TPU v7x, 32 devices: a whole 2x2x4 slice. The times are simulated.
32 devices in a mesh: dp: 8 (over y, x, core), tensor: 4 (over z).
Axes of the slice: x: 2, y: 2, z: 4, core: 2. Of those that a mesh axis runs over, the one named last changes fastest.
Arguments:
- tokens: bfloat16 [16384, 3072], P(('dp', 'tensor')), may hold values from -6 to 6
- cotangent: bfloat16 [16384, 3072], P(('dp', 'tensor')), may hold values from -6 to 6
- segments: int32 [16384], P(('dp', 'tensor')), may hold values from 0 to 2, as said below
- positions: int32 [16384], P(('dp', 'tensor')), may hold values from 0 to 2046, as said below
- counts: int32 [8], P('dp'), may hold values from 1536 to 2048, as said below
- query_weight: bfloat16 [3072, 3072], P('dp', 'tensor'), may hold values from -0.109375 to 0.109375
- key_projection_weight: bfloat16 [3072, 1024], P('dp', 'tensor'), may hold values from -0.109375 to 0.109375
- value_projection_weight: bfloat16 [3072, 1024], P('dp', 'tensor'), may hold values from -0.109375 to 0.109375
- out_weight: bfloat16 [3072, 3072], P('tensor', 'dp'), may hold values from -2.5 to 2.5
- attn_gain: bfloat16 [3072], P('dp'), may hold values from 0.099609375 to 1.8984375
- gate_weight: bfloat16 [3072, 8192], P('dp', 'tensor'), may hold values from -0.109375 to 0.109375
- up_weight: bfloat16 [3072, 8192], P('dp', 'tensor'), may hold values from -0.109375 to 0.109375
- down_weight: bfloat16 [8192, 3072], P('tensor', 'dp'), may hold values from -0.0625 to 0.0625
- mlp_gain: bfloat16 [3072], P('dp'), may hold values from 0.099609375 to 1.8984375
Outputs:
- output: bfloat16 [16384, 3072], P(('dp', 'tensor'))
- grad_tokens: float32 [16384, 3072], P(('dp', 'tensor'))
- grad_query_weight: float32 [3072, 3072], P('dp', 'tensor')
- grad_key_weight: float32 [3072, 1024], P('dp', 'tensor')
- grad_value_weight: float32 [3072, 1024], P('dp', 'tensor')
- grad_out_weight: float32 [3072, 3072], P('tensor', 'dp')
- grad_attn_gain: float32 [3072], P('dp')
- grad_gate_weight: float32 [3072, 8192], P('dp', 'tensor')
- grad_up_weight: float32 [3072, 8192], P('dp', 'tensor')
- grad_down_weight: float32 [8192, 3072], P('tensor', 'dp')
- grad_mlp_gain: float32 [3072], P('dp')
Inputs may be any that keep to these rules, and one draw needn't show every extreme that they name: `segments`: within each group of 2048 rows, segment numbers start at 0 and never fall; rows past the group's live count continue its last segment. positions start at 0 at the beginning of each segment and rise by one a row. `counts`: some group is full.
All inputs are finite; a program needn't handle non-finite values.
Results may differ from a plain program's by a relative error of at most 0.013.
Values may be sent and summed in bfloat16 or wider, within the bound.
A program may use at most 384 MiB of HBM per device.

v0:
```python
import jax
import jax.numpy as jnp
from jax import lax
from jax.sharding import PartitionSpec as P

HEAD_SIZE = 128


EPSILON = 1e-05
ROPE_BASE = 500000.0
MASKED = -1e30


def rope_tables(place):
    half_size = HEAD_SIZE // 2
    freqs = ROPE_BASE ** (-(jnp.arange(half_size, dtype=jnp.float32) * 2.0) / HEAD_SIZE)
    angles = place.astype(jnp.float32)[:, None] * freqs[None, :]
    return (jnp.cos(angles)[:, None, :], jnp.sin(angles)[:, None, :])


def apply_rotary(vector, cosine_table, sine_table):
    half_size = vector.shape[-1] // 2
    first = vector[..., :half_size]
    second = vector[..., half_size:]
    return jnp.concatenate(
        [first * cosine_table - second * sine_table, second * cosine_table + first * sine_table],
        axis=-1,
    )


def norm_inverse(source):
    return lax.rsqrt(jnp.mean(source * source, axis=-1, keepdims=True) + EPSILON)


def norm_back(grad_normed, source, inverse, gain):
    unit_rows = source * inverse
    gain_term = jnp.sum(grad_normed * unit_rows, axis=0)
    scaled = grad_normed * gain
    grad_source = inverse * (
        scaled - unit_rows * jnp.mean(scaled * unit_rows, axis=-1, keepdims=True)
    )
    return (grad_source, gain_term)


def shards(
    tokens,
    cotangent,
    segments,
    positions,
    counts,
    query_weight,
    key_projection_weight,
    value_projection_weight,
    out_weight,
    attn_gain,
    gate_weight,
    up_weight,
    down_weight,
    mlp_gain,
):
    f32 = jnp.float32
    bf16 = jnp.bfloat16
    row_count = tokens.shape[0]
    every_row_count = row_count * lax.axis_size("tensor")
    heads_q = query_weight.shape[1] // HEAD_SIZE
    heads_kv = key_projection_weight.shape[1] // HEAD_SIZE
    head_groups = heads_q // heads_kv
    score_scale = HEAD_SIZE ** (-0.5)
    live_count = counts[0]
    own_index = lax.axis_index("tensor") * row_count + jnp.arange(row_count, dtype=jnp.int32)
    live_mask = (own_index < live_count).astype(f32)[:, None]
    query_full, key_full, value_full, out_full, gain_one = (
        lax.all_gather(query_weight, "dp", axis=0, tiled=True),
        lax.all_gather(key_projection_weight, "dp", axis=0, tiled=True),
        lax.all_gather(value_projection_weight, "dp", axis=0, tiled=True),
        lax.all_gather(out_weight, "dp", axis=1, tiled=True),
        lax.all_gather(attn_gain, "dp", axis=0, tiled=True),
    )
    gate_full, up_full, down_full, gain_two = (
        lax.all_gather(gate_weight, "dp", axis=0, tiled=True),
        lax.all_gather(up_weight, "dp", axis=0, tiled=True),
        lax.all_gather(down_weight, "dp", axis=1, tiled=True),
        lax.all_gather(mlp_gain, "dp", axis=0, tiled=True),
    )
    source = tokens.astype(f32)
    inv_one = norm_inverse(source)
    first_normalized = (source * inv_one * gain_one.astype(f32)).astype(bf16)
    gathered_one, seg_all, place_all = (
        lax.all_gather(first_normalized, "tensor", axis=0, tiled=True),
        lax.all_gather(segments, "tensor", axis=0, tiled=True),
        lax.all_gather(positions, "tensor", axis=0, tiled=True),
    )
    cosine_table, sine_table = rope_tables(place_all)
    query_rows = apply_rotary(
        jnp.dot(gathered_one, query_full, preferred_element_type=f32).reshape(
            every_row_count, heads_q, HEAD_SIZE
        ),
        cosine_table,
        sine_table,
    ).astype(bf16)
    key_rows = apply_rotary(
        jnp.dot(gathered_one, key_full, preferred_element_type=f32).reshape(
            every_row_count, heads_kv, HEAD_SIZE
        ),
        cosine_table,
        sine_table,
    ).astype(bf16)
    value_rows = (
        jnp.dot(gathered_one, value_full, preferred_element_type=f32)
        .astype(bf16)
        .reshape(every_row_count, heads_kv, HEAD_SIZE)
    )
    index_all = jnp.arange(every_row_count, dtype=jnp.int32)
    live_all = index_all < live_count
    rows_per_block = 512
    block_count = every_row_count // rows_per_block
    starts = jnp.arange(block_count, dtype=jnp.int32) * rows_per_block

    def block_scores(begin_row):
        query_blk = lax.dynamic_slice_in_dim(query_rows, begin_row, rows_per_block, 0).reshape(
            rows_per_block, heads_kv, head_groups, HEAD_SIZE
        )
        seg_blk = lax.dynamic_slice_in_dim(seg_all, begin_row, rows_per_block, 0)
        place_blk = lax.dynamic_slice_in_dim(place_all, begin_row, rows_per_block, 0)
        index_blk = lax.dynamic_slice_in_dim(index_all, begin_row, rows_per_block, 0)
        scores = (
            jnp.einsum("bkgd,nkd->kgbn", query_blk, key_rows, preferred_element_type=f32)
            * score_scale
        )
        allowed = (seg_blk[:, None] == seg_all[None, :]) & (
            place_all[None, :] <= place_blk[:, None]
        )
        allowed = allowed & (live_all[None, :] | (index_all[None, :] == index_blk[:, None]))
        return (query_blk, jnp.where(allowed[None, None], scores, MASKED))

    def forward_block(begin_row):
        query_blk, scores = block_scores(begin_row)
        row_peak = jnp.max(scores, axis=-1, keepdims=True)
        exp_scores = jnp.exp(scores - row_peak)
        row_totals = jnp.sum(exp_scores, axis=-1, keepdims=True)
        probs = (exp_scores / row_totals).astype(bf16)
        block_out = jnp.einsum("kgbn,nkd->bkgd", probs, value_rows, preferred_element_type=f32)
        return (
            block_out.reshape(rows_per_block, heads_q * HEAD_SIZE),
            (row_peak + jnp.log(row_totals))[..., 0],
        )

    block_outs, log_totals = lax.map(forward_block, starts)
    attended = block_outs.reshape(every_row_count, heads_q * HEAD_SIZE).astype(bf16)
    piece = attended
    hidden = source + lax.psum_scatter(
        jnp.dot(piece, out_full, preferred_element_type=f32),
        "tensor",
        scatter_dimension=0,
        tiled=True,
    )
    inv_two = norm_inverse(hidden)
    normed_two = (hidden * inv_two * gain_two.astype(f32)).astype(bf16)
    gathered_two = lax.all_gather(normed_two, "tensor", axis=0, tiled=True)
    gate_proj = jnp.dot(gathered_two, gate_full, preferred_element_type=f32)
    up_proj = jnp.dot(gathered_two, up_full, preferred_element_type=f32)
    sigmoid_gate = jax.nn.sigmoid(gate_proj)
    activated = gate_proj * sigmoid_gate
    mixed_act = (activated * up_proj).astype(bf16)
    piece = mixed_act
    result = hidden + lax.psum_scatter(
        jnp.dot(piece, down_full, preferred_element_type=f32),
        "tensor",
        scatter_dimension=0,
        tiled=True,
    )
    output = (result * live_mask).astype(bf16)
    query_back, key_back, value_back, out_back, gain_one_back = (
        lax.all_gather(query_weight, "dp", axis=0, tiled=True),
        lax.all_gather(key_projection_weight, "dp", axis=0, tiled=True),
        lax.all_gather(value_projection_weight, "dp", axis=0, tiled=True),
        lax.all_gather(out_weight, "dp", axis=1, tiled=True),
        lax.all_gather(attn_gain, "dp", axis=0, tiled=True),
    )
    gate_back, up_back, down_back, gain_two_back = (
        lax.all_gather(gate_weight, "dp", axis=0, tiled=True),
        lax.all_gather(up_weight, "dp", axis=0, tiled=True),
        lax.all_gather(down_weight, "dp", axis=1, tiled=True),
        lax.all_gather(mlp_gain, "dp", axis=0, tiled=True),
    )
    grad_result = cotangent.astype(f32) * live_mask
    grad_rows_two = lax.all_gather(grad_result.astype(bf16), "tensor", axis=0, tiled=True)
    grad_down = jnp.einsum("rf,rd->fd", mixed_act, grad_rows_two, preferred_element_type=f32)
    grad_mixed = jnp.einsum("rd,fd->rf", grad_rows_two, down_back, preferred_element_type=f32)
    grad_gate = (
        grad_mixed * up_proj * sigmoid_gate * (1.0 + gate_proj * (1.0 - sigmoid_gate))
    ).astype(bf16)
    grad_up = (grad_mixed * activated).astype(bf16)
    grad_gate_w = jnp.einsum("rd,rf->df", gathered_two, grad_gate, preferred_element_type=f32)
    grad_up_w = jnp.einsum("rd,rf->df", gathered_two, grad_up, preferred_element_type=f32)
    grad_normed_two = lax.psum_scatter(
        jnp.einsum("rf,df->rd", grad_gate, gate_back, preferred_element_type=f32)
        + jnp.einsum("rf,df->rd", grad_up, up_back, preferred_element_type=f32),
        "tensor",
        scatter_dimension=0,
        tiled=True,
    )
    grad_hidden_norm, gain_two_term = norm_back(
        grad_normed_two, hidden, inv_two, gain_two_back.astype(f32)
    )
    grad_hidden = grad_result + grad_hidden_norm
    grad_rows_one = lax.all_gather(grad_hidden.astype(bf16), "tensor", axis=0, tiled=True)
    grad_out_w = jnp.einsum("ra,rd->ad", attended, grad_rows_one, preferred_element_type=f32)
    grad_attended = jnp.einsum(
        "rd,ad->ra", grad_rows_one, out_back, preferred_element_type=f32
    ).astype(bf16)
    grad_attended = grad_attended.reshape(every_row_count, heads_kv, head_groups, HEAD_SIZE)

    def backward_block(carry, items):
        grad_keys, grad_values = carry
        begin_row, lse_blk = items
        query_blk, scores = block_scores(begin_row)
        probs = jnp.exp(scores - lse_blk[..., None])
        grad_blk = lax.dynamic_slice_in_dim(grad_attended, begin_row, rows_per_block, 0)
        grad_probs = jnp.einsum("bkgd,nkd->kgbn", grad_blk, value_rows, preferred_element_type=f32)
        delta = jnp.sum(probs * grad_probs, axis=-1, keepdims=True)
        grad_scores = (probs * (grad_probs - delta)).astype(bf16)
        grad_query_blk = (
            jnp.einsum("kgbn,nkd->bkgd", grad_scores, key_rows, preferred_element_type=f32)
            * score_scale
        )
        grad_keys = (
            grad_keys
            + jnp.einsum("kgbn,bkgd->nkd", grad_scores, query_blk, preferred_element_type=f32)
            * score_scale
        )
        grad_values = grad_values + jnp.einsum(
            "kgbn,bkgd->nkd", probs.astype(bf16), grad_blk, preferred_element_type=f32
        )
        return ((grad_keys, grad_values), grad_query_blk)

    zero_kv = jnp.zeros((every_row_count, heads_kv, HEAD_SIZE), f32)
    (grad_keys, grad_values), grad_queries = lax.scan(
        backward_block, (zero_kv, zero_kv), (starts, log_totals)
    )
    grad_queries = grad_queries.reshape(every_row_count, heads_q, HEAD_SIZE)
    grad_q_low = (
        apply_rotary(grad_queries, cosine_table, -sine_table)
        .astype(bf16)
        .reshape(every_row_count, heads_q * HEAD_SIZE)
    )
    grad_k_low = (
        apply_rotary(grad_keys, cosine_table, -sine_table)
        .astype(bf16)
        .reshape(every_row_count, heads_kv * HEAD_SIZE)
    )
    grad_v_low = grad_values.astype(bf16).reshape(every_row_count, heads_kv * HEAD_SIZE)
    grad_query_w = jnp.einsum("rd,rh->dh", gathered_one, grad_q_low, preferred_element_type=f32)
    grad_key_w = jnp.einsum("rd,rh->dh", gathered_one, grad_k_low, preferred_element_type=f32)
    grad_value_w = jnp.einsum("rd,rh->dh", gathered_one, grad_v_low, preferred_element_type=f32)
    grad_normed_one = lax.psum_scatter(
        jnp.einsum("rh,dh->rd", grad_q_low, query_back, preferred_element_type=f32)
        + jnp.einsum("rh,dh->rd", grad_k_low, key_back, preferred_element_type=f32)
        + jnp.einsum("rh,dh->rd", grad_v_low, value_back, preferred_element_type=f32),
        "tensor",
        scatter_dimension=0,
        tiled=True,
    )
    grad_input_norm, gain_one_term = norm_back(
        grad_normed_one, source, inv_one, gain_one_back.astype(f32)
    )
    grad_tokens = grad_hidden + grad_input_norm
    gain_one_sum, gain_two_sum = lax.psum((gain_one_term, gain_two_term), "tensor")
    grad_parts = (
        lax.psum_scatter(grad_query_w, "dp", scatter_dimension=0, tiled=True),
        lax.psum_scatter(grad_key_w, "dp", scatter_dimension=0, tiled=True),
        lax.psum_scatter(grad_value_w, "dp", scatter_dimension=0, tiled=True),
        lax.psum_scatter(grad_out_w, "dp", scatter_dimension=1, tiled=True),
        lax.psum_scatter(gain_one_sum, "dp", scatter_dimension=0, tiled=True),
        lax.psum_scatter(grad_gate_w, "dp", scatter_dimension=0, tiled=True),
        lax.psum_scatter(grad_up_w, "dp", scatter_dimension=0, tiled=True),
        lax.psum_scatter(grad_down, "dp", scatter_dimension=1, tiled=True),
        lax.psum_scatter(gain_two_sum, "dp", scatter_dimension=0, tiled=True),
    )
    return (
        output,
        grad_tokens,
        grad_parts[0],
        grad_parts[1],
        grad_parts[2],
        grad_parts[3],
        grad_parts[4],
        grad_parts[5],
        grad_parts[6],
        grad_parts[7],
        grad_parts[8],
    )


def solution(mesh):
    in_specs = (
        P(("dp", "tensor"), None),
        P(("dp", "tensor"), None),
        P(("dp", "tensor")),
        P(("dp", "tensor")),
        P("dp"),
        P("dp", "tensor"),
        P("dp", "tensor"),
        P("dp", "tensor"),
        P("tensor", "dp"),
        P("dp"),
        P("dp", "tensor"),
        P("dp", "tensor"),
        P("tensor", "dp"),
        P("dp"),
    )
    out_specs = (
        P(("dp", "tensor"), None),
        P(("dp", "tensor"), None),
        P("dp", "tensor"),
        P("dp", "tensor"),
        P("dp", "tensor"),
        P("tensor", "dp"),
        P("dp"),
        P("dp", "tensor"),
        P("dp", "tensor"),
        P("tensor", "dp"),
        P("dp"),
    )
    return jax.shard_map(shards, mesh=mesh, in_specs=in_specs, out_specs=out_specs, check_vma=False)
```

profile of v0, /device:TPU:0, one launch (start us, length us, event | category | flops | bytes accessed | tf_op | source)
XLA Modules:
  0.0 4350.3 jit_solution(16986061215583990875)
XLA Ops:
  29.1 12.1 all-gather
  41.2 12.2 all-gather.1
  56.8 201.9 %all-gather.16.cloned.1.call-done = bf16[2048,3072]{1,0:T(8,128)(2,1)} async-done(((bf16[512,3072]{1,0:T(8,128)(2,1)}), bf16[2048,3072]{1,0:T(8,128)(2,1)}) %all-gather.16.cloned.1.call-update) | async-done | bytes 12582928 | tf_op jit(solution)/shard_map/all_gather | solution.py:89
  268.7 29.0 all-gather.18.cloned.1.call-done
  297.7 14.8 fusion.57
  327.2 15.8 subtract_convert_fusion.1
  356.5 173.1 %while.30 = (s32[]{:T(128)}, bf16[4,512,768]{2,1,0:T(8,128)(2,1)}, f32[4,2,3,512]{3,2,1,0:T(4,128)}, s32[4]{0:T(128)S(1)}, s32[2048]{0:T(1024)S(1)}, /*index=5*/...) while((s32[]{:T(128)}, bf16[4,512,768]{2,1,0:T(8,128)(2,1)}, ...), condition=%wide.region_4.5_spmd.clone.clone, body=%wide.region_1.4_spmd.clone.clone.sunk | while | flops 3303013376 | bytes 92424424 | solution.py:148
  374.1 12.1 fusion.139
  386.2 11.7 fusion.140
  406.7 10.7 bitcast_reduce_fusion.2
  417.4 12.1 fusion.139
  429.5 11.7 fusion.140
  460.7 12.1 fusion.139
  472.8 11.7 fusion.140
  493.3 10.7 bitcast_reduce_fusion.2
  504.0 12.1 fusion.139
  516.1 11.7 fusion.140
  529.7 17.8 fusion.59
  557.4 404.7 %reduce-scatter.12.cloned.1.call-done = f32[512,3072]{1,0:T(8,128)} async-done(((f32[2048,3072]{1,0:T(8,128)}), f32[512,3072]{1,0:T(8,128)}) %reduce-scatter.12.cloned.1.call-update) | async-done | bytes 6291472 | tf_op jit(solution)/shard_map/reduce_scatter | solution.py:151
  976.7 61.4 %all-gather.30.cloned.1.call-done = bf16[3072,2048]{1,0:T(8,128)(2,1)} async-done(((bf16[384,2048]{1,0:T(8,128)(2,1)}), bf16[3072,2048]{1,0:T(8,128)(2,1)}) %all-gather.30.cloned.1.call-update) | async-done | bytes 12582928 | tf_op jit(solution)/shard_map/all_gather | solution.py:81
  1038.1 220.5 %all-gather.26.cloned.1.call-done = bf16[2048,3072]{1,0:T(8,128)(2,1)} async-done(((bf16[512,3072]{1,0:T(8,128)(2,1)}), bf16[2048,3072]{1,0:T(8,128)(2,1)}) %all-gather.26.cloned.1.call-update) | async-done | bytes 12582928 | tf_op jit(solution)/shard_map/all_gather | solution.py:159
  1258.6 34.9 fusion.61
  1293.4 37.5 all-gather.28.cloned.1.call-done
  1331.0 34.5 fusion.60
  1365.4 185.9 %all-gather.34.cloned.1.call-done = bf16[2048,3072]{1,0:T(8,128)(2,1)} async-done(((bf16[512,3072]{1,0:T(8,128)(2,1)}), bf16[2048,3072]{1,0:T(8,128)(2,1)}) %all-gather.34.cloned.1.call-update) | async-done | bytes 12582928 | tf_op jit(solution)/shard_map/all_gather | solution.py:187
  1551.3 74.8 %all-gather.32.cloned.1.call-done = bf16[2048,3072]{1,0:T(8,128)(2,1)} async-done(((bf16[2048,384]{1,0:T(8,128)(2,1)}), bf16[2048,3072]{1,0:T(8,128)(2,1)}) %all-gather.32.cloned.1.call-update) | async-done | bytes 12582928 | tf_op jit(solution)/shard_map/all_gather | solution.py:82
  1626.1 46.8 %multiply_convert_fusion = (bf16[2048,2048]{1,0:T(8,128)(2,1)}, bf16[2048,2048]{1,0:T(8,128)(2,1)}, bf16[2048,2048]{1,0:T(8,128)(2,1)}) fusion(f32[2048,2048]{1,0:T(8,128)} %fusion.60, f32[2048,2048]{1,0:T(8,128)} %fusion.61, bf16[2048,3072]{1,0:T(8,128)(2,1)} %all-gather.34.cloned.1.call-done, bf16[2048,3072]{1,0:T(8,128)(2,1)} %all-gather.32.cloned.1.call-done), kind=kOutput, calls=%fused_computation.52 | convolution fusion | flops 25832718336 | bytes 83886080 | tf_op jit(solution)/shard_map/rd,fd->rf/dot_general | solution.py:189
  1672.9 34.3 fusion.63
  1707.3 36.4 convolution_add_fusion
  1743.7 34.6 fusion.62
  1778.4 379.8 %reduce-scatter.16.cloned.1.call-done = f32[512,3072]{1,0:T(8,128)} async-done(((f32[2048,3072]{1,0:T(8,128)}), f32[512,3072]{1,0:T(8,128)}) %reduce-scatter.16.cloned.1.call-update) | async-done | bytes 6291472 | tf_op jit(solution)/shard_map/reduce_scatter | solution.py:196
  2164.4 412.4 %reduce-scatter.14.cloned.1.call-done = f32[512,3072]{1,0:T(8,128)} async-done(((f32[2048,3072]{1,0:T(8,128)}), f32[512,3072]{1,0:T(8,128)}) %reduce-scatter.14.cloned.1.call-update) | async-done | bytes 6291472 | tf_op jit(solution)/shard_map/reduce_scatter | solution.py:166
  2576.8 10.8 fusion.55
  2592.4 215.4 %all-gather.36.cloned.1.call-done = bf16[2048,3072]{1,0:T(8,128)(2,1)} async-done(((bf16[512,3072]{1,0:T(8,128)(2,1)}), bf16[2048,3072]{1,0:T(8,128)(2,1)}) %all-gather.36.cloned.1.call-update) | async-done | bytes 12582928 | tf_op jit(solution)/shard_map/all_gather | solution.py:207
  2807.8 15.4 convolution_convert_fusion
  2823.3 296.4 %while.31 = (s32[]{:T(128)}, f32[2048,2,128]{0,2,1:T(8,128)}, f32[2048,2,128]{0,2,1:T(8,128)}, f32[4,512,2,3,128]{4,1,0,3,2:T(8,128)}, s32[4]{0:T(128)S(1)}, /*i...) while((s32[]{:T(128)}, f32[2048,2,128]{0,2,1:T(8,128)}, ...), condition=%wide.region_12.13_spmd.clone.clone, body=%wide.region_10.12_spmd.clone.clone.sunk | while | flops 8156740608 | bytes 227674416 | solution.py:238
  2841.2 13.2 fusion.153
  2854.4 18.5 fusion.150
  2873.0 17.2 fusion.151
  2914.8 13.7 fusion.153
  2928.5 18.5 fusion.150
  2947.0 17.2 fusion.151
  2988.9 13.7 fusion.153
  3002.6 18.5 fusion.150
  3021.1 17.2 fusion.151
  3063.0 13.6 fusion.153
  3076.6 18.5 fusion.150
  3095.1 17.2 fusion.151
  3157.1 26.9 add_add_fusion
  3184.1 35.0 fusion.72
  3219.2 34.0 fusion.71
  3253.3 34.4 fusion.70
  3309.7 16.1 fusion.69
  3327.7 15.3 fusion.66
  3344.9 251.9 %reduce-scatter.18.cloned.1.call-done = f32[512,3072]{1,0:T(8,128)} async-done(((f32[2048,3072]{1,0:T(8,128)}), f32[512,3072]{1,0:T(8,128)}) %reduce-scatter.18.cloned.1.call-update) | async-done | bytes 6291472 | tf_op jit(solution)/shard_map/reduce_scatter | solution.py:256
  3600.7 24.0 all-reduce.2
  3624.9 13.1 all-reduce.3
  3645.4 114.1 %reduce-scatter.32.cloned.1.call-done = f32[2048,384]{1,0:T(8,128)} async-done(((f32[2048,3072]{1,0:T(8,128)}), f32[2048,384]{1,0:T(8,128)}) %reduce-scatter.32.cloned.1.call-update) | async-done | bytes 3145744 | tf_op jit(solution)/shard_map/reduce_scatter | solution.py:277
  3759.6 160.9 %reduce-scatter.30.cloned.1.call-done = f32[384,2048]{1,0:T(8,128)} async-done(((f32[3072,2048]{1,0:T(8,128)}), f32[384,2048]{1,0:T(8,128)}) %reduce-scatter.30.cloned.1.call-update) | async-done | bytes 3145744 | tf_op jit(solution)/shard_map/reduce_scatter | solution.py:276
  3920.5 161.0 %reduce-scatter.28.cloned.1.call-done = f32[384,2048]{1,0:T(8,128)} async-done(((f32[3072,2048]{1,0:T(8,128)}), f32[384,2048]{1,0:T(8,128)}) %reduce-scatter.28.cloned.1.call-update) | async-done | bytes 3145744 | tf_op jit(solution)/shard_map/reduce_scatter | solution.py:275
  4081.5 50.2 %reduce-scatter.24.cloned.1.call-done = f32[384,256]{1,0:T(8,128)} async-done(((f32[3072,256]{1,0:T(8,128)}), f32[384,256]{1,0:T(8,128)}) %reduce-scatter.24.cloned.1.call-update) | async-done | bytes 393232 | tf_op jit(solution)/shard_map/reduce_scatter | solution.py:272
  4131.7 50.5 %reduce-scatter.22.cloned.1.call-done = f32[384,256]{1,0:T(8,128)} async-done(((f32[3072,256]{1,0:T(8,128)}), f32[384,256]{1,0:T(8,128)}) %reduce-scatter.22.cloned.1.call-update) | async-done | bytes 393232 | tf_op jit(solution)/shard_map/reduce_scatter | solution.py:271
  4182.1 80.6 %reduce-scatter.26.cloned.1.call-done = f32[768,384]{1,0:T(8,128)} async-done(((f32[768,3072]{1,0:T(8,128)}), f32[768,384]{1,0:T(8,128)}) %reduce-scatter.26.cloned.1.call-update) | async-done | bytes 1179664 | tf_op jit(solution)/shard_map/reduce_scatter | solution.py:273
  4262.7 80.6 %reduce-scatter.20.cloned.1.call-done = f32[384,768]{1,0:T(8,128)} async-done(((f32[3072,768]{1,0:T(8,128)}), f32[384,768]{1,0:T(8,128)}) %reduce-scatter.20.cloned.1.call-update) | async-done | bytes 1179664 | tf_op jit(solution)/shard_map/reduce_scatter | solution.py:270
  (295 shorter events, 311.2 us)
Async XLA Ops:
  7.2 49.7 %all-gather.20.cloned.1.call-start = ((), (), s32[]{:S(2)}) async-start(), calls=%async_computation.13 | async-start | bytes 1769472 | tf_op jit(solution)/shard_map/all_gather | solution.py:74
  7.9 250.8 %all-gather.16.cloned.1.call-start = ((), (), s32[]{:S(2)}) async-start(), calls=%async_computation.11 | async-start | bytes 15728640 | tf_op jit(solution)/shard_map/all_gather | solution.py:89
  19.0 10.0 copy-start.38
  19.0 22.1 copy-start.39
  27.1 270.7 %all-gather.18.cloned.1.call-start = ((), (), s32[]{:S(2)}) async-start(), calls=%async_computation.12 | async-start | bytes 5308416 | tf_op jit(solution)/shard_map/all_gather | solution.py:73
  27.8 318.6 %all-gather.22.cloned.1.call-start = ((), (), s32[]{:S(2)}) async-start(), calls=%async_computation.14 | async-start | bytes 1769472 | tf_op jit(solution)/shard_map/all_gather | solution.py:75
  28.4 501.3 %all-gather.24.cloned.1.call-start = ((), (), s32[]{:S(2)}) async-start(), calls=%async_computation.15 | async-start | bytes 5308416 | tf_op jit(solution)/shard_map/all_gather | solution.py:76
  29.0 933.1 %reduce-scatter.12.cloned.1.call-start = ((), (), s32[]{:S(2)}) async-start(), calls=%async_computation.16 | async-start | bytes 31457280 | tf_op jit(solution)/shard_map/reduce_scatter | solution.py:151
  56.1 209.5 %copy-start.11 = (f32[2048,64]{0,1:T(8,128)}, f32[2048,64]{0,1:T(8,128)S(1)}, u32[]{:S(2)}) copy-start(f32[2048,64]{0,1:T(8,128)S(1)} %get-tuple-element.467) | copy-start | bytes 1572868
  56.5 270.7 %copy-start.10 = (f32[2048,64]{1,0:T(8,128)}, f32[2048,64]{1,0:T(8,128)S(1)}, u32[]{:S(2)}) copy-start(f32[2048,64]{1,0:T(8,128)S(1)} %copy.67) | copy-start | bytes 1572868
  374.1 12.1 copy-start.26
  417.4 12.1 copy-start.26
  460.7 12.1 copy-start.26
  504.0 12.1 copy-start.26
  529.7 17.9 copy-start.3
  529.7 17.9 copy-start.20
  529.7 17.9 copy-start.24
  529.7 17.9 copy-start.42
  547.5 414.6 %copy-start.6 = (bf16[512,3072]{1,0:T(8,128)(2,1)S(1)}, bf16[512,3072]{1,0:T(8,128)(2,1)}, u32[]{:S(2)}) copy-start(bf16[512,3072]{1,0:T(8,128)(2,1)} %param.18) | copy-start | bytes 9437188
  547.6 490.5 %all-gather.30.cloned.1.call-start = ((), (), s32[]{:S(2)}) async-start(), calls=%async_computation.19 | async-start | bytes 14155776 | tf_op jit(solution)/shard_map/all_gather | solution.py:81
  548.3 710.2 %all-gather.26.cloned.1.call-start = ((), (), s32[]{:S(2)}) async-start(), calls=%async_computation.17 | async-start | bytes 15728640 | tf_op jit(solution)/shard_map/all_gather | solution.py:159
  557.4 408.4 %copy-start.29 = (f32[8,1,384]{2,1,0:T(1,128)}, f32[8,1,384]{2,1,0:T(1,128)S(1)}, u32[]{:S(2)}) copy-start(f32[8,1,384]{2,1,0:T(1,128)S(1)} %convert_element_type.109) | copy-start | bytes 36868
  968.5 4.7 copy-start.8
  971.2 359.8 %all-gather.28.cloned.1.call-start = ((), (), s32[]{:S(2)}) async-start(), calls=%async_computation.18 | async-start | bytes 14155776 | tf_op jit(solution)/shard_map/all_gather | solution.py:80
  971.9 579.4 %all-gather.34.cloned.1.call-start = ((), (), s32[]{:S(2)}) async-start(), calls=%async_computation.22 | async-start | bytes 15728640 | tf_op jit(solution)/shard_map/all_gather | solution.py:187
  975.9 650.2 %all-gather.32.cloned.1.call-start = ((), (), s32[]{:S(2)}) async-start(), calls=%async_computation.20 | async-start | bytes 14155776 | tf_op jit(solution)/shard_map/all_gather | solution.py:82
  976.6 1181.6 %reduce-scatter.16.cloned.1.call-start = ((), (), s32[]{:S(2)}) async-start(), calls=%async_computation.23 | async-start | bytes 31457280 | tf_op jit(solution)/shard_map/reduce_scatter | solution.py:196
  1743.7 833.1 %reduce-scatter.14.cloned.1.call-start = ((), (), s32[]{:S(2)}) async-start(), calls=%async_computation.21 | async-start | bytes 31457280 | tf_op jit(solution)/shard_map/reduce_scatter | solution.py:166
  1778.3 379.9 %copy-start.30 = (f32[8,1,384]{2,1,0:T(1,128)S(1)}, f32[8,1,384]{2,1,0:T(1,128)}, u32[]{:S(2)}) copy-start(f32[8,1,384]{2,1,0:T(1,128)} %copy-done.29) | copy-start | bytes 36868
  1778.3 379.9 %copy-start.35 = (f32[512]{0:T(512)S(1)}, f32[512]{0:T(512)}, u32[]{:S(2)}) copy-start(f32[512]{0:T(512)} %copy-done.34) | copy-start | bytes 6148
  1778.4 798.4 %copy-start.9 = (bf16[512,3072]{1,0:T(8,128)(2,1)S(1)}, bf16[512,3072]{1,0:T(8,128)(2,1)}, u32[]{:S(2)}) copy-start(bf16[512,3072]{1,0:T(8,128)(2,1)} %param.19) | copy-start | bytes 9437188
  1778.4 798.4 %copy-start.37 = (f32[512]{0:T(512)S(1)}, f32[512]{0:T(512)}, u32[]{:S(2)}) copy-start(f32[512]{0:T(512)} %copy-done.36) | copy-start | bytes 6148
  1778.4 1029.4 %all-gather.36.cloned.1.call-start = ((), (), s32[]{:S(2)}) async-start(), calls=%async_computation.24 | async-start | bytes 15728640 | tf_op jit(solution)/shard_map/all_gather | solution.py:207
  2587.6 1009.1 %reduce-scatter.18.cloned.1.call-start = ((), (), s32[]{:S(2)}) async-start(), calls=%async_computation.25 | async-start | bytes 31457280 | tf_op jit(solution)/shard_map/reduce_scatter | solution.py:256
  2592.4 230.9 %copy-start.4 = (bf16[2048,2,128]{2,0,1:T(8,128)(2,1)S(1)}, bf16[2048,2,128]{2,0,1:T(8,128)(2,1)}, u32[]{:S(2)}) copy-start(bf16[2048,2,128]{2,0,1:T(8,128)(2,1)} %copy-done.3) | copy-start | bytes 3145732
  2592.4 230.9 %copy-start.21 = (s32[2048]{0:T(1024)S(1)}, s32[2048]{0:T(1024)}, u32[]{:S(2)}) copy-start(s32[2048]{0:T(1024)} %copy-done.20) | copy-start | bytes 24580
  2592.4 230.9 %copy-start.25 = (s32[2048]{0:T(1024)S(1)}, s32[2048]{0:T(1024)}, u32[]{:S(2)}) copy-start(s32[2048]{0:T(1024)} %copy-done.24) | copy-start | bytes 24580
  2592.4 230.9 %copy-start.43 = (s32[4]{0:T(128)S(1)}, s32[4]{0:T(128)}, u32[]{:S(2)}) copy-start(s32[4]{0:T(128)} %copy-done.42) | copy-start | bytes 52
  2872.9 17.2 copy-start
  2947.0 17.2 copy-start
  2966.6 4.6 copy-start.1
  3021.1 17.2 copy-start
  3040.7 4.6 copy-start.1
  3095.1 17.2 copy-start
  3114.7 4.6 copy-start.1
  3126.0 8.2 copy-start.2
  3126.0 8.2 copy-start.12
  3126.0 8.2 copy-start.17
  3136.4 10.5 copy-start.13
  3136.5 10.3 copy-start.15
  3136.6 10.3 copy-start.23
  3146.9 10.2 copy-start.18
  3184.1 575.5 %reduce-scatter.32.cloned.1.call-start = ((), (), s32[]{:S(2)}) async-start(), calls=%async_computation.32 | async-start | bytes 28311552 | tf_op jit(solution)/shard_map/reduce_scatter | solution.py:277
  3219.2 701.4 %reduce-scatter.30.cloned.1.call-start = ((), (), s32[]{:S(2)}) async-start(), calls=%async_computation.31 | async-start | bytes 28311552 | tf_op jit(solution)/shard_map/reduce_scatter | solution.py:276
  3253.3 828.2 %reduce-scatter.28.cloned.1.call-start = ((), (), s32[]{:S(2)}) async-start(), calls=%async_computation.30 | async-start | bytes 28311552 | tf_op jit(solution)/shard_map/reduce_scatter | solution.py:275
  3287.8 11.8 copy-start.16
  3287.8 843.9 %reduce-scatter.24.cloned.1.call-start = ((), (), s32[]{:S(2)}) async-start(), calls=%async_computation.28 | async-start | bytes 3538944 | tf_op jit(solution)/shard_map/reduce_scatter | solution.py:272
  3299.1 883.0 %reduce-scatter.22.cloned.1.call-start = ((), (), s32[]{:S(2)}) async-start(), calls=%async_computation.27 | async-start | bytes 3538944 | tf_op jit(solution)/shard_map/reduce_scatter | solution.py:271
  3309.7 953.1 %reduce-scatter.26.cloned.1.call-start = ((), (), s32[]{:S(2)}) async-start(), calls=%async_computation.29 | async-start | bytes 10616832 | tf_op jit(solution)/shard_map/reduce_scatter | solution.py:273
  3325.8 1017.5 %reduce-scatter.20.cloned.1.call-start = ((), (), s32[]{:S(2)}) async-start(), calls=%async_computation.26 | async-start | bytes 10616832 | tf_op jit(solution)/shard_map/reduce_scatter | solution.py:270
  3343.0 253.8 %copy-start.7 = (bf16[512,3072]{1,0:T(8,128)(2,1)S(1)}, bf16[512,3072]{1,0:T(8,128)(2,1)}, u32[]{:S(2)}) copy-start(bf16[512,3072]{1,0:T(8,128)(2,1)} %param.18) | copy-start | bytes 9437188
  3343.0 253.8 %copy-start.28 = (f32[8,1,384]{2,1,0:T(1,128)S(1)}, f32[8,1,384]{2,1,0:T(1,128)}, u32[]{:S(2)}) copy-start(f32[8,1,384]{2,1,0:T(1,128)} %copy-done.27) | copy-start | bytes 36868
  3343.0 253.8 %copy-start.33 = (f32[512]{0:T(512)S(1)}, f32[512]{0:T(512)}, u32[]{:S(2)}) copy-start(f32[512]{0:T(512)} %copy-done.32) | copy-start | bytes 6148
  3343.0 257.7 %copy-start.31 = (f32[3072]{0:T(1024)S(1)}, f32[3072]{0:T(1024)}, u32[]{:S(2)}) copy-start(f32[3072]{0:T(1024)} %get-tuple-element.385) | copy-start | bytes 36868
  (11 other events, 20.8 us)
Sparse Core Ops, SparseCore 0:
  9.9 28.3 all-gather.19
  40.5 218.1 all-gather.15
  260.6 37.0 all-gather.17
  299.5 25.6 all-gather.21
  326.9 39.7 all-gather.23
  547.7 414.3 reduce-scatter.11
  964.1 73.9 all-gather.29
  1040.3 218.1 all-gather.25
  1260.6 70.3 all-gather.27
  1333.0 218.2 all-gather.33
  1553.3 72.7 all-gather.31
  1743.8 414.3 reduce-scatter.15
  2160.6 416.1 reduce-scatter.13
  2587.7 220.0 all-gather.35
  3184.2 412.5 reduce-scatter.17
  3600.8 158.7 reduce-scatter.31
  3763.6 156.8 reduce-scatter.29
  3924.6 156.8 reduce-scatter.27
  4085.4 46.2 reduce-scatter.23
  4135.9 46.2 reduce-scatter.21
  4186.2 76.4 reduce-scatter.25
  4266.8 76.4 reduce-scatter.19
where the time goes:
time: 4350 us
  waiting for transfers between devices  3180 us (73%)
  matrix products  775 us (18%)
  other arithmetic  222 us (5%)
  blocking collectives  80.7 us (2%)
  local copies, waits for them, and re-layouts  60.4 us (1%)
    reduce_scatter x1, waiting for transfers between devices, shards(): lax.psum_scatter(jnp.dot(piece, down_full, preferred_element_type=f32), '...  412 us
    reduce_scatter x1, waiting for transfers between devices, shards(): lax.psum_scatter(jnp.dot(piece, out_full, preferred_element_type=f32), 't...  405 us
    reduce_scatter x1, waiting for transfers between devices, shards(): lax.psum_scatter(jnp.einsum('rf,df->rd', grad_gate, gate_back, preferred_...  380 us
    reduce_scatter x1, waiting for transfers between devices, shards(): lax.psum_scatter(jnp.einsum('rh,dh->rd', grad_q_low, query_back, preferre...  252 us
    all_gather x1, waiting for transfers between devices, shards(): gathered_two = lax.all_gather(normed_two, 'tensor', axis=0, tiled=True)  220 us
    all_gather x1, waiting for transfers between devices, shards(): lax.all_gather(grad_hidden.astype(bf16), 'tensor', axis=0, tiled=True)  215 us
    all_gather x1, waiting for transfers between devices, shards(): lax.all_gather(first_normalized, 'tensor', axis=0, tiled=True)  202 us
    all_gather x1, waiting for transfers between devices, shards(): lax.all_gather(grad_result.astype(bf16), 'tensor', axis=0, tiled=True)  186 us
  transfers between devices with their start and end apart: 22, of which 19 were waited for; matrix products, arithmetic and copies ran while one was open for 12% of the time, Pallas kernels for 0%

commit v1 on v0

v1 whole, which is shorter than its diff:
```python
import functools
import math

import jax
import jax.numpy as jnp
import numpy as np
from jax import lax
from jax.experimental import pallas as pl
from jax.experimental.pallas import tpu as pltpu
from jax.sharding import PartitionSpec as P

HEAD_SIZE = 128
EPSILON = 1e-05
ROPE_BASE = 500000.0
MASKED = -1e30
F32 = jnp.float32
BF16 = jnp.bfloat16
NT = (((1,), (1,)), ((), ()))
NN = (((1,), (0,)), ((), ()))
TN = (((0,), (0,)), ((), ()))


def dot(a, b, dims, out=F32):
    return lax.dot_general(a, b, dims, preferred_element_type=F32).astype(out)


def after(value, *others):
    return lax.optimization_barrier((value, *others))[0]


def arrival_order(n):
    return [
        [s for d in range(1, n) for s in (i - d, i + d) if 0 <= s < n]
        for i in range(n)
    ]


def pick(place, choices):
    distinct = []
    for value in choices:
        if not any(value is other for other in distinct):
            distinct.append(value)
    out = distinct[0]
    for value in distinct[1:]:
        here = functools.reduce(
            jnp.logical_or, [place == i for i, c in enumerate(choices) if c is value]
        )
        out = jnp.where(here, value, out)
    return out


def travel(items, work=lambda: ()):
    arrays = lax.optimization_barrier(tuple(array for array, _ in items))
    moved = [lax.ppermute(array, "tensor", pairs) for array, (_, pairs) in zip(arrays, items)]
    out = lax.optimization_barrier((*moved, *work()))
    return list(out[: len(moved)])


def line_gather(own, n, use, fill=lambda step: (), along=lambda step: ()):
    place = lax.axis_index("tensor")
    order = arrival_order(n)
    right = left = own
    from_left, from_right = [own], [own]
    slots, used, others = [own], [], []
    for d in range(1, n):

        def work():
            used.append(use(d - 1, slots[d - 1]))
            return (used[-1], *fill(d))

        right, left, *more = travel(
            [
                (right, [(i, i + 1) for i in range(d - 1, n - 1)]),
                (left, [(i + 1, i) for i in range(n - d)]),
                *along(d),
            ],
            work,
        )
        others += more
        from_left.append(right)
        from_right.append(left)
        slots.append(
            pick(
                place,
                [
                    from_left[i - order[i][d - 1]] if order[i][d - 1] < i else from_right[order[i][d - 1] - i]
                    for i in range(n)
                ],
            )
        )
    used.append(use(n - 1, slots[-1]))
    return slots, used, others


def line_reduce(part, n, fill=lambda step, parts: (), along=lambda step: ()):
    place = lax.axis_index("tensor")
    parts = [None] * n
    parts[n - 1] = lax.optimization_barrier(part(n - 1))
    order = [[i] + row for i, row in enumerate(arrival_order(n))]
    right = left = None
    others = []
    for k in range(1, n):
        to_right = pick(
            place,
            [parts[order[i].index(i + n - k)] if i < k else parts[n - k] for i in range(n)],
        )
        to_left = pick(
            place,
            [parts[order[i].index(i - n + k)] if i >= n - k else parts[n - k] for i in range(n)],
        )
        if right is not None:
            to_right = (to_right.astype(F32) + right.astype(F32)).astype(BF16)
            to_left = (to_left.astype(F32) + left.astype(F32)).astype(BF16)

        def work():
            if k == 1:
                for s in range(n - 2, -1, -1):
                    parts[s] = lax.optimization_barrier(part(s))
            return (*fill(k, parts), *(parts[: n - 1] if k == 1 else ()))

        right, left, *more = travel(
            [
                (to_right, [(i, i + 1) for i in range(k)]),
                (to_left, [(n - 1 - i, n - 2 - i) for i in range(k)]),
                *along(k),
            ],
            work,
        )
        others += more
    return parts[0].astype(F32) + (right.astype(F32) + left.astype(F32)), others


def pairs_of(n):
    return [(i, i ^ 1) for i in range(n)]


def attend_forward(n, heads, rows, c, place_ref, *refs):
    chunks = refs[:n]
    cos_ref, sin_ref, qseg_ref, kseg_ref, o_ref, rot_ref, lse_ref, vt, acc, stat = refs[n:]
    hd = HEAD_SIZE
    kc, vc = heads * hd, (heads + 1) * hd
    for s in range(n):
        at = pl.ds(pl.multiple_of(place_ref[s] * rows, rows), rows)
        cos, sin = cos_ref[at, :], sin_ref[at, :]
        for h in range(heads + 1):
            u = chunks[s][:, h * hd : (h + 1) * hd]
            rot_ref[at, h * hd : (h + 1) * hd] = (u * cos + pltpu.roll(u, hd // 2, 1) * sin).astype(BF16)
        v = chunks[s][:, vc : vc + hd]
        rot_ref[at, vc : vc + hd] = v.astype(BF16)
        vt[:, at] = v.T.astype(BF16)

    def block(i, j, diagonal):
        qi = pl.ds(pl.multiple_of(i * rows, rows), rows)
        kj = pl.ds(pl.multiple_of(j * rows, rows), rows)
        k = rot_ref[kj, kc : kc + hd]
        allowed = kseg_ref[kj, :] == qseg_ref[:, qi]
        if diagonal:
            kr = lax.broadcasted_iota(jnp.int32, (rows, rows), 0)
            qr = lax.broadcasted_iota(jnp.int32, (rows, rows), 1)
            allowed = (allowed & (kr < qr)) | (kr == qr)
        for h in range(heads):
            q = rot_ref[qi, h * hd : (h + 1) * hd]
            scores = jnp.where(allowed, dot(k, q, NT) * c, MASKED)
            m = stat[h : h + 1, :]
            top = jnp.maximum(m, jnp.max(scores, axis=0, keepdims=True))
            p = jnp.exp2(scores - top)
            alpha = jnp.exp2(m - top)
            stat[h : h + 1, :] = top
            total = alpha * stat[8 + h : 9 + h, :] + jnp.sum(p, axis=0, keepdims=True)
            stat[8 + h : 9 + h, :] = total
            new = alpha * acc[h] + dot(vt[:, kj], p.astype(BF16), NN)
            if diagonal:
                at = pl.ds(pl.multiple_of(place_ref[n + i] * rows, rows), rows)
                o_ref[at, h * hd : (h + 1) * hd] = (new / total).T.astype(BF16)
                lse_ref[0, h : h + 1, qi] = top + jnp.log2(total)
            else:
                acc[h] = new

    @pl.loop(0, n)
    def _(i):
        stat[0:8, :] = jnp.full((8, rows), MASKED, F32)
        stat[8:16, :] = jnp.zeros((8, rows), F32)
        acc[...] = jnp.zeros_like(acc)

        @pl.loop(0, i)
        def _(j):
            block(i, j, False)

        block(i, i, True)


def attend_backward(n, heads, rows, c, place_ref, *refs):
    gas = refs[:n]
    rot_ref, o_ref, lse_ref, cos_ref, sin_ref, qseg_ref, kseg_ref, d_ref, go, dqt, delta, dk, dv, kt = refs[n:]
    hd = HEAD_SIZE
    scale = hd**-0.5
    kc, vc = heads * hd, (heads + 1) * hd
    for s in range(n):
        at = pl.ds(pl.multiple_of(place_ref[s] * rows, rows), rows)
        for h in range(heads):
            g = gas[s][:, h * hd : (h + 1) * hd]
            o = o_ref[s * rows : (s + 1) * rows, h * hd : (h + 1) * hd]
            go[at, h * hd : (h + 1) * hd] = g
            both = (g.astype(F32) * o.astype(F32)).T
            delta[h : h + 1, at] = jnp.sum(both, axis=0, keepdims=True)
        kt[:, at] = rot_ref[at, kc : kc + hd].astype(F32).T.astype(BF16)
    dqt[...] = jnp.zeros_like(dqt)

    def block(i, j, diagonal):
        qi = pl.ds(pl.multiple_of(i * rows, rows), rows)
        kj = pl.ds(pl.multiple_of(j * rows, rows), rows)
        k = rot_ref[kj, kc : kc + hd]
        v = rot_ref[kj, vc : vc + hd]
        allowed = kseg_ref[kj, :] == qseg_ref[:, qi]
        if diagonal:
            kr = lax.broadcasted_iota(jnp.int32, (rows, rows), 0)
            qr = lax.broadcasted_iota(jnp.int32, (rows, rows), 1)
            allowed = (allowed & (kr < qr)) | (kr == qr)
        for h in range(heads):
            cols = slice(h * hd, (h + 1) * hd)
            q = rot_ref[qi, cols]
            g = go[qi, cols]
            scores = jnp.where(allowed, dot(k, q, NT) * c, MASKED)
            p = jnp.exp2(scores - lse_ref[0, h : h + 1, qi])
            gp = dot(v, g, NT)
            ds = (p * (gp - delta[h : h + 1, qi])).astype(BF16)
            new_v = dot(p.astype(BF16), g, NN)
            new_k = dot(ds, q, NN)
            if diagonal and h == 0:
                dv[...] = new_v
                dk[...] = new_k
            else:
                dv[...] += new_v
                dk[...] += new_k
            dqt[h * hd : (h + 1) * hd, qi] += dot(kt[:, kj], ds, NN)

    def unrotate(u, at):
        return u * cos_ref[at, :] - pltpu.roll(u, hd // 2, 1) * sin_ref[at, :]

    @pl.loop(0, n)
    def _(j):
        block(j, j, True)

        @pl.loop(j + 1, n)
        def _(i):
            block(i, j, False)

        kj = pl.ds(pl.multiple_of(j * rows, rows), rows)
        to = pl.ds(pl.multiple_of(place_ref[n + j] * rows, rows), rows)
        for h in range(heads):
            u = dqt[h * hd : (h + 1) * hd, kj].T * scale
            d_ref[to, h * hd : (h + 1) * hd] = unrotate(u, kj).astype(BF16)
        d_ref[to, kc : kc + hd] = unrotate(dk[...] * scale, kj).astype(BF16)
        d_ref[to, vc : vc + hd] = dv[...].astype(BF16)


def attention_calls(n, rows, heads_q, heads_kv):
    heads = heads_q // heads_kv
    every = n * rows
    wide = (heads + 2) * HEAD_SIZE
    c = HEAD_SIZE**-0.5 * math.log2(math.e)
    whole = lambda shape: pl.BlockSpec(shape, lambda g, place: (0, 0))
    by_head = lambda r, w: pl.BlockSpec((r, w), lambda g, place: (0, g))
    tables = [
        whole((every, HEAD_SIZE)),
        whole((every, HEAD_SIZE)),
        whole((1, every)),
        whole((every, 1)),
    ]
    lse_spec = pl.BlockSpec((1, 8, every), lambda g, place: (g, 0, 0))
    pairs = every * (every + rows) // 2 * heads_q
    params = pltpu.CompilerParams(vmem_limit_bytes=58 << 20)
    forward = pl.pallas_call(
        functools.partial(attend_forward, n, heads, rows, c),
        grid_spec=pltpu.PrefetchScalarGridSpec(
            num_scalar_prefetch=1,
            grid=(heads_kv,),
            in_specs=[by_head(rows, wide)] * n + tables,
            out_specs=[by_head(every, heads * HEAD_SIZE), by_head(every, wide), lse_spec],
            scratch_shapes=[
                pltpu.VMEM((HEAD_SIZE, every), BF16),
                pltpu.VMEM((heads, HEAD_SIZE, rows), F32),
                pltpu.VMEM((16, rows), F32),
            ],
        ),
        out_shape=[
            jax.ShapeDtypeStruct((every, heads_q * HEAD_SIZE), BF16),
            jax.ShapeDtypeStruct((every, heads_kv * wide), BF16),
            jax.ShapeDtypeStruct((heads_kv, 8, every), F32),
        ],
        compiler_params=params,
        cost_estimate=pl.CostEstimate(
            flops=pairs * 4 * HEAD_SIZE, transcendentals=pairs, bytes_accessed=every * heads_kv * wide * 8
        ),
    )
    backward = pl.pallas_call(
        functools.partial(attend_backward, n, heads, rows, c),
        grid_spec=pltpu.PrefetchScalarGridSpec(
            num_scalar_prefetch=1,
            grid=(heads_kv,),
            in_specs=[by_head(rows, heads * HEAD_SIZE)] * n
            + [by_head(every, wide), by_head(every, heads * HEAD_SIZE), lse_spec]
            + tables,
            out_specs=by_head(every, wide),
            scratch_shapes=[
                pltpu.VMEM((every, heads * HEAD_SIZE), BF16),
                pltpu.VMEM((heads * HEAD_SIZE, every), F32),
                pltpu.VMEM((8, every), F32),
                pltpu.VMEM((rows, HEAD_SIZE), F32),
                pltpu.VMEM((rows, HEAD_SIZE), F32),
                pltpu.VMEM((HEAD_SIZE, every), BF16),
            ],
        ),
        out_shape=jax.ShapeDtypeStruct((every, heads_kv * wide), BF16),
        compiler_params=params,
        cost_estimate=pl.CostEstimate(
            flops=pairs * 10 * HEAD_SIZE, transcendentals=pairs, bytes_accessed=every * heads_kv * wide * 10
        ),
    )
    return forward, backward


def gated_kernel(x_ref, gate_ref, up_ref, gm_ref, *refs):
    mixed_ref, dg_ref, du_ref = refs[-3:]
    x = x_ref[...]
    step = 256 if mixed_ref.shape[1] % 256 == 0 else mixed_ref.shape[1]
    for c in range(0, mixed_ref.shape[1], step):
        at = slice(c, c + step)
        gate = dot(x, gate_ref[:, at], NN)
        up = dot(x, up_ref[:, at], NN)
        gm = gm_ref[:, at]
        sig = 1.0 / (1.0 + jnp.exp(-gate))
        act = gate * sig
        mixed_ref[:, at] = (act * up).astype(BF16)
        du_ref[:, at] = (gm * act).astype(BF16)
        dg_ref[:, at] = (gm * up * sig * (1.0 + gate * (1.0 - sig))).astype(BF16)


def gated(x, w_gate, w_up, gm, part, before=None):
    rows, width = x.shape
    hidden = w_gate.shape[1]
    tile = 512 if hidden % 512 == 0 else hidden
    weight = pl.BlockSpec((width, tile), lambda j: (0, j))
    here = pl.BlockSpec((rows, tile), lambda j: (part, j))
    before = () if before is None else tuple(before)
    return pl.pallas_call(
        gated_kernel,
        grid=(hidden // tile,),
        in_specs=[pl.BlockSpec((rows, width), lambda j: (0, 0)), weight, weight, here]
        + [pl.BlockSpec(memory_space=pl.ANY)] * len(before),
        out_specs=[here] * 3,
        out_shape=[jax.ShapeDtypeStruct((2 * rows, hidden), BF16)] * 3,
        input_output_aliases={4 + i: i for i in range(len(before))},
        compiler_params=pltpu.CompilerParams(vmem_limit_bytes=50 << 20),
        cost_estimate=pl.CostEstimate(
            flops=4 * rows * width * hidden,
            transcendentals=rows * hidden,
            bytes_accessed=4 * width * hidden + 2 * rows * width + 10 * rows * hidden,
        ),
    )(x, w_gate, w_up, gm, *before)


def spread_kernel(count, *refs):
    total = None
    for a_ref, w_ref in zip(refs[:count], refs[count : 2 * count]):
        term = lax.dot_general(a_ref[...], w_ref[...], NT, preferred_element_type=F32)
        total = term if total is None else total + term
    refs[-1][...] = total.astype(refs[-1].dtype)


def spread(acts, weights, part, out):
    rows, hidden = acts[0].shape[0] // 2, acts[0].shape[1]
    width = weights[0].shape[0]
    tile = 256 if width % 256 == 0 else width
    count = len(acts)
    return pl.pallas_call(
        functools.partial(spread_kernel, count),
        grid=(width // tile,),
        in_specs=[pl.BlockSpec((rows, hidden), lambda j: (part, 0))] * count
        + [pl.BlockSpec((tile, hidden), lambda j: (j, 0))] * count,
        out_specs=pl.BlockSpec((rows, tile), lambda j: (0, j)),
        out_shape=jax.ShapeDtypeStruct((rows, width), out),
        compiler_params=pltpu.CompilerParams(vmem_limit_bytes=50 << 20),
        cost_estimate=pl.CostEstimate(
            flops=2 * count * rows * width * hidden,
            transcendentals=0,
            bytes_accessed=count * 2 * hidden * (rows + width) + 4 * rows * width,
        ),
    )(*acts, *weights)


def norm_inverse(source):
    return lax.rsqrt(jnp.mean(source * source, axis=-1, keepdims=True) + EPSILON)


def norm_back(grad_normed, source, inverse, gain):
    unit_rows = source * inverse
    gain_term = jnp.sum(grad_normed * unit_rows, axis=0)
    scaled = grad_normed * gain
    grad_source = inverse * (scaled - unit_rows * jnp.mean(scaled * unit_rows, axis=-1, keepdims=True))
    return (grad_source, gain_term)


def shards(
    tokens,
    cotangent,
    segments,
    positions,
    counts,
    query_weight,
    key_projection_weight,
    value_projection_weight,
    out_weight,
    attn_gain,
    gate_weight,
    up_weight,
    down_weight,
    mlp_gain,
):
    n = lax.axis_size("tensor")
    place = lax.axis_index("tensor")
    rows, width = tokens.shape
    every = rows * n
    heads_q = query_weight.shape[1] // HEAD_SIZE
    heads_kv = key_projection_weight.shape[1] // HEAD_SIZE
    heads = heads_q // heads_kv
    qw, hd = heads * HEAD_SIZE, HEAD_SIZE
    wide = qw + 2 * hd
    slices = n // 2

    def gather(shard):
        return lax.all_gather(shard, "dp", axis=0, tiled=True)

    own_qkv = jnp.concatenate(
        [
            part
            for g in range(heads_kv)
            for part in (
                query_weight[:, g * qw : (g + 1) * qw],
                key_projection_weight[:, g * hd : (g + 1) * hd],
                value_projection_weight[:, g * hd : (g + 1) * hd],
            )
        ],
        axis=1,
    )
    w_qkv = gather(own_qkv)
    w_out = gather(out_weight.T)
    gains = lax.all_gather(jnp.stack([attn_gain, mlp_gain]), "dp", axis=1, tiled=True).astype(F32)
    gain_one, gain_two = gains[0], gains[1]
    down_t = down_weight.T

    def to_others(shard):
        return [(shard, [((i + 2 * k) % n, i) for i in range(n)]) for k in range(1, slices)]

    def to_owners(sums):
        return [(one, [(i, (i + 2 * k) % n) for i in range(n)]) for k, one in enumerate(sums, 1)]

    w_down = [gather(down_t)]
    w_gate = [gather(gate_weight)]
    w_up = [gather(up_weight)]

    live_count = counts[0]
    own_index = place * rows + jnp.arange(rows, dtype=jnp.int32)
    live = (own_index < live_count).astype(F32)[:, None]
    labels = lax.all_gather(jnp.stack([segments, positions]), "tensor", axis=1, tiled=True)
    seg_all, place_all = labels[0], labels[1]
    index_all = jnp.arange(every, dtype=jnp.int32)
    key_seg = jnp.where(index_all < live_count, seg_all, -1)[:, None]
    query_seg = seg_all[None, :]
    freqs = ROPE_BASE ** (-(jnp.arange(hd // 2, dtype=F32) * 2.0) / hd)
    angles = place_all.astype(F32)[:, None] * freqs[None, :]
    cos, sin = jnp.cos(angles), jnp.sin(angles)
    cos = jnp.concatenate([cos, cos], axis=1)
    sin = jnp.concatenate([-sin, sin], axis=1)
    order = np.array([[i] + row for i, row in enumerate(arrival_order(n))], np.int32)
    where_is = np.argsort(order, axis=1).astype(np.int32)
    slot_table = jnp.asarray(np.concatenate([order, where_is], axis=1))[place]
    attend, attend_back = attention_calls(n, rows, heads_q, heads_kv)
    tables = (cos, sin, query_seg, key_seg)

    source = tokens.astype(F32)
    inv_one = norm_inverse(source)
    normed_one = (source * inv_one * gain_one).astype(BF16)
    grad_result = cotangent.astype(F32) * live
    grad_low = grad_result.astype(BF16)
    slots_one, projected, moved = line_gather(
        after(normed_one, labels),
        n,
        lambda s, shard: dot(shard, w_qkv, NN),
        lambda step: tables if step == 1 else (),
        lambda step: to_others(down_t) if step == n - 1 else (),
    )
    w_down += [gather(shard) for shard in moved]
    projected[n - 1] = after(projected[n - 1], w_out, w_down[0])
    kept = []

    def attention():
        kept.extend(attend(slot_table, *projected, *tables))
        return kept

    gates, lows = lax.optimization_barrier((gate_weight, grad_low, projected[n - 1]))[:2]
    *moved, grad_theirs = travel([*to_others(gates), (lows, pairs_of(n))], attention)
    attended, rotated, lse = kept
    w_gate += [gather(shard) for shard in moved]
    grad_two = jnp.concatenate([grad_low, grad_theirs], axis=0)
    grad_mixed = []

    def while_out(step, parts):
        if step == 1:
            grad_mixed.append(dot(grad_two, w_down[0], NN))
            return (w_gate[0], grad_mixed[0])
        if step == 2:
            grad_mixed.extend(dot(grad_two, w, NN) for w in w_down[1:])
            return (w_up[0], *grad_mixed[1:])
        return ()

    summed, moved = line_reduce(
        lambda s: dot(after(attended, *moved)[s * rows : (s + 1) * rows], w_out, NT, BF16),
        n,
        while_out,
        lambda step: to_others(up_weight) if step == 1 else (),
    )
    w_up += [gather(shard) for shard in moved]
    hidden = source + summed

    inv_two = norm_inverse(hidden)
    normed_two = (hidden * inv_two * gain_two).astype(BF16)
    mine = []

    def own_rows():
        mine.extend(gated(normed_two, g, u, gm, 0) for g, u, gm in zip(w_gate, w_up, grad_mixed))
        return [one[0] for one in mine]

    (two_theirs,) = travel([(normed_two, pairs_of(n))], own_rows)
    both = [
        gated(two_theirs, g, u, gm, 1, before) for g, u, gm, before in zip(w_gate, w_up, grad_mixed, mine)
    ]
    mixed, grad_gate, grad_up = zip(*both)
    two = jnp.concatenate([normed_two, two_theirs], axis=0)
    d_down = [None] * slices
    d_down[1:] = [dot(grad_two, m, TN, BF16) for m in mixed[1:]]
    grads, weights = list(grad_gate + grad_up), w_gate + w_up
    theirs = spread([after(grads[0], *d_down[1:])] + grads[1:], weights, 1, BF16)
    ours, d_up, d_gate = [], [None] * slices, [None] * slices

    def own_sums():
        ours.append(spread(grads, weights, 0, F32))
        d_up[1:] = [dot(two, g, TN, BF16) for g in grad_up[1:]]
        return (ours[0], *d_up[1:])

    (from_theirs,) = travel([(theirs, pairs_of(n))], own_sums)
    grad_normed_two = ours[0] + from_theirs.astype(F32)
    grad_hidden_norm, gain_two_term = norm_back(grad_normed_two, hidden, inv_two, gain_two)
    grad_hidden = grad_result + grad_hidden_norm

    def owner_sum(partial):
        return lax.psum_scatter(partial, "dp", scatter_dimension=0, tiled=True)

    results = []

    def while_gather(step):
        if step == 1:
            d_gate[1:] = [dot(two, g, TN, BF16) for g in grad_gate[1:]]
            d_down[0] = dot(grad_two, mixed[0], TN, BF16)
            return (*d_gate[1:], d_down[0])
        if step == 2:
            d_up[0] = dot(two, grad_up[0], TN, BF16)
            d_gate[0] = dot(two, grad_gate[0], TN, BF16)
            return (d_up[0], d_gate[0])
        results.extend((spread(mixed, w_down, 1, BF16), spread(mixed, w_down, 0, F32)))
        return results

    sums_down = [owner_sum(d) for d in d_down[1:]]
    slots_back, grad_attended, back_down = line_gather(
        grad_hidden.astype(BF16),
        n,
        lambda s, shard: dot(shard, w_out, NN, BF16),
        while_gather,
        lambda step: to_owners(sums_down) if step == n - 1 else (),
    )
    kept = []

    def attention_back():
        kept.append(attend_back(slot_table, *grad_attended, rotated, attended, lse, *tables))
        return kept

    (from_partner,) = travel([(after(results[0], grad_attended[n - 1]), pairs_of(n))], attention_back)
    grad_qkv = kept[0]
    result = hidden + (results[1] + from_partner.astype(F32))
    output = (result * live).astype(BF16)
    d_qkv = dot(jnp.concatenate(slots_one, axis=0), grad_qkv, TN, BF16)
    d_out = dot(jnp.concatenate(slots_back, axis=0), after(attended, grad_qkv), TN, BF16)
    gain_terms = []

    def while_reduce(step, parts):
        if step == 1:
            return (d_qkv, d_out)
        if step == 2:
            gain_one_term = sum(
                jnp.sum(one.astype(F32) * part.astype(F32), axis=0) for one, part in zip(slots_one, parts)
            )
            gain_terms.append(jnp.stack([gain_one_term / gain_one, gain_two_term]))
            return (gain_terms[0], output)
        return ()

    sums_up = [owner_sum(d) for d in d_up[1:]]
    sums_gate = [owner_sum(d) for d in d_gate[1:]]
    grad_normed_one, back_up = line_reduce(
        lambda s: dot(after(grad_qkv, from_partner)[s * rows : (s + 1) * rows], w_qkv, NT, BF16),
        n,
        while_reduce,
        lambda step: to_owners(sums_up) if step == 1 else (),
    )
    back_gate = travel(to_owners([after(one, grad_normed_one) for one in sums_gate]))

    def whole(first, back):
        return sum((one.astype(F32) for one in back), owner_sum(first).astype(F32))

    grad_down_w = whole(d_down[0], back_down).T
    grad_up_w = whole(d_up[0], back_up)
    grad_gate_w = whole(d_gate[0], back_gate)
    grad_out_w = owner_sum(d_out).astype(F32).T
    grad_qkv_w = owner_sum(d_qkv).astype(F32)
    grad_input_norm, _ = norm_back(grad_normed_one, source, inv_one, gain_one)
    grad_tokens = grad_hidden + grad_input_norm
    gain_sums = lax.psum(after(gain_terms[0], *back_gate), ("dp", "tensor"))
    owned = attn_gain.shape[0]
    gain_own = lax.dynamic_slice_in_dim(gain_sums, lax.axis_index("dp") * owned, owned, 1)

    def columns(offset, size):
        return jnp.concatenate(
            [grad_qkv_w[:, g * wide + offset : g * wide + offset + size] for g in range(heads_kv)], axis=1
        )

    return (
        output,
        grad_tokens,
        columns(0, qw),
        columns(qw, hd),
        columns(qw + hd, hd),
        grad_out_w,
        gain_own[0],
        grad_gate_w,
        grad_up_w,
        grad_down_w,
        gain_own[1],
    )


def solution(mesh):
    rows = P(("dp", "tensor"), None)
    row = P(("dp", "tensor"))
    down_cols = P("tensor", "dp")
    cols = P("dp", "tensor")
    return jax.shard_map(
        shards,
        mesh=mesh,
        in_specs=(rows, rows, row, row, P("dp"), cols, cols, cols, down_cols, P("dp"), cols, cols, down_cols, P("dp")),
        out_specs=(rows, rows, cols, cols, cols, down_cols, P("dp"), cols, cols, down_cols, P("dp")),
        check_vma=False,
    )
```

time: 4350 us -> 1820 us (0.42)
  waiting for transfers between devices: 3180 us -> 897 us
  matrix products: 775 us -> 292 us
  Pallas kernels: 0 us -> 295 us
  other arithmetic: 222 us -> 125 us
  starting transfers between devices: 1.47 us -> 86.9 us
    reduce_scatter x11 -> x8, waiting for transfers between devices: 2150 us -> 0.03 us  [owner_sum(): return lax.psum_scatter(partial, 'dp', scatter_dimension=0, tiled=True)]
    all_gather x11 -> x8, waiting for transfers between devices: 1030 us -> 7.25 us  [gather(): return lax.all_gather(shard, 'dp', axis=0, tiled=True)]
    ppermute x0 -> x34, waiting for transfers between devices: none -> 887 us  [travel(): lax.ppermute(array, 'tensor', pairs)]
    dot_general x49 -> x26, matrix products: 775 us -> 292 us  [dot(): return lax.dot_general(a, b, dims, preferred_element_type=F32).astype(out)]
    pallas_call x0 -> x10, Pallas kernels: none -> 295 us  [the longest x4 115 us: spread(): pl.pallas_call(functools.partial(spread_kernel, count), grid=(width // ti...]
    ppermute x0 -> x34, starting transfers between devices: none -> 86.1 us  [travel(): lax.ppermute(array, 'tensor', pairs)]
    convert_element_type x13 -> x11, other arithmetic: 91.5 us -> 58.8 us  [the longest x4 30.9 us: line_reduce(): to_left = (to_left.astype(F32) + left.astype(F32)).astype(BF16)]
  transfers between devices with their start and end apart: 22 -> 50, of which waited for: 19 -> 24; matrix products, arithmetic and copies ran while one was open for 12% -> 23% of each run, Pallas kernels for 0% -> 15%
where the time goes in v1:
time: 1820 us; the launch traced here: 1810 us
  waiting for transfers between devices  897 us (49%)
  Pallas kernels  295 us (16%)
  matrix products  292 us (16%)
  other arithmetic  125 us (7%)
  starting transfers between devices  86.9 us (5%)
  blocking collectives  63 us (3%)
  local copies, waits for them, and re-layouts  31.3 us (2%)
    ppermute x34, waiting for transfers between devices, travel(): lax.ppermute(array, 'tensor', pairs)  887 us
    dot_general x26, matrix products, dot(): return lax.dot_general(a, b, dims, preferred_element_type=F32).astype(out)  292 us
    pallas_call x4, Pallas kernels, spread(): pl.pallas_call(functools.partial(spread_kernel, count), grid=(width // ti...  115 us
    ppermute x34, starting transfers between devices, travel(): lax.ppermute(array, 'tensor', pairs)  86.1 us
    pallas_call x4, Pallas kernels, gated(): pl.pallas_call(gated_kernel, grid=(hidden // tile,), in_specs=[pl.BlockSp...  80.8 us
    pallas_call x1, Pallas kernels, attention_back(): attend_back(slot_table, *grad_attended, rotated, attended, lse, *tables)  56 us
    pallas_call x1, Pallas kernels, attention(): kept.extend(attend(slot_table, *projected, *tables))  43.1 us
    psum x1, blocking collectives, shards(): gain_sums = lax.psum(after(gain_terms[0], *back_gate), ('dp', 'tensor'))  39.2 us
  transfers between devices with their start and end apart: 50, of which 24 were waited for; matrix products, arithmetic and copies ran while one was open for 23% of the time, Pallas kernels for 15%

profile of v1, /device:TPU:0, one launch (start us, length us, event | category | flops | bytes accessed | tf_op | source)
XLA Modules:
  0.0 1805.4 jit_solution(11190078599161341035)
XLA Ops:
  21.1 10.4 all_gather.30
  31.5 13.4 all_gather.31
  64.8 7.2 all-gather.9.cloned.1.call-done
  72.0 9.9 fusion.54.refs_0_
  81.9 35.8 %collective-permute-done = bf16[512,3072]{1,0:T(8,128)(2,1)} collective-permute-done((bf16[512,3072]{1,0:T(8,128)(2,1)}, bf16[512,3072]{1,0:T(8,128)(2,1)}, u32[]{:S(2)}, u32[]{:S(2)}) %collective-permute-start) | collective-permute-done | bytes 3145760 | tf_op jit(solution)/shard_map/ppermute | solution.py:54
  137.5 57.3 %collective-permute-done.3 = bf16[512,3072]{1,0:T(8,128)(2,1)} collective-permute-done((bf16[512,3072]{1,0:T(8,128)(2,1)}, bf16[512,3072]{1,0:T(8,128)(2,1)}, u32[]{:S(2)}, u32[]{:S(2)}) %collective-permute-start.3) | collective-permute-done | bytes 3145760 | tf_op jit(solution)/shard_map/ppermute | solution.py:54
  208.8 56.2 %collective-permute-done.6 = bf16[384,2048]{1,0:T(8,128)(2,1)} collective-permute-done((bf16[384,2048]{1,0:T(8,128)(2,1)S(1)}, bf16[384,2048]{1,0:T(8,128)(2,1)}, u32[]{:S(2)}, u32[]{:S(2)}) %collective-permute-start.6) | collective-permute-done | bytes 1572896 | tf_op jit(solution)/shard_map/ppermute | solution.py:54
  265.0 33.4 %collective-permute-done.5 = bf16[512,3072]{1,0:T(8,128)(2,1)} collective-permute-done((bf16[512,3072]{1,0:T(8,128)(2,1)}, bf16[512,3072]{1,0:T(8,128)(2,1)}, u32[]{:S(2)}, u32[]{:S(2)}) %collective-permute-start.5) | collective-permute-done | bytes 3145760 | tf_op jit(solution)/shard_map/ppermute | solution.py:54
  316.1 43.1 %shard_map.230 = (bf16[2048,768]{1,0:T(8,128)(2,1)}, bf16[2048,1280]{1,0:T(8,128)(2,1)}, f32[2,8,2048]{2,1,0:T(8,128)}) custom-call(s32[8]{0:T(128)} %dynamic-slice_bitcast_fusion.place_ref, f32[512,1280]{1,0:T(8,128)} %fusion.54.refs_0_, f32[512,1280]{1,0:T(8,128)} %fusion.55.refs_1_, f32[512,1280]{1,0:T(8,128)} %fusion.56.refs_2_, ...), custom_call_target="tpu_custom_call" | custom-call | flops 8053063680 | bytes 20971520 | tf_op jit(solution)/shard_map/pallas_call | solution.py:498
  359.2 55.4 %collective-permute-done.7 = bf16[384,2048]{1,0:T(8,128)(2,1)} collective-permute-done((bf16[384,2048]{1,0:T(8,128)(2,1)}, bf16[384,2048]{1,0:T(8,128)(2,1)}, u32[]{:S(2)}, u32[]{:S(2)}) %collective-permute-start.7) | collective-permute-done | bytes 1572896 | tf_op jit(solution)/shard_map/ppermute | solution.py:54
  416.9 7.0 convolution_convert_fusion.6
  430.0 18.1 %fusion.49.gm_ref = f32[1024,2048]{1,0:T(8,128)} fusion(bf16[3072,2048]{1,0:T(8,128)(2,1)} %all-gather.13.cloned.1.call-done.refs_2_, bf16[512,3072]{1,0:T(8,128)(2,1)} %collective-permute-done.8, bf16[512,3072]{1,0:T(8,128)(2,1)S(1)} %copy-done.20), kind=kOutput, calls=%fused_computation.129 | convolution fusion | flops 12897484800 | bytes 27262976 | tf_op jit(solution)/shard_map/dot_general | solution.py:24
  460.2 66.4 %collective-permute-done.11 = bf16[384,2048]{1,0:T(8,128)(2,1)} collective-permute-done((bf16[384,2048]{1,0:T(8,128)(2,1)}, bf16[384,2048]{1,0:T(8,128)(2,1)}, u32[]{:S(2)}, u32[]{:S(2)}) %collective-permute-start.11) | collective-permute-done | bytes 1572896 | tf_op jit(solution)/shard_map/ppermute | solution.py:54
  526.6 7.5 add_convert_fusion.5
  534.2 7.9 collective-permute-start.12
  544.4 18.8 %fusion.48.gm_ref = f32[1024,2048]{1,0:T(8,128)} fusion(bf16[3072,2048]{1,0:T(8,128)(2,1)} %all-gather.19.cloned.1.call-done.refs_3_, bf16[512,3072]{1,0:T(8,128)(2,1)} %collective-permute-done.8, bf16[512,3072]{1,0:T(8,128)(2,1)} %fusion.31), kind=kOutput, calls=%fused_computation.128 | convolution fusion | flops 12897484800 | bytes 27262976 | tf_op jit(solution)/shard_map/dot_general | solution.py:24
  563.2 41.6 %collective-permute-done.12 = bf16[512,3072]{1,0:T(8,128)(2,1)} collective-permute-done((bf16[512,3072]{1,0:T(8,128)(2,1)}, bf16[512,3072]{1,0:T(8,128)(2,1)}, u32[]{:S(2)}, u32[]{:S(2)}) %collective-permute-start.12) | collective-permute-done | bytes 3145760 | tf_op jit(solution)/shard_map/ppermute | solution.py:54
  604.8 6.5 add_convert_fusion.3
  611.3 8.1 collective-permute-start.14
  621.1 62.3 %collective-permute-done.14 = bf16[512,3072]{1,0:T(8,128)(2,1)S(1)} collective-permute-done((bf16[512,3072]{1,0:T(8,128)(2,1)S(1)}, bf16[512,3072]{1,0:T(8,128)(2,1)S(1)}, u32[]{:S(2)}, u32[]{:S(2)}) %collective-permute-start.14) | collective-permute-done | bytes 3145760 | tf_op jit(solution)/shard_map/ppermute | solution.py:54
  694.0 21.0 %shard_map.231 = (bf16[1024,2048]{1,0:T(8,128)(2,1)}, bf16[1024,2048]{1,0:T(8,128)(2,1)}, bf16[1024,2048]{1,0:T(8,128)(2,1)}) custom-call(bf16[512,3072]{1,0:T(8,128)(2,1)} %multiply_convert_fusion.1.x_ref, bf16[3072,2048]{1,0:T(8,128)(2,1)} %all-gather.15.cloned.1.call-done.gate_ref.refs_4_, ...), custom_call_target="tpu_custom_call" | custom-call | flops 12884901888 | bytes 38797312 | tf_op jit(solution)/shard_map/pallas_call | solution.py:346
  715.0 21.0 %shard_map.232 = (bf16[1024,2048]{1,0:T(8,128)(2,1)}, bf16[1024,2048]{1,0:T(8,128)(2,1)}, bf16[1024,2048]{1,0:T(8,128)(2,1)}) custom-call(bf16[512,3072]{1,0:T(8,128)(2,1)} %multiply_convert_fusion.1.x_ref, bf16[3072,2048]{1,0:T(8,128)(2,1)} %all-gather.21.cloned.1.call-done.gate_ref.refs_5_, ...), custom_call_target="tpu_custom_call" | custom-call | flops 12884901888 | bytes 38797312 | tf_op jit(solution)/shard_map/pallas_call | solution.py:346
  736.0 23.6 %collective-permute-done.16.x_ref = bf16[512,3072]{1,0:T(8,128)(2,1)S(1)} collective-permute-done((bf16[512,3072]{1,0:T(8,128)(2,1)}, bf16[512,3072]{1,0:T(8,128)(2,1)S(1)}, u32[]{:S(2)}, u32[]{:S(2)}) %collective-permute-start.16) | collective-permute-done | bytes 3145760 | tf_op jit(solution)/shard_map/ppermute | solution.py:54
  759.6 19.2 %shard_map.234 = (bf16[1024,2048]{1,0:T(8,128)(2,1)}, bf16[1024,2048]{1,0:T(8,128)(2,1)}, bf16[1024,2048]{1,0:T(8,128)(2,1)}) custom-call(bf16[512,3072]{1,0:T(8,128)(2,1)S(1)} %collective-permute-done.16.x_ref, bf16[3072,2048]{1,0:T(8,128)(2,1)} %all-gather.21.cloned.1.call-done.gate_ref.refs_5_, ...), custom_call_target="tpu_custom_call", output_to_operand_aliasing={{0}: (4, {}), {1}: (5, {}), {2}: (6, {})} | custom-call | flops 12884901888 | bytes 38797312 | tf_op jit(solution)/shard_map/pallas_call | solution.py:346
  778.8 19.1 %convolution_convert_fusion.5 = bf16[3072,2048]{1,0:T(8,128)(2,1)} fusion(bf16[1024,2048]{1,0:T(8,128)(2,1)} %get-tuple-element.148.refs_1_, bf16[512,3072]{1,0:T(8,128)(2,1)} %collective-permute-done.8, bf16[512,3072]{1,0:T(8,128)(2,1)S(1)} %copy-done.21), kind=kOutput, calls=%fused_computation.22 | convolution fusion | flops 12903776256 | bytes 23068672 | tf_op jit(solution)/shard_map/dot_general | solution.py:24
  798.0 18.9 %convolution_convert_fusion.4 = bf16[3072,2048]{1,0:T(8,128)(2,1)} fusion(bf16[1024,2048]{1,0:T(8,128)(2,1)} %get-tuple-element.152.refs_3_, bf16[512,3072]{1,0:T(8,128)(2,1)S(1)} %collective-permute-done.16.x_ref, bf16[512,3072]{1,0:T(8,128)(2,1)} %multiply_convert_fusion.1.x_ref), kind=kOutput, calls=%fused_computation.21 | convolution fusion | flops 12903776256 | bytes 23068672 | tf_op jit(solution)/shard_map/dot_general | solution.py:24
  817.0 19.6 %shard_map.233 = (bf16[1024,2048]{1,0:T(8,128)(2,1)}, bf16[1024,2048]{1,0:T(8,128)(2,1)}, bf16[1024,2048]{1,0:T(8,128)(2,1)}) custom-call(bf16[512,3072]{1,0:T(8,128)(2,1)S(1)} %collective-permute-done.16.x_ref, bf16[3072,2048]{1,0:T(8,128)(2,1)} %all-gather.15.cloned.1.call-done.gate_ref.refs_4_, ...), custom_call_target="tpu_custom_call", output_to_operand_aliasing={{0}: (4, {}), {1}: (5, {}), {2}: (6, {})} | custom-call | flops 12884901888 | bytes 38797312 | tf_op jit(solution)/shard_map/pallas_call | solution.py:346
  836.5 19.0 %convolution_convert_fusion.2 = bf16[3072,2048]{1,0:T(8,128)(2,1)} fusion(bf16[1024,2048]{1,0:T(8,128)(2,1)} %get-tuple-element.145.refs_0_, bf16[512,3072]{1,0:T(8,128)(2,1)} %collective-permute-done.8, bf16[512,3072]{1,0:T(8,128)(2,1)S(1)} %copy-done.22), kind=kOutput, calls=%fused_computation.19 | convolution fusion | flops 12903776256 | bytes 23068672 | tf_op jit(solution)/shard_map/dot_general | solution.py:24
  855.6 36.1 %shard_map.238 = bf16[512,3072]{1,0:T(8,128)(2,1)} custom-call(bf16[1024,2048]{1,0:T(8,128)(2,1)} %get-tuple-element.153.refs_0_, bf16[1024,2048]{1,0:T(8,128)(2,1)} %get-tuple-element.150.refs_1_, bf16[1024,2048]{1,0:T(8,128)(2,1)} %get-tuple-element.151.refs_2_, bf16[1024,2048]{1,0:T(8,128)(2,1)} %get-tuple-element.152.refs_3_, ...), custom_call_target="tpu_custom_call" | custom-call | flops 25769803776 | bytes 65011712 | tf_op jit(solution)/shard_map/pallas_call | solution.py:376
  892.8 17.6 convolution_convert_fusion.1
  910.5 35.8 %shard_map.237 = f32[512,3072]{1,0:T(8,128)} custom-call(bf16[1024,2048]{1,0:T(8,128)(2,1)} %get-tuple-element.153.refs_0_, bf16[1024,2048]{1,0:T(8,128)(2,1)} %get-tuple-element.150.refs_1_, bf16[1024,2048]{1,0:T(8,128)(2,1)} %get-tuple-element.151.refs_2_, bf16[1024,2048]{1,0:T(8,128)(2,1)} %get-tuple-element.152.refs_3_, ...), custom_call_target="tpu_custom_call" | custom-call | flops 25769803776 | bytes 65011712 | tf_op jit(solution)/shard_map/pallas_call | solution.py:376
  946.3 11.7 collective-permute-done.17
  957.9 7.5 multiply_reduce_fusion
  965.4 7.8 fusion.50
  979.6 18.0 convolution_convert_fusion.3
  997.7 8.8 convolution_convert_fusion.17.refs_0_
  1006.5 34.4 %collective-permute-done.18 = bf16[512,3072]{1,0:T(8,128)(2,1)} collective-permute-done((bf16[512,3072]{1,0:T(8,128)(2,1)}, bf16[512,3072]{1,0:T(8,128)(2,1)}, u32[]{:S(2)}, u32[]{:S(2)}) %collective-permute-start.18) | collective-permute-done | bytes 3145760 | tf_op jit(solution)/shard_map/ppermute | solution.py:54
  1050.2 17.8 convolution_convert_fusion
  1070.2 7.1 convolution_convert_fusion.16.refs_1_
  1077.3 41.6 %collective-permute-done.21 = bf16[512,3072]{1,0:T(8,128)(2,1)} collective-permute-done((bf16[512,3072]{1,0:T(8,128)(2,1)}, bf16[512,3072]{1,0:T(8,128)(2,1)}, u32[]{:S(2)}, u32[]{:S(2)}) %collective-permute-start.21) | collective-permute-done | bytes 3145760 | tf_op jit(solution)/shard_map/ppermute | solution.py:54
  1121.1 22.5 %shard_map.235 = f32[512,3072]{1,0:T(8,128)} custom-call(bf16[1024,2048]{1,0:T(8,128)(2,1)} %get-tuple-element.145.refs_0_, bf16[1024,2048]{1,0:T(8,128)(2,1)} %get-tuple-element.148.refs_1_, bf16[3072,2048]{1,0:T(8,128)(2,1)} %all-gather.13.cloned.1.call-done.refs_2_, bf16[3072,2048]{1,0:T(8,128)(2,1)} %all-gather.19.cloned.1.call-done.refs_3_), custom_call_target="tpu_custom_call" | custom-call | flops 12884901888 | bytes 35651584 | tf_op jit(solution)/shard_map/pallas_call | solution.py:376
  1143.7 20.6 %shard_map.236 = bf16[512,3072]{1,0:T(8,128)(2,1)S(1)} custom-call(bf16[1024,2048]{1,0:T(8,128)(2,1)} %get-tuple-element.145.refs_0_, bf16[1024,2048]{1,0:T(8,128)(2,1)} %get-tuple-element.148.refs_1_, bf16[3072,2048]{1,0:T(8,128)(2,1)} %all-gather.13.cloned.1.call-done.refs_2_, bf16[3072,2048]{1,0:T(8,128)(2,1)} %all-gather.19.cloned.1.call-done.refs_3_), custom_call_target="tpu_custom_call" | custom-call | flops 12884901888 | bytes 35651584 | tf_op jit(solution)/shard_map/pallas_call | solution.py:376
  1171.3 59.5 %collective-permute-done.24 = bf16[384,2048]{1,0:T(8,128)(2,1)S(1)} collective-permute-done((bf16[384,2048]{1,0:T(8,128)(2,1)}, bf16[384,2048]{1,0:T(8,128)(2,1)S(1)}, u32[]{:S(2)}, u32[]{:S(2)}) %collective-permute-start.24) | collective-permute-done | bytes 1572896 | tf_op jit(solution)/shard_map/ppermute | solution.py:54
  1237.8 56.0 %shard_map.239 = bf16[2048,1280]{1,0:T(8,128)(2,1)} custom-call(s32[8]{0:T(128)} %dynamic-slice_bitcast_fusion.place_ref, bf16[512,768]{1,0:T(8,128)(2,1)} %convolution_convert_fusion.17.refs_0_, bf16[512,768]{1,0:T(8,128)(2,1)} %convolution_convert_fusion.16.refs_1_, bf16[512,768]{1,0:T(8,128)(2,1)} %convolution_convert_fusion.15.refs_2_, ...), custom_call_target="tpu_custom_call" | custom-call | flops 20132659200 | bytes 26214400 | tf_op jit(solution)/shard_map/pallas_call | solution.py:584
  1293.8 15.5 fusion.32
  1309.4 22.7 %fusion.16 = bf16[3072,1280]{1,0:T(8,128)(2,1)} fusion(bf16[2048,1280]{1,0:T(8,128)(2,1)} %shard_map.239, bf16[512,3072]{1,0:T(8,128)(2,1)} %copy-done.9, bf16[512,3072]{1,0:T(8,128)(2,1)} %copy-done.7, bf16[512,3072]{1,0:T(8,128)(2,1)} %copy-done.5, bf16[512,3072]{1,0:T(8,128)(2,1)} %fusion.25), kind=kOutput, calls=%fused_computation.16 | convolution fusion | flops 16160391168 | bytes 25690112 | tf_op jit(solution)/shard_map/dot_general | solution.py:24
  1334.3 68.4 %collective-permute-done.25 = bf16[512,3072]{1,0:T(8,128)(2,1)} collective-permute-done((bf16[512,3072]{1,0:T(8,128)(2,1)S(1)}, bf16[512,3072]{1,0:T(8,128)(2,1)}, u32[]{:S(2)}, u32[]{:S(2)}) %collective-permute-start.25) | collective-permute-done | bytes 3145760 | tf_op jit(solution)/shard_map/ppermute | solution.py:54
  1402.7 9.6 convolution_convert_fusion.10
  1420.2 8.6 convolution_convert_fusion.11
  1428.8 8.0 convolution_convert_fusion.13
  1436.9 10.7 convolution_convert_fusion.12
  1447.6 69.0 %collective-permute-done.28 = bf16[384,2048]{1,0:T(8,128)(2,1)S(1)} collective-permute-done((bf16[384,2048]{1,0:T(8,128)(2,1)}, bf16[384,2048]{1,0:T(8,128)(2,1)S(1)}, u32[]{:S(2)}, u32[]{:S(2)}) %collective-permute-start.28) | collective-permute-done | bytes 1572896 | tf_op jit(solution)/shard_map/ppermute | solution.py:54
  1516.6 10.9 add_convert_fusion.1
  1527.5 7.6 collective-permute-start.29
  1541.8 9.5 multiply_convert_fusion
  1552.0 46.9 %collective-permute-done.29 = bf16[512,3072]{1,0:T(8,128)(2,1)} collective-permute-done((bf16[512,3072]{1,0:T(8,128)(2,1)}, bf16[512,3072]{1,0:T(8,128)(2,1)}, u32[]{:S(2)}, u32[]{:S(2)}) %collective-permute-start.29) | collective-permute-done | bytes 3145760 | tf_op jit(solution)/shard_map/ppermute | solution.py:54
  1598.9 6.0 fusion.24
  1604.9 8.6 collective-permute-start.31
  1633.1 43.1 %collective-permute-done.31 = bf16[512,3072]{1,0:T(8,128)(2,1)} collective-permute-done((bf16[512,3072]{1,0:T(8,128)(2,1)}, bf16[512,3072]{1,0:T(8,128)(2,1)}, u32[]{:S(2)}, u32[]{:S(2)}) %collective-permute-start.31) | collective-permute-done | bytes 3145760 | tf_op jit(solution)/shard_map/ppermute | solution.py:54
  1676.2 5.8 collective-permute-done.32
  1682.0 6.9 fusion.26
  1690.3 7.5 fusion.29
  1697.8 56.5 %collective-permute-done.33 = bf16[384,2048]{1,0:T(8,128)(2,1)} collective-permute-done((bf16[384,2048]{1,0:T(8,128)(2,1)}, bf16[384,2048]{1,0:T(8,128)(2,1)}, u32[]{:S(2)}, u32[]{:S(2)}) %collective-permute-start.33) | collective-permute-done | bytes 1572896 | tf_op jit(solution)/shard_map/ppermute | solution.py:54
  1754.4 39.2 %psum.7 = f32[2,3072]{1,0:T(2,128)S(1)} all-reduce(f32[2,3072]{1,0:T(2,128)S(1)} %copy-done.34), channel_id=1, replica_groups=mesh['dp'=8,'tensor'=4] {'dp','tensor'}, use_global_device_ids=true, to_apply=%region_14.15 | all-reduce | flops 6144 | bytes 49152 | tf_op jit(solution)/shard_map/psum | solution.py:626
  (271 shorter events, 198.1 us)
Async XLA Ops:
  7.2 64.9 %all-gather.9.cloned.1.call-start = ((), (), s32[]{:S(2)}) async-start(), calls=%async_computation.8 | async-start | bytes 8847360 | tf_op jit(solution)/shard_map/all_gather | solution.py:432
  17.0 297.9 %all-gather.11.cloned.1.call-start = ((), (), s32[]{:S(2)}) async-start(), calls=%async_computation.9 | async-start | bytes 5308416 | tf_op jit(solution)/shard_map/all_gather | solution.py:432
  17.7 297.2 %all-gather.13.cloned.1.call-start = ((), (), s32[]{:S(2)}) async-start(), calls=%async_computation.10 | async-start | bytes 14155776 | tf_op jit(solution)/shard_map/all_gather | solution.py:432
  20.4 439.8 %all-gather.15.cloned.1.call-start = ((), (), s32[]{:S(2)}) async-start(), calls=%async_computation.11 | async-start | bytes 14155776 | tf_op jit(solution)/shard_map/all_gather | solution.py:432
  21.0 523.4 %all-gather.19.cloned.1.call-start = ((), (), s32[]{:S(2)}) async-start(), calls=%async_computation.13 | async-start | bytes 14155776 | tf_op jit(solution)/shard_map/all_gather | solution.py:432
  45.6 644.5 %copy-start.28 = (f32[1,3072]{1,0:T(1,128)}, f32[1,3072]{1,0:T(1,128)S(1)}, u32[]{:S(2)}) copy-start(f32[1,3072]{1,0:T(1,128)S(1)} %get-tuple-element.240) | copy-start | bytes 36868
  49.0 68.7 %collective-permute-start = (bf16[512,3072]{1,0:T(8,128)(2,1)}, bf16[512,3072]{1,0:T(8,128)(2,1)}, u32[]{:S(2)}, u32[]{:S(2)}) collective-permute-start(bf16[512,3072]{1,0:T(8,128)(2,1)} %fusion.25), channel_id=1, source_target_pairs={{0,1},{1,2},{2,3},{4,5},{5,6},{6,7},{8,9},{9,10},{10,11},{12,13},{... | collective-permute-start | bytes 9437192 | tf_op jit(solution)/shard_map/ppermute | solution.py:54
  54.1 69.4 %collective-permute-start.1 = (bf16[512,3072]{1,0:T(8,128)(2,1)}, bf16[512,3072]{1,0:T(8,128)(2,1)}, u32[]{:S(2)}, u32[]{:S(2)}) collective-permute-start(bf16[512,3072]{1,0:T(8,128)(2,1)} %fusion.25), channel_id=1, source_target_pairs={{1,0},{2,1},{3,2},{5,4},{6,5},{7,6},{9,8},{10,9},{11,10},{13,12},{... | collective-permute-start | bytes 9437192 | tf_op jit(solution)/shard_map/ppermute | solution.py:54
  123.5 14.0 collective-permute-start.2
  125.8 69.0 %collective-permute-start.3 = (bf16[512,3072]{1,0:T(8,128)(2,1)}, bf16[512,3072]{1,0:T(8,128)(2,1)}, u32[]{:S(2)}, u32[]{:S(2)}) collective-permute-start(bf16[512,3072]{1,0:T(8,128)(2,1)} %collective-permute-done.1), channel_id=1, source_target_pairs={{1,0},{2,1},{5,4},{6,5},{9,8},{10,9},{13,12},{14,13},{17,16},{18,1... | collective-permute-start | bytes 9437192 | tf_op jit(solution)/shard_map/ppermute | solution.py:54
  131.8 66.7 %copy-start.14 = (bf16[2048,384]{0,1:T(8,128)(2,1)S(1)}, bf16[2048,384]{0,1:T(8,128)(2,1)}, u32[]{:S(2)}) copy-start(bf16[2048,384]{0,1:T(8,128)(2,1)} %copy.36) | copy-start | bytes 4718596
  194.8 70.2 %collective-permute-start.4 = (bf16[512,3072]{1,0:T(8,128)(2,1)}, bf16[512,3072]{1,0:T(8,128)(2,1)}, u32[]{:S(2)}, u32[]{:S(2)}) collective-permute-start(bf16[512,3072]{1,0:T(8,128)(2,1)} %collective-permute-done.2), channel_id=1, source_target_pairs={{2,3},{6,7},{10,11},{14,15},{18,19},{22,23},{26,27},{30,31}} | collective-permute-start | bytes 9437192 | tf_op jit(solution)/shard_map/ppermute | solution.py:54
  197.2 101.2 %collective-permute-start.5 = (bf16[512,3072]{1,0:T(8,128)(2,1)}, bf16[512,3072]{1,0:T(8,128)(2,1)}, u32[]{:S(2)}, u32[]{:S(2)}) collective-permute-start(bf16[512,3072]{1,0:T(8,128)(2,1)} %collective-permute-done.3), channel_id=1, source_target_pairs={{1,0},{5,4},{9,8},{13,12},{17,16},{21,20},{25,24},{29,28}} | collective-permute-start | bytes 9437192 | tf_op jit(solution)/shard_map/ppermute | solution.py:54
  198.5 66.5 %collective-permute-start.6 = (bf16[384,2048]{1,0:T(8,128)(2,1)S(1)}, bf16[384,2048]{1,0:T(8,128)(2,1)}, u32[]{:S(2)}, u32[]{:S(2)}) collective-permute-start(bf16[384,2048]{1,0:T(8,128)(2,1)S(1)} %bitcast.57), channel_id=1, source_target_pairs={{2,0},{3,1},{0,2},{1,3},{6,4},{7,5},{4,6},{5,7},{10,8},{11,9},{8,1... | collective-permute-start | bytes 4718600 | tf_op jit(solution)/shard_map/ppermute | solution.py:54
  298.4 264.8 %all-gather.17.cloned.1.call-start = ((), (), s32[]{:S(2)}) async-start(), calls=%async_computation.12 | async-start | bytes 14155776 | tf_op jit(solution)/shard_map/all_gather | solution.py:432
  299.0 416.0 %all-gather.21.cloned.1.call-start = ((), (), s32[]{:S(2)}) async-start(), calls=%async_computation.14 | async-start | bytes 14155776 | tf_op jit(solution)/shard_map/all_gather | solution.py:432
  314.9 101.9 %collective-permute-start.8 = (bf16[512,3072]{1,0:T(8,128)(2,1)}, bf16[512,3072]{1,0:T(8,128)(2,1)}, u32[]{:S(2)}, u32[]{:S(2)}) collective-permute-start(bf16[512,3072]{1,0:T(8,128)(2,1)} %fusion.31), channel_id=1, source_target_pairs={{0,1},{1,0},{2,3},{3,2},{4,5},{5,4},{6,7},{7,6},{8,9},{9,8},{10,11... | collective-permute-start | bytes 9437192 | tf_op jit(solution)/shard_map/ppermute | solution.py:54
  314.9 99.7 %collective-permute-start.7 = (bf16[384,2048]{1,0:T(8,128)(2,1)}, bf16[384,2048]{1,0:T(8,128)(2,1)}, u32[]{:S(2)}, u32[]{:S(2)}) collective-permute-start(bf16[384,2048]{1,0:T(8,128)(2,1)} %param.25), channel_id=1, source_target_pairs={{2,0},{3,1},{0,2},{1,3},{6,4},{7,5},{4,6},{5,7},{10,8},{11,9},{8,1... | collective-permute-start | bytes 4718600 | tf_op jit(solution)/shard_map/ppermute | solution.py:54
  416.9 298.1 %all-gather.23.cloned.1.call-start = ((), (), s32[]{:S(2)}) async-start(), calls=%async_computation.15 | async-start | bytes 14155776 | tf_op jit(solution)/shard_map/all_gather | solution.py:432
  423.9 102.6 %collective-permute-start.9 = (bf16[512,3072]{1,0:T(8,128)(2,1)}, bf16[512,3072]{1,0:T(8,128)(2,1)}, u32[]{:S(2)}, u32[]{:S(2)}) collective-permute-start(bf16[512,3072]{1,0:T(8,128)(2,1)} %convolution_convert_fusion.6), channel_id=1, source_target_pairs={{0,1},{4,5},{8,9},{12,13},{16,17},{20,21},{24,25},{28,29}} | collective-permute-start | bytes 9437192 | tf_op jit(solution)/shard_map/ppermute | solution.py:54
  427.4 99.2 %collective-permute-start.10 = (bf16[512,3072]{1,0:T(8,128)(2,1)}, bf16[512,3072]{1,0:T(8,128)(2,1)}, u32[]{:S(2)}, u32[]{:S(2)}) collective-permute-start(bf16[512,3072]{1,0:T(8,128)(2,1)} %convolution_convert_fusion.6), channel_id=1, source_target_pairs={{3,2},{7,6},{11,10},{15,14},{19,18},{23,22},{27,26},{31,30}} | collective-permute-start | bytes 9437192 | tf_op jit(solution)/shard_map/ppermute | solution.py:54
  430.0 96.6 %collective-permute-start.11 = (bf16[384,2048]{1,0:T(8,128)(2,1)}, bf16[384,2048]{1,0:T(8,128)(2,1)}, u32[]{:S(2)}, u32[]{:S(2)}) collective-permute-start(bf16[384,2048]{1,0:T(8,128)(2,1)} %param.26), channel_id=1, source_target_pairs={{2,0},{3,1},{0,2},{1,3},{6,4},{7,5},{4,6},{5,7},{10,8},{11,9},{8,1... | collective-permute-start | bytes 4718600 | tf_op jit(solution)/shard_map/ppermute | solution.py:54
  526.6 592.3 %reduce-scatter.9.cloned.1.call-start = ((), (), s32[]{:S(2)}) async-start(), calls=%async_computation.16 | async-start | bytes 14155776 | tf_op jit(solution)/shard_map/reduce_scatter | solution.py:557
  534.2 70.6 %collective-permute-start.12 = (bf16[512,3072]{1,0:T(8,128)(2,1)}, bf16[512,3072]{1,0:T(8,128)(2,1)}, u32[]{:S(2)}, u32[]{:S(2)}) collective-permute-start(bf16[512,3072]{1,0:T(8,128)(2,1)} %get-tuple-element.130), channel_id=1, source_target_pairs={{0,1},{1,2},{4,5},{5,6},{8,9},{9,10},{12,13},{13,14},{16,17},{17,1... | collective-permute-start | bytes 9437192 | tf_op jit(solution)/shard_map/ppermute | solution.py:54
  542.1 62.7 %collective-permute-start.13 = (bf16[512,3072]{1,0:T(8,128)(2,1)}, bf16[512,3072]{1,0:T(8,128)(2,1)}, u32[]{:S(2)}, u32[]{:S(2)}) collective-permute-start(bf16[512,3072]{1,0:T(8,128)(2,1)} %get-tuple-element.131), channel_id=1, source_target_pairs={{3,2},{2,1},{7,6},{6,5},{11,10},{10,9},{15,14},{14,13},{19,18},{18... | collective-permute-start | bytes 9437192 | tf_op jit(solution)/shard_map/ppermute | solution.py:54
  563.2 124.6 %copy-start.19 = (bf16[512,3072]{1,0:T(8,128)(2,1)S(1)}, bf16[512,3072]{1,0:T(8,128)(2,1)}, u32[]{:S(2)}) copy-start(bf16[512,3072]{1,0:T(8,128)(2,1)} %convolution_convert_fusion.9) | copy-start | bytes 9437188
  611.3 72.2 %collective-permute-start.14 = (bf16[512,3072]{1,0:T(8,128)(2,1)S(1)}, bf16[512,3072]{1,0:T(8,128)(2,1)S(1)}, u32[]{:S(2)}, u32[]{:S(2)}) collective-permute-start(bf16[512,3072]{1,0:T(8,128)(2,1)S(1)} %get-tuple-element.135), channel_id=1, source_target_pairs={{0,1},{1,2},{2,3},{4,5},{5,6},{6,7},{8,9},{9,10},{10,11},{12,13},{... | collective-permute-start | bytes 9437192 | tf_op jit(solution)/shard_map/ppermute | solution.py:54
  619.4 68.3 %collective-permute-start.15 = (bf16[512,3072]{1,0:T(8,128)(2,1)S(1)}, bf16[512,3072]{1,0:T(8,128)(2,1)S(1)}, u32[]{:S(2)}, u32[]{:S(2)}) collective-permute-start(bf16[512,3072]{1,0:T(8,128)(2,1)S(1)} %get-tuple-element.136), channel_id=1, source_target_pairs={{3,2},{2,1},{1,0},{7,6},{6,5},{5,4},{11,10},{10,9},{9,8},{15,14},{... | collective-permute-start | bytes 9437192 | tf_op jit(solution)/shard_map/ppermute | solution.py:54
  693.8 65.7 %collective-permute-start.16 = (bf16[512,3072]{1,0:T(8,128)(2,1)}, bf16[512,3072]{1,0:T(8,128)(2,1)S(1)}, u32[]{:S(2)}, u32[]{:S(2)}) collective-permute-start(bf16[512,3072]{1,0:T(8,128)(2,1)} %multiply_convert_fusion.1.x_ref), channel_id=1, source_target_pairs={{0,1},{1,0},{2,3},{3,2},{4,5},{5,4},{6,7},{7,6},{8,9},{9,8},{10,11... | collective-permute-start | bytes 9437192 | tf_op jit(solution)/shard_map/ppermute | solution.py:54
  797.9 614.3 %reduce-scatter.11.cloned.1.call-start = ((), (), s32[]{:S(2)}) async-start(), calls=%async_computation.17 | async-start | bytes 14155776 | tf_op jit(solution)/shard_map/reduce_scatter | solution.py:557
  816.9 797.9 %reduce-scatter.23.cloned.1.call-start = ((), (), s32[]{:S(2)}) async-start(), calls=%async_computation.23 | async-start | bytes 14155776 | tf_op jit(solution)/shard_map/reduce_scatter | solution.py:557
  855.6 764.2 %reduce-scatter.21.cloned.1.call-start = ((), (), s32[]{:S(2)}) async-start(), calls=%async_computation.22 | async-start | bytes 14155776 | tf_op jit(solution)/shard_map/reduce_scatter | solution.py:557
  891.7 66.2 %collective-permute-start.17 = (bf16[512,3072]{1,0:T(8,128)(2,1)}, bf16[512,3072]{1,0:T(8,128)(2,1)}, u32[]{:S(2)}, u32[]{:S(2)}) collective-permute-start(bf16[512,3072]{1,0:T(8,128)(2,1)} %shard_map.238), channel_id=1, source_target_pairs={{0,1},{1,0},{2,3},{3,2},{4,5},{5,4},{6,7},{7,6},{8,9},{9,8},{10,11... | collective-permute-start | bytes 9437192 | tf_op jit(solution)/shard_map/ppermute | solution.py:54
  910.4 713.5 %reduce-scatter.15.cloned.1.call-start = ((), (), s32[]{:S(2)}) async-start(), calls=%async_computation.19 | async-start | bytes 5308416 | tf_op jit(solution)/shard_map/reduce_scatter | solution.py:557
  973.3 67.6 %collective-permute-start.18 = (bf16[512,3072]{1,0:T(8,128)(2,1)}, bf16[512,3072]{1,0:T(8,128)(2,1)}, u32[]{:S(2)}, u32[]{:S(2)}) collective-permute-start(bf16[512,3072]{1,0:T(8,128)(2,1)} %get-tuple-element.156), channel_id=1, source_target_pairs={{0,1},{1,2},{2,3},{4,5},{5,6},{6,7},{8,9},{9,10},{10,11},{12,13},{... | collective-permute-start | bytes 9437192 | tf_op jit(solution)/shard_map/ppermute | solution.py:54
  978.3 68.3 %collective-permute-start.19 = (bf16[512,3072]{1,0:T(8,128)(2,1)}, bf16[512,3072]{1,0:T(8,128)(2,1)}, u32[]{:S(2)}, u32[]{:S(2)}) collective-permute-start(bf16[512,3072]{1,0:T(8,128)(2,1)} %get-tuple-element.156), channel_id=1, source_target_pairs={{1,0},{2,1},{3,2},{5,4},{6,5},{7,6},{9,8},{10,9},{11,10},{13,12},{... | collective-permute-start | bytes 9437192 | tf_op jit(solution)/shard_map/ppermute | solution.py:54
  1046.6 30.7 %collective-permute-start.20 = (bf16[512,3072]{1,0:T(8,128)(2,1)}, bf16[512,3072]{1,0:T(8,128)(2,1)}, u32[]{:S(2)}, u32[]{:S(2)}) collective-permute-start(bf16[512,3072]{1,0:T(8,128)(2,1)} %collective-permute-done.18), channel_id=1, source_target_pairs={{1,2},{2,3},{5,6},{6,7},{9,10},{10,11},{13,14},{14,15},{17,18},{18... | collective-permute-start | bytes 9437192 | tf_op jit(solution)/shard_map/ppermute | solution.py:54
  1048.9 70.0 %collective-permute-start.21 = (bf16[512,3072]{1,0:T(8,128)(2,1)}, bf16[512,3072]{1,0:T(8,128)(2,1)}, u32[]{:S(2)}, u32[]{:S(2)}) collective-permute-start(bf16[512,3072]{1,0:T(8,128)(2,1)} %collective-permute-done.19), channel_id=1, source_target_pairs={{1,0},{2,1},{5,4},{6,5},{9,8},{10,9},{13,12},{14,13},{17,16},{18,1... | collective-permute-start | bytes 9437192 | tf_op jit(solution)/shard_map/ppermute | solution.py:54
  1118.9 111.9 %collective-permute-start.22 = (bf16[512,3072]{1,0:T(8,128)(2,1)}, bf16[512,3072]{1,0:T(8,128)(2,1)S(1)}, u32[]{:S(2)}, u32[]{:S(2)}) collective-permute-start(bf16[512,3072]{1,0:T(8,128)(2,1)} %collective-permute-done.20), channel_id=1, source_target_pairs={{2,3},{6,7},{10,11},{14,15},{18,19},{22,23},{26,27},{30,31}} | collective-permute-start | bytes 9437192 | tf_op jit(solution)/shard_map/ppermute | solution.py:54
  1119.8 112.2 %collective-permute-start.23 = (bf16[512,3072]{1,0:T(8,128)(2,1)}, bf16[512,3072]{1,0:T(8,128)(2,1)S(1)}, u32[]{:S(2)}, u32[]{:S(2)}) collective-permute-start(bf16[512,3072]{1,0:T(8,128)(2,1)} %collective-permute-done.21), channel_id=1, source_target_pairs={{1,0},{5,4},{9,8},{13,12},{17,16},{21,20},{25,24},{29,28}} | collective-permute-start | bytes 9437192 | tf_op jit(solution)/shard_map/ppermute | solution.py:54
  1164.3 66.6 %collective-permute-start.24 = (bf16[384,2048]{1,0:T(8,128)(2,1)}, bf16[384,2048]{1,0:T(8,128)(2,1)S(1)}, u32[]{:S(2)}, u32[]{:S(2)}) collective-permute-start(bf16[384,2048]{1,0:T(8,128)(2,1)} %reduce-scatter.9.cloned.1.call-done), channel_id=1, source_target_pairs={{0,2},{1,3},{2,0},{3,1},{4,6},{5,7},{6,4},{7,5},{8,10},{9,11},{10,... | collective-permute-start | bytes 4718600 | tf_op jit(solution)/shard_map/ppermute | solution.py:54
  1309.3 319.5 %reduce-scatter.13.cloned.1.call-start = ((), (), s32[]{:S(2)}) async-start(), calls=%async_computation.18 | async-start | bytes 8847360 | tf_op jit(solution)/shard_map/reduce_scatter | solution.py:557
  1332.2 356.7 %reduce-scatter.17.cloned.1.call-start = ((), (), s32[]{:S(2)}) async-start(), calls=%async_computation.20 | async-start | bytes 14155776 | tf_op jit(solution)/shard_map/reduce_scatter | solution.py:557
  1332.7 461.6 %reduce-scatter.19.cloned.1.call-start = ((), (), s32[]{:S(2)}) async-start(), calls=%async_computation.21 | async-start | bytes 14155776 | tf_op jit(solution)/shard_map/reduce_scatter | solution.py:557
  1333.3 86.8 %copy-start.31 = (bf16[2,3072]{1,0:T(2,128)(2,1)S(1)}, bf16[2,3072]{1,0:T(2,128)(2,1)}, u32[]{:S(2)}) copy-start(bf16[2,3072]{1,0:T(2,128)(2,1)} %copy-done.30) | copy-start | bytes 36868
  1333.3 69.3 %collective-permute-start.25 = (bf16[512,3072]{1,0:T(8,128)(2,1)S(1)}, bf16[512,3072]{1,0:T(8,128)(2,1)}, u32[]{:S(2)}, u32[]{:S(2)}) collective-permute-start(bf16[512,3072]{1,0:T(8,128)(2,1)S(1)} %shard_map.236), channel_id=1, source_target_pairs={{0,1},{1,0},{2,3},{3,2},{4,5},{5,4},{6,7},{7,6},{8,9},{9,8},{10,11... | collective-permute-start | bytes 9437192 | tf_op jit(solution)/shard_map/ppermute | solution.py:54
  1412.2 104.3 %collective-permute-start.26 = (bf16[512,3072]{1,0:T(8,128)(2,1)}, bf16[512,3072]{1,0:T(8,128)(2,1)}, u32[]{:S(2)}, u32[]{:S(2)}) collective-permute-start(bf16[512,3072]{1,0:T(8,128)(2,1)} %convolution_convert_fusion.10), channel_id=1, source_target_pairs={{0,1},{4,5},{8,9},{12,13},{16,17},{20,21},{24,25},{28,29}} | collective-permute-start | bytes 9437192 | tf_op jit(solution)/shard_map/ppermute | solution.py:54
  1417.6 99.0 %collective-permute-start.27 = (bf16[512,3072]{1,0:T(8,128)(2,1)}, bf16[512,3072]{1,0:T(8,128)(2,1)}, u32[]{:S(2)}, u32[]{:S(2)}) collective-permute-start(bf16[512,3072]{1,0:T(8,128)(2,1)} %convolution_convert_fusion.10), channel_id=1, source_target_pairs={{3,2},{7,6},{11,10},{15,14},{19,18},{23,22},{27,26},{31,30}} | collective-permute-start | bytes 9437192 | tf_op jit(solution)/shard_map/ppermute | solution.py:54
  1428.8 87.8 %collective-permute-start.28 = (bf16[384,2048]{1,0:T(8,128)(2,1)}, bf16[384,2048]{1,0:T(8,128)(2,1)S(1)}, u32[]{:S(2)}, u32[]{:S(2)}) collective-permute-start(bf16[384,2048]{1,0:T(8,128)(2,1)} %reduce-scatter.11.cloned.1.call-done), channel_id=1, source_target_pairs={{0,2},{1,3},{2,0},{3,1},{4,6},{5,7},{6,4},{7,5},{8,10},{9,11},{10,... | collective-permute-start | bytes 4718600 | tf_op jit(solution)/shard_map/ppermute | solution.py:54
  1436.8 100.8 %copy-start.11 = (bf16[512,3072]{1,0:T(8,128)(2,1)}, bf16[512,3072]{1,0:T(8,128)(2,1)S(1)}, u32[]{:S(2)}) copy-start(bf16[512,3072]{1,0:T(8,128)(2,1)S(1)} %convolution_convert_fusion.13) | copy-start | bytes 9437188
  1436.8 79.7 %copy-start.8 = (bf16[512,3072]{1,0:T(8,128)(2,1)S(1)}, bf16[512,3072]{1,0:T(8,128)(2,1)}, u32[]{:S(2)}) copy-start(bf16[512,3072]{1,0:T(8,128)(2,1)} %copy-done.7) | copy-start | bytes 9437188
  1436.8 79.7 %copy-start.10 = (bf16[512,3072]{1,0:T(8,128)(2,1)S(1)}, bf16[512,3072]{1,0:T(8,128)(2,1)}, u32[]{:S(2)}) copy-start(bf16[512,3072]{1,0:T(8,128)(2,1)} %copy-done.9) | copy-start | bytes 9437188
  1436.9 104.9 %slice-start = ((s8[6291456]{0:T(1024)(128)(4,1)}), s8[4194304]{0:T(1024)(128)(4,1)S(1)}, s32[]{:S(2)}) async-start(s8[6291456]{0:T(1024)(128)(4,1)} %bitcast.54), calls=%async_computation.24 | async-start | bytes 8388608
  1447.6 94.2 %slice-start.1 = ((s8[6291456]{0:T(1024)(128)(4,1)}), s8[2097152]{0:T(1024)(128)(4,1)S(1)}, s32[]{:S(2)}) async-start(s8[6291456]{0:T(1024)(128)(4,1)} %bitcast.54), calls=%async_computation.25 | async-start | bytes 4194304
  1527.5 71.4 %collective-permute-start.29 = (bf16[512,3072]{1,0:T(8,128)(2,1)}, bf16[512,3072]{1,0:T(8,128)(2,1)}, u32[]{:S(2)}, u32[]{:S(2)}) collective-permute-start(bf16[512,3072]{1,0:T(8,128)(2,1)} %get-tuple-element.177), channel_id=1, source_target_pairs={{0,1},{1,2},{4,5},{5,6},{8,9},{9,10},{12,13},{13,14},{16,17},{17,1... | collective-permute-start | bytes 9437192 | tf_op jit(solution)/shard_map/ppermute | solution.py:54
  1535.1 63.8 %collective-permute-start.30 = (bf16[512,3072]{1,0:T(8,128)(2,1)}, bf16[512,3072]{1,0:T(8,128)(2,1)}, u32[]{:S(2)}, u32[]{:S(2)}) collective-permute-start(bf16[512,3072]{1,0:T(8,128)(2,1)} %get-tuple-element.178), channel_id=1, source_target_pairs={{3,2},{2,1},{7,6},{6,5},{11,10},{10,9},{15,14},{14,13},{19,18},{18... | collective-permute-start | bytes 9437192 | tf_op jit(solution)/shard_map/ppermute | solution.py:54
  1541.8 57.1 %copy-start.13 = (bf16[512,3072]{1,0:T(8,128)(2,1)S(1)}, bf16[512,3072]{1,0:T(8,128)(2,1)}, u32[]{:S(2)}) copy-start(bf16[512,3072]{1,0:T(8,128)(2,1)} %convolution_convert_fusion.12) | copy-start | bytes 9437188
  1604.9 71.2 %collective-permute-start.31 = (bf16[512,3072]{1,0:T(8,128)(2,1)}, bf16[512,3072]{1,0:T(8,128)(2,1)}, u32[]{:S(2)}, u32[]{:S(2)}) collective-permute-start(bf16[512,3072]{1,0:T(8,128)(2,1)} %get-tuple-element.181), channel_id=1, source_target_pairs={{0,1},{1,2},{2,3},{4,5},{5,6},{6,7},{8,9},{9,10},{10,11},{12,13},{... | collective-permute-start | bytes 9437192 | tf_op jit(solution)/shard_map/ppermute | solution.py:54
  1613.5 68.4 %collective-permute-start.32 = (bf16[512,3072]{1,0:T(8,128)(2,1)}, bf16[512,3072]{1,0:T(8,128)(2,1)}, u32[]{:S(2)}, u32[]{:S(2)}) collective-permute-start(bf16[512,3072]{1,0:T(8,128)(2,1)} %get-tuple-element.182), channel_id=1, source_target_pairs={{3,2},{2,1},{1,0},{7,6},{6,5},{5,4},{11,10},{10,9},{9,8},{15,14},{... | collective-permute-start | bytes 9437192 | tf_op jit(solution)/shard_map/ppermute | solution.py:54
  1626.0 55.9 %copy-start.2 = (bf16[512,3072]{1,0:T(8,128)(2,1)S(1)}, bf16[512,3072]{1,0:T(8,128)(2,1)}, u32[]{:S(2)}) copy-start(bf16[512,3072]{1,0:T(8,128)(2,1)} %param.15) | copy-start | bytes 9437188
  1626.0 55.9 %copy-start.33 = (f32[1,3072]{1,0:T(1,128)S(1)}, f32[1,3072]{1,0:T(1,128)}, u32[]{:S(2)}) copy-start(f32[1,3072]{1,0:T(1,128)} %copy-done.32) | copy-start | bytes 36868
  1626.0 55.9 %copy-start.42 = (f32[512]{0:T(512)S(1)}, f32[512]{0:T(512)}, u32[]{:S(2)}) copy-start(f32[512]{0:T(512)} %copy-done.41) | copy-start | bytes 6148
  1688.9 65.5 %collective-permute-start.33 = (bf16[384,2048]{1,0:T(8,128)(2,1)}, bf16[384,2048]{1,0:T(8,128)(2,1)}, u32[]{:S(2)}, u32[]{:S(2)}) collective-permute-start(bf16[384,2048]{1,0:T(8,128)(2,1)} %reduce-scatter.17.cloned.1.call-done), channel_id=1, source_target_pairs={{0,2},{1,3},{2,0},{3,1},{4,6},{5,7},{6,4},{7,5},{8,10},{9,11},{10,... | collective-permute-start | bytes 4718600 | tf_op jit(solution)/shard_map/ppermute | solution.py:54
  1690.3 64.1 %copy-start.34 = (f32[2,3072]{1,0:T(2,128)S(1)}, f32[2,3072]{1,0:T(2,128)}, u32[]{:S(2)}) copy-start(f32[2,3072]{1,0:T(2,128)} %pad_maximum_fusion.7) | copy-start | bytes 73732
  (43 other events, 708.4 us)
Sparse Core Ops, SparseCore 0:
  17.1 54.8 all-gather.8
  73.9 39.7 all-gather.10
  116.1 72.1 all-gather.12
  190.1 72.1 all-gather.14
  298.6 69.3 all-gather.18
  369.7 72.1 all-gather.16
  443.8 72.1 all-gather.20
  526.7 73.2 all-gather.22
  798.0 90.0 reduce-scatter.8
  891.5 92.3 reduce-scatter.10
  987.4 92.3 reduce-scatter.22
  1083.2 92.3 reduce-scatter.20
  1309.5 53.5 reduce-scatter.14
  1366.8 69.3 reduce-scatter.12
  1439.5 92.3 reduce-scatter.16
  1535.3 92.3 reduce-scatter.18

commit v2 on v1

--- a/solution.py
+++ b/solution.py
@@ -18,6 +18,7 @@
 NT = (((1,), (1,)), ((), ()))
 NN = (((1,), (0,)), ((), ()))
 TN = (((0,), (0,)), ((), ()))
+HIDES = pl.CostEstimate(flops=1, transcendentals=0, bytes_accessed=1)
 
 
 def dot(a, b, dims, out=F32):
@@ -49,26 +50,25 @@
     return out
 
 
-def travel(items, work=lambda: ()):
+def travel(items, work=lambda gate: ()):
     arrays = lax.optimization_barrier(tuple(array for array, _ in items))
     moved = [lax.ppermute(array, "tensor", pairs) for array, (_, pairs) in zip(arrays, items)]
-    out = lax.optimization_barrier((*moved, *work()))
-    return list(out[: len(moved)])
-
-
-def line_gather(own, n, use, fill=lambda step: (), along=lambda step: ()):
+    out = lax.optimization_barrier((*moved, *work(arrays[0])))
+    return list(out[: len(moved)]), list(out[len(moved) :])
+
+
+def line_gather(own, n, use, fill=lambda step, gate: (), along=lambda step: (), took=lambda step, arrived, filled: None):
     place = lax.axis_index("tensor")
     order = arrival_order(n)
     right = left = own
     from_left, from_right = [own], [own]
-    slots, used, others = [own], [], []
+    slots, used = [own], []
     for d in range(1, n):
 
-        def work():
-            used.append(use(d - 1, slots[d - 1]))
-            return (used[-1], *fill(d))
-
-        right, left, *more = travel(
+        def work(gate):
+            return (use(d - 1, slots[d - 1]), *fill(d, gate))
+
+        (right, left, *more), (result, *filled) = travel(
             [
                 (right, [(i, i + 1) for i in range(d - 1, n - 1)]),
                 (left, [(i + 1, i) for i in range(n - d)]),
@@ -76,7 +76,8 @@
             ],
             work,
         )
-        others += more
+        used.append(result)
+        took(d, more, filled)
         from_left.append(right)
         from_right.append(left)
         slots.append(
@@ -89,36 +90,38 @@
             )
         )
     used.append(use(n - 1, slots[-1]))
-    return slots, used, others
-
-
-def line_reduce(part, n, fill=lambda step, parts: (), along=lambda step: ()):
+    return slots, used
+
+
+def line_reduce(part, n, fill=lambda step, gate: (), along=lambda step: (), took=lambda step, arrived, filled: None):
     place = lax.axis_index("tensor")
     parts = [None] * n
     parts[n - 1] = lax.optimization_barrier(part(n - 1))
     order = [[i] + row for i, row in enumerate(arrival_order(n))]
     right = left = None
-    others = []
+
+    def add(value, *sums):
+        if right is None:
+            return value
+        return (value.astype(F32) + sum(one.astype(F32) for one in sums)).astype(BF16)
+
     for k in range(1, n):
-        to_right = pick(
-            place,
-            [parts[order[i].index(i + n - k)] if i < k else parts[n - k] for i in range(n)],
-        )
-        to_left = pick(
-            place,
-            [parts[order[i].index(i - n + k)] if i >= n - k else parts[n - k] for i in range(n)],
-        )
-        if right is not None:
-            to_right = (to_right.astype(F32) + right.astype(F32)).astype(BF16)
-            to_left = (to_left.astype(F32) + left.astype(F32)).astype(BF16)
-
-        def work():
-            if k == 1:
-                for s in range(n - 2, -1, -1):
-                    parts[s] = lax.optimization_barrier(part(s))
-            return (*fill(k, parts), *(parts[: n - 1] if k == 1 else ()))
-
-        right, left, *more = travel(
+        rightward = [parts[order[i].index(i + n - k)] if i < k else parts[n - k] for i in range(n)]
+        leftward = [parts[order[i].index(i - n + k)] if i >= n - k else parts[n - k] for i in range(n)]
+        if 2 * k <= n:
+            choice = [r if i < k else l for i, (r, l) in enumerate(zip(rightward, leftward))]
+            to_right = to_left = add(pick(place, choice), right, left)
+        else:
+            to_right, to_left = add(pick(place, rightward), right), add(pick(place, leftward), left)
+
+        coming = list(range(n - 2, 0, -1)) if k == 1 else []
+        if k == n - 1:
+            coming.append(0)
+
+        def work(gate):
+            return (*(part(s) for s in coming), *fill(k, gate))
+
+        (right, left, *more), worked = travel(
             [
                 (to_right, [(i, i + 1) for i in range(k)]),
                 (to_left, [(n - 1 - i, n - 2 - i) for i in range(k)]),
@@ -126,12 +129,19 @@
             ],
             work,
         )
-        others += more
-    return parts[0].astype(F32) + (right.astype(F32) + left.astype(F32)), others
-
-
-def pairs_of(n):
-    return [(i, i ^ 1) for i in range(n)]
+        for s, one in zip(coming, worked):
+            parts[s] = one
+        took(k, more, worked[len(coming) :])
+    return parts[0].astype(F32) + (right.astype(F32) + left.astype(F32))
+
+
+def halves(n, pairs):
+    ends = [(a, b) for a, b in pairs if a < n // 4 or a >= n - n // 4]
+    return ends, [pair for pair in pairs if pair not in ends]
+
+
+def joined(first, second):
+    return first + second
 
 
 def attend_forward(n, heads, rows, c, place_ref, *refs):
@@ -268,7 +278,6 @@
         whole((every, 1)),
     ]
     lse_spec = pl.BlockSpec((1, 8, every), lambda g, place: (g, 0, 0))
-    pairs = every * (every + rows) // 2 * heads_q
     params = pltpu.CompilerParams(vmem_limit_bytes=58 << 20)
     forward = pl.pallas_call(
         functools.partial(attend_forward, n, heads, rows, c),
@@ -289,9 +298,7 @@
             jax.ShapeDtypeStruct((heads_kv, 8, every), F32),
         ],
         compiler_params=params,
-        cost_estimate=pl.CostEstimate(
-            flops=pairs * 4 * HEAD_SIZE, transcendentals=pairs, bytes_accessed=every * heads_kv * wide * 8
-        ),
+        cost_estimate=HIDES,
     )
     backward = pl.pallas_call(
         functools.partial(attend_backward, n, heads, rows, c),
@@ -313,9 +320,7 @@
         ),
         out_shape=jax.ShapeDtypeStruct((every, heads_kv * wide), BF16),
         compiler_params=params,
-        cost_estimate=pl.CostEstimate(
-            flops=pairs * 10 * HEAD_SIZE, transcendentals=pairs, bytes_accessed=every * heads_kv * wide * 10
-        ),
+        cost_estimate=HIDES,
     )
     return forward, backward
 
@@ -352,11 +357,7 @@
         out_shape=[jax.ShapeDtypeStruct((2 * rows, hidden), BF16)] * 3,
         input_output_aliases={4 + i: i for i in range(len(before))},
         compiler_params=pltpu.CompilerParams(vmem_limit_bytes=50 << 20),
-        cost_estimate=pl.CostEstimate(
-            flops=4 * rows * width * hidden,
-            transcendentals=rows * hidden,
-            bytes_accessed=4 * width * hidden + 2 * rows * width + 10 * rows * hidden,
-        ),
+        cost_estimate=HIDES,
     )(x, w_gate, w_up, gm, *before)
 
 
@@ -368,7 +369,7 @@
     refs[-1][...] = total.astype(refs[-1].dtype)
 
 
-def spread(acts, weights, part, out):
+def spread(acts, weights, part, out, cost=HIDES):
     rows, hidden = acts[0].shape[0] // 2, acts[0].shape[1]
     width = weights[0].shape[0]
     tile = 256 if width % 256 == 0 else width
@@ -381,11 +382,7 @@
         out_specs=pl.BlockSpec((rows, tile), lambda j: (0, j)),
         out_shape=jax.ShapeDtypeStruct((rows, width), out),
         compiler_params=pltpu.CompilerParams(vmem_limit_bytes=50 << 20),
-        cost_estimate=pl.CostEstimate(
-            flops=2 * count * rows * width * hidden,
-            transcendentals=0,
-            bytes_accessed=count * 2 * hidden * (rows + width) + 4 * rows * width,
-        ),
+        cost_estimate=cost,
     )(*acts, *weights)
 
 
@@ -395,10 +392,8 @@
 
 def norm_back(grad_normed, source, inverse, gain):
     unit_rows = source * inverse
-    gain_term = jnp.sum(grad_normed * unit_rows, axis=0)
     scaled = grad_normed * gain
-    grad_source = inverse * (scaled - unit_rows * jnp.mean(scaled * unit_rows, axis=-1, keepdims=True))
-    return (grad_source, gain_term)
+    return inverse * (scaled - unit_rows * jnp.mean(scaled * unit_rows, axis=-1, keepdims=True))
 
 
 def shards(
@@ -449,11 +444,15 @@
     gain_one, gain_two = gains[0], gains[1]
     down_t = down_weight.T
 
-    def to_others(shard):
-        return [(shard, [((i + 2 * k) % n, i) for i in range(n)]) for k in range(1, slices)]
-
-    def to_owners(sums):
-        return [(one, [(i, (i + 2 * k) % n) for i in range(n)]) for k, one in enumerate(sums, 1)]
+    partners = halves(n, [(i, i ^ 1) for i in range(n)])
+    outward = [halves(n, [((i + 2 * k) % n, i) for i in range(n)]) for k in range(1, slices)]
+    homeward = [halves(n, [(i, (i + 2 * k) % n) for i in range(n)]) for k in range(1, slices)]
+
+    def to_others(shard, half):
+        return [(shard, pairs[half]) for pairs in outward]
+
+    def to_owners(sums, half):
+        return [(one, pairs[half]) for one, pairs in zip(sums, homeward)]
 
     w_down = [gather(down_t)]
     w_gate = [gather(gate_weight)]
@@ -483,149 +482,216 @@
     normed_one = (source * inv_one * gain_one).astype(BF16)
     grad_result = cotangent.astype(F32) * live
     grad_low = grad_result.astype(BF16)
-    slots_one, projected, moved = line_gather(
+    more = slices - 1
+    early = []
+    slots_one, projected = line_gather(
         after(normed_one, labels),
         n,
         lambda s, shard: dot(shard, w_qkv, NN),
-        lambda step: tables if step == 1 else (),
-        lambda step: to_others(down_t) if step == n - 1 else (),
-    )
-    w_down += [gather(shard) for shard in moved]
+        lambda step, gate: tables if step == 1 else (),
+        lambda step: {
+            n - 2: [(grad_low, partners[0])],
+            n - 1: to_others(down_t, 0) + to_others(gate_weight, 0),
+        }.get(step, ()),
+        lambda step, arrived, filled: early.extend(arrived),
+    )
+    low_ends, down_ends, gate_ends = early[0], early[1 : 1 + more], early[1 + more :]
     projected[n - 1] = after(projected[n - 1], w_out, w_down[0])
-    kept = []
-
-    def attention():
-        kept.extend(attend(slot_table, *projected, *tables))
-        return kept
-
-    gates, lows = lax.optimization_barrier((gate_weight, grad_low, projected[n - 1]))[:2]
-    *moved, grad_theirs = travel([*to_others(gates), (lows, pairs_of(n))], attention)
-    attended, rotated, lse = kept
-    w_gate += [gather(shard) for shard in moved]
-    grad_two = jnp.concatenate([grad_low, grad_theirs], axis=0)
-    grad_mixed = []
-
-    def while_out(step, parts):
+
+    def attention(gate):
+        return attend(slot_table, *projected, *tables)
+
+    downs, ups = lax.optimization_barrier((down_t, up_weight, projected[n - 1]))[:2]
+    moved, (attended, rotated, lse) = travel(to_others(downs, 1) + to_others(ups, 0), attention)
+    w_down += [gather(joined(a, b)) for a, b in zip(down_ends, moved[:more])]
+    up_ends = moved[more:]
+    grad_mixed, lows = [], []
+
+    def while_out(step, gate):
         if step == 1:
-            grad_mixed.append(dot(grad_two, w_down[0], NN))
-            return (w_gate[0], grad_mixed[0])
+            return (w_gate[0],)
+        if step == n - 1:
+            theirs = joined(low_ends, lows[0])
+            lows.append(theirs)
+            return (w_up[0], *(dot(jnp.concatenate([grad_low, theirs], axis=0), w, NN) for w in w_down))
+        return ()
+
+    def along_out(step):
+        if step == 1:
+            return to_others(gate_weight, 1) + to_others(up_weight, 1)
         if step == 2:
-            grad_mixed.extend(dot(grad_two, w, NN) for w in w_down[1:])
-            return (w_up[0], *grad_mixed[1:])
+            return [(grad_low, partners[1])]
         return ()
 
-    summed, moved = line_reduce(
-        lambda s: dot(after(attended, *moved)[s * rows : (s + 1) * rows], w_out, NT, BF16),
-        n,
-        while_out,
-        lambda step: to_others(up_weight) if step == 1 else (),
-    )
-    w_up += [gather(shard) for shard in moved]
+    def took_out(step, arrived, filled):
+        if step == 1:
+            w_gate.extend(gather(joined(a, b)) for a, b in zip(gate_ends, arrived[:more]))
+            w_up.extend(gather(joined(a, b)) for a, b in zip(up_ends, arrived[more:]))
+        elif step == n - 1:
+            grad_mixed.extend(filled[1:])
+        else:
+            lows.extend(arrived)
+
+    summed = line_reduce(
+        lambda s: dot(attended[s * rows : (s + 1) * rows], w_out, NT, BF16), n, while_out, along_out, took_out
+    )
     hidden = source + summed
+    grad_two = jnp.concatenate([grad_low, lows[1]], axis=0)
 
     inv_two = norm_inverse(hidden)
     normed_two = (hidden * inv_two * gain_two).astype(BF16)
-    mine = []
-
-    def own_rows():
-        mine.extend(gated(normed_two, g, u, gm, 0) for g, u, gm in zip(w_gate, w_up, grad_mixed))
-        return [one[0] for one in mine]
-
-    (two_theirs,) = travel([(normed_two, pairs_of(n))], own_rows)
-    both = [
-        gated(two_theirs, g, u, gm, 1, before) for g, u, gm, before in zip(w_gate, w_up, grad_mixed, mine)
-    ]
-    mixed, grad_gate, grad_up = zip(*both)
+
+    def own_rows(gate):
+        return [one for g, u, gm in zip(w_gate, w_up, grad_mixed) for one in gated(gate, g, u, gm, 0)]
+
+    (two_theirs,), mine = travel([(normed_two, partners[0] + partners[1])], own_rows)
     two = jnp.concatenate([normed_two, two_theirs], axis=0)
-    d_down = [None] * slices
-    d_down[1:] = [dot(grad_two, m, TN, BF16) for m in mixed[1:]]
-    grads, weights = list(grad_gate + grad_up), w_gate + w_up
-    theirs = spread([after(grads[0], *d_down[1:])] + grads[1:], weights, 1, BF16)
-    ours, d_up, d_gate = [], [None] * slices, [None] * slices
-
-    def own_sums():
-        ours.append(spread(grads, weights, 0, F32))
-        d_up[1:] = [dot(two, g, TN, BF16) for g in grad_up[1:]]
-        return (ours[0], *d_up[1:])
-
-    (from_theirs,) = travel([(theirs, pairs_of(n))], own_sums)
-    grad_normed_two = ours[0] + from_theirs.astype(F32)
-    grad_hidden_norm, gain_two_term = norm_back(grad_normed_two, hidden, inv_two, gain_two)
+    mixed, grad_gate, grad_up, d_down = [None] * slices, [None] * slices, [None] * slices, [None] * slices
+    rows_in = two_theirs
+    for k in range(slices - 1, -1, -1):
+        mixed[k], grad_gate[k], grad_up[k] = gated(rows_in, w_gate[k], w_up[k], grad_mixed[k], 1, mine[3 * k : 3 * k + 3])
+        if k > 0:
+            d_down[k] = dot(grad_two, mixed[k], TN, BF16)
+            rows_in = after(two_theirs, d_down[k])
+    grads, weights = grad_gate + grad_up, w_gate + w_up
+    theirs = spread(grads, weights, 1, BF16)
+    d_up, d_gate = [None] * slices, [None] * slices
+
+    def own_sums(gate):
+        return (
+            spread([after(grads[0], gate)] + grads[1:], weights, 0, F32),
+            *(dot(two, after(g, gate), TN, BF16) for g in grad_up[1:]),
+        )
+
+    (from_theirs,), (ours, *d_up[1:]) = travel([(theirs, partners[0] + partners[1])], own_sums)
+    grad_normed_two = ours + from_theirs.astype(F32)
+    grad_hidden_norm = norm_back(grad_normed_two, hidden, inv_two, gain_two)
     grad_hidden = grad_result + grad_hidden_norm
 
     def owner_sum(partial):
         return lax.psum_scatter(partial, "dp", scatter_dimension=0, tiled=True)
 
-    results = []
-
-    def while_gather(step):
+    results, early = [], []
+
+    def d_of(left, right, gate):
+        return dot(left, after(right, gate), TN, BF16)
+
+    def result_rows(part, out, gate, cost=HIDES):
+        return spread([after(mixed[0], gate), *mixed[1:]], w_down, part, out, cost)
+
+    def while_gather(step, gate):
         if step == 1:
-            d_gate[1:] = [dot(two, g, TN, BF16) for g in grad_gate[1:]]
-            d_down[0] = dot(grad_two, mixed[0], TN, BF16)
-            return (*d_gate[1:], d_down[0])
+            flops = 2 * rows * width * slices * gate_weight.shape[1]
+            cost = pl.CostEstimate(flops=flops, transcendentals=0, bytes_accessed=flops // rows)
+            return (result_rows(1, BF16, gate, cost), *(d_of(two, g, gate) for g in grad_gate[1:]))
         if step == 2:
-            d_up[0] = dot(two, grad_up[0], TN, BF16)
-            d_gate[0] = dot(two, grad_gate[0], TN, BF16)
-            return (d_up[0], d_gate[0])
-        results.extend((spread(mixed, w_down, 1, BF16), spread(mixed, w_down, 0, F32)))
-        return results
-
-    sums_down = [owner_sum(d) for d in d_down[1:]]
-    slots_back, grad_attended, back_down = line_gather(
+            return (result_rows(0, F32, gate), d_of(grad_two, mixed[0], gate))
+        if step == n - 1:
+            return (d_of(two, grad_up[0], gate),)
+        return ()
+
+    def took_gather(step, arrived, filled):
+        early.extend(arrived)
+        if step == 1:
+            results.append(filled[0])
+            d_gate[1:] = filled[1:]
+        elif step == 2:
+            results.append(filled[0])
+            d_down[0] = filled[1]
+        elif step == n - 1:
+            d_up[0] = filled[0]
+
+    sums = [jnp.concatenate([owner_sum(a), owner_sum(b)], axis=1) for a, b in zip(d_down[1:], d_up[1:])]
+    slots_back, grad_attended = line_gather(
         grad_hidden.astype(BF16),
         n,
         lambda s, shard: dot(shard, w_out, NN, BF16),
         while_gather,
-        lambda step: to_owners(sums_down) if step == n - 1 else (),
-    )
-    kept = []
-
-    def attention_back():
-        kept.append(attend_back(slot_table, *grad_attended, rotated, attended, lse, *tables))
-        return kept
-
-    (from_partner,) = travel([(after(results[0], grad_attended[n - 1]), pairs_of(n))], attention_back)
-    grad_qkv = kept[0]
-    result = hidden + (results[1] + from_partner.astype(F32))
-    output = (result * live).astype(BF16)
-    d_qkv = dot(jnp.concatenate(slots_one, axis=0), grad_qkv, TN, BF16)
-    d_out = dot(jnp.concatenate(slots_back, axis=0), after(attended, grad_qkv), TN, BF16)
-    gain_terms = []
-
-    def while_reduce(step, parts):
+        lambda step: {
+            2: [(results[0], partners[0])] if results else (),
+            n - 1: to_owners(sums, 0),
+        }.get(step, ()),
+        took_gather,
+    )
+    result_ends, sum_ends = early[0], early[1:]
+
+    def attention_back(gate):
+        return (
+            attend_back(slot_table, *grad_attended, rotated, attended, lse, *tables),
+            d_of(two, grad_gate[0], gate),
+            sum_down,
+        )
+
+    sums_gate = [owner_sum(d) for d in d_gate[1:]]
+    sum_down, sum_up = owner_sum(d_down[0]), owner_sum(d_up[0])
+    leaving = [after(one, grad_attended[n - 1]) for one in sums_gate]
+    moved, (grad_qkv, d_gate[0], _) = travel(to_owners(leaving, 0) + to_owners(leaving, 1), attention_back)
+    back_gate = [joined(a, b) for a, b in zip(moved[:more], moved[more:])]
+    back_down, back_up, outputs, d_own = [], [], [], []
+    sum_gate = owner_sum(d_gate[0])
+
+    def while_reduce(step, gate):
         if step == 1:
-            return (d_qkv, d_out)
+            return (d_of(jnp.concatenate(slots_one, axis=0), grad_qkv, gate), sum_up)
         if step == 2:
-            gain_one_term = sum(
-                jnp.sum(one.astype(F32) * part.astype(F32), axis=0) for one, part in zip(slots_one, parts)
-            )
-            gain_terms.append(jnp.stack([gain_one_term / gain_one, gain_two_term]))
-            return (gain_terms[0], output)
+            return (d_of(jnp.concatenate(slots_back, axis=0), attended, gate), sum_gate)
+        if step == n - 1:
+            from_partner = joined(result_ends, outputs[0])
+            result = hidden + (results[1] + after(from_partner, gate).astype(F32))
+            return ((result * live).astype(BF16),)
         return ()
 
-    sums_up = [owner_sum(d) for d in d_up[1:]]
-    sums_gate = [owner_sum(d) for d in d_gate[1:]]
-    grad_normed_one, back_up = line_reduce(
-        lambda s: dot(after(grad_qkv, from_partner)[s * rows : (s + 1) * rows], w_qkv, NT, BF16),
+    def along_reduce(step):
+        if step == 1:
+            return to_owners(sums, 1)
+        if step == 2:
+            return [(results[0], partners[1])]
+        return ()
+
+    def took_reduce(step, arrived, filled):
+        if step == 1:
+            for a, b in zip(sum_ends, arrived):
+                back = joined(a, b)
+                back_down.append(back[:, : down_t.shape[1]])
+                back_up.append(back[:, down_t.shape[1] :])
+            d_own.append(filled[0])
+        elif step == 2:
+            outputs.extend(arrived)
+            d_own.append(filled[0])
+        elif step == n - 1:
+            outputs.append(filled[0])
+
+    grad_normed_one = line_reduce(
+        lambda s: dot(grad_qkv[s * rows : (s + 1) * rows], w_qkv, NT, BF16),
         n,
         while_reduce,
-        lambda step: to_owners(sums_up) if step == 1 else (),
-    )
-    back_gate = travel(to_owners([after(one, grad_normed_one) for one in sums_gate]))
+        along_reduce,
+        took_reduce,
+    )
+    output = outputs[1]
 
     def whole(first, back):
-        return sum((one.astype(F32) for one in back), owner_sum(first).astype(F32))
-
-    grad_down_w = whole(d_down[0], back_down).T
-    grad_up_w = whole(d_up[0], back_up)
-    grad_gate_w = whole(d_gate[0], back_gate)
-    grad_out_w = owner_sum(d_out).astype(F32).T
-    grad_qkv_w = owner_sum(d_qkv).astype(F32)
-    grad_input_norm, _ = norm_back(grad_normed_one, source, inv_one, gain_one)
+        return sum((one.astype(F32) for one in back), first.astype(F32))
+
+    grad_down_w = whole(sum_down, back_down).T
+    grad_up_w = whole(sum_up, back_up)
+    grad_gate_w = whole(sum_gate, back_gate)
+    sum_qkv = owner_sum(d_own[0])
+    grad_qkv_w = sum_qkv.astype(F32)
+    grad_out_w = owner_sum(after(d_own[1], sum_qkv)).astype(F32).T
+    grad_input_norm = norm_back(grad_normed_one, source, inv_one, gain_one)
     grad_tokens = grad_hidden + grad_input_norm
-    gain_sums = lax.psum(after(gain_terms[0], *back_gate), ("dp", "tensor"))
-    owned = attn_gain.shape[0]
-    gain_own = lax.dynamic_slice_in_dim(gain_sums, lax.axis_index("dp") * owned, owned, 1)
+
+    def along_row(weight, grad):
+        return jnp.sum(weight.astype(F32) * grad, axis=1)
+
+    gain_parts = jnp.stack(
+        [
+            along_row(own_qkv, grad_qkv_w),
+            along_row(gate_weight, grad_gate_w) + along_row(up_weight, grad_up_w),
+        ]
+    )
+    gain_own = lax.psum(gain_parts, "tensor") / jnp.stack([attn_gain, mlp_gain]).astype(F32)
 
     def columns(offset, size):
         return jnp.concatenate(

time: 1820 us -> 1460 us (0.80)
  waiting for transfers between devices: 897 us -> 485 us
  starting transfers between devices: 86.9 us -> 134 us
  blocking collectives: 63 us -> 35.2 us
    ppermute x34 -> x40, waiting for transfers between devices: 887 us -> 419 us  [travel(): lax.ppermute(array, 'tensor', pairs)]
    ppermute x34 -> x40, starting transfers between devices: 86.1 us -> 133 us  [travel(): lax.ppermute(array, 'tensor', pairs)]
    reduce_scatter x8, waiting for transfers between devices: 0.03 us -> 42.2 us  [owner_sum(): return lax.psum_scatter(partial, 'dp', scatter_dimension=0, tiled=True)]
    psum x1, blocking collectives: 39.2 us -> 11.5 us  [shards(): lax.psum(gain_parts, 'tensor')]
    convert_element_type x6 -> x5, other arithmetic: 40.4 us -> 34.9 us  [the longest x4 28.3 us: add(): (value.astype(F32) + sum((one.astype(F32) for one in sums))).astype(BF16)]
  transfers between devices with their start and end apart: 50 -> 56, of which waited for: 24 -> 27; matrix products, arithmetic and copies ran while one was open for 23% -> 30% of each run, Pallas kernels for 15% -> 19%
where the time goes in v2:
time: 1460 us; the launch traced here: 1450 us
  waiting for transfers between devices  485 us (33%)
  matrix products  304 us (21%)
  Pallas kernels  303 us (21%)
  other arithmetic  142 us (10%)
  starting transfers between devices  134 us (9%)
  blocking collectives  35.2 us (2%)
  local copies, waits for them, and re-layouts  33.7 us (2%)
  between operations  15.7 us (1%)
    ppermute x40, waiting for transfers between devices, travel(): lax.ppermute(array, 'tensor', pairs)  419 us
    dot_general x26, matrix products, dot(): return lax.dot_general(a, b, dims, preferred_element_type=F32).astype(out)  304 us
    ppermute x40, starting transfers between devices, travel(): lax.ppermute(array, 'tensor', pairs)  133 us
    pallas_call x4, Pallas kernels, spread(): pl.pallas_call(functools.partial(spread_kernel, count), grid=(width // ti...  118 us
    pallas_call x4, Pallas kernels, gated(): pl.pallas_call(gated_kernel, grid=(hidden // tile,), in_specs=[pl.BlockSp...  86.3 us
    pallas_call x1, Pallas kernels, attention_back(): attend_back(slot_table, *grad_attended, rotated, attended, lse, *tables)  56 us
    pallas_call x1, Pallas kernels, attention(): return attend(slot_table, *projected, *tables)  43.2 us
    reduce_scatter x8, waiting for transfers between devices, owner_sum(): return lax.psum_scatter(partial, 'dp', scatter_dimension=0, tiled=True)  42.2 us
  transfers between devices with their start and end apart: 56, of which 27 were waited for; matrix products, arithmetic and copies ran while one was open for 30% of the time, Pallas kernels for 19%

profile of v2, /device:TPU:0, one launch (start us, length us, event | category | flops | bytes accessed | tf_op | source)
XLA Modules:
  0.0 1453.5 jit_solution(16479911564933114596)
XLA Ops:
  18.2 10.4 all_gather.30
  28.6 13.4 all_gather.31
  68.9 9.9 fusion.51.refs_0_
  78.8 35.5 %collective-permute-done = bf16[512,3072]{1,0:T(8,128)(2,1)} collective-permute-done((bf16[512,3072]{1,0:T(8,128)(2,1)}, bf16[512,3072]{1,0:T(8,128)(2,1)}, u32[]{:S(2)}, u32[]{:S(2)}) %collective-permute-start) | collective-permute-done | bytes 3145760 | tf_op jit(solution)/shard_map/ppermute | solution.py:55
  123.7 7.3 collective-permute-start.4
  140.9 50.4 %collective-permute-done.3 = bf16[512,3072]{1,0:T(8,128)(2,1)} collective-permute-done((bf16[512,3072]{1,0:T(8,128)(2,1)}, bf16[512,3072]{1,0:T(8,128)(2,1)}, u32[]{:S(2)}, u32[]{:S(2)}) %collective-permute-start.3) | collective-permute-done | bytes 3145760 | tf_op jit(solution)/shard_map/ppermute | solution.py:55
  194.6 7.7 collective-permute-start.7
  206.0 9.2 fusion.53.refs_2_
  215.2 21.8 %collective-permute-done.7 = bf16[384,2048]{1,0:T(8,128)(2,1)S(1)} collective-permute-done((bf16[384,2048]{1,0:T(8,128)(2,1)S(1)}, bf16[384,2048]{1,0:T(8,128)(2,1)S(1)}, u32[]{:S(2)}, u32[]{:S(2)}) %collective-permute-start.7) | collective-permute-done | bytes 1572896 | tf_op jit(solution)/shard_map/ppermute | solution.py:55
  237.0 27.3 %collective-permute-done.8 = bf16[384,2048]{1,0:T(8,128)(2,1)S(1)} collective-permute-done((bf16[384,2048]{1,0:T(8,128)(2,1)}, bf16[384,2048]{1,0:T(8,128)(2,1)S(1)}, u32[]{:S(2)}, u32[]{:S(2)}) %collective-permute-start.8) | collective-permute-done | bytes 1572896 | tf_op jit(solution)/shard_map/ppermute | solution.py:55
  268.0 8.0 fusion.54.refs_3_
  277.4 9.5 collective-permute-start.10
  288.2 43.2 %shard_map.230 = (bf16[2048,768]{1,0:T(8,128)(2,1)}, bf16[2048,1280]{1,0:T(8,128)(2,1)}, f32[2,8,2048]{2,1,0:T(8,128)}) custom-call(s32[8]{0:T(128)} %dynamic-slice_bitcast_fusion.place_ref, f32[512,1280]{1,0:T(8,128)} %fusion.51.refs_0_, f32[512,1280]{1,0:T(8,128)} %fusion.52.refs_1_, f32[512,1280]{1,0:T(8,128)} %fusion.53.refs_2_, ...), custom_call_target="tpu_custom_call" | custom-call | flops 1 | bytes 1 | tf_op jit(solution)/shard_map/pallas_call | solution.py:502
  331.4 13.3 collective-permute-done.9
  348.6 7.0 convolution_convert_fusion.9
  374.0 27.5 %collective-permute-done.13 = bf16[384,2048]{1,0:T(8,128)(2,1)} collective-permute-done((bf16[384,2048]{1,0:T(8,128)(2,1)}, bf16[384,2048]{1,0:T(8,128)(2,1)}, u32[]{:S(2)}, u32[]{:S(2)}) %collective-permute-start.13) | collective-permute-done | bytes 1572896 | tf_op jit(solution)/shard_map/ppermute | solution.py:55
  401.5 29.7 %collective-permute-done.14 = bf16[384,2048]{1,0:T(8,128)(2,1)} collective-permute-done((bf16[384,2048]{1,0:T(8,128)(2,1)}, bf16[384,2048]{1,0:T(8,128)(2,1)}, u32[]{:S(2)}, u32[]{:S(2)}) %collective-permute-start.14) | collective-permute-done | bytes 1572896 | tf_op jit(solution)/shard_map/ppermute | solution.py:55
  449.4 6.9 convolution_convert_fusion.6
  456.4 54.8 %collective-permute-done.15 = bf16[512,3072]{1,0:T(8,128)(2,1)S(1)} collective-permute-done((bf16[512,3072]{1,0:T(8,128)(2,1)S(1)}, bf16[512,3072]{1,0:T(8,128)(2,1)S(1)}, u32[]{:S(2)}, u32[]{:S(2)}) %collective-permute-start.15) | collective-permute-done | bytes 3145760 | tf_op jit(solution)/shard_map/ppermute | solution.py:55
  531.8 17.4 %fusion.46.gm_ref = f32[1024,2048]{1,0:T(8,128)} fusion(bf16[3072,2048]{1,0:T(8,128)(2,1)S(1)} %bitcast.55, bf16[512,3072]{1,0:T(8,128)(2,1)S(1)} %add.152, bf16[512,3072]{1,0:T(8,128)(2,1)} %fusion.28), kind=kOutput, calls=%fused_computation.123 | convolution fusion | flops 12897484800 | bytes 27262976 | tf_op jit(solution)/shard_map/dot_general | solution.py:25
  549.2 18.9 %fusion.45.gm_ref = f32[1024,2048]{1,0:T(8,128)} fusion(bf16[3072,2048]{1,0:T(8,128)(2,1)} %all-gather.19.cloned.1.call-done.refs_3_, bf16[512,3072]{1,0:T(8,128)(2,1)} %copy-done.24, bf16[512,3072]{1,0:T(8,128)(2,1)} %fusion.28), kind=kOutput, calls=%fused_computation.122 | convolution fusion | flops 12897484800 | bytes 27262976 | tf_op jit(solution)/shard_map/dot_general | solution.py:25
  568.1 18.3 %collective-permute-done.18 = bf16[512,3072]{1,0:T(8,128)(2,1)} collective-permute-done((bf16[512,3072]{1,0:T(8,128)(2,1)}, bf16[512,3072]{1,0:T(8,128)(2,1)}, u32[]{:S(2)}, u32[]{:S(2)}) %collective-permute-start.18) | collective-permute-done | bytes 3145760 | tf_op jit(solution)/shard_map/ppermute | solution.py:55
  600.5 21.3 %shard_map.231 = (bf16[1024,2048]{1,0:T(8,128)(2,1)}, bf16[1024,2048]{1,0:T(8,128)(2,1)}, bf16[1024,2048]{1,0:T(8,128)(2,1)}) custom-call(bf16[512,3072]{1,0:T(8,128)(2,1)S(1)} %multiply_convert_fusion.1.x_ref, bf16[3072,2048]{1,0:T(8,128)(2,1)} %all-gather.15.cloned.1.call-done.gate_ref.refs_4_, ...), custom_call_target="tpu_custom_call" | custom-call | flops 1 | bytes 1 | tf_op jit(solution)/shard_map/pallas_call | solution.py:351
  621.8 17.7 %all-gather.23.cloned.1.call-done.up_ref.refs_7_ = bf16[3072,2048]{1,0:T(8,128)(2,1)} async-done(((bf16[384,2048]{1,0:T(8,128)(2,1)}), bf16[3072,2048]{1,0:T(8,128)(2,1)}) %all-gather.23.cloned.1.call-update) | async-done | bytes 12582928 | tf_op jit(solution)/shard_map/all_gather | solution.py:427
  639.6 19.1 %shard_map.232 = (bf16[1024,2048]{1,0:T(8,128)(2,1)}, bf16[1024,2048]{1,0:T(8,128)(2,1)}, bf16[1024,2048]{1,0:T(8,128)(2,1)}) custom-call(bf16[512,3072]{1,0:T(8,128)(2,1)S(1)} %multiply_convert_fusion.1.x_ref, bf16[3072,2048]{1,0:T(8,128)(2,1)} %all-gather.21.cloned.1.call-done.gate_ref.refs_5_, ...), custom_call_target="tpu_custom_call" | custom-call | flops 1 | bytes 1 | tf_op jit(solution)/shard_map/pallas_call | solution.py:351
  664.9 21.1 %shard_map.233 = (bf16[1024,2048]{1,0:T(8,128)(2,1)}, bf16[1024,2048]{1,0:T(8,128)(2,1)}, bf16[1024,2048]{1,0:T(8,128)(2,1)}) custom-call(bf16[512,3072]{1,0:T(8,128)(2,1)} %collective-permute-done.20.x_ref, bf16[3072,2048]{1,0:T(8,128)(2,1)} %all-gather.21.cloned.1.call-done.gate_ref.refs_5_, ...), custom_call_target="tpu_custom_call", output_to_operand_aliasing={{0}: (4, {}), {1}: (5, {}), {2}: (6, {})} | custom-call | flops 1 | bytes 1 | tf_op jit(solution)/shard_map/pallas_call | solution.py:351
  686.0 18.9 %convolution_convert_fusion.5 = bf16[3072,2048]{1,0:T(8,128)(2,1)} fusion(bf16[1024,2048]{1,0:T(8,128)(2,1)} %get-tuple-element.222.refs_1_, bf16[512,3072]{1,0:T(8,128)(2,1)S(1)} %copy-done.25, bf16[512,3072]{1,0:T(8,128)(2,1)} %fusion.28), kind=kOutput, calls=%fused_computation.22 | convolution fusion | flops 12903776256 | bytes 23068672 | tf_op jit(solution)/shard_map/dot_general | solution.py:25
  705.0 24.8 %shard_map.234 = (bf16[1024,2048]{1,0:T(8,128)(2,1)}, bf16[1024,2048]{1,0:T(8,128)(2,1)}, bf16[1024,2048]{1,0:T(8,128)(2,1)}) custom-call(bf16[512,3072]{1,0:T(8,128)(2,1)} %collective-permute-done.20.x_ref, bf16[3072,2048]{1,0:T(8,128)(2,1)} %all-gather.15.cloned.1.call-done.gate_ref.refs_4_, ...), custom_call_target="tpu_custom_call", output_to_operand_aliasing={{0}: (4, {}), {1}: (5, {}), {2}: (6, {})} | custom-call | flops 1 | bytes 1 | tf_op jit(solution)/shard_map/pallas_call | solution.py:351
  729.8 36.0 %shard_map.235 = bf16[512,3072]{1,0:T(8,128)(2,1)} custom-call(bf16[1024,2048]{1,0:T(8,128)(2,1)} %get-tuple-element.265.refs_0_, bf16[1024,2048]{1,0:T(8,128)(2,1)} %get-tuple-element.239.refs_1_, bf16[1024,2048]{1,0:T(8,128)(2,1)} %get-tuple-element.254.refs_2_, bf16[1024,2048]{1,0:T(8,128)(2,1)} %get-tuple-element.232.refs_3_, ...), custom_call_target="tpu_custom_call" | custom-call | flops 1 | bytes 1 | tf_op jit(solution)/shard_map/pallas_call | solution.py:377
  765.8 35.9 %shard_map.236 = f32[512,3072]{1,0:T(8,128)} custom-call(bf16[1024,2048]{1,0:T(8,128)(2,1)} %get-tuple-element.265.refs_0_, bf16[1024,2048]{1,0:T(8,128)(2,1)} %get-tuple-element.239.refs_1_, bf16[1024,2048]{1,0:T(8,128)(2,1)} %get-tuple-element.254.refs_2_, bf16[1024,2048]{1,0:T(8,128)(2,1)} %get-tuple-element.232.refs_3_, ...), custom_call_target="tpu_custom_call" | custom-call | flops 1 | bytes 1 | tf_op jit(solution)/shard_map/pallas_call | solution.py:377
  801.7 17.6 %convolution_convert_fusion.4 = bf16[3072,2048]{1,0:T(8,128)(2,1)} fusion(bf16[1024,2048]{1,0:T(8,128)(2,1)S(1)} %copy-done.7, bf16[512,3072]{1,0:T(8,128)(2,1)} %collective-permute-done.20.x_ref, bf16[512,3072]{1,0:T(8,128)(2,1)S(1)} %multiply_convert_fusion.1.x_ref), kind=kOutput, calls=%fused_computation.21 | convolution fusion | flops 12903776256 | bytes 23068672 | tf_op jit(solution)/shard_map/dot_general | solution.py:25
  819.4 8.4 collective-permute-done.21
  827.8 7.0 multiply_reduce_fusion
  834.8 14.5 %fusion.47 = (bf16[512,3072]{1,0:T(8,128)(2,1)}, f32[512,3072]{1,0:T(8,128)}) fusion(f32[512]{0:T(512)S(1)} %broadcast_multiply_fusion.1, f32[512,3072]{1,0:T(8,128)} %copy-done.2, f32[3072]{0:T(1024)S(1)} %bitcast.64, f32[512,3072]{1,0:T(8,128)} %shard_map.236, bf16[512,3072]{1,0:T(8,128)(2,1)} %collective-permute-done.21, f32[512]{0:T(512)S(1)} %add_rsqrt_fusion, ...), kind=kLoop, calls=%fused_computation.124 | loop fusion | flops 17301504 | bytes 28329984 | tf_op jit(solution)/shard_map/convert_element_type | solution.py:606
  855.8 21.3 %shard_map.237 = bf16[512,3072]{1,0:T(8,128)(2,1)S(1)} custom-call(bf16[1024,2048]{1,0:T(8,128)(2,1)} %get-tuple-element.247.refs_0_, bf16[1024,2048]{1,0:T(8,128)(2,1)} %get-tuple-element.222.refs_1_, bf16[3072,2048]{1,0:T(8,128)(2,1)} %all-gather.13.cloned.1.call-done.refs_2_, bf16[3072,2048]{1,0:T(8,128)(2,1)} %all-gather.19.cloned.1.call-done.refs_3_), custom_call_target="tpu_custom_call" | custom-call | flops 12884901888 | bytes 25165824 | tf_op jit(solution)/shard_map/pallas_call | solution.py:377
  884.3 17.6 %convolution_convert_fusion.3 = bf16[3072,2048]{1,0:T(8,128)(2,1)} fusion(bf16[1024,2048]{1,0:T(8,128)(2,1)S(1)} %copy-done.6, bf16[512,3072]{1,0:T(8,128)(2,1)} %collective-permute-done.20.x_ref, bf16[512,3072]{1,0:T(8,128)(2,1)S(1)} %multiply_convert_fusion.1.x_ref), kind=kOutput, calls=%fused_computation.20 | convolution fusion | flops 12903776256 | bytes 23068672 | tf_op jit(solution)/shard_map/dot_general | solution.py:25
  902.0 17.5 %collective-permute-done.23 = bf16[512,3072]{1,0:T(8,128)(2,1)} collective-permute-done((bf16[512,3072]{1,0:T(8,128)(2,1)}, bf16[512,3072]{1,0:T(8,128)(2,1)}, u32[]{:S(2)}, u32[]{:S(2)}) %collective-permute-start.23) | collective-permute-done | bytes 3145760 | tf_op jit(solution)/shard_map/ppermute | solution.py:55
  923.3 9.7 collective-permute-start.26
  933.0 24.5 %shard_map.238 = f32[512,3072]{1,0:T(8,128)} custom-call(bf16[1024,2048]{1,0:T(8,128)(2,1)} %get-tuple-element.247.refs_0_, bf16[1024,2048]{1,0:T(8,128)(2,1)} %get-tuple-element.222.refs_1_, bf16[3072,2048]{1,0:T(8,128)(2,1)} %all-gather.13.cloned.1.call-done.refs_2_, bf16[3072,2048]{1,0:T(8,128)(2,1)} %all-gather.19.cloned.1.call-done.refs_3_), custom_call_target="tpu_custom_call" | custom-call | flops 1 | bytes 1 | tf_op jit(solution)/shard_map/pallas_call | solution.py:377
  959.8 7.2 convolution_convert_fusion.16.refs_1_
  967.0 18.6 %convolution_convert_fusion.2 = bf16[3072,2048]{1,0:T(8,128)(2,1)} fusion(bf16[1024,2048]{1,0:T(8,128)(2,1)S(1)} %copy-done.8, bf16[512,3072]{1,0:T(8,128)(2,1)} %copy-done.24, bf16[512,3072]{1,0:T(8,128)(2,1)} %fusion.28), kind=kOutput, calls=%fused_computation.19 | convolution fusion | flops 12903776256 | bytes 23068672 | tf_op jit(solution)/shard_map/dot_general | solution.py:25
  985.6 7.0 collective-permute-done.25
  1005.2 10.1 collective-permute-start.29
  1024.4 18.7 %convolution_convert_fusion.1 = bf16[3072,2048]{1,0:T(8,128)(2,1)} fusion(bf16[1024,2048]{1,0:T(8,128)(2,1)S(1)} %copy-done.5, bf16[512,3072]{1,0:T(8,128)(2,1)} %collective-permute-done.20.x_ref, bf16[512,3072]{1,0:T(8,128)(2,1)S(1)} %multiply_convert_fusion.1.x_ref), kind=kOutput, calls=%fused_computation.18 | convolution fusion | flops 12903776256 | bytes 23068672 | tf_op jit(solution)/shard_map/dot_general | solution.py:25
  1043.1 26.7 %collective-permute-done.28 = bf16[512,3072]{1,0:T(8,128)(2,1)} collective-permute-done((bf16[512,3072]{1,0:T(8,128)(2,1)}, bf16[512,3072]{1,0:T(8,128)(2,1)}, u32[]{:S(2)}, u32[]{:S(2)}) %collective-permute-start.28) | collective-permute-done | bytes 3145760 | tf_op jit(solution)/shard_map/ppermute | solution.py:55
  1086.2 9.5 collective-permute-start.30
  1095.7 56.0 %shard_map.239 = bf16[2048,1280]{1,0:T(8,128)(2,1)} custom-call(s32[8]{0:T(128)} %dynamic-slice_bitcast_fusion.place_ref, bf16[512,768]{1,0:T(8,128)(2,1)} %convolution_convert_fusion.17.refs_0_, bf16[512,768]{1,0:T(8,128)(2,1)} %convolution_convert_fusion.16.refs_1_, bf16[512,768]{1,0:T(8,128)(2,1)} %convolution_convert_fusion.15.refs_2_, ...), custom_call_target="tpu_custom_call" | custom-call | flops 1 | bytes 1 | tf_op jit(solution)/shard_map/pallas_call | solution.py:620
  1151.7 19.3 %convolution_convert_fusion = bf16[3072,2048]{1,0:T(8,128)(2,1)} fusion(bf16[1024,2048]{1,0:T(8,128)(2,1)} %get-tuple-element.265.refs_0_, bf16[512,3072]{1,0:T(8,128)(2,1)} %collective-permute-done.20.x_ref, bf16[512,3072]{1,0:T(8,128)(2,1)S(1)} %multiply_convert_fusion.1.x_ref), kind=kOutput, calls=%fused_computation.17 | convolution fusion | flops 12903776256 | bytes 23068672 | tf_op jit(solution)/shard_map/dot_general | solution.py:25
  1171.3 9.8 convolution_convert_fusion.13
  1189.5 9.6 convolution_convert_fusion.11
  1199.2 9.2 convolution_convert_fusion.12
  1208.3 20.3 %fusion.16 = bf16[3072,1280]{1,0:T(8,128)(2,1)} fusion(bf16[2048,1280]{1,0:T(8,128)(2,1)S(1)} %bitcast.60, bf16[512,3072]{1,0:T(8,128)(2,1)} %copy-done.22, bf16[512,3072]{1,0:T(8,128)(2,1)S(1)} %copy-done.21, bf16[512,3072]{1,0:T(8,128)(2,1)S(1)} %copy-done.19, bf16[512,3072]{1,0:T(8,128)(2,1)} %fusion.22), kind=kOutput, calls=%fused_computation.16 | convolution fusion | flops 16160391168 | bytes 25690112 | tf_op jit(solution)/shard_map/dot_general | solution.py:25
  1228.6 24.5 %collective-permute-done.34 = bf16[384,4096]{1,0:T(8,128)(2,1)} collective-permute-done((bf16[384,4096]{1,0:T(8,128)(2,1)}, bf16[384,4096]{1,0:T(8,128)(2,1)}, u32[]{:S(2)}, u32[]{:S(2)}) %collective-permute-start.34) | collective-permute-done | bytes 3145760 | tf_op jit(solution)/shard_map/ppermute | solution.py:55
  1253.6 8.4 add_convert_fusion.2
  1265.6 7.9 collective-permute-start.35
  1273.5 15.6 %fusion.29 = bf16[3072,768]{1,0:T(8,128)(2,1)} fusion(bf16[2048,768]{1,0:T(8,128)(2,1)} %get-tuple-element.280.refs_5_, bf16[512,3072]{1,0:T(8,128)(2,1)} %copy-done.26, bf16[512,3072]{1,0:T(8,128)(2,1)} %select_select_fusion.1, bf16[512,3072]{1,0:T(8,128)(2,1)} %copy-done.23, bf16[512,3072]{1,0:T(8,128)(2,1)} %get-tuple-element.236), kind=kOutput, calls=%fused_computation.52 | convolution fusion | flops 9716367360 | bytes 20447232 | tf_op jit(solution)/shard_map/dot_general | solution.py:25
  1289.1 15.5 %reduce-scatter.19.cloned.1.call-done = bf16[384,2048]{1,0:T(8,128)(2,1)} async-done(((bf16[3072,2048]{1,0:T(8,128)(2,1)}), bf16[384,2048]{1,0:T(8,128)(2,1)}) %reduce-scatter.19.cloned.1.call-update) | async-done | bytes 1572880 | tf_op jit(solution)/shard_map/reduce_scatter | solution.py:572
  1304.6 22.4 %collective-permute-done.37 = bf16[512,3072]{1,0:T(8,128)(2,1)} collective-permute-done((bf16[512,3072]{1,0:T(8,128)(2,1)S(1)}, bf16[512,3072]{1,0:T(8,128)(2,1)}, u32[]{:S(2)}, u32[]{:S(2)}) %collective-permute-start.37) | collective-permute-done | bytes 3145760 | tf_op jit(solution)/shard_map/ppermute | solution.py:55
  1330.1 9.1 add_convert_fusion
  1340.5 10.1 collective-permute-start.38
  1350.6 26.7 %reduce-scatter.21.cloned.1.call-done = bf16[384,1280]{1,0:T(8,128)(2,1)} async-done(((bf16[3072,1280]{1,0:T(8,128)(2,1)}), bf16[384,1280]{1,0:T(8,128)(2,1)}) %reduce-scatter.21.cloned.1.call-update) | async-done | bytes 983056 | tf_op jit(solution)/shard_map/reduce_scatter | solution.py:572
  1377.3 9.5 convolution_convert_fusion.10
  1420.7 8.2 fusion.26
  1429.3 11.5 psum.7
  (299 shorter events, 265.8 us)
Async XLA Ops:
  7.2 61.8 %all-gather.9.cloned.1.call-start = ((), (), s32[]{:S(2)}) async-start(), calls=%async_computation.8 | async-start | bytes 8847360 | tf_op jit(solution)/shard_map/all_gather | solution.py:427
  13.9 262.2 %all-gather.11.cloned.1.call-start = ((), (), s32[]{:S(2)}) async-start(), calls=%async_computation.9 | async-start | bytes 5308416 | tf_op jit(solution)/shard_map/all_gather | solution.py:427
  14.7 27.3 %copy-start.3 = (bf16[512,3072]{1,0:T(8,128)(2,1)S(1)}, bf16[512,3072]{1,0:T(8,128)(2,1)}, u32[]{:S(2)}) copy-start(bf16[512,3072]{1,0:T(8,128)(2,1)} %param.15) | copy-start | bytes 9437188
  14.7 261.4 %all-gather.13.cloned.1.call-start = ((), (), s32[]{:S(2)}) async-start(), calls=%async_computation.10 | async-start | bytes 14155776 | tf_op jit(solution)/shard_map/all_gather | solution.py:427
  17.5 356.5 %all-gather.15.cloned.1.call-start = ((), (), s32[]{:S(2)}) async-start(), calls=%async_computation.11 | async-start | bytes 14155776 | tf_op jit(solution)/shard_map/all_gather | solution.py:427
  18.1 531.1 %all-gather.19.cloned.1.call-start = ((), (), s32[]{:S(2)}) async-start(), calls=%async_computation.13 | async-start | bytes 14155776 | tf_op jit(solution)/shard_map/all_gather | solution.py:427
  45.6 68.7 %collective-permute-start = (bf16[512,3072]{1,0:T(8,128)(2,1)}, bf16[512,3072]{1,0:T(8,128)(2,1)}, u32[]{:S(2)}, u32[]{:S(2)}) collective-permute-start(bf16[512,3072]{1,0:T(8,128)(2,1)} %fusion.22), channel_id=1, source_target_pairs={{0,1},{1,2},{2,3},{4,5},{5,6},{6,7},{8,9},{9,10},{10,11},{12,13},{... | collective-permute-start | bytes 9437192 | tf_op jit(solution)/shard_map/ppermute | solution.py:55
  50.8 69.3 %collective-permute-start.1 = (bf16[512,3072]{1,0:T(8,128)(2,1)}, bf16[512,3072]{1,0:T(8,128)(2,1)}, u32[]{:S(2)}, u32[]{:S(2)}) collective-permute-start(bf16[512,3072]{1,0:T(8,128)(2,1)} %fusion.22), channel_id=1, source_target_pairs={{1,0},{2,1},{3,2},{5,4},{6,5},{7,6},{9,8},{10,9},{11,10},{13,12},{... | collective-permute-start | bytes 9437192 | tf_op jit(solution)/shard_map/ppermute | solution.py:55
  120.1 20.8 %collective-permute-start.2 = (bf16[512,3072]{1,0:T(8,128)(2,1)}, bf16[512,3072]{1,0:T(8,128)(2,1)}, u32[]{:S(2)}, u32[]{:S(2)}) collective-permute-start(bf16[512,3072]{1,0:T(8,128)(2,1)} %collective-permute-done), channel_id=1, source_target_pairs={{1,2},{2,3},{5,6},{6,7},{9,10},{10,11},{13,14},{14,15},{17,18},{18... | collective-permute-start | bytes 9437192 | tf_op jit(solution)/shard_map/ppermute | solution.py:55
  122.4 68.8 %collective-permute-start.3 = (bf16[512,3072]{1,0:T(8,128)(2,1)}, bf16[512,3072]{1,0:T(8,128)(2,1)}, u32[]{:S(2)}, u32[]{:S(2)}) collective-permute-start(bf16[512,3072]{1,0:T(8,128)(2,1)} %collective-permute-done.1), channel_id=1, source_target_pairs={{1,0},{2,1},{5,4},{6,5},{9,8},{10,9},{13,12},{14,13},{17,16},{18,1... | collective-permute-start | bytes 9437192 | tf_op jit(solution)/shard_map/ppermute | solution.py:55
  123.7 68.7 %collective-permute-start.4 = (bf16[512,3072]{1,0:T(8,128)(2,1)}, bf16[512,3072]{1,0:T(8,128)(2,1)}, u32[]{:S(2)}, u32[]{:S(2)}) collective-permute-start(bf16[512,3072]{1,0:T(8,128)(2,1)} %fusion.28), channel_id=1, source_target_pairs={{0,1},{3,2},{4,5},{7,6},{8,9},{11,10},{12,13},{15,14},{16,17},{19,... | collective-permute-start | bytes 9437192 | tf_op jit(solution)/shard_map/ppermute | solution.py:55
  135.2 59.4 %copy-start.14 = (bf16[2048,384]{0,1:T(8,128)(2,1)S(1)}, bf16[2048,384]{0,1:T(8,128)(2,1)}, u32[]{:S(2)}) copy-start(bf16[2048,384]{0,1:T(8,128)(2,1)} %copy.35) | copy-start | bytes 4718596
  192.4 71.9 %collective-permute-start.5 = (bf16[512,3072]{1,0:T(8,128)(2,1)}, bf16[512,3072]{1,0:T(8,128)(2,1)S(1)}, u32[]{:S(2)}, u32[]{:S(2)}) collective-permute-start(bf16[512,3072]{1,0:T(8,128)(2,1)} %collective-permute-done.2), channel_id=1, source_target_pairs={{2,3},{6,7},{10,11},{14,15},{18,19},{22,23},{26,27},{30,31}} | collective-permute-start | bytes 9437192 | tf_op jit(solution)/shard_map/ppermute | solution.py:55
  193.3 72.2 %collective-permute-start.6 = (bf16[512,3072]{1,0:T(8,128)(2,1)}, bf16[512,3072]{1,0:T(8,128)(2,1)S(1)}, u32[]{:S(2)}, u32[]{:S(2)}) collective-permute-start(bf16[512,3072]{1,0:T(8,128)(2,1)} %collective-permute-done.3), channel_id=1, source_target_pairs={{1,0},{5,4},{9,8},{13,12},{17,16},{21,20},{25,24},{29,28}} | collective-permute-start | bytes 9437192 | tf_op jit(solution)/shard_map/ppermute | solution.py:55
  194.6 42.4 %collective-permute-start.7 = (bf16[384,2048]{1,0:T(8,128)(2,1)S(1)}, bf16[384,2048]{1,0:T(8,128)(2,1)S(1)}, u32[]{:S(2)}, u32[]{:S(2)}) collective-permute-start(bf16[384,2048]{1,0:T(8,128)(2,1)S(1)} %bitcast.58), channel_id=1, source_target_pairs={{3,1},{0,2},{7,5},{4,6},{11,9},{8,10},{15,13},{12,14},{19,17},{16,... | collective-permute-start | bytes 4718600 | tf_op jit(solution)/shard_map/ppermute | solution.py:55
  202.3 62.0 %collective-permute-start.8 = (bf16[384,2048]{1,0:T(8,128)(2,1)}, bf16[384,2048]{1,0:T(8,128)(2,1)S(1)}, u32[]{:S(2)}, u32[]{:S(2)}) collective-permute-start(bf16[384,2048]{1,0:T(8,128)(2,1)} %param.25), channel_id=1, source_target_pairs={{3,1},{0,2},{7,5},{4,6},{11,9},{8,10},{15,13},{12,14},{19,17},{16,... | collective-permute-start | bytes 4718600 | tf_op jit(solution)/shard_map/ppermute | solution.py:55
  237.0 27.3 %copy-start.30 = (bf16[384,2048]{1,0:T(8,128)(2,1)}, bf16[384,2048]{1,0:T(8,128)(2,1)S(1)}, u32[]{:S(2)}) copy-start(bf16[384,2048]{1,0:T(8,128)(2,1)S(1)} %collective-permute-done.7) | copy-start | bytes 4718596
  276.1 68.6 %collective-permute-start.9 = (bf16[384,2048]{1,0:T(8,128)(2,1)}, bf16[384,2048]{1,0:T(8,128)(2,1)}, u32[]{:S(2)}, u32[]{:S(2)}) collective-permute-start(bf16[384,2048]{1,0:T(8,128)(2,1)} %bitcast.57), channel_id=1, source_target_pairs={{2,0},{1,3},{6,4},{5,7},{10,8},{9,11},{14,12},{13,15},{18,16},{17,... | collective-permute-start | bytes 4718600 | tf_op jit(solution)/shard_map/ppermute | solution.py:55
  277.4 67.3 %collective-permute-start.10 = (bf16[384,2048]{1,0:T(8,128)(2,1)}, bf16[384,2048]{1,0:T(8,128)(2,1)}, u32[]{:S(2)}, u32[]{:S(2)}) collective-permute-start(bf16[384,2048]{1,0:T(8,128)(2,1)} %param.26), channel_id=1, source_target_pairs={{3,1},{0,2},{7,5},{4,6},{11,9},{8,10},{15,13},{12,14},{19,17},{16,... | collective-permute-start | bytes 4718600 | tf_op jit(solution)/shard_map/ppermute | solution.py:55
  288.2 56.5 %copy-start.31 = (bf16[384,2048]{1,0:T(8,128)(2,1)S(1)}, bf16[384,2048]{1,0:T(8,128)(2,1)}, u32[]{:S(2)}) copy-start(bf16[384,2048]{1,0:T(8,128)(2,1)} %copy-done.30) | copy-start | bytes 4718596
  347.9 220.1 %all-gather.17.cloned.1.call-start = ((), (), s32[]{:S(2)}) async-start(), calls=%async_computation.12 | async-start | bytes 14155776 | tf_op jit(solution)/shard_map/all_gather | solution.py:427
  348.5 273.3 %all-gather.21.cloned.1.call-start = ((), (), s32[]{:S(2)}) async-start(), calls=%async_computation.14 | async-start | bytes 14155776 | tf_op jit(solution)/shard_map/all_gather | solution.py:427
  355.6 75.6 %collective-permute-start.11 = (bf16[512,3072]{1,0:T(8,128)(2,1)}, bf16[512,3072]{1,0:T(8,128)(2,1)}, u32[]{:S(2)}, u32[]{:S(2)}) collective-permute-start(bf16[512,3072]{1,0:T(8,128)(2,1)} %convolution_convert_fusion.9), channel_id=1, source_target_pairs={{0,1},{4,5},{8,9},{12,13},{16,17},{20,21},{24,25},{28,29}} | collective-permute-start | bytes 9437192 | tf_op jit(solution)/shard_map/ppermute | solution.py:55
  358.8 72.4 %collective-permute-start.12 = (bf16[512,3072]{1,0:T(8,128)(2,1)}, bf16[512,3072]{1,0:T(8,128)(2,1)}, u32[]{:S(2)}, u32[]{:S(2)}) collective-permute-start(bf16[512,3072]{1,0:T(8,128)(2,1)} %convolution_convert_fusion.9), channel_id=1, source_target_pairs={{3,2},{7,6},{11,10},{15,14},{19,18},{23,22},{27,26},{31,30}} | collective-permute-start | bytes 9437192 | tf_op jit(solution)/shard_map/ppermute | solution.py:55
  361.1 40.4 %collective-permute-start.13 = (bf16[384,2048]{1,0:T(8,128)(2,1)}, bf16[384,2048]{1,0:T(8,128)(2,1)}, u32[]{:S(2)}, u32[]{:S(2)}) collective-permute-start(bf16[384,2048]{1,0:T(8,128)(2,1)} %param.25), channel_id=1, source_target_pairs={{2,0},{1,3},{6,4},{5,7},{10,8},{9,11},{14,12},{13,15},{18,16},{17,... | collective-permute-start | bytes 4718600 | tf_op jit(solution)/shard_map/ppermute | solution.py:55
  362.4 68.8 %collective-permute-start.14 = (bf16[384,2048]{1,0:T(8,128)(2,1)}, bf16[384,2048]{1,0:T(8,128)(2,1)}, u32[]{:S(2)}, u32[]{:S(2)}) collective-permute-start(bf16[384,2048]{1,0:T(8,128)(2,1)} %param.26), channel_id=1, source_target_pairs={{2,0},{1,3},{6,4},{5,7},{10,8},{9,11},{14,12},{13,15},{18,16},{17,... | collective-permute-start | bytes 4718600 | tf_op jit(solution)/shard_map/ppermute | solution.py:55
  435.0 204.6 %all-gather.23.cloned.1.call-start = ((), (), s32[]{:S(2)}) async-start(), calls=%async_computation.15 | async-start | bytes 14155776 | tf_op jit(solution)/shard_map/all_gather | solution.py:427
  438.7 559.1 %reduce-scatter.11.cloned.1.call-start = ((), (), s32[]{:S(2)}) async-start(), calls=%async_computation.17 | async-start | bytes 14155776 | tf_op jit(solution)/shard_map/reduce_scatter | solution.py:572
  445.4 71.3 %copy-start.11 = (bf16[512,3072]{1,0:T(8,128)(2,1)S(1)}, bf16[512,3072]{1,0:T(8,128)(2,1)}, u32[]{:S(2)}) copy-start(bf16[512,3072]{1,0:T(8,128)(2,1)} %convolution_convert_fusion.8) | copy-start | bytes 9437188
  445.4 71.3 %copy-start.28 = (bf16[512,3072]{1,0:T(8,128)(2,1)S(1)}, bf16[512,3072]{1,0:T(8,128)(2,1)}, u32[]{:S(2)}) copy-start(bf16[512,3072]{1,0:T(8,128)(2,1)} %convolution_convert_fusion.7) | copy-start | bytes 9437188
  445.4 65.8 %collective-permute-start.15 = (bf16[512,3072]{1,0:T(8,128)(2,1)S(1)}, bf16[512,3072]{1,0:T(8,128)(2,1)S(1)}, u32[]{:S(2)}, u32[]{:S(2)}) collective-permute-start(bf16[512,3072]{1,0:T(8,128)(2,1)S(1)} %add_convert_fusion.5), channel_id=1, source_target_pairs={{0,1},{1,2},{4,5},{5,6},{8,9},{9,10},{12,13},{13,14},{16,17},{17,1... | collective-permute-start | bytes 9437192 | tf_op jit(solution)/shard_map/ppermute | solution.py:55
  447.1 64.0 %collective-permute-start.16 = (bf16[512,3072]{1,0:T(8,128)(2,1)S(1)}, bf16[512,3072]{1,0:T(8,128)(2,1)S(1)}, u32[]{:S(2)}, u32[]{:S(2)}) collective-permute-start(bf16[512,3072]{1,0:T(8,128)(2,1)S(1)} %add_convert_fusion.5), channel_id=1, source_target_pairs={{3,2},{2,1},{7,6},{6,5},{11,10},{10,9},{15,14},{14,13},{19,18},{18... | collective-permute-start | bytes 9437192 | tf_op jit(solution)/shard_map/ppermute | solution.py:55
  448.1 68.6 %collective-permute-start.17 = (bf16[512,3072]{1,0:T(8,128)(2,1)}, bf16[512,3072]{1,0:T(8,128)(2,1)S(1)}, u32[]{:S(2)}, u32[]{:S(2)}) collective-permute-start(bf16[512,3072]{1,0:T(8,128)(2,1)} %fusion.28), channel_id=1, source_target_pairs={{1,0},{2,3},{5,4},{6,7},{9,8},{10,11},{13,12},{14,15},{17,16},{18,... | collective-permute-start | bytes 9437192 | tf_op jit(solution)/shard_map/ppermute | solution.py:55
  521.1 65.3 %collective-permute-start.18 = (bf16[512,3072]{1,0:T(8,128)(2,1)}, bf16[512,3072]{1,0:T(8,128)(2,1)}, u32[]{:S(2)}, u32[]{:S(2)}) collective-permute-start(bf16[512,3072]{1,0:T(8,128)(2,1)} %get-tuple-element.197), channel_id=1, source_target_pairs={{0,1},{1,2},{2,3},{4,5},{5,6},{6,7},{8,9},{9,10},{10,11},{12,13},{... | collective-permute-start | bytes 9437192 | tf_op jit(solution)/shard_map/ppermute | solution.py:55
  524.7 67.4 %collective-permute-start.19 = (bf16[512,3072]{1,0:T(8,128)(2,1)}, bf16[512,3072]{1,0:T(8,128)(2,1)}, u32[]{:S(2)}, u32[]{:S(2)}) collective-permute-start(bf16[512,3072]{1,0:T(8,128)(2,1)} %get-tuple-element.198), channel_id=1, source_target_pairs={{3,2},{2,1},{1,0},{7,6},{6,5},{5,4},{11,10},{10,9},{9,8},{15,14},{... | collective-permute-start | bytes 9437192 | tf_op jit(solution)/shard_map/ppermute | solution.py:55
  600.5 64.4 %collective-permute-start.20 = (bf16[512,3072]{1,0:T(8,128)(2,1)S(1)}, bf16[512,3072]{1,0:T(8,128)(2,1)}, u32[]{:S(2)}, u32[]{:S(2)}) collective-permute-start(bf16[512,3072]{1,0:T(8,128)(2,1)S(1)} %multiply_convert_fusion.1.x_ref), channel_id=1, source_target_pairs={{0,1},{3,2},{1,0},{2,3},{4,5},{7,6},{5,4},{6,7},{8,9},{11,10},{9,8... | collective-permute-start | bytes 9437192 | tf_op jit(solution)/shard_map/ppermute | solution.py:55
  705.0 295.7 %reduce-scatter.13.cloned.1.call-start = ((), (), s32[]{:S(2)}) async-start(), calls=%async_computation.18 | async-start | bytes 14155776 | tf_op jit(solution)/shard_map/reduce_scatter | solution.py:572
  765.8 35.9 %copy-start.7 = (bf16[1024,2048]{1,0:T(8,128)(2,1)S(1)}, bf16[1024,2048]{1,0:T(8,128)(2,1)}, u32[]{:S(2)}) copy-start(bf16[1024,2048]{1,0:T(8,128)(2,1)} %get-tuple-element.232.refs_3_) | copy-start | bytes 12582916
  765.8 61.9 %collective-permute-start.21 = (bf16[512,3072]{1,0:T(8,128)(2,1)}, bf16[512,3072]{1,0:T(8,128)(2,1)}, u32[]{:S(2)}, u32[]{:S(2)}) collective-permute-start(bf16[512,3072]{1,0:T(8,128)(2,1)} %shard_map.235), channel_id=1, source_target_pairs={{0,1},{3,2},{1,0},{2,3},{4,5},{7,6},{5,4},{6,7},{8,9},{11,10},{9,8... | collective-permute-start | bytes 9437192 | tf_op jit(solution)/shard_map/ppermute | solution.py:55
  827.8 257.1 %reduce-scatter.9.cloned.1.call-start = ((), (), s32[]{:S(2)}) async-start(), calls=%async_computation.16 | async-start | bytes 14155776 | tf_op jit(solution)/shard_map/reduce_scatter | solution.py:572
  849.4 70.2 %collective-permute-start.22 = (bf16[512,3072]{1,0:T(8,128)(2,1)}, bf16[512,3072]{1,0:T(8,128)(2,1)}, u32[]{:S(2)}, u32[]{:S(2)}) collective-permute-start(bf16[512,3072]{1,0:T(8,128)(2,1)} %get-tuple-element.236), channel_id=1, source_target_pairs={{0,1},{1,2},{2,3},{4,5},{5,6},{6,7},{8,9},{9,10},{10,11},{12,13},{... | collective-permute-start | bytes 9437192 | tf_op jit(solution)/shard_map/ppermute | solution.py:55
  854.2 65.3 %collective-permute-start.23 = (bf16[512,3072]{1,0:T(8,128)(2,1)}, bf16[512,3072]{1,0:T(8,128)(2,1)}, u32[]{:S(2)}, u32[]{:S(2)}) collective-permute-start(bf16[512,3072]{1,0:T(8,128)(2,1)} %get-tuple-element.236), channel_id=1, source_target_pairs={{1,0},{2,1},{3,2},{5,4},{6,5},{7,6},{9,8},{10,9},{11,10},{13,12},{... | collective-permute-start | bytes 9437192 | tf_op jit(solution)/shard_map/ppermute | solution.py:55
  919.5 251.5 %reduce-scatter.15.cloned.1.call-start = ((), (), s32[]{:S(2)}) async-start(), calls=%async_computation.19 | async-start | bytes 14155776 | tf_op jit(solution)/shard_map/reduce_scatter | solution.py:572
  919.6 74.2 %collective-permute-start.24 = (bf16[512,3072]{1,0:T(8,128)(2,1)}, bf16[512,3072]{1,0:T(8,128)(2,1)}, u32[]{:S(2)}, u32[]{:S(2)}) collective-permute-start(bf16[512,3072]{1,0:T(8,128)(2,1)} %collective-permute-done.22), channel_id=1, source_target_pairs={{1,2},{2,3},{5,6},{6,7},{9,10},{10,11},{13,14},{14,15},{17,18},{18... | collective-permute-start | bytes 9437192 | tf_op jit(solution)/shard_map/ppermute | solution.py:55
  922.0 70.6 %collective-permute-start.25 = (bf16[512,3072]{1,0:T(8,128)(2,1)}, bf16[512,3072]{1,0:T(8,128)(2,1)}, u32[]{:S(2)}, u32[]{:S(2)}) collective-permute-start(bf16[512,3072]{1,0:T(8,128)(2,1)} %collective-permute-done.23), channel_id=1, source_target_pairs={{1,0},{2,1},{5,4},{6,5},{9,8},{10,9},{13,12},{14,13},{17,16},{18,1... | collective-permute-start | bytes 9437192 | tf_op jit(solution)/shard_map/ppermute | solution.py:55
  923.3 70.5 %collective-permute-start.26 = (bf16[512,3072]{1,0:T(8,128)(2,1)}, bf16[512,3072]{1,0:T(8,128)(2,1)}, u32[]{:S(2)}, u32[]{:S(2)}) collective-permute-start(bf16[512,3072]{1,0:T(8,128)(2,1)} %copy-done), channel_id=1, source_target_pairs={{0,1},{3,2},{4,5},{7,6},{8,9},{11,10},{12,13},{15,14},{16,17},{19,... | collective-permute-start | bytes 9437192 | tf_op jit(solution)/shard_map/ppermute | solution.py:55
  993.8 259.3 %reduce-scatter.17.cloned.1.call-start = ((), (), s32[]{:S(2)}) async-start(), calls=%async_computation.20 | async-start | bytes 14155776 | tf_op jit(solution)/shard_map/reduce_scatter | solution.py:572
  1003.6 66.2 %collective-permute-start.28 = (bf16[512,3072]{1,0:T(8,128)(2,1)}, bf16[512,3072]{1,0:T(8,128)(2,1)}, u32[]{:S(2)}, u32[]{:S(2)}) collective-permute-start(bf16[512,3072]{1,0:T(8,128)(2,1)} %collective-permute-done.25), channel_id=1, source_target_pairs={{1,0},{5,4},{9,8},{13,12},{17,16},{21,20},{25,24},{29,28}} | collective-permute-start | bytes 9437192 | tf_op jit(solution)/shard_map/ppermute | solution.py:55
  1005.2 69.7 %collective-permute-start.29 = (bf16[384,4096]{1,0:T(8,128)(2,1)}, bf16[384,4096]{1,0:T(8,128)(2,1)}, u32[]{:S(2)}, u32[]{:S(2)}) collective-permute-start(bf16[384,4096]{1,0:T(8,128)(2,1)} %constant_dynamic-update-slice_fusion), channel_id=1, source_target_pairs={{0,2},{3,1},{4,6},{7,5},{8,10},{11,9},{12,14},{15,13},{16,18},{19,... | collective-permute-start | bytes 9437192 | tf_op jit(solution)/shard_map/ppermute | solution.py:55
  1015.3 59.5 %collective-permute-start.27 = (bf16[512,3072]{1,0:T(8,128)(2,1)}, bf16[512,3072]{1,0:T(8,128)(2,1)}, u32[]{:S(2)}, u32[]{:S(2)}) collective-permute-start(bf16[512,3072]{1,0:T(8,128)(2,1)} %collective-permute-done.24), channel_id=1, source_target_pairs={{2,3},{6,7},{10,11},{14,15},{18,19},{22,23},{26,27},{30,31}} | collective-permute-start | bytes 9437192 | tf_op jit(solution)/shard_map/ppermute | solution.py:55
  1074.9 229.7 %reduce-scatter.19.cloned.1.call-start = ((), (), s32[]{:S(2)}) async-start(), calls=%async_computation.21 | async-start | bytes 14155776 | tf_op jit(solution)/shard_map/reduce_scatter | solution.py:572
  1084.9 86.1 %collective-permute-start.31 = (bf16[384,2048]{1,0:T(8,128)(2,1)}, bf16[384,2048]{1,0:T(8,128)(2,1)}, u32[]{:S(2)}, u32[]{:S(2)}) collective-permute-start(bf16[384,2048]{1,0:T(8,128)(2,1)} %reduce-scatter.9.cloned.1.call-done), channel_id=1, source_target_pairs={{1,3},{2,0},{5,7},{6,4},{9,11},{10,8},{13,15},{14,12},{17,19},{18,... | collective-permute-start | bytes 4718600 | tf_op jit(solution)/shard_map/ppermute | solution.py:55
  1086.2 84.8 %collective-permute-start.30 = (bf16[384,2048]{1,0:T(8,128)(2,1)}, bf16[384,2048]{1,0:T(8,128)(2,1)}, u32[]{:S(2)}, u32[]{:S(2)}) collective-permute-start(bf16[384,2048]{1,0:T(8,128)(2,1)} %reduce-scatter.9.cloned.1.call-done), channel_id=1, source_target_pairs={{0,2},{3,1},{4,6},{7,5},{8,10},{11,9},{12,14},{15,13},{16,18},{19,... | collective-permute-start | bytes 4718600 | tf_op jit(solution)/shard_map/ppermute | solution.py:55
  1171.0 206.3 %reduce-scatter.21.cloned.1.call-start = ((), (), s32[]{:S(2)}) async-start(), calls=%async_computation.22 | async-start | bytes 8847360 | tf_op jit(solution)/shard_map/reduce_scatter | solution.py:572
  1171.3 27.9 %slice-start.5 = ((s8[5242880]{0:T(1024)(128)(4,1)}), s8[4194304]{0:T(1024)(128)(4,1)S(1)}, s32[]{:S(2)}) async-start(s8[5242880]{0:T(1024)(128)(4,1)} %bitcast.59), calls=%async_computation.29 | async-start | bytes 8388608
  1181.1 72.0 %collective-permute-start.32 = (bf16[512,3072]{1,0:T(8,128)(2,1)}, bf16[512,3072]{1,0:T(8,128)(2,1)}, u32[]{:S(2)}, u32[]{:S(2)}) collective-permute-start(bf16[512,3072]{1,0:T(8,128)(2,1)} %convolution_convert_fusion.13), channel_id=1, source_target_pairs={{0,1},{4,5},{8,9},{12,13},{16,17},{20,21},{24,25},{28,29}} | collective-permute-start | bytes 9437192 | tf_op jit(solution)/shard_map/ppermute | solution.py:55
  1185.8 42.8 %collective-permute-start.33 = (bf16[512,3072]{1,0:T(8,128)(2,1)}, bf16[512,3072]{1,0:T(8,128)(2,1)}, u32[]{:S(2)}, u32[]{:S(2)}) collective-permute-start(bf16[512,3072]{1,0:T(8,128)(2,1)} %convolution_convert_fusion.13), channel_id=1, source_target_pairs={{3,2},{7,6},{11,10},{15,14},{19,18},{23,22},{27,26},{31,30}} | collective-permute-start | bytes 9437192 | tf_op jit(solution)/shard_map/ppermute | solution.py:55
  1188.2 64.9 %collective-permute-start.34 = (bf16[384,4096]{1,0:T(8,128)(2,1)}, bf16[384,4096]{1,0:T(8,128)(2,1)}, u32[]{:S(2)}, u32[]{:S(2)}) collective-permute-start(bf16[384,4096]{1,0:T(8,128)(2,1)} %constant_dynamic-update-slice_fusion), channel_id=1, source_target_pairs={{1,3},{2,0},{5,7},{6,4},{9,11},{10,8},{13,15},{14,12},{17,19},{18,... | collective-permute-start | bytes 9437192 | tf_op jit(solution)/shard_map/ppermute | solution.py:55
  1253.1 191.1 %reduce-scatter.23.cloned.1.call-start = ((), (), s32[]{:S(2)}) async-start(), calls=%async_computation.23 | async-start | bytes 5308416 | tf_op jit(solution)/shard_map/reduce_scatter | solution.py:572
  1262.0 42.6 %collective-permute-start.36 = (bf16[512,3072]{1,0:T(8,128)(2,1)}, bf16[512,3072]{1,0:T(8,128)(2,1)}, u32[]{:S(2)}, u32[]{:S(2)}) collective-permute-start(bf16[512,3072]{1,0:T(8,128)(2,1)} %add_convert_fusion.2), channel_id=1, source_target_pairs={{3,2},{2,1},{7,6},{6,5},{11,10},{10,9},{15,14},{14,13},{19,18},{18... | collective-permute-start | bytes 9437192 | tf_op jit(solution)/shard_map/ppermute | solution.py:55
  1264.3 62.7 %collective-permute-start.37 = (bf16[512,3072]{1,0:T(8,128)(2,1)S(1)}, bf16[512,3072]{1,0:T(8,128)(2,1)}, u32[]{:S(2)}, u32[]{:S(2)}) collective-permute-start(bf16[512,3072]{1,0:T(8,128)(2,1)S(1)} %copy-done.1), channel_id=1, source_target_pairs={{1,0},{2,3},{5,4},{6,7},{9,8},{10,11},{13,12},{14,15},{17,16},{18,... | collective-permute-start | bytes 9437192 | tf_op jit(solution)/shard_map/ppermute | solution.py:55
  1265.6 64.5 %collective-permute-start.35 = (bf16[512,3072]{1,0:T(8,128)(2,1)}, bf16[512,3072]{1,0:T(8,128)(2,1)}, u32[]{:S(2)}, u32[]{:S(2)}) collective-permute-start(bf16[512,3072]{1,0:T(8,128)(2,1)} %add_convert_fusion.2), channel_id=1, source_target_pairs={{0,1},{1,2},{4,5},{5,6},{8,9},{9,10},{12,13},{13,14},{16,17},{17,1... | collective-permute-start | bytes 9437192 | tf_op jit(solution)/shard_map/ppermute | solution.py:55
  1339.2 75.7 %collective-permute-start.39 = (bf16[512,3072]{1,0:T(8,128)(2,1)}, bf16[512,3072]{1,0:T(8,128)(2,1)}, u32[]{:S(2)}, u32[]{:S(2)}) collective-permute-start(bf16[512,3072]{1,0:T(8,128)(2,1)} %get-tuple-element.285), channel_id=1, source_target_pairs={{3,2},{2,1},{1,0},{7,6},{6,5},{5,4},{11,10},{10,9},{9,8},{15,14},{... | collective-permute-start | bytes 9437192 | tf_op jit(solution)/shard_map/ppermute | solution.py:55
  1340.5 74.4 %collective-permute-start.38 = (bf16[512,3072]{1,0:T(8,128)(2,1)}, bf16[512,3072]{1,0:T(8,128)(2,1)}, u32[]{:S(2)}, u32[]{:S(2)}) collective-permute-start(bf16[512,3072]{1,0:T(8,128)(2,1)} %get-tuple-element.284), channel_id=1, source_target_pairs={{0,1},{1,2},{2,3},{4,5},{5,6},{6,7},{8,9},{9,10},{10,11},{12,13},{... | collective-permute-start | bytes 9437192 | tf_op jit(solution)/shard_map/ppermute | solution.py:55
  (53 other events, 478.7 us)
Sparse Core Ops, SparseCore 0:
  14.0 54.8 all-gather.8
  70.8 39.7 all-gather.10
  112.5 72.1 all-gather.12
  186.4 72.1 all-gather.14
  348.1 69.4 all-gather.18
  419.3 72.1 all-gather.16
  493.3 72.1 all-gather.20
  567.4 72.1 all-gather.22
  705.1 90.0 reduce-scatter.10
  827.9 93.2 reduce-scatter.12
  924.6 92.3 reduce-scatter.8
  1020.4 92.3 reduce-scatter.14
  1116.4 92.3 reduce-scatter.16
  1212.1 92.3 reduce-scatter.18
  1307.9 69.4 reduce-scatter.20
  1381.0 53.8 reduce-scatter.22

commit v3 on v2

--- a/solution.py
+++ b/solution.py
@@ -66,7 +66,7 @@
     for d in range(1, n):
 
         def work(gate):
-            return (use(d - 1, slots[d - 1]), *fill(d, gate))
+            return (use(d - 1, after(slots[d - 1], gate) if d > 1 else own), *fill(d, gate))
 
         (right, left, *more), (result, *filled) = travel(
             [
@@ -100,6 +100,10 @@
     order = [[i] + row for i, row in enumerate(arrival_order(n))]
     right = left = None
 
+    def sent(k):
+        ways = [order[i].index(i + n - k) for i in range(k)] + [order[i].index(i - n + k) for i in range(n - k, n)]
+        return sorted(set(ways), reverse=True)
+
     def add(value, *sums):
         if right is None:
             return value
@@ -114,9 +118,7 @@
         else:
             to_right, to_left = add(pick(place, rightward), right), add(pick(place, leftward), left)
 
-        coming = list(range(n - 2, 0, -1)) if k == 1 else []
-        if k == n - 1:
-            coming.append(0)
+        coming = [0] if k == n - 1 else [s for s in sent(k + 1) if parts[s] is None]
 
         def work(gate):
             return (*(part(s) for s in coming), *fill(k, gate))
@@ -132,7 +134,7 @@
         for s, one in zip(coming, worked):
             parts[s] = one
         took(k, more, worked[len(coming) :])
-    return parts[0].astype(F32) + (right.astype(F32) + left.astype(F32))
+    return parts[0], right, left
 
 
 def halves(n, pairs):
@@ -278,6 +280,7 @@
         whole((every, 1)),
     ]
     lse_spec = pl.BlockSpec((1, 8, every), lambda g, place: (g, 0, 0))
+    pairs = every * every * heads_q
     params = pltpu.CompilerParams(vmem_limit_bytes=58 << 20)
     forward = pl.pallas_call(
         functools.partial(attend_forward, n, heads, rows, c),
@@ -320,7 +323,7 @@
         ),
         out_shape=jax.ShapeDtypeStruct((every, heads_kv * wide), BF16),
         compiler_params=params,
-        cost_estimate=HIDES,
+        cost_estimate=pl.CostEstimate(flops=pairs * 10 * HEAD_SIZE, transcendentals=pairs, bytes_accessed=every * wide * 20),
     )
     return forward, backward
 
@@ -341,24 +344,25 @@
         dg_ref[:, at] = (gm * up * sig * (1.0 + gate * (1.0 - sig))).astype(BF16)
 
 
-def gated(x, w_gate, w_up, gm, part, before=None):
+def gated(x, w_both, gm, part, before=None):
     rows, width = x.shape
-    hidden = w_gate.shape[1]
+    hidden = w_both.shape[1] // 2
     tile = 512 if hidden % 512 == 0 else hidden
-    weight = pl.BlockSpec((width, tile), lambda j: (0, j))
+    tiles = hidden // tile
+    weight = [pl.BlockSpec((width, tile), lambda j: (0, j)), pl.BlockSpec((width, tile), lambda j: (0, j + tiles))]
     here = pl.BlockSpec((rows, tile), lambda j: (part, j))
     before = () if before is None else tuple(before)
     return pl.pallas_call(
         gated_kernel,
-        grid=(hidden // tile,),
-        in_specs=[pl.BlockSpec((rows, width), lambda j: (0, 0)), weight, weight, here]
+        grid=(tiles,),
+        in_specs=[pl.BlockSpec((rows, width), lambda j: (0, 0)), *weight, here]
         + [pl.BlockSpec(memory_space=pl.ANY)] * len(before),
         out_specs=[here] * 3,
         out_shape=[jax.ShapeDtypeStruct((2 * rows, hidden), BF16)] * 3,
         input_output_aliases={4 + i: i for i in range(len(before))},
         compiler_params=pltpu.CompilerParams(vmem_limit_bytes=50 << 20),
         cost_estimate=HIDES,
-    )(x, w_gate, w_up, gm, *before)
+    )(x, w_both, w_both, gm, *before)
 
 
 def spread_kernel(count, *refs):
@@ -369,31 +373,93 @@
     refs[-1][...] = total.astype(refs[-1].dtype)
 
 
-def spread(acts, weights, part, out, cost=HIDES):
+def spread(acts, weights, part, out, cost=HIDES, piece=0, pieces=1):
     rows, hidden = acts[0].shape[0] // 2, acts[0].shape[1]
-    width = weights[0].shape[0]
+    width = weights[0][0].shape[0] // pieces
     tile = 256 if width % 256 == 0 else width
+    tiles = width // tile
     count = len(acts)
+
+    def column_block(which):
+        return pl.BlockSpec((tile, hidden), lambda j: (j + piece * tiles, which))
+
     return pl.pallas_call(
         functools.partial(spread_kernel, count),
-        grid=(width // tile,),
+        grid=(tiles,),
         in_specs=[pl.BlockSpec((rows, hidden), lambda j: (part, 0))] * count
-        + [pl.BlockSpec((tile, hidden), lambda j: (j, 0))] * count,
+        + [column_block(which) for _, which in weights],
         out_specs=pl.BlockSpec((rows, tile), lambda j: (0, j)),
         out_shape=jax.ShapeDtypeStruct((rows, width), out),
         compiler_params=pltpu.CompilerParams(vmem_limit_bytes=50 << 20),
         cost_estimate=cost,
-    )(*acts, *weights)
+    )(*acts, *[array for array, _ in weights])
 
 
 def norm_inverse(source):
     return lax.rsqrt(jnp.mean(source * source, axis=-1, keepdims=True) + EPSILON)
 
 
-def norm_back(grad_normed, source, inverse, gain):
+def norm_back_kernel(places, masked, gain_ref, source_ref, straight_ref, *refs):
+    grads, refs = refs[: len(places)], refs[len(places) :]
+    source = source_ref[...].astype(F32)
+    width = source.shape[1]
+    inverse = lax.rsqrt(jnp.mean(source * source, axis=-1, keepdims=True) + EPSILON)
+    pieces = []
+    for half in range(2):
+        at = slice(half * width // 2, (half + 1) * width // 2)
+        terms = [
+            ref[:, at] if count == 2 else ref[...]
+            for ref, (first, count) in zip(grads, places)
+            if first <= half < first + count
+        ]
+        pieces.append(sum(term.astype(F32) for term in terms))
+    scaled = jnp.concatenate(pieces, axis=1) * gain_ref[...]
     unit_rows = source * inverse
-    scaled = grad_normed * gain
-    return inverse * (scaled - unit_rows * jnp.mean(scaled * unit_rows, axis=-1, keepdims=True))
+    grad = inverse * (scaled - unit_rows * jnp.mean(scaled * unit_rows, axis=-1, keepdims=True))
+    straight = straight_ref[...].astype(F32)
+    if masked:
+        straight = straight * refs[0][...]
+    total = straight + grad
+    if masked:
+        refs[1][...] = total
+        refs[2][...] = total.astype(BF16)
+    else:
+        refs[0][...] = total
+
+
+def norm_back(grads, source, gain, straight, mask, low):
+    rows, width = source.shape
+    tile = 64 if rows % 64 == 0 else rows
+    block = lambda wide: pl.BlockSpec((tile, wide), lambda i: (i, 0))
+    masked = mask is not None
+    out_shape = [jax.ShapeDtypeStruct((rows, width), F32)] + [jax.ShapeDtypeStruct((rows, width), BF16)] * low
+    return pl.pallas_call(
+        functools.partial(norm_back_kernel, [place for _, *place in grads], masked),
+        grid=(rows // tile,),
+        in_specs=[pl.BlockSpec((1, width), lambda i: (0, 0)), block(width), block(width)]
+        + [block(array.shape[1]) for array, _, _ in grads]
+        + [block(1)] * masked,
+        out_specs=[block(width)] * len(out_shape) if low else block(width),
+        out_shape=out_shape if low else out_shape[0],
+        compiler_params=pltpu.CompilerParams(vmem_limit_bytes=40 << 20),
+        cost_estimate=HIDES,
+    )(gain[None, :], source, straight, *[array for array, _, _ in grads], *([mask] if masked else []))
+
+
+def turn_kernel(x_ref, o_ref):
+    o_ref[...] = x_ref[...].astype(F32).T
+
+
+def turned(array, first, size):
+    rows = array.shape[0]
+    return pl.pallas_call(
+        turn_kernel,
+        grid=(size // HEAD_SIZE,),
+        in_specs=[pl.BlockSpec((rows, HEAD_SIZE), lambda j: (0, j + first // HEAD_SIZE))],
+        out_specs=pl.BlockSpec((HEAD_SIZE, rows), lambda j: (j, 0)),
+        out_shape=jax.ShapeDtypeStruct((size, rows), F32),
+        cost_estimate=HIDES,
+    )(array)
 
 
 def shards(
@@ -455,8 +521,8 @@
         return [(one, pairs[half]) for one, pairs in zip(sums, homeward)]
 
     w_down = [gather(down_t)]
-    w_gate = [gather(gate_weight)]
-    w_up = [gather(up_weight)]
+    both_weight = jnp.concatenate([gate_weight, up_weight], axis=1)
+    w_both = [gather(both_weight)]
 
     live_count = counts[0]
     own_index = place * rows + jnp.arange(rows, dtype=jnp.int32)
@@ -491,82 +557,87 @@
         lambda step, gate: tables if step == 1 else (),
         lambda step: {
             n - 2: [(grad_low, partners[0])],
-            n - 1: to_others(down_t, 0) + to_others(gate_weight, 0),
+            n - 1: to_others(both_weight, 0),
         }.get(step, ()),
         lambda step, arrived, filled: early.extend(arrived),
     )
-    low_ends, down_ends, gate_ends = early[0], early[1 : 1 + more], early[1 + more :]
+    low_ends, both_ends = early[0], early[1:]
     projected[n - 1] = after(projected[n - 1], w_out, w_down[0])
 
     def attention(gate):
         return attend(slot_table, *projected, *tables)
 
-    downs, ups = lax.optimization_barrier((down_t, up_weight, projected[n - 1]))[:2]
-    moved, (attended, rotated, lse) = travel(to_others(downs, 1) + to_others(ups, 0), attention)
-    w_down += [gather(joined(a, b)) for a, b in zip(down_ends, moved[:more])]
-    up_ends = moved[more:]
+    downs = after(down_t, projected[n - 1])
+    moved, (attended, rotated, lse) = travel([(downs, a + b) for a, b in outward], attention)
+    w_down += [gather(shard) for shard in moved]
     grad_mixed, lows = [], []
 
     def while_out(step, gate):
         if step == 1:
-            return (w_gate[0],)
+            return (w_both[0],)
         if step == n - 1:
             theirs = joined(low_ends, lows[0])
             lows.append(theirs)
-            return (w_up[0], *(dot(jnp.concatenate([grad_low, theirs], axis=0), w, NN) for w in w_down))
+            return tuple(dot(jnp.concatenate([grad_low, theirs], axis=0), w, NN) for w in w_down)
         return ()
 
     def along_out(step):
         if step == 1:
-            return to_others(gate_weight, 1) + to_others(up_weight, 1)
+            return to_others(both_weight, 1)
         if step == 2:
             return [(grad_low, partners[1])]
         return ()
 
     def took_out(step, arrived, filled):
         if step == 1:
-            w_gate.extend(gather(joined(a, b)) for a, b in zip(gate_ends, arrived[:more]))
-            w_up.extend(gather(joined(a, b)) for a, b in zip(up_ends, arrived[more:]))
+            w_both.extend(gather(joined(a, b)) for a, b in zip(both_ends, arrived))
         elif step == n - 1:
-            grad_mixed.extend(filled[1:])
+            grad_mixed.extend(filled)
         else:
             lows.extend(arrived)
 
     summed = line_reduce(
         lambda s: dot(attended[s * rows : (s + 1) * rows], w_out, NT, BF16), n, while_out, along_out, took_out
     )
-    hidden = source + summed
+    hidden = source + sum(term.astype(F32) for term in summed)
     grad_two = jnp.concatenate([grad_low, lows[1]], axis=0)
 
     inv_two = norm_inverse(hidden)
     normed_two = (hidden * inv_two * gain_two).astype(BF16)
 
     def own_rows(gate):
-        return [one for g, u, gm in zip(w_gate, w_up, grad_mixed) for one in gated(gate, g, u, gm, 0)]
-
-    (two_theirs,), mine = travel([(normed_two, partners[0] + partners[1])], own_rows)
+        made = [one for w, gm in zip(w_both, grad_mixed) for one in gated(gate, w, gm, 0)]
+        return [spread(made[1::3] + made[2::3], weights, 0, F32), *made]
+
+    swap = partners[0] + partners[1]
+    weights = [(w, 0) for w in w_both] + [(w, 1) for w in w_both]
+    (two_theirs,), (ours, *mine) = travel([(normed_two, swap)], own_rows)
     two = jnp.concatenate([normed_two, two_theirs], axis=0)
     mixed, grad_gate, grad_up, d_down = [None] * slices, [None] * slices, [None] * slices, [None] * slices
     rows_in = two_theirs
     for k in range(slices - 1, -1, -1):
-        mixed[k], grad_gate[k], grad_up[k] = gated(rows_in, w_gate[k], w_up[k], grad_mixed[k], 1, mine[3 * k : 3 * k + 3])
+        mixed[k], grad_gate[k], grad_up[k] = gated(rows_in, w_both[k], grad_mixed[k], 1, mine[3 * k : 3 * k + 3])
         if k > 0:
             d_down[k] = dot(grad_two, mixed[k], TN, BF16)
             rows_in = after(two_theirs, d_down[k])
-    grads, weights = grad_gate + grad_up, w_gate + w_up
-    theirs = spread(grads, weights, 1, BF16)
+    grads = grad_gate + grad_up
     d_up, d_gate = [None] * slices, [None] * slices
 
-    def own_sums(gate):
+    def second_half(gate):
         return (
-            spread([after(grads[0], gate)] + grads[1:], weights, 0, F32),
+            spread([after(grads[0], gate)] + grads[1:], weights, 1, BF16, HIDES, 1, 2),
             *(dot(two, after(g, gate), TN, BF16) for g in grad_up[1:]),
         )
 
-    (from_theirs,), (ours, *d_up[1:]) = travel([(theirs, partners[0] + partners[1])], own_sums)
-    grad_normed_two = ours + from_theirs.astype(F32)
-    grad_hidden_norm = norm_back(grad_normed_two, hidden, inv_two, gain_two)
-    grad_hidden = grad_result + grad_hidden_norm
+    def gate_weights(gate):
+        return tuple(dot(two, after(g, gate), TN, BF16) for g in grad_gate[1:])
+
+    theirs = spread(grads, weights, 1, BF16, HIDES, 0, 2)
+    (from_first,), (theirs, *d_up[1:]) = travel([(theirs, swap)], second_half)
+    (from_second,), d_gate[1:] = travel([(theirs, swap)], gate_weights)
+    grad_hidden, grad_hidden_low = norm_back(
+        [(ours, 0, 2), (from_first, 0, 1), (from_second, 1, 1)], hidden, gain_two, cotangent, live, True
+    )
 
     def owner_sum(partial):
         return lax.psum_scatter(partial, "dp", scatter_dimension=0, tiled=True)
@@ -577,33 +648,38 @@
         return dot(left, after(right, gate), TN, BF16)
 
     def result_rows(part, out, gate, cost=HIDES):
-        return spread([after(mixed[0], gate), *mixed[1:]], w_down, part, out, cost)
+        return spread([after(mixed[0], gate), *mixed[1:]], [(w, 0) for w in w_down], part, out, cost)
 
     def while_gather(step, gate):
         if step == 1:
             flops = 2 * rows * width * slices * gate_weight.shape[1]
             cost = pl.CostEstimate(flops=flops, transcendentals=0, bytes_accessed=flops // rows)
-            return (result_rows(1, BF16, gate, cost), *(d_of(two, g, gate) for g in grad_gate[1:]))
+            return (result_rows(1, BF16, gate, cost), d_of(grad_two, mixed[0], gate))
         if step == 2:
-            return (result_rows(0, F32, gate), d_of(grad_two, mixed[0], gate))
+            return (result_rows(0, F32, gate), d_of(two, grad_up[0], gate), *joined_sums())
         if step == n - 1:
-            return (d_of(two, grad_up[0], gate),)
+            return (d_of(two, grad_gate[0], gate),)
         return ()
 
     def took_gather(step, arrived, filled):
         early.extend(arrived)
         if step == 1:
             results.append(filled[0])
-            d_gate[1:] = filled[1:]
+            d_down[0] = filled[1]
         elif step == 2:
             results.append(filled[0])
-            d_down[0] = filled[1]
+            d_up[0] = filled[1]
+            sums.extend(filled[2:])
         elif step == n - 1:
-            d_up[0] = filled[0]
-
-    sums = [jnp.concatenate([owner_sum(a), owner_sum(b)], axis=1) for a, b in zip(d_down[1:], d_up[1:])]
+            d_gate[0] = filled[0]
+
+    sums = []
+
+    def joined_sums():
+        return [jnp.concatenate([owner_sum(a), owner_sum(b)], axis=1) for a, b in zip(d_down[1:], d_up[1:])]
+
     slots_back, grad_attended = line_gather(
-        grad_hidden.astype(BF16),
+        grad_hidden_low,
         n,
         lambda s, shard: dot(shard, w_out, NN, BF16),
         while_gather,
@@ -617,24 +693,25 @@
 
     def attention_back(gate):
         return (
-            attend_back(slot_table, *grad_attended, rotated, attended, lse, *tables),
-            d_of(two, grad_gate[0], gate),
+            attend_back(after(slot_table, gate), *grad_attended, rotated, attended, lse, *tables),
+            d_of(jnp.concatenate(slots_back, axis=0), attended, gate),
             sum_down,
         )
 
     sums_gate = [owner_sum(d) for d in d_gate[1:]]
-    sum_down, sum_up = owner_sum(d_down[0]), owner_sum(d_up[0])
+    sum_down, sum_up, sum_gate = owner_sum(d_down[0]), owner_sum(d_up[0]), owner_sum(d_gate[0])
     leaving = [after(one, grad_attended[n - 1]) for one in sums_gate]
-    moved, (grad_qkv, d_gate[0], _) = travel(to_owners(leaving, 0) + to_owners(leaving, 1), attention_back)
-    back_gate = [joined(a, b) for a, b in zip(moved[:more], moved[more:])]
-    back_down, back_up, outputs, d_own = [], [], [], []
-    sum_gate = owner_sum(d_gate[0])
+    back_gate, (grad_qkv, d_out, _) = travel(
+        [(one, a + b) for one, (a, b) in zip(leaving, homeward)], attention_back
+    )
+    back_down, back_up, outputs, d_attention = [], [], [], []
 
     def while_reduce(step, gate):
         if step == 1:
-            return (d_of(jnp.concatenate(slots_one, axis=0), grad_qkv, gate), sum_up)
+            d_qkv = d_of(jnp.concatenate(slots_one, axis=0), grad_qkv, gate)
+            return (jnp.concatenate([d_qkv, d_out], axis=1), sum_up)
         if step == 2:
-            return (d_of(jnp.concatenate(slots_back, axis=0), attended, gate), sum_gate)
+            return (sum_gate,)
         if step == n - 1:
             from_partner = joined(result_ends, outputs[0])
             result = hidden + (results[1] + after(from_partner, gate).astype(F32))
@@ -654,10 +731,9 @@
                 back = joined(a, b)
                 back_down.append(back[:, : down_t.shape[1]])
                 back_up.append(back[:, down_t.shape[1] :])
-            d_own.append(filled[0])
+            d_attention.append(filled[0])
         elif step == 2:
             outputs.extend(arrived)
-            d_own.append(filled[0])
         elif step == n - 1:
             outputs.append(filled[0])
 
@@ -673,14 +749,14 @@
     def whole(first, back):
         return sum((one.astype(F32) for one in back), first.astype(F32))
 
+    all_heads = own_qkv.shape[1]
     grad_down_w = whole(sum_down, back_down).T
+    grad_gate_w = whole(sum_gate, back_gate)
     grad_up_w = whole(sum_up, back_up)
-    grad_gate_w = whole(sum_gate, back_gate)
-    sum_qkv = owner_sum(d_own[0])
-    grad_qkv_w = sum_qkv.astype(F32)
-    grad_out_w = owner_sum(after(d_own[1], sum_qkv)).astype(F32).T
-    grad_input_norm = norm_back(grad_normed_one, source, inv_one, gain_one)
-    grad_tokens = grad_hidden + grad_input_norm
+    sum_attention = owner_sum(d_attention[0])
+    grad_qkv_w = sum_attention[:, :all_heads].astype(F32)
+    grad_out_w = turned(sum_attention, all_heads, out_weight.shape[0])
+    grad_tokens = norm_back([(term, 0, 2) for term in grad_normed_one], tokens, gain_one, grad_hidden, None, False)
 
     def along_row(weight, grad):
         return jnp.sum(weight.astype(F32) * grad, axis=1)

time: 1460 us -> 1440 us (0.986)
  Pallas kernels: 303 us -> 334 us
  other arithmetic: 142 us -> 117 us
  starting transfers between devices: 134 us -> 114 us
    pallas_call x9 -> x13, Pallas kernels: 260 us -> 291 us  [the longest x5 120 us: spread(): pl.pallas_call(functools.partial(spread_kernel, count), grid=(tiles,), in...]
    ppermute x40 -> x37, waiting for transfers between devices: 419 us -> 449 us  [travel(): lax.ppermute(array, 'tensor', pairs)]
    all_gather x8 -> x6, waiting for transfers between devices: 22.2 us -> 0.8 us  [gather(): return lax.all_gather(shard, 'dp', axis=0, tiled=True)]
    ppermute x40 -> x37, starting transfers between devices: 133 us -> 113 us  [travel(): lax.ppermute(array, 'tensor', pairs)]
    reduce_scatter x8 -> x7, waiting for transfers between devices: 42.2 us -> 22.6 us  [owner_sum(): return lax.psum_scatter(partial, 'dp', scatter_dimension=0, tiled=True)]
  transfers between devices with their start and end apart: 56 -> 50, of which waited for: 27 -> 27; matrix products, arithmetic and copies ran while one was open for 30% -> 29% of each run, Pallas kernels for 19% -> 21%
where the time goes in v3:
time: 1440 us; the launch traced here: 1430 us
  waiting for transfers between devices  474 us (33%)
  Pallas kernels  334 us (23%)
  matrix products  312 us (22%)
  other arithmetic  117 us (8%)
  starting transfers between devices  114 us (8%)
  local copies, waits for them, and re-layouts  36 us (2%)
  blocking collectives  32.1 us (2%)
  between operations  15.6 us (1%)
    ppermute x37, waiting for transfers between devices, travel(): lax.ppermute(array, 'tensor', pairs)  449 us
    dot_general x26, matrix products, dot(): return lax.dot_general(a, b, dims, preferred_element_type=F32).astype(out)  312 us
    pallas_call x5, Pallas kernels, spread(): pl.pallas_call(functools.partial(spread_kernel, count), grid=(tiles,), in...  120 us
    ppermute x37, starting transfers between devices, travel(): lax.ppermute(array, 'tensor', pairs)  113 us
    pallas_call x4, Pallas kernels, gated(): pl.pallas_call(gated_kernel, grid=(tiles,), in_specs=[pl.BlockSpec((rows,...  87.3 us
    pallas_call x1, Pallas kernels, attention_back(): attend_back(after(slot_table, gate), *grad_attended, rotated, attended, l...  55.6 us
    pallas_call x1, Pallas kernels, attention(): return attend(slot_table, *projected, *tables)  43.1 us
  transfers between devices with their start and end apart: 50, of which 27 were waited for; matrix products, arithmetic and copies ran while one was open for 29% of the time, Pallas kernels for 21%

profile of v3, /device:TPU:0, one launch (start us, length us, event | category | flops | bytes accessed | tf_op | source)
XLA Modules:
  0.0 1434.6 jit_solution(2275797690451701521)
XLA Ops:
  22.0 10.4 all_gather.24
  32.4 13.4 all_gather.25
  69.0 9.9 fusion.44.refs_0_
  78.9 39.2 %collective-permute-done = bf16[512,3072]{1,0:T(8,128)(2,1)} collective-permute-done((bf16[512,3072]{1,0:T(8,128)(2,1)}, bf16[512,3072]{1,0:T(8,128)(2,1)}, u32[]{:S(2)}, u32[]{:S(2)}) %collective-permute-start) | collective-permute-done | bytes 3145760 | tf_op jit(solution)/shard_map/ppermute | solution.py:55
  127.4 7.0 collective-permute-start.4
  144.4 50.8 %collective-permute-done.3 = bf16[512,3072]{1,0:T(8,128)(2,1)} collective-permute-done((bf16[512,3072]{1,0:T(8,128)(2,1)}, bf16[512,3072]{1,0:T(8,128)(2,1)}, u32[]{:S(2)}, u32[]{:S(2)}) %collective-permute-start.3) | collective-permute-done | bytes 3145760 | tf_op jit(solution)/shard_map/ppermute | solution.py:55
  198.5 9.2 collective-permute-start.7
  210.0 9.2 fusion.46.refs_2_
  219.1 45.3 %collective-permute-done.6 = bf16[512,3072]{1,0:T(8,128)(2,1)S(1)} collective-permute-done((bf16[512,3072]{1,0:T(8,128)(2,1)}, bf16[512,3072]{1,0:T(8,128)(2,1)S(1)}, u32[]{:S(2)}, u32[]{:S(2)}) %collective-permute-start.6) | collective-permute-done | bytes 3145760 | tf_op jit(solution)/shard_map/ppermute | solution.py:55
  270.9 8.2 fusion.47.refs_3_
  285.6 43.1 %shard_map.230 = (bf16[2048,768]{1,0:T(8,128)(2,1)}, bf16[2048,1280]{1,0:T(8,128)(2,1)}, f32[2,8,2048]{2,1,0:T(8,128)}) custom-call(s32[8]{0:T(128)} %dynamic-slice_bitcast_fusion.place_ref, f32[512,1280]{1,0:T(8,128)} %fusion.44.refs_0_, f32[512,1280]{1,0:T(8,128)} %fusion.45.refs_1_, f32[512,1280]{1,0:T(8,128)} %fusion.46.refs_2_, ...), custom_call_target="tpu_custom_call" | custom-call | flops 1 | bytes 1 | tf_op jit(solution)/shard_map/pallas_call | solution.py:568
  328.7 17.9 %collective-permute-done.8 = bf16[384,2048]{1,0:T(8,128)(2,1)} collective-permute-done((bf16[384,2048]{1,0:T(8,128)(2,1)}, bf16[384,2048]{1,0:T(8,128)(2,1)}, u32[]{:S(2)}, u32[]{:S(2)}) %collective-permute-start.8) | collective-permute-done | bytes 1572896 | tf_op jit(solution)/shard_map/ppermute | solution.py:55
  354.1 7.7 collective-permute-start.9
  361.8 6.9 convolution_convert_fusion.8
  370.3 55.5 %collective-permute-done.11 = bf16[384,4096]{1,0:T(8,128)(2,1)S(1)} collective-permute-done((bf16[384,4096]{1,0:T(8,128)(2,1)}, bf16[384,4096]{1,0:T(8,128)(2,1)S(1)}, u32[]{:S(2)}, u32[]{:S(2)}) %collective-permute-start.11) | collective-permute-done | bytes 3145760 | tf_op jit(solution)/shard_map/ppermute | solution.py:55
  433.4 6.5 add_convert_fusion.5
  451.3 6.6 convolution_convert_fusion.6
  457.9 51.6 %collective-permute-done.12 = bf16[512,3072]{1,0:T(8,128)(2,1)S(1)} collective-permute-done((bf16[512,3072]{1,0:T(8,128)(2,1)S(1)}, bf16[512,3072]{1,0:T(8,128)(2,1)S(1)}, u32[]{:S(2)}, u32[]{:S(2)}) %collective-permute-start.12) | collective-permute-done | bytes 3145760 | tf_op jit(solution)/shard_map/ppermute | solution.py:55
  529.1 17.3 %fusion.40.gm_ref = f32[1024,2048]{1,0:T(8,128)} fusion(bf16[3072,2048]{1,0:T(8,128)(2,1)S(1)} %bitcast.56, bf16[512,3072]{1,0:T(8,128)(2,1)S(1)} %add.134, bf16[512,3072]{1,0:T(8,128)(2,1)} %multiply_convert_fusion.2), kind=kOutput, calls=%fused_computation.114 | convolution fusion | flops 12897484800 | bytes 27262976 | tf_op jit(solution)/shard_map/dot_general | solution.py:25
  546.3 19.1 %fusion.39.gm_ref = f32[1024,2048]{1,0:T(8,128)} fusion(bf16[3072,2048]{1,0:T(8,128)(2,1)} %all-gather.15.cloned.1.call-done.refs_3_, bf16[512,3072]{1,0:T(8,128)(2,1)} %copy-done.24, bf16[512,3072]{1,0:T(8,128)(2,1)} %multiply_convert_fusion.2), kind=kOutput, calls=%fused_computation.113 | convolution fusion | flops 12897484800 | bytes 27262976 | tf_op jit(solution)/shard_map/dot_general | solution.py:25
  565.4 21.0 %collective-permute-done.15 = bf16[512,3072]{1,0:T(8,128)(2,1)} collective-permute-done((bf16[512,3072]{1,0:T(8,128)(2,1)}, bf16[512,3072]{1,0:T(8,128)(2,1)}, u32[]{:S(2)}, u32[]{:S(2)}) %collective-permute-start.15) | collective-permute-done | bytes 3145760 | tf_op jit(solution)/shard_map/ppermute | solution.py:55
  600.6 21.2 %shard_map.231 = (bf16[1024,2048]{1,0:T(8,128)(2,1)}, bf16[1024,2048]{1,0:T(8,128)(2,1)}, bf16[1024,2048]{1,0:T(8,128)(2,1)}) custom-call(bf16[512,3072]{1,0:T(8,128)(2,1)} %multiply_convert_fusion.1.x_ref, bf16[3072,4096]{1,0:T(8,128)(2,1)} %all-gather.13.cloned.1.call-done.gate_ref.up_ref.refs_4_.refs_6_, ...), custom_call_target="tpu_custom_call" | custom-call | flops 1 | bytes 1 | tf_op jit(solution)/shard_map/pallas_call | solution.py:355
  621.8 21.0 %shard_map.232 = (bf16[1024,2048]{1,0:T(8,128)(2,1)}, bf16[1024,2048]{1,0:T(8,128)(2,1)}, bf16[1024,2048]{1,0:T(8,128)(2,1)}) custom-call(bf16[512,3072]{1,0:T(8,128)(2,1)} %multiply_convert_fusion.1.x_ref, bf16[3072,4096]{1,0:T(8,128)(2,1)} %all-gather.17.cloned.1.call-done.gate_ref.up_ref.refs_5_.refs_7_, ...), custom_call_target="tpu_custom_call" | custom-call | flops 1 | bytes 1 | tf_op jit(solution)/shard_map/pallas_call | solution.py:355
  642.8 34.6 %shard_map.233.refs_0_ = f32[512,3072]{1,0:T(8,128)} custom-call(bf16[1024,2048]{1,0:T(8,128)(2,1)} %get-tuple-element.217.refs_0_.refs_1_, bf16[1024,2048]{1,0:T(8,128)(2,1)} %get-tuple-element.212.refs_1_, bf16[1024,2048]{1,0:T(8,128)(2,1)} %get-tuple-element.218.refs_2_, bf16[1024,2048]{1,0:T(8,128)(2,1)} %get-tuple-element.213.refs_3_.refs_2_, ...), custom_call_target="tpu_custom_call" | custom-call | flops 1 | bytes 1 | tf_op jit(solution)/shard_map/pallas_call | solution.py:386
  677.4 21.2 %shard_map.234 = (bf16[1024,2048]{1,0:T(8,128)(2,1)}, bf16[1024,2048]{1,0:T(8,128)(2,1)}, bf16[1024,2048]{1,0:T(8,128)(2,1)}) custom-call(bf16[512,3072]{1,0:T(8,128)(2,1)} %collective-permute-done.17.x_ref, ...), custom_call_target="tpu_custom_call", output_to_operand_aliasing={{0}: (4, {}), {1}: (5, {}), {2}: (6, {})} | custom-call | flops 1 | bytes 1 | tf_op jit(solution)/shard_map/pallas_call | solution.py:355
  698.7 19.4 %convolution_convert_fusion.5 = bf16[3072,2048]{1,0:T(8,128)(2,1)} fusion(bf16[1024,2048]{1,0:T(8,128)(2,1)} %get-tuple-element.214.refs_1_, bf16[512,3072]{1,0:T(8,128)(2,1)S(1)} %copy-done.25, bf16[512,3072]{1,0:T(8,128)(2,1)} %multiply_convert_fusion.2), kind=kOutput, calls=%fused_computation.23 | convolution fusion | flops 12903776256 | bytes 23068672 | tf_op jit(solution)/shard_map/dot_general | solution.py:25
  718.1 23.9 %shard_map.235 = (bf16[1024,2048]{1,0:T(8,128)(2,1)}, bf16[1024,2048]{1,0:T(8,128)(2,1)}, bf16[1024,2048]{1,0:T(8,128)(2,1)}) custom-call(bf16[512,3072]{1,0:T(8,128)(2,1)} %collective-permute-done.17.x_ref, ...), custom_call_target="tpu_custom_call", output_to_operand_aliasing={{0}: (4, {}), {1}: (5, {}), {2}: (6, {})} | custom-call | flops 1 | bytes 1 | tf_op jit(solution)/shard_map/pallas_call | solution.py:355
  742.0 21.1 %shard_map.236 = bf16[512,1536]{1,0:T(8,128)(2,1)} custom-call(bf16[1024,2048]{1,0:T(8,128)(2,1)} %get-tuple-element.253.refs_0_, bf16[1024,2048]{1,0:T(8,128)(2,1)} %get-tuple-element.226.refs_1_, bf16[1024,2048]{1,0:T(8,128)(2,1)} %get-tuple-element.244.refs_2_, bf16[1024,2048]{1,0:T(8,128)(2,1)} %get-tuple-element.224.refs_3_, ...), custom_call_target="tpu_custom_call" | custom-call | flops 1 | bytes 1 | tf_op jit(solution)/shard_map/pallas_call | solution.py:386
  765.3 19.8 %shard_map.237 = bf16[512,1536]{1,0:T(8,128)(2,1)S(1)} custom-call(bf16[1024,2048]{1,0:T(8,128)(2,1)} %get-tuple-element.253.refs_0_, bf16[1024,2048]{1,0:T(8,128)(2,1)} %get-tuple-element.226.refs_1_, bf16[1024,2048]{1,0:T(8,128)(2,1)} %get-tuple-element.244.refs_2_, bf16[1024,2048]{1,0:T(8,128)(2,1)} %get-tuple-element.224.refs_3_, ...), custom_call_target="tpu_custom_call" | custom-call | flops 1 | bytes 1 | tf_op jit(solution)/shard_map/pallas_call | solution.py:386
  786.3 18.6 %convolution_convert_fusion.4 = bf16[3072,2048]{1,0:T(8,128)(2,1)} fusion(bf16[1024,2048]{1,0:T(8,128)(2,1)S(1)} %copy-done.10, bf16[512,3072]{1,0:T(8,128)(2,1)} %collective-permute-done.17.x_ref, bf16[512,3072]{1,0:T(8,128)(2,1)} %multiply_convert_fusion.1.x_ref), kind=kOutput, calls=%fused_computation.22 | convolution fusion | flops 12903776256 | bytes 23068672 | tf_op jit(solution)/shard_map/dot_general | solution.py:25
  805.2 20.7 %convolution_convert_fusion.3 = bf16[3072,2048]{1,0:T(8,128)(2,1)} fusion(bf16[1024,2048]{1,0:T(8,128)(2,1)} %get-tuple-element.226.refs_1_, bf16[512,3072]{1,0:T(8,128)(2,1)} %collective-permute-done.17.x_ref, bf16[512,3072]{1,0:T(8,128)(2,1)} %multiply_convert_fusion.1.x_ref), kind=kOutput, calls=%fused_computation.21 | convolution fusion | flops 12903776256 | bytes 23068672 | tf_op jit(solution)/shard_map/dot_general | solution.py:25
  825.9 10.1 collective-permute-done.19.refs_2_
  838.0 12.6 shard_map.238
  855.9 22.1 %shard_map.239 = bf16[512,3072]{1,0:T(8,128)(2,1)} custom-call(bf16[1024,2048]{1,0:T(8,128)(2,1)} %get-tuple-element.243.refs_0_, bf16[1024,2048]{1,0:T(8,128)(2,1)} %get-tuple-element.214.refs_1_, bf16[3072,2048]{1,0:T(8,128)(2,1)} %all-gather.11.cloned.1.call-done.refs_2_, bf16[3072,2048]{1,0:T(8,128)(2,1)} %all-gather.15.cloned.1.call-done.refs_3_), custom_call_target="tpu_custom_call" | custom-call | flops 12884901888 | bytes 25165824 | tf_op jit(solution)/shard_map/pallas_call | solution.py:386
  878.0 7.1 convolution_convert_fusion.17.refs_0_
  885.1 17.9 %convolution_convert_fusion.2 = bf16[3072,2048]{1,0:T(8,128)(2,1)} fusion(bf16[1024,2048]{1,0:T(8,128)(2,1)S(1)} %copy-done.11, bf16[512,3072]{1,0:T(8,128)(2,1)S(1)} %copy-done.26, bf16[512,3072]{1,0:T(8,128)(2,1)} %multiply_convert_fusion.2), kind=kOutput, calls=%fused_computation.20 | convolution fusion | flops 12903776256 | bytes 23068672 | tf_op jit(solution)/shard_map/dot_general | solution.py:25
  903.1 12.5 collective-permute-done.20
  928.3 7.7 collective-permute-start.24
  942.1 22.6 %shard_map.240 = f32[512,3072]{1,0:T(8,128)} custom-call(bf16[1024,2048]{1,0:T(8,128)(2,1)} %get-tuple-element.243.refs_0_, bf16[1024,2048]{1,0:T(8,128)(2,1)} %get-tuple-element.214.refs_1_, bf16[3072,2048]{1,0:T(8,128)(2,1)} %all-gather.11.cloned.1.call-done.refs_2_, bf16[3072,2048]{1,0:T(8,128)(2,1)} %all-gather.15.cloned.1.call-done.refs_3_), custom_call_target="tpu_custom_call" | custom-call | flops 1 | bytes 1 | tf_op jit(solution)/shard_map/pallas_call | solution.py:386
  964.7 18.7 %convolution_convert_fusion.1 = bf16[3072,2048]{1,0:T(8,128)(2,1)} fusion(bf16[1024,2048]{1,0:T(8,128)(2,1)S(1)} %copy-done.9, bf16[512,3072]{1,0:T(8,128)(2,1)} %collective-permute-done.17.x_ref, bf16[512,3072]{1,0:T(8,128)(2,1)} %multiply_convert_fusion.1.x_ref), kind=kOutput, calls=%fused_computation.19 | convolution fusion | flops 12903776256 | bytes 23068672 | tf_op jit(solution)/shard_map/dot_general | solution.py:25
  987.3 8.8 collective-permute-done.23
  1003.5 11.2 collective-permute-start.27
  1014.8 7.1 convolution_convert_fusion.15.refs_2_
  1021.9 19.2 %convolution_convert_fusion = bf16[3072,2048]{1,0:T(8,128)(2,1)} fusion(bf16[1024,2048]{1,0:T(8,128)(2,1)S(1)} %copy-done.8, bf16[512,3072]{1,0:T(8,128)(2,1)} %collective-permute-done.17.x_ref, bf16[512,3072]{1,0:T(8,128)(2,1)} %multiply_convert_fusion.1.x_ref), kind=kOutput, calls=%fused_computation.18 | convolution fusion | flops 12903776256 | bytes 23068672 | tf_op jit(solution)/shard_map/dot_general | solution.py:25
  1041.1 27.8 %collective-permute-done.26 = bf16[512,3072]{1,0:T(8,128)(2,1)} collective-permute-done((bf16[512,3072]{1,0:T(8,128)(2,1)}, bf16[512,3072]{1,0:T(8,128)(2,1)}, u32[]{:S(2)}, u32[]{:S(2)}) %collective-permute-start.26) | collective-permute-done | bytes 3145760 | tf_op jit(solution)/shard_map/ppermute | solution.py:55
  1090.3 55.6 %shard_map.241 = bf16[2048,1280]{1,0:T(8,128)(2,1)} custom-call(s32[8]{0:T(128)} %dynamic-slice_bitcast_fusion.place_ref, bf16[512,768]{1,0:T(8,128)(2,1)} %convolution_convert_fusion.17.refs_0_, bf16[512,768]{1,0:T(8,128)(2,1)} %convolution_convert_fusion.16.refs_1_, bf16[512,768]{1,0:T(8,128)(2,1)} %convolution_convert_fusion.15.refs_2_, ...), custom_call_target="tpu_custom_call" | custom-call | flops 32212254720 | bytes 26214400 | tf_op jit(solution)/shard_map/pallas_call | solution.py:696
  1145.9 15.9 %fusion.22 = bf16[3072,768]{1,0:T(8,128)(2,1)} fusion(bf16[2048,768]{1,0:T(8,128)(2,1)} %get-tuple-element.263.refs_5_, bf16[512,3072]{1,0:T(8,128)(2,1)} %copy-done.31, bf16[512,3072]{1,0:T(8,128)(2,1)} %copy-done.28, bf16[512,3072]{1,0:T(8,128)(2,1)} %copy-done.27, bf16[512,3072]{1,0:T(8,128)(2,1)} %get-tuple-element.233), kind=kOutput, calls=%fused_computation.42 | convolution fusion | flops 9716367360 | bytes 20447232 | tf_op jit(solution)/shard_map/dot_general | solution.py:25
  1161.8 9.8 convolution_convert_fusion.13
  1178.3 20.8 %fusion.16 = bf16[3072,1280]{1,0:T(8,128)(2,1)S(1)} fusion(bf16[2048,1280]{1,0:T(8,128)(2,1)} %shard_map.241, bf16[512,3072]{1,0:T(8,128)(2,1)} %copy-done.23, bf16[512,3072]{1,0:T(8,128)(2,1)} %copy-done.22, bf16[512,3072]{1,0:T(8,128)(2,1)S(1)} %copy-done.21, bf16[512,3072]{1,0:T(8,128)(2,1)} %fusion.21), kind=kOutput, calls=%fused_computation.17 | convolution fusion | flops 16160391168 | bytes 25690112 | tf_op jit(solution)/shard_map/dot_general | solution.py:25
  1199.1 8.6 pad_maximum_fusion
  1207.7 11.8 convolution_convert_fusion.12
  1219.6 13.0 collective-permute-done.29
  1232.5 9.1 collective-permute-done.31
  1241.6 8.3 add_convert_fusion.2
  1257.0 9.7 convolution_convert_fusion.11
  1266.7 22.6 %reduce-scatter.18.cloned.1.call-done = bf16[384,2048]{1,0:T(8,128)(2,1)} async-done(((bf16[3072,2048]{1,0:T(8,128)(2,1)}), bf16[384,2048]{1,0:T(8,128)(2,1)}) %reduce-scatter.18.cloned.1.call-update) | async-done | bytes 1572880 | tf_op jit(solution)/shard_map/reduce_scatter | solution.py:643
  1289.3 20.9 %collective-permute-done.32 = bf16[512,3072]{1,0:T(8,128)(2,1)} collective-permute-done((bf16[512,3072]{1,0:T(8,128)(2,1)}, bf16[512,3072]{1,0:T(8,128)(2,1)}, u32[]{:S(2)}, u32[]{:S(2)}) %collective-permute-start.32) | collective-permute-done | bytes 3145760 | tf_op jit(solution)/shard_map/ppermute | solution.py:55
  1310.2 8.1 collective-permute-done.34
  1318.3 8.9 add_convert_fusion
  1332.2 10.0 convolution_convert_fusion.10.refs_0_
  1364.3 7.8 multiply_convert_fusion
  1372.1 17.4 %collective-permute-done.35.refs_1_ = bf16[512,3072]{1,0:T(8,128)(2,1)} collective-permute-done((bf16[512,3072]{1,0:T(8,128)(2,1)}, bf16[512,3072]{1,0:T(8,128)(2,1)}, u32[]{:S(2)}, u32[]{:S(2)}) %collective-permute-start.35) | collective-permute-done | bytes 3145760 | tf_op jit(solution)/shard_map/ppermute | solution.py:55
  1395.3 10.8 shard_map.242
  1409.7 8.4 psum.7
  (261 shorter events, 259.2 us)
Async XLA Ops:
  7.2 61.8 %all-gather.7.cloned.1.call-start = ((), (), s32[]{:S(2)}) async-start(), calls=%async_computation.7 | async-start | bytes 8847360 | tf_op jit(solution)/shard_map/all_gather | solution.py:493
  13.9 265.2 %all-gather.9.cloned.1.call-start = ((), (), s32[]{:S(2)}) async-start(), calls=%async_computation.8 | async-start | bytes 5308416 | tf_op jit(solution)/shard_map/all_gather | solution.py:493
  14.7 264.5 %all-gather.11.cloned.1.call-start = ((), (), s32[]{:S(2)}) async-start(), calls=%async_computation.9 | async-start | bytes 14155776 | tf_op jit(solution)/shard_map/all_gather | solution.py:493
  17.4 410.2 %all-gather.13.cloned.1.call-start = ((), (), s32[]{:S(2)}) async-start(), calls=%async_computation.10 | async-start | bytes 28311552 | tf_op jit(solution)/shard_map/all_gather | solution.py:493
  18.9 13.5 copy-start.42
  18.9 26.9 %copy-start = (bf16[512,3072]{1,0:T(8,128)(2,1)S(1)}, bf16[512,3072]{1,0:T(8,128)(2,1)}, u32[]{:S(2)}) copy-start(bf16[512,3072]{1,0:T(8,128)(2,1)} %source_ref.1) | copy-start | bytes 9437188
  21.8 524.5 %all-gather.15.cloned.1.call-start = ((), (), s32[]{:S(2)}) async-start(), calls=%async_computation.11 | async-start | bytes 14155776 | tf_op jit(solution)/shard_map/all_gather | solution.py:493
  49.3 68.7 %collective-permute-start = (bf16[512,3072]{1,0:T(8,128)(2,1)}, bf16[512,3072]{1,0:T(8,128)(2,1)}, u32[]{:S(2)}, u32[]{:S(2)}) collective-permute-start(bf16[512,3072]{1,0:T(8,128)(2,1)} %fusion.21), channel_id=1, source_target_pairs={{0,1},{1,2},{2,3},{4,5},{5,6},{6,7},{8,9},{9,10},{10,11},{12,13},{... | collective-permute-start | bytes 9437192 | tf_op jit(solution)/shard_map/ppermute | solution.py:55
  54.4 69.4 %collective-permute-start.1 = (bf16[512,3072]{1,0:T(8,128)(2,1)}, bf16[512,3072]{1,0:T(8,128)(2,1)}, u32[]{:S(2)}, u32[]{:S(2)}) collective-permute-start(bf16[512,3072]{1,0:T(8,128)(2,1)} %fusion.21), channel_id=1, source_target_pairs={{1,0},{2,1},{3,2},{5,4},{6,5},{7,6},{9,8},{10,9},{11,10},{13,12},{... | collective-permute-start | bytes 9437192 | tf_op jit(solution)/shard_map/ppermute | solution.py:55
  123.8 20.6 %collective-permute-start.2 = (bf16[512,3072]{1,0:T(8,128)(2,1)}, bf16[512,3072]{1,0:T(8,128)(2,1)}, u32[]{:S(2)}, u32[]{:S(2)}) collective-permute-start(bf16[512,3072]{1,0:T(8,128)(2,1)} %collective-permute-done), channel_id=1, source_target_pairs={{1,2},{2,3},{5,6},{6,7},{9,10},{10,11},{13,14},{14,15},{17,18},{18... | collective-permute-start | bytes 9437192 | tf_op jit(solution)/shard_map/ppermute | solution.py:55
  126.2 69.0 %collective-permute-start.3 = (bf16[512,3072]{1,0:T(8,128)(2,1)}, bf16[512,3072]{1,0:T(8,128)(2,1)}, u32[]{:S(2)}, u32[]{:S(2)}) collective-permute-start(bf16[512,3072]{1,0:T(8,128)(2,1)} %collective-permute-done.1), channel_id=1, source_target_pairs={{1,0},{2,1},{5,4},{6,5},{9,8},{10,9},{13,12},{14,13},{17,16},{18,1... | collective-permute-start | bytes 9437192 | tf_op jit(solution)/shard_map/ppermute | solution.py:55
  127.4 68.9 %collective-permute-start.4 = (bf16[512,3072]{1,0:T(8,128)(2,1)}, bf16[512,3072]{1,0:T(8,128)(2,1)}, u32[]{:S(2)}, u32[]{:S(2)}) collective-permute-start(bf16[512,3072]{1,0:T(8,128)(2,1)} %multiply_convert_fusion.2), channel_id=1, source_target_pairs={{0,1},{3,2},{4,5},{7,6},{8,9},{11,10},{12,13},{15,14},{16,17},{19,... | collective-permute-start | bytes 9437192 | tf_op jit(solution)/shard_map/ppermute | solution.py:55
  196.3 22.8 %collective-permute-start.5 = (bf16[512,3072]{1,0:T(8,128)(2,1)}, bf16[512,3072]{1,0:T(8,128)(2,1)S(1)}, u32[]{:S(2)}, u32[]{:S(2)}) collective-permute-start(bf16[512,3072]{1,0:T(8,128)(2,1)} %collective-permute-done.2), channel_id=1, source_target_pairs={{2,3},{6,7},{10,11},{14,15},{18,19},{22,23},{26,27},{30,31}} | collective-permute-start | bytes 9437192 | tf_op jit(solution)/shard_map/ppermute | solution.py:55
  197.2 67.3 %collective-permute-start.6 = (bf16[512,3072]{1,0:T(8,128)(2,1)}, bf16[512,3072]{1,0:T(8,128)(2,1)S(1)}, u32[]{:S(2)}, u32[]{:S(2)}) collective-permute-start(bf16[512,3072]{1,0:T(8,128)(2,1)} %collective-permute-done.3), channel_id=1, source_target_pairs={{1,0},{5,4},{9,8},{13,12},{17,16},{21,20},{25,24},{29,28}} | collective-permute-start | bytes 9437192 | tf_op jit(solution)/shard_map/ppermute | solution.py:55
  198.5 70.0 %collective-permute-start.7 = (bf16[384,4096]{1,0:T(8,128)(2,1)}, bf16[384,4096]{1,0:T(8,128)(2,1)}, u32[]{:S(2)}, u32[]{:S(2)}) collective-permute-start(bf16[384,4096]{1,0:T(8,128)(2,1)} %constant_dynamic-update-slice_fusion), channel_id=1, source_target_pairs={{3,1},{0,2},{7,5},{4,6},{11,9},{8,10},{15,13},{12,14},{19,17},{16,... | collective-permute-start | bytes 9437192 | tf_op jit(solution)/shard_map/ppermute | solution.py:55
  279.1 67.5 %collective-permute-start.8 = (bf16[384,2048]{1,0:T(8,128)(2,1)}, bf16[384,2048]{1,0:T(8,128)(2,1)}, u32[]{:S(2)}, u32[]{:S(2)}) collective-permute-start(bf16[384,2048]{1,0:T(8,128)(2,1)} %bitcast.58), channel_id=1, source_target_pairs={{3,1},{0,2},{2,0},{1,3},{7,5},{4,6},{6,4},{5,7},{11,9},{8,10},{10,... | collective-permute-start | bytes 4718600 | tf_op jit(solution)/shard_map/ppermute | solution.py:55
  346.7 275.2 %all-gather.17.cloned.1.call-start = ((), (), s32[]{:S(2)}) async-start(), calls=%async_computation.12 | async-start | bytes 28311552 | tf_op jit(solution)/shard_map/all_gather | solution.py:493
  351.9 16.7 %copy-start.29 = (bf16[512,3072]{1,0:T(8,128)(2,1)}, bf16[512,3072]{1,0:T(8,128)(2,1)S(1)}, u32[]{:S(2)}) copy-start(bf16[512,3072]{1,0:T(8,128)(2,1)S(1)} %convolution_convert_fusion.9) | copy-start | bytes 9437188
  351.9 16.7 %collective-permute-start.10 = (bf16[512,3072]{1,0:T(8,128)(2,1)S(1)}, bf16[512,3072]{1,0:T(8,128)(2,1)S(1)}, u32[]{:S(2)}, u32[]{:S(2)}) collective-permute-start(bf16[512,3072]{1,0:T(8,128)(2,1)S(1)} %convolution_convert_fusion.9), channel_id=1, source_target_pairs={{3,2},{7,6},{11,10},{15,14},{19,18},{23,22},{27,26},{31,30}} | collective-permute-start | bytes 9437192 | tf_op jit(solution)/shard_map/ppermute | solution.py:55
  352.8 73.0 %collective-permute-start.11 = (bf16[384,4096]{1,0:T(8,128)(2,1)}, bf16[384,4096]{1,0:T(8,128)(2,1)S(1)}, u32[]{:S(2)}, u32[]{:S(2)}) collective-permute-start(bf16[384,4096]{1,0:T(8,128)(2,1)} %constant_dynamic-update-slice_fusion), channel_id=1, source_target_pairs={{2,0},{1,3},{6,4},{5,7},{10,8},{9,11},{14,12},{13,15},{18,16},{17,... | collective-permute-start | bytes 9437192 | tf_op jit(solution)/shard_map/ppermute | solution.py:55
  354.1 73.5 %collective-permute-start.9 = (bf16[512,3072]{1,0:T(8,128)(2,1)S(1)}, bf16[512,3072]{1,0:T(8,128)(2,1)}, u32[]{:S(2)}, u32[]{:S(2)}) collective-permute-start(bf16[512,3072]{1,0:T(8,128)(2,1)S(1)} %convolution_convert_fusion.9), channel_id=1, source_target_pairs={{0,1},{4,5},{8,9},{12,13},{16,17},{20,21},{24,25},{28,29}} | collective-permute-start | bytes 9437192 | tf_op jit(solution)/shard_map/ppermute | solution.py:55
  433.4 550.0 %reduce-scatter.10.cloned.1.call-start = ((), (), s32[]{:S(2)}) async-start(), calls=%async_computation.14 | async-start | bytes 14155776 | tf_op jit(solution)/shard_map/reduce_scatter | solution.py:643
  439.9 69.6 %collective-permute-start.12 = (bf16[512,3072]{1,0:T(8,128)(2,1)S(1)}, bf16[512,3072]{1,0:T(8,128)(2,1)S(1)}, u32[]{:S(2)}, u32[]{:S(2)}) collective-permute-start(bf16[512,3072]{1,0:T(8,128)(2,1)S(1)} %add_convert_fusion.5), channel_id=1, source_target_pairs={{0,1},{1,2},{4,5},{5,6},{8,9},{9,10},{12,13},{13,14},{16,17},{17,1... | collective-permute-start | bytes 9437192 | tf_op jit(solution)/shard_map/ppermute | solution.py:55
  443.7 65.8 %collective-permute-start.13 = (bf16[512,3072]{1,0:T(8,128)(2,1)S(1)}, bf16[512,3072]{1,0:T(8,128)(2,1)S(1)}, u32[]{:S(2)}, u32[]{:S(2)}) collective-permute-start(bf16[512,3072]{1,0:T(8,128)(2,1)S(1)} %add_convert_fusion.5), channel_id=1, source_target_pairs={{3,2},{2,1},{7,6},{6,5},{11,10},{10,9},{15,14},{14,13},{19,18},{18... | collective-permute-start | bytes 9437192 | tf_op jit(solution)/shard_map/ppermute | solution.py:55
  444.5 70.4 %collective-permute-start.14 = (bf16[512,3072]{1,0:T(8,128)(2,1)}, bf16[512,3072]{1,0:T(8,128)(2,1)S(1)}, u32[]{:S(2)}, u32[]{:S(2)}) collective-permute-start(bf16[512,3072]{1,0:T(8,128)(2,1)} %multiply_convert_fusion.2), channel_id=1, source_target_pairs={{1,0},{2,3},{5,4},{6,7},{9,8},{10,11},{13,12},{14,15},{17,16},{18,... | collective-permute-start | bytes 9437192 | tf_op jit(solution)/shard_map/ppermute | solution.py:55
  451.3 63.6 %copy-start.12 = (bf16[512,3072]{1,0:T(8,128)(2,1)S(1)}, bf16[512,3072]{1,0:T(8,128)(2,1)}, u32[]{:S(2)}) copy-start(bf16[512,3072]{1,0:T(8,128)(2,1)} %convolution_convert_fusion.8) | copy-start | bytes 9437188
  514.9 14.2 slice-start.2
  514.9 14.2 slice-start.3
  519.3 67.1 %collective-permute-start.15 = (bf16[512,3072]{1,0:T(8,128)(2,1)}, bf16[512,3072]{1,0:T(8,128)(2,1)}, u32[]{:S(2)}, u32[]{:S(2)}) collective-permute-start(bf16[512,3072]{1,0:T(8,128)(2,1)} %get-tuple-element.192), channel_id=1, source_target_pairs={{0,1},{1,2},{2,3},{4,5},{5,6},{6,7},{8,9},{9,10},{10,11},{12,13},{... | collective-permute-start | bytes 9437192 | tf_op jit(solution)/shard_map/ppermute | solution.py:55
  522.9 69.3 %collective-permute-start.16 = (bf16[512,3072]{1,0:T(8,128)(2,1)}, bf16[512,3072]{1,0:T(8,128)(2,1)}, u32[]{:S(2)}, u32[]{:S(2)}) collective-permute-start(bf16[512,3072]{1,0:T(8,128)(2,1)} %get-tuple-element.193), channel_id=1, source_target_pairs={{3,2},{2,1},{1,0},{7,6},{6,5},{5,4},{11,10},{10,9},{9,8},{15,14},{... | collective-permute-start | bytes 9437192 | tf_op jit(solution)/shard_map/ppermute | solution.py:55
  546.3 45.9 %copy-start.19 = (bf16[512,3072]{1,0:T(8,128)(2,1)S(1)}, bf16[512,3072]{1,0:T(8,128)(2,1)}, u32[]{:S(2)}) copy-start(bf16[512,3072]{1,0:T(8,128)(2,1)} %convolution_convert_fusion.6) | copy-start | bytes 9437188
  600.6 76.8 %collective-permute-start.17 = (bf16[512,3072]{1,0:T(8,128)(2,1)}, bf16[512,3072]{1,0:T(8,128)(2,1)}, u32[]{:S(2)}, u32[]{:S(2)}) collective-permute-start(bf16[512,3072]{1,0:T(8,128)(2,1)} %multiply_convert_fusion.1.x_ref), channel_id=1, source_target_pairs={{0,1},{3,2},{1,0},{2,3},{4,5},{7,6},{5,4},{6,7},{8,9},{11,10},{9,8... | collective-permute-start | bytes 9437192 | tf_op jit(solution)/shard_map/ppermute | solution.py:55
  677.4 21.2 %copy-start.25 = (bf16[512,3072]{1,0:T(8,128)(2,1)S(1)}, bf16[512,3072]{1,0:T(8,128)(2,1)}, u32[]{:S(2)}) copy-start(bf16[512,3072]{1,0:T(8,128)(2,1)} %copy-done.24) | copy-start | bytes 9437188
  718.0 265.4 %reduce-scatter.12.cloned.1.call-start = ((), (), s32[]{:S(2)}) async-start(), calls=%async_computation.15 | async-start | bytes 14155776 | tf_op jit(solution)/shard_map/reduce_scatter | solution.py:643
  763.0 23.2 %copy-start.10 = (bf16[1024,2048]{1,0:T(8,128)(2,1)S(1)}, bf16[1024,2048]{1,0:T(8,128)(2,1)}, u32[]{:S(2)}) copy-start(bf16[1024,2048]{1,0:T(8,128)(2,1)} %get-tuple-element.224.refs_3_) | copy-start | bytes 12582916
  763.1 41.8 %collective-permute-start.18 = (bf16[512,1536]{1,0:T(8,128)(2,1)}, bf16[512,1536]{1,0:T(8,128)(2,1)}, u32[]{:S(2)}, u32[]{:S(2)}) collective-permute-start(bf16[512,1536]{1,0:T(8,128)(2,1)} %shard_map.236), channel_id=1, source_target_pairs={{0,1},{3,2},{1,0},{2,3},{4,5},{7,6},{5,4},{6,7},{8,9},{11,10},{9,8... | collective-permute-start | bytes 4718600 | tf_op jit(solution)/shard_map/ppermute | solution.py:55
  804.9 280.1 %reduce-scatter.8.cloned.1.call-start = ((), (), s32[]{:S(2)}) async-start(), calls=%async_computation.13 | async-start | bytes 14155776 | tf_op jit(solution)/shard_map/reduce_scatter | solution.py:643
  804.9 31.0 %collective-permute-start.19 = (bf16[512,1536]{1,0:T(8,128)(2,1)}, bf16[512,1536]{1,0:T(8,128)(2,1)}, u32[]{:S(2)}, u32[]{:S(2)}) collective-permute-start(bf16[512,1536]{1,0:T(8,128)(2,1)} %copy-done.4), channel_id=1, source_target_pairs={{0,1},{3,2},{1,0},{2,3},{4,5},{7,6},{5,4},{6,7},{8,9},{11,10},{9,8... | collective-permute-start | bytes 4718600 | tf_op jit(solution)/shard_map/ppermute | solution.py:55
  836.0 325.8 %reduce-scatter.14.cloned.1.call-start = ((), (), s32[]{:S(2)}) async-start(), calls=%async_computation.16 | async-start | bytes 14155776 | tf_op jit(solution)/shard_map/reduce_scatter | solution.py:643
  850.6 64.9 %collective-permute-start.20 = (bf16[512,3072]{1,0:T(8,128)(2,1)}, bf16[512,3072]{1,0:T(8,128)(2,1)}, u32[]{:S(2)}, u32[]{:S(2)}) collective-permute-start(bf16[512,3072]{1,0:T(8,128)(2,1)} %get-tuple-element.233), channel_id=1, source_target_pairs={{0,1},{1,2},{2,3},{4,5},{5,6},{6,7},{8,9},{9,10},{10,11},{12,13},{... | collective-permute-start | bytes 9437192 | tf_op jit(solution)/shard_map/ppermute | solution.py:55
  854.6 66.6 %collective-permute-start.21 = (bf16[512,3072]{1,0:T(8,128)(2,1)}, bf16[512,3072]{1,0:T(8,128)(2,1)}, u32[]{:S(2)}, u32[]{:S(2)}) collective-permute-start(bf16[512,3072]{1,0:T(8,128)(2,1)} %get-tuple-element.233), channel_id=1, source_target_pairs={{1,0},{2,1},{3,2},{5,4},{6,5},{7,6},{9,8},{10,9},{11,10},{13,12},{... | collective-permute-start | bytes 9437192 | tf_op jit(solution)/shard_map/ppermute | solution.py:55
  921.3 320.3 %reduce-scatter.16.cloned.1.call-start = ((), (), s32[]{:S(2)}) async-start(), calls=%async_computation.17 | async-start | bytes 14155776 | tf_op jit(solution)/shard_map/reduce_scatter | solution.py:643
  921.4 66.0 %collective-permute-start.22 = (bf16[512,3072]{1,0:T(8,128)(2,1)}, bf16[512,3072]{1,0:T(8,128)(2,1)}, u32[]{:S(2)}, u32[]{:S(2)}) collective-permute-start(bf16[512,3072]{1,0:T(8,128)(2,1)} %collective-permute-done.20), channel_id=1, source_target_pairs={{1,2},{2,3},{5,6},{6,7},{9,10},{10,11},{13,14},{14,15},{17,18},{18... | collective-permute-start | bytes 9437192 | tf_op jit(solution)/shard_map/ppermute | solution.py:55
  927.0 69.1 %collective-permute-start.23 = (bf16[512,3072]{1,0:T(8,128)(2,1)}, bf16[512,3072]{1,0:T(8,128)(2,1)}, u32[]{:S(2)}, u32[]{:S(2)}) collective-permute-start(bf16[512,3072]{1,0:T(8,128)(2,1)} %collective-permute-done.21), channel_id=1, source_target_pairs={{1,0},{2,1},{5,4},{6,5},{9,8},{10,9},{13,12},{14,13},{17,16},{18,1... | collective-permute-start | bytes 9437192 | tf_op jit(solution)/shard_map/ppermute | solution.py:55
  928.3 69.0 %collective-permute-start.24 = (bf16[512,3072]{1,0:T(8,128)(2,1)}, bf16[512,3072]{1,0:T(8,128)(2,1)}, u32[]{:S(2)}, u32[]{:S(2)}) collective-permute-start(bf16[512,3072]{1,0:T(8,128)(2,1)} %shard_map.239), channel_id=1, source_target_pairs={{0,1},{3,2},{4,5},{7,6},{8,9},{11,10},{12,13},{15,14},{16,17},{19,... | collective-permute-start | bytes 9437192 | tf_op jit(solution)/shard_map/ppermute | solution.py:55
  942.1 22.6 %copy-start.9 = (bf16[1024,2048]{1,0:T(8,128)(2,1)S(1)}, bf16[1024,2048]{1,0:T(8,128)(2,1)}, u32[]{:S(2)}) copy-start(bf16[1024,2048]{1,0:T(8,128)(2,1)} %get-tuple-element.244.refs_2_) | copy-start | bytes 12582916
  997.3 292.0 %reduce-scatter.18.cloned.1.call-start = ((), (), s32[]{:S(2)}) async-start(), calls=%async_computation.18 | async-start | bytes 14155776 | tf_op jit(solution)/shard_map/reduce_scatter | solution.py:643
  997.4 43.7 %collective-permute-start.25 = (bf16[512,3072]{1,0:T(8,128)(2,1)}, bf16[512,3072]{1,0:T(8,128)(2,1)}, u32[]{:S(2)}, u32[]{:S(2)}) collective-permute-start(bf16[512,3072]{1,0:T(8,128)(2,1)} %collective-permute-done.22), channel_id=1, source_target_pairs={{2,3},{6,7},{10,11},{14,15},{18,19},{22,23},{26,27},{30,31}} | collective-permute-start | bytes 9437192 | tf_op jit(solution)/shard_map/ppermute | solution.py:55
  1002.0 19.9 %copy-start.8 = (bf16[1024,2048]{1,0:T(8,128)(2,1)S(1)}, bf16[1024,2048]{1,0:T(8,128)(2,1)}, u32[]{:S(2)}) copy-start(bf16[1024,2048]{1,0:T(8,128)(2,1)} %get-tuple-element.253.refs_0_) | copy-start | bytes 12582916
  1002.0 66.9 %collective-permute-start.26 = (bf16[512,3072]{1,0:T(8,128)(2,1)}, bf16[512,3072]{1,0:T(8,128)(2,1)}, u32[]{:S(2)}, u32[]{:S(2)}) collective-permute-start(bf16[512,3072]{1,0:T(8,128)(2,1)} %collective-permute-done.23), channel_id=1, source_target_pairs={{1,0},{5,4},{9,8},{13,12},{17,16},{21,20},{25,24},{29,28}} | collective-permute-start | bytes 9437192 | tf_op jit(solution)/shard_map/ppermute | solution.py:55
  1003.5 70.9 %collective-permute-start.27 = (bf16[384,4096]{1,0:T(8,128)(2,1)}, bf16[384,4096]{1,0:T(8,128)(2,1)}, u32[]{:S(2)}, u32[]{:S(2)}) collective-permute-start(bf16[384,4096]{1,0:T(8,128)(2,1)} %pad_maximum_fusion.3), channel_id=1, source_target_pairs={{0,2},{3,1},{4,6},{7,5},{8,10},{11,9},{12,14},{15,13},{16,18},{19,... | collective-permute-start | bytes 9437192 | tf_op jit(solution)/shard_map/ppermute | solution.py:55
  1074.4 331.7 %reduce-scatter.20.cloned.1.call-start = ((), (), s32[]{:S(2)}) async-start(), calls=%async_computation.19 | async-start | bytes 14155776 | tf_op jit(solution)/shard_map/reduce_scatter | solution.py:643
  1085.0 76.8 %collective-permute-start.28 = (bf16[384,2048]{1,0:T(8,128)(2,1)}, bf16[384,2048]{1,0:T(8,128)(2,1)}, u32[]{:S(2)}, u32[]{:S(2)}) collective-permute-start(bf16[384,2048]{1,0:T(8,128)(2,1)} %reduce-scatter.8.cloned.1.call-done), channel_id=1, source_target_pairs={{0,2},{3,1},{1,3},{2,0},{4,6},{7,5},{5,7},{6,4},{8,10},{11,9},{9,1... | collective-permute-start | bytes 4718600 | tf_op jit(solution)/shard_map/ppermute | solution.py:55
  1161.8 16.5 %copy-start.21 = (bf16[512,3072]{1,0:T(8,128)(2,1)S(1)}, bf16[512,3072]{1,0:T(8,128)(2,1)}, u32[]{:S(2)}) copy-start(bf16[512,3072]{1,0:T(8,128)(2,1)} %copy-done.20) | copy-start | bytes 9437188
  1171.6 60.9 %collective-permute-start.29 = (bf16[512,3072]{1,0:T(8,128)(2,1)}, bf16[512,3072]{1,0:T(8,128)(2,1)}, u32[]{:S(2)}, u32[]{:S(2)}) collective-permute-start(bf16[512,3072]{1,0:T(8,128)(2,1)} %convolution_convert_fusion.13), channel_id=1, source_target_pairs={{0,1},{4,5},{8,9},{12,13},{16,17},{20,21},{24,25},{28,29}} | collective-permute-start | bytes 9437192 | tf_op jit(solution)/shard_map/ppermute | solution.py:55
  1174.6 58.0 %collective-permute-start.30 = (bf16[512,3072]{1,0:T(8,128)(2,1)}, bf16[512,3072]{1,0:T(8,128)(2,1)}, u32[]{:S(2)}, u32[]{:S(2)}) collective-permute-start(bf16[512,3072]{1,0:T(8,128)(2,1)} %convolution_convert_fusion.13), channel_id=1, source_target_pairs={{3,2},{7,6},{11,10},{15,14},{19,18},{23,22},{27,26},{31,30}} | collective-permute-start | bytes 9437192 | tf_op jit(solution)/shard_map/ppermute | solution.py:55
  1177.0 64.6 %collective-permute-start.31 = (bf16[384,4096]{1,0:T(8,128)(2,1)}, bf16[384,4096]{1,0:T(8,128)(2,1)}, u32[]{:S(2)}, u32[]{:S(2)}) collective-permute-start(bf16[384,4096]{1,0:T(8,128)(2,1)} %pad_maximum_fusion.3), channel_id=1, source_target_pairs={{1,3},{2,0},{5,7},{6,4},{9,11},{10,8},{13,15},{14,12},{17,19},{18,... | collective-permute-start | bytes 9437192 | tf_op jit(solution)/shard_map/ppermute | solution.py:55
  1249.9 60.3 %collective-permute-start.32 = (bf16[512,3072]{1,0:T(8,128)(2,1)}, bf16[512,3072]{1,0:T(8,128)(2,1)}, u32[]{:S(2)}, u32[]{:S(2)}) collective-permute-start(bf16[512,3072]{1,0:T(8,128)(2,1)} %add_convert_fusion.2), channel_id=1, source_target_pairs={{0,1},{1,2},{4,5},{5,6},{8,9},{9,10},{12,13},{13,14},{16,17},{17,1... | collective-permute-start | bytes 9437192 | tf_op jit(solution)/shard_map/ppermute | solution.py:55
  1253.2 57.0 %collective-permute-start.33 = (bf16[512,3072]{1,0:T(8,128)(2,1)}, bf16[512,3072]{1,0:T(8,128)(2,1)}, u32[]{:S(2)}, u32[]{:S(2)}) collective-permute-start(bf16[512,3072]{1,0:T(8,128)(2,1)} %add_convert_fusion.2), channel_id=1, source_target_pairs={{3,2},{2,1},{7,6},{6,5},{11,10},{10,9},{15,14},{14,13},{19,18},{18... | collective-permute-start | bytes 9437192 | tf_op jit(solution)/shard_map/ppermute | solution.py:55
  1255.5 62.8 %collective-permute-start.34 = (bf16[512,3072]{1,0:T(8,128)(2,1)}, bf16[512,3072]{1,0:T(8,128)(2,1)}, u32[]{:S(2)}, u32[]{:S(2)}) collective-permute-start(bf16[512,3072]{1,0:T(8,128)(2,1)} %shard_map.239), channel_id=1, source_target_pairs={{1,0},{2,3},{5,4},{6,7},{9,8},{10,11},{13,12},{14,15},{17,16},{18,... | collective-permute-start | bytes 9437192 | tf_op jit(solution)/shard_map/ppermute | solution.py:55
  1327.2 62.3 %collective-permute-start.35 = (bf16[512,3072]{1,0:T(8,128)(2,1)}, bf16[512,3072]{1,0:T(8,128)(2,1)}, u32[]{:S(2)}, u32[]{:S(2)}) collective-permute-start(bf16[512,3072]{1,0:T(8,128)(2,1)} %get-tuple-element.282), channel_id=1, source_target_pairs={{0,1},{1,2},{2,3},{4,5},{5,6},{6,7},{8,9},{9,10},{10,11},{12,13},{... | collective-permute-start | bytes 9437192 | tf_op jit(solution)/shard_map/ppermute | solution.py:55
  1330.9 64.4 %collective-permute-start.36 = (bf16[512,3072]{1,0:T(8,128)(2,1)}, bf16[512,3072]{1,0:T(8,128)(2,1)}, u32[]{:S(2)}, u32[]{:S(2)}) collective-permute-start(bf16[512,3072]{1,0:T(8,128)(2,1)} %get-tuple-element.283), channel_id=1, source_target_pairs={{3,2},{2,1},{1,0},{7,6},{6,5},{5,4},{11,10},{10,9},{9,8},{15,14},{... | collective-permute-start | bytes 9437192 | tf_op jit(solution)/shard_map/ppermute | solution.py:55
  1364.3 31.0 %copy-start.3 = (bf16[512,3072]{1,0:T(8,128)(2,1)S(1)}, bf16[512,3072]{1,0:T(8,128)(2,1)}, u32[]{:S(2)}) copy-start(bf16[512,3072]{1,0:T(8,128)(2,1)} %convolution_convert_fusion.10.refs_0_) | copy-start | bytes 9437188
  1364.3 31.0 %copy-start.6 = (f32[1,3072]{1,0:T(1,128)S(1)}, f32[1,3072]{1,0:T(1,128)}, u32[]{:S(2)}) copy-start(f32[1,3072]{1,0:T(1,128)} %copy-done.5) | copy-start | bytes 36868
  (38 other events, 215.9 us)
Sparse Core Ops, SparseCore 0:
  14.0 54.9 all-gather.6
  70.8 39.7 all-gather.8
  112.5 72.1 all-gather.10
  186.4 125.3 all-gather.12
  346.8 69.6 all-gather.14
  433.5 124.2 all-gather.16
  718.2 91.6 reduce-scatter.9
  813.4 92.3 reduce-scatter.11
  909.3 92.3 reduce-scatter.7
  1005.1 92.3 reduce-scatter.13
  1101.0 92.4 reduce-scatter.15
  1196.8 92.3 reduce-scatter.17
  1292.8 92.3 reduce-scatter.19

commit v4 on v3

--- a/solution.py
+++ b/solution.py
@@ -57,7 +57,7 @@
     return list(out[: len(moved)]), list(out[len(moved) :])
 
 
-def line_gather(own, n, use, fill=lambda step, gate: (), along=lambda step: (), took=lambda step, arrived, filled: None):
+def line_gather(own, n, use, arrive=lambda shard, gate: shard, fill=lambda step, gate: (), along=lambda step: (), took=lambda step, arrived, filled: None):
     place = lax.axis_index("tensor")
     order = arrival_order(n)
     right = left = own
@@ -66,7 +66,8 @@
     for d in range(1, n):
 
         def work(gate):
-            return (use(d - 1, after(slots[d - 1], gate) if d > 1 else own), *fill(d, gate))
+            slots[d - 1] = arrive(after(slots[d - 1], gate), gate)
+            return (use(d - 1, slots[d - 1]), *fill(d, gate))
 
         (right, left, *more), (result, *filled) = travel(
             [
@@ -89,6 +90,7 @@
                 ],
             )
         )
+    slots[-1] = arrive(slots[-1], slots[-1])
     used.append(use(n - 1, slots[-1]))
     return slots, used
 
@@ -506,8 +508,7 @@
     )
     w_qkv = gather(own_qkv)
     w_out = gather(out_weight.T)
-    gains = lax.all_gather(jnp.stack([attn_gain, mlp_gain]), "dp", axis=1, tiled=True).astype(F32)
-    gain_one, gain_two = gains[0], gains[1]
+    gains = []
     down_t = down_weight.T
 
     partners = halves(n, [(i, i ^ 1) for i in range(n)])
@@ -544,16 +545,23 @@
     tables = (cos, sin, query_seg, key_seg)
 
     source = tokens.astype(F32)
-    inv_one = norm_inverse(source)
-    normed_one = (source * inv_one * gain_one).astype(BF16)
+    unit_one = (source * norm_inverse(source)).astype(BF16)
+
+    def gained(shard, gate):
+        if not gains:
+            both = lax.all_gather(after(jnp.stack([attn_gain, mlp_gain]), gate), "dp", axis=1, tiled=True)
+            gains.extend(both.astype(F32))
+        return (shard.astype(F32) * gains[0]).astype(BF16)
+
     grad_result = cotangent.astype(F32) * live
     grad_low = grad_result.astype(BF16)
     more = slices - 1
     early = []
     slots_one, projected = line_gather(
-        after(normed_one, labels),
+        after(unit_one, labels),
         n,
         lambda s, shard: dot(shard, w_qkv, NN),
+        gained,
         lambda step, gate: tables if step == 1 else (),
         lambda step: {
             n - 2: [(grad_low, partners[0])],
@@ -562,6 +570,7 @@
         lambda step, arrived, filled: early.extend(arrived),
     )
     low_ends, both_ends = early[0], early[1:]
+    gain_one, gain_two = gains
     projected[n - 1] = after(projected[n - 1], w_out, w_down[0])
 
     def attention(gate):
@@ -570,11 +579,13 @@
     downs = after(down_t, projected[n - 1])
     moved, (attended, rotated, lse) = travel([(downs, a + b) for a, b in outward], attention)
     w_down += [gather(shard) for shard in moved]
-    grad_mixed, lows = [], []
+    grad_mixed, lows, both_rest = [], [], []
 
     def while_out(step, gate):
         if step == 1:
             return (w_both[0],)
+        if step == 2:
+            return tuple(joined(a, after(b, gate)) for a, b in zip(both_ends, both_rest))
         if step == n - 1:
             theirs = joined(low_ends, lows[0])
             lows.append(theirs)
@@ -590,11 +601,12 @@
 
     def took_out(step, arrived, filled):
         if step == 1:
-            w_both.extend(gather(joined(a, b)) for a, b in zip(both_ends, arrived))
+            both_rest.extend(arrived)
         elif step == n - 1:
             grad_mixed.extend(filled)
-        else:
+        elif step == 2:
             lows.extend(arrived)
+            w_both.extend(gather(shard) for shard in filled)
 
     summed = line_reduce(
         lambda s: dot(attended[s * rows : (s + 1) * rows], w_out, NT, BF16), n, while_out, along_out, took_out
@@ -682,6 +694,7 @@
         grad_hidden_low,
         n,
         lambda s, shard: dot(shard, w_out, NN, BF16),
+        lambda shard, gate: shard,
         while_gather,
         lambda step: {
             2: [(results[0], partners[0])] if results else (),
@@ -694,14 +707,13 @@
     def attention_back(gate):
         return (
             attend_back(after(slot_table, gate), *grad_attended, rotated, attended, lse, *tables),
-            d_of(jnp.concatenate(slots_back, axis=0), attended, gate),
             sum_down,
         )
 
     sums_gate = [owner_sum(d) for d in d_gate[1:]]
     sum_down, sum_up, sum_gate = owner_sum(d_down[0]), owner_sum(d_up[0]), owner_sum(d_gate[0])
     leaving = [after(one, grad_attended[n - 1]) for one in sums_gate]
-    back_gate, (grad_qkv, d_out, _) = travel(
+    back_gate, (grad_qkv, _) = travel(
         [(one, a + b) for one, (a, b) in zip(leaving, homeward)], attention_back
     )
     back_down, back_up, outputs, d_attention = [], [], [], []
@@ -709,6 +721,7 @@
     def while_reduce(step, gate):
         if step == 1:
             d_qkv = d_of(jnp.concatenate(slots_one, axis=0), grad_qkv, gate)
+            d_out = d_of(jnp.concatenate(slots_back, axis=0), attended, gate)
             return (jnp.concatenate([d_qkv, d_out], axis=1), sum_up)
         if step == 2:
             return (sum_gate,)

time: 1440 us -> 1470 us (1.021)
  other arithmetic: 117 us -> 132 us
  transfers between devices with their start and end apart: 50 -> 50, of which waited for: 27 -> 29; matrix products, arithmetic and copies ran while one was open for 29% -> 29% of each run, Pallas kernels for 21% -> 21%
where the time goes in v4:
time: 1470 us; the launch traced here: 1460 us
  waiting for transfers between devices  483 us (33%)
  Pallas kernels  335 us (23%)
  matrix products  312 us (21%)
  other arithmetic  132 us (9%)
  starting transfers between devices  118 us (8%)
  local copies, waits for them, and re-layouts  35.1 us (2%)
  blocking collectives  32.7 us (2%)
  between operations  15.5 us (1%)
    ppermute x37, waiting for transfers between devices, travel(): lax.ppermute(array, 'tensor', pairs)  460 us
    dot_general x26, matrix products, dot(): return lax.dot_general(a, b, dims, preferred_element_type=F32).astype(out)  312 us
    pallas_call x5, Pallas kernels, spread(): pl.pallas_call(functools.partial(spread_kernel, count), grid=(tiles,), in...  119 us
    ppermute x37, starting transfers between devices, travel(): lax.ppermute(array, 'tensor', pairs)  117 us
    pallas_call x4, Pallas kernels, gated(): pl.pallas_call(gated_kernel, grid=(tiles,), in_specs=[pl.BlockSpec((rows,...  87 us
    pallas_call x1, Pallas kernels, attention_back(): attend_back(after(slot_table, gate), *grad_attended, rotated, attended, l...  56.5 us
    pallas_call x1, Pallas kernels, attention(): return attend(slot_table, *projected, *tables)  43.8 us
    convert_element_type x4, other arithmetic, add(): (value.astype(F32) + sum((one.astype(F32) for one in sums))).astype(BF16)  31.2 us
  transfers between devices with their start and end apart: 50, of which 29 were waited for; matrix products, arithmetic and copies ran while one was open for 29% of the time, Pallas kernels for 21%

profile of v4, /device:TPU:0, one launch (start us, length us, event | category | flops | bytes accessed | tf_op | source)
XLA Modules:
  0.0 1462.9 jit_solution(13110492207214211560)
XLA Ops:
  21.7 14.8 %all_gather.24 = s32[2,2048]{1,0:T(2,128)S(1)} all-gather(s32[2,512]{1,0:T(2,128)S(1)} %pad_add_fusion), channel_id=1, replica_groups=mesh['dp'=8,'tensor'=4] {'tensor'}, dimensions={1}, use_global_device_ids=true | all-gather | bytes 20480 | tf_op jit(solution)/shard_map/all_gather | solution.py:531
  50.4 9.5 all_gather.25
  75.5 10.4 fusion.43.refs_0_
  85.9 22.6 %collective-permute-done = bf16[512,3072]{1,0:T(8,128)(2,1)} collective-permute-done((bf16[512,3072]{1,0:T(8,128)(2,1)}, bf16[512,3072]{1,0:T(8,128)(2,1)}, u32[]{:S(2)}, u32[]{:S(2)}) %collective-permute-start) | collective-permute-done | bytes 3145760 | tf_op jit(solution)/shard_map/ppermute | solution.py:55
  134.4 50.3 %collective-permute-done.3 = bf16[512,3072]{1,0:T(8,128)(2,1)} collective-permute-done((bf16[512,3072]{1,0:T(8,128)(2,1)}, bf16[512,3072]{1,0:T(8,128)(2,1)}, u32[]{:S(2)}, u32[]{:S(2)}) %collective-permute-start.3) | collective-permute-done | bytes 3145760 | tf_op jit(solution)/shard_map/ppermute | solution.py:55
  188.0 9.4 collective-permute-start.7
  200.9 9.2 fusion.45.refs_2_
  210.1 43.4 %collective-permute-done.6 = bf16[512,3072]{1,0:T(8,128)(2,1)S(1)} collective-permute-done((bf16[512,3072]{1,0:T(8,128)(2,1)}, bf16[512,3072]{1,0:T(8,128)(2,1)S(1)}, u32[]{:S(2)}, u32[]{:S(2)}) %collective-permute-start.6) | collective-permute-done | bytes 3145760 | tf_op jit(solution)/shard_map/ppermute | solution.py:55
  260.1 8.1 fusion.46.refs_3_
  275.1 43.8 %shard_map.230 = (bf16[2048,768]{1,0:T(8,128)(2,1)}, bf16[2048,1280]{1,0:T(8,128)(2,1)}, f32[2,8,2048]{2,1,0:T(8,128)}) custom-call(s32[8]{0:T(128)} %dynamic-slice_bitcast_fusion.place_ref, f32[512,1280]{1,0:T(8,128)} %fusion.43.refs_0_, f32[512,1280]{1,0:T(8,128)} %fusion.44.refs_1_, f32[512,1280]{1,0:T(8,128)} %fusion.45.refs_2_, ...), custom_call_target="tpu_custom_call" | custom-call | flops 1 | bytes 1 | tf_op jit(solution)/shard_map/pallas_call | solution.py:577
  318.9 16.1 %collective-permute-done.8 = bf16[384,2048]{1,0:T(8,128)(2,1)} collective-permute-done((bf16[384,2048]{1,0:T(8,128)(2,1)}, bf16[384,2048]{1,0:T(8,128)(2,1)}, u32[]{:S(2)}, u32[]{:S(2)}) %collective-permute-start.8) | collective-permute-done | bytes 1572896 | tf_op jit(solution)/shard_map/ppermute | solution.py:55
  342.9 8.7 collective-permute-start.9
  351.6 6.9 convolution_convert_fusion.8
  360.1 54.2 %collective-permute-done.11 = bf16[384,4096]{1,0:T(8,128)(2,1)} collective-permute-done((bf16[384,4096]{1,0:T(8,128)(2,1)}, bf16[384,4096]{1,0:T(8,128)(2,1)}, u32[]{:S(2)}, u32[]{:S(2)}) %collective-permute-start.11) | collective-permute-done | bytes 3145760 | tf_op jit(solution)/shard_map/ppermute | solution.py:55
  416.4 8.0 add_convert_fusion.5
  434.2 6.9 convolution_convert_fusion.7
  446.9 47.9 %collective-permute-done.12 = bf16[512,3072]{1,0:T(8,128)(2,1)} collective-permute-done((bf16[512,3072]{1,0:T(8,128)(2,1)}, bf16[512,3072]{1,0:T(8,128)(2,1)}, u32[]{:S(2)}, u32[]{:S(2)}) %collective-permute-start.12) | collective-permute-done | bytes 3145760 | tf_op jit(solution)/shard_map/ppermute | solution.py:55
  494.8 8.0 collective-permute-done.14
  503.0 7.2 convolution_convert_fusion.6
  527.8 17.4 %fusion.39.gm_ref = f32[1024,2048]{1,0:T(8,128)} fusion(bf16[3072,2048]{1,0:T(8,128)(2,1)S(1)} %bitcast.59, bf16[512,3072]{1,0:T(8,128)(2,1)S(1)} %add.135, bf16[512,3072]{1,0:T(8,128)(2,1)} %multiply_convert_fusion.5), kind=kOutput, calls=%fused_computation.116 | convolution fusion | flops 12897484800 | bytes 27262976 | tf_op jit(solution)/shard_map/dot_general | solution.py:25
  545.2 18.9 %fusion.38.gm_ref = f32[1024,2048]{1,0:T(8,128)} fusion(bf16[3072,2048]{1,0:T(8,128)(2,1)} %all-gather.15.cloned.1.call-done.refs_3_, bf16[512,3072]{1,0:T(8,128)(2,1)} %copy-done.23, bf16[512,3072]{1,0:T(8,128)(2,1)} %multiply_convert_fusion.5), kind=kOutput, calls=%fused_computation.115 | convolution fusion | flops 12897484800 | bytes 27262976 | tf_op jit(solution)/shard_map/dot_general | solution.py:25
  564.1 19.5 %collective-permute-done.15 = bf16[512,3072]{1,0:T(8,128)(2,1)} collective-permute-done((bf16[512,3072]{1,0:T(8,128)(2,1)}, bf16[512,3072]{1,0:T(8,128)(2,1)}, u32[]{:S(2)}, u32[]{:S(2)}) %collective-permute-start.15) | collective-permute-done | bytes 3145760 | tf_op jit(solution)/shard_map/ppermute | solution.py:55
  598.4 21.3 %shard_map.231 = (bf16[1024,2048]{1,0:T(8,128)(2,1)}, bf16[1024,2048]{1,0:T(8,128)(2,1)}, bf16[1024,2048]{1,0:T(8,128)(2,1)}) custom-call(bf16[512,3072]{1,0:T(8,128)(2,1)} %multiply_convert_fusion.1.x_ref, bf16[3072,4096]{1,0:T(8,128)(2,1)} %all-gather.13.cloned.1.call-done.gate_ref.up_ref.refs_4_.refs_6_, ...), custom_call_target="tpu_custom_call" | custom-call | flops 1 | bytes 1 | tf_op jit(solution)/shard_map/pallas_call | solution.py:357
  619.7 6.9 all-gather.17.cloned.1.call-done.gate_ref.up_ref.refs_5_.refs_7_
  626.6 21.0 %shard_map.232 = (bf16[1024,2048]{1,0:T(8,128)(2,1)}, bf16[1024,2048]{1,0:T(8,128)(2,1)}, bf16[1024,2048]{1,0:T(8,128)(2,1)}) custom-call(bf16[512,3072]{1,0:T(8,128)(2,1)} %multiply_convert_fusion.1.x_ref, bf16[3072,4096]{1,0:T(8,128)(2,1)} %all-gather.17.cloned.1.call-done.gate_ref.up_ref.refs_5_.refs_7_, ...), custom_call_target="tpu_custom_call" | custom-call | flops 1 | bytes 1 | tf_op jit(solution)/shard_map/pallas_call | solution.py:357
  647.6 34.6 %shard_map.233.refs_0_ = f32[512,3072]{1,0:T(8,128)} custom-call(bf16[1024,2048]{1,0:T(8,128)(2,1)} %get-tuple-element.225.refs_0_.refs_1_, bf16[1024,2048]{1,0:T(8,128)(2,1)} %get-tuple-element.220.refs_1_, bf16[1024,2048]{1,0:T(8,128)(2,1)} %get-tuple-element.226.refs_2_, bf16[1024,2048]{1,0:T(8,128)(2,1)} %get-tuple-element.221.refs_3_.refs_2_, ...), custom_call_target="tpu_custom_call" | custom-call | flops 1 | bytes 1 | tf_op jit(solution)/shard_map/pallas_call | solution.py:388
  682.2 21.1 %shard_map.234 = (bf16[1024,2048]{1,0:T(8,128)(2,1)}, bf16[1024,2048]{1,0:T(8,128)(2,1)}, bf16[1024,2048]{1,0:T(8,128)(2,1)}) custom-call(bf16[512,3072]{1,0:T(8,128)(2,1)} %collective-permute-done.17.x_ref, ...), custom_call_target="tpu_custom_call", output_to_operand_aliasing={{0}: (4, {}), {1}: (5, {}), {2}: (6, {})} | custom-call | flops 1 | bytes 1 | tf_op jit(solution)/shard_map/pallas_call | solution.py:357
  703.3 19.3 %convolution_convert_fusion.5 = bf16[3072,2048]{1,0:T(8,128)(2,1)} fusion(bf16[1024,2048]{1,0:T(8,128)(2,1)} %get-tuple-element.222.refs_1_, bf16[512,3072]{1,0:T(8,128)(2,1)S(1)} %copy-done.24, bf16[512,3072]{1,0:T(8,128)(2,1)} %multiply_convert_fusion.5), kind=kOutput, calls=%fused_computation.23 | convolution fusion | flops 12903776256 | bytes 23068672 | tf_op jit(solution)/shard_map/dot_general | solution.py:25
  722.7 23.7 %shard_map.235 = (bf16[1024,2048]{1,0:T(8,128)(2,1)}, bf16[1024,2048]{1,0:T(8,128)(2,1)}, bf16[1024,2048]{1,0:T(8,128)(2,1)}) custom-call(bf16[512,3072]{1,0:T(8,128)(2,1)} %collective-permute-done.17.x_ref, ...), custom_call_target="tpu_custom_call", output_to_operand_aliasing={{0}: (4, {}), {1}: (5, {}), {2}: (6, {})} | custom-call | flops 1 | bytes 1 | tf_op jit(solution)/shard_map/pallas_call | solution.py:357
  746.4 20.4 %shard_map.236 = bf16[512,1536]{1,0:T(8,128)(2,1)} custom-call(bf16[1024,2048]{1,0:T(8,128)(2,1)} %get-tuple-element.262.refs_0_, bf16[1024,2048]{1,0:T(8,128)(2,1)} %get-tuple-element.234.refs_1_, bf16[1024,2048]{1,0:T(8,128)(2,1)} %get-tuple-element.253.refs_2_, bf16[1024,2048]{1,0:T(8,128)(2,1)} %get-tuple-element.232.refs_3_, ...), custom_call_target="tpu_custom_call" | custom-call | flops 1 | bytes 1 | tf_op jit(solution)/shard_map/pallas_call | solution.py:388
  768.3 19.9 %shard_map.237 = bf16[512,1536]{1,0:T(8,128)(2,1)S(1)} custom-call(bf16[1024,2048]{1,0:T(8,128)(2,1)} %get-tuple-element.262.refs_0_, bf16[1024,2048]{1,0:T(8,128)(2,1)} %get-tuple-element.234.refs_1_, bf16[1024,2048]{1,0:T(8,128)(2,1)} %get-tuple-element.253.refs_2_, bf16[1024,2048]{1,0:T(8,128)(2,1)} %get-tuple-element.232.refs_3_, ...), custom_call_target="tpu_custom_call" | custom-call | flops 1 | bytes 1 | tf_op jit(solution)/shard_map/pallas_call | solution.py:388
  789.4 18.6 %convolution_convert_fusion.4 = bf16[3072,2048]{1,0:T(8,128)(2,1)} fusion(bf16[1024,2048]{1,0:T(8,128)(2,1)S(1)} %copy-done.8, bf16[512,3072]{1,0:T(8,128)(2,1)} %collective-permute-done.17.x_ref, bf16[512,3072]{1,0:T(8,128)(2,1)} %multiply_convert_fusion.1.x_ref), kind=kOutput, calls=%fused_computation.22 | convolution fusion | flops 12903776256 | bytes 23068672 | tf_op jit(solution)/shard_map/dot_general | solution.py:25
  809.0 20.8 %convolution_convert_fusion.3 = bf16[3072,2048]{1,0:T(8,128)(2,1)} fusion(bf16[1024,2048]{1,0:T(8,128)(2,1)} %get-tuple-element.234.refs_1_, bf16[512,3072]{1,0:T(8,128)(2,1)} %collective-permute-done.17.x_ref, bf16[512,3072]{1,0:T(8,128)(2,1)} %multiply_convert_fusion.1.x_ref), kind=kOutput, calls=%fused_computation.21 | convolution fusion | flops 12903776256 | bytes 23068672 | tf_op jit(solution)/shard_map/dot_general | solution.py:25
  829.8 14.9 %collective-permute-done.19.refs_2_ = bf16[512,1536]{1,0:T(8,128)(2,1)} collective-permute-done((bf16[512,1536]{1,0:T(8,128)(2,1)}, bf16[512,1536]{1,0:T(8,128)(2,1)}, u32[]{:S(2)}, u32[]{:S(2)}) %collective-permute-start.19) | collective-permute-done | bytes 1572896 | tf_op jit(solution)/shard_map/ppermute | solution.py:55
  846.8 13.0 shard_map.238
  865.0 21.7 %shard_map.239 = bf16[512,3072]{1,0:T(8,128)(2,1)} custom-call(bf16[1024,2048]{1,0:T(8,128)(2,1)} %get-tuple-element.252.refs_0_, bf16[1024,2048]{1,0:T(8,128)(2,1)} %get-tuple-element.222.refs_1_, bf16[3072,2048]{1,0:T(8,128)(2,1)} %all-gather.11.cloned.1.call-done.refs_2_, bf16[3072,2048]{1,0:T(8,128)(2,1)} %all-gather.15.cloned.1.call-done.refs_3_), custom_call_target="tpu_custom_call" | custom-call | flops 12884901888 | bytes 25165824 | tf_op jit(solution)/shard_map/pallas_call | solution.py:388
  886.7 7.0 convolution_convert_fusion.17.refs_0_
  893.7 18.1 %convolution_convert_fusion.2 = bf16[3072,2048]{1,0:T(8,128)(2,1)} fusion(bf16[1024,2048]{1,0:T(8,128)(2,1)S(1)} %copy-done.9, bf16[512,3072]{1,0:T(8,128)(2,1)S(1)} %copy-done.25, bf16[512,3072]{1,0:T(8,128)(2,1)} %multiply_convert_fusion.5), kind=kOutput, calls=%fused_computation.20 | convolution fusion | flops 12903776256 | bytes 23068672 | tf_op jit(solution)/shard_map/dot_general | solution.py:25
  911.8 16.6 %collective-permute-done.20 = bf16[512,3072]{1,0:T(8,128)(2,1)} collective-permute-done((bf16[512,3072]{1,0:T(8,128)(2,1)}, bf16[512,3072]{1,0:T(8,128)(2,1)}, u32[]{:S(2)}, u32[]{:S(2)}) %collective-permute-start.20) | collective-permute-done | bytes 3145760 | tf_op jit(solution)/shard_map/ppermute | solution.py:55
  940.1 7.0 collective-permute-start.24
  952.9 22.6 %shard_map.240 = f32[512,3072]{1,0:T(8,128)} custom-call(bf16[1024,2048]{1,0:T(8,128)(2,1)} %get-tuple-element.252.refs_0_, bf16[1024,2048]{1,0:T(8,128)(2,1)} %get-tuple-element.222.refs_1_, bf16[3072,2048]{1,0:T(8,128)(2,1)} %all-gather.11.cloned.1.call-done.refs_2_, bf16[3072,2048]{1,0:T(8,128)(2,1)} %all-gather.15.cloned.1.call-done.refs_3_), custom_call_target="tpu_custom_call" | custom-call | flops 1 | bytes 1 | tf_op jit(solution)/shard_map/pallas_call | solution.py:388
  975.5 18.7 %convolution_convert_fusion.1 = bf16[3072,2048]{1,0:T(8,128)(2,1)} fusion(bf16[1024,2048]{1,0:T(8,128)(2,1)S(1)} %copy-done.7, bf16[512,3072]{1,0:T(8,128)(2,1)} %collective-permute-done.17.x_ref, bf16[512,3072]{1,0:T(8,128)(2,1)} %multiply_convert_fusion.1.x_ref), kind=kOutput, calls=%fused_computation.19 | convolution fusion | flops 12903776256 | bytes 23068672 | tf_op jit(solution)/shard_map/dot_general | solution.py:25
  998.1 11.4 collective-permute-done.23
  1017.1 11.4 collective-permute-start.27
  1034.7 18.6 %convolution_convert_fusion = bf16[3072,2048]{1,0:T(8,128)(2,1)} fusion(bf16[1024,2048]{1,0:T(8,128)(2,1)S(1)} %copy-done.6, bf16[512,3072]{1,0:T(8,128)(2,1)} %collective-permute-done.17.x_ref, bf16[512,3072]{1,0:T(8,128)(2,1)} %multiply_convert_fusion.1.x_ref), kind=kOutput, calls=%fused_computation.18 | convolution fusion | flops 12903776256 | bytes 23068672 | tf_op jit(solution)/shard_map/dot_general | solution.py:25
  1053.3 31.4 %collective-permute-done.26 = bf16[512,3072]{1,0:T(8,128)(2,1)} collective-permute-done((bf16[512,3072]{1,0:T(8,128)(2,1)}, bf16[512,3072]{1,0:T(8,128)(2,1)}, u32[]{:S(2)}, u32[]{:S(2)}) %collective-permute-start.26) | collective-permute-done | bytes 3145760 | tf_op jit(solution)/shard_map/ppermute | solution.py:55
  1104.5 56.5 %shard_map.241 = bf16[2048,1280]{1,0:T(8,128)(2,1)} custom-call(s32[8]{0:T(128)} %dynamic-slice_bitcast_fusion.place_ref, bf16[512,768]{1,0:T(8,128)(2,1)} %convolution_convert_fusion.17.refs_0_, bf16[512,768]{1,0:T(8,128)(2,1)} %convolution_convert_fusion.16.refs_1_, bf16[512,768]{1,0:T(8,128)(2,1)} %convolution_convert_fusion.15.refs_2_, ...), custom_call_target="tpu_custom_call" | custom-call | flops 32212254720 | bytes 26214400 | tf_op jit(solution)/shard_map/pallas_call | solution.py:709
  1167.0 9.8 convolution_convert_fusion.13
  1183.8 21.7 %fusion.16 = bf16[3072,1280]{1,0:T(8,128)(2,1)} fusion(bf16[2048,1280]{1,0:T(8,128)(2,1)} %shard_map.241, bf16[512,3072]{1,0:T(8,128)(2,1)S(1)} %copy-done.17, bf16[512,3072]{1,0:T(8,128)(2,1)} %copy-done.22, bf16[512,3072]{1,0:T(8,128)(2,1)S(1)} %copy-done.21, bf16[512,3072]{1,0:T(8,128)(2,1)S(1)} %copy-done.19), kind=kOutput, calls=%fused_computation.17 | convolution fusion | flops 16160391168 | bytes 25690112 | tf_op jit(solution)/shard_map/dot_general | solution.py:25
  1205.5 16.6 %fusion.21 = bf16[3072,768]{1,0:T(8,128)(2,1)} fusion(bf16[2048,768]{1,0:T(8,128)(2,1)} %get-tuple-element.278.refs_5_, bf16[512,3072]{1,0:T(8,128)(2,1)} %copy-done.28, bf16[512,3072]{1,0:T(8,128)(2,1)} %copy-done.27, bf16[512,3072]{1,0:T(8,128)(2,1)} %copy-done.26, bf16[512,3072]{1,0:T(8,128)(2,1)} %get-tuple-element.242), kind=kOutput, calls=%fused_computation.45 | convolution fusion | flops 9716367360 | bytes 20447232 | tf_op jit(solution)/shard_map/dot_general | solution.py:25
  1222.1 11.3 pad_maximum_fusion
  1233.4 9.6 convolution_convert_fusion.12
  1246.3 8.9 collective-permute-done.31
  1255.3 8.1 add_convert_fusion.2
  1269.9 9.6 convolution_convert_fusion.11
  1279.5 15.2 %reduce-scatter.18.cloned.1.call-done = bf16[384,2048]{1,0:T(8,128)(2,1)} async-done(((bf16[3072,2048]{1,0:T(8,128)(2,1)}), bf16[384,2048]{1,0:T(8,128)(2,1)}) %reduce-scatter.18.cloned.1.call-update) | async-done | bytes 1572880 | tf_op jit(solution)/shard_map/reduce_scatter | solution.py:655
  1294.7 37.3 %collective-permute-done.32 = bf16[512,3072]{1,0:T(8,128)(2,1)} collective-permute-done((bf16[512,3072]{1,0:T(8,128)(2,1)}, bf16[512,3072]{1,0:T(8,128)(2,1)}, u32[]{:S(2)}, u32[]{:S(2)}) %collective-permute-start.32) | collective-permute-done | bytes 3145760 | tf_op jit(solution)/shard_map/ppermute | solution.py:55
  1332.0 8.0 collective-permute-done.34
  1340.0 8.4 add_convert_fusion
  1354.0 9.7 convolution_convert_fusion.10.refs_0_
  1386.0 7.6 multiply_convert_fusion
  1393.6 23.3 %collective-permute-done.35.refs_1_ = bf16[512,3072]{1,0:T(8,128)(2,1)} collective-permute-done((bf16[512,3072]{1,0:T(8,128)(2,1)}, bf16[512,3072]{1,0:T(8,128)(2,1)}, u32[]{:S(2)}, u32[]{:S(2)}) %collective-permute-start.35) | collective-permute-done | bytes 3145760 | tf_op jit(solution)/shard_map/ppermute | solution.py:55
  1422.6 10.9 shard_map.242
  1437.1 8.4 psum.7
  (260 shorter events, 285.4 us)
Async XLA Ops:
  7.2 68.3 %all-gather.7.cloned.1.call-start = ((), (), s32[]{:S(2)}) async-start(), calls=%async_computation.7 | async-start | bytes 8847360 | tf_op jit(solution)/shard_map/all_gather | solution.py:495
  13.9 254.3 %all-gather.9.cloned.1.call-start = ((), (), s32[]{:S(2)}) async-start(), calls=%async_computation.8 | async-start | bytes 5308416 | tf_op jit(solution)/shard_map/all_gather | solution.py:495
  14.6 253.5 %all-gather.11.cloned.1.call-start = ((), (), s32[]{:S(2)}) async-start(), calls=%async_computation.9 | async-start | bytes 14155776 | tf_op jit(solution)/shard_map/all_gather | solution.py:495
  17.3 399.1 %all-gather.13.cloned.1.call-start = ((), (), s32[]{:S(2)}) async-start(), calls=%async_computation.10 | async-start | bytes 28311552 | tf_op jit(solution)/shard_map/all_gather | solution.py:495
  18.7 17.8 %copy-start = (bf16[512,3072]{1,0:T(8,128)(2,1)S(1)}, bf16[512,3072]{1,0:T(8,128)(2,1)}, u32[]{:S(2)}) copy-start(bf16[512,3072]{1,0:T(8,128)(2,1)} %source_ref.1) | copy-start | bytes 9437188
  21.6 523.5 %all-gather.15.cloned.1.call-start = ((), (), s32[]{:S(2)}) async-start(), calls=%async_computation.11 | async-start | bytes 14155776 | tf_op jit(solution)/shard_map/all_gather | solution.py:495
  39.9 68.6 %collective-permute-start = (bf16[512,3072]{1,0:T(8,128)(2,1)}, bf16[512,3072]{1,0:T(8,128)(2,1)}, u32[]{:S(2)}, u32[]{:S(2)}) collective-permute-start(bf16[512,3072]{1,0:T(8,128)(2,1)} %fusion.20), channel_id=1, source_target_pairs={{0,1},{1,2},{2,3},{4,5},{5,6},{6,7},{8,9},{9,10},{10,11},{12,13},{... | collective-permute-start | bytes 9437192 | tf_op jit(solution)/shard_map/ppermute | solution.py:55
  45.3 68.9 %collective-permute-start.1 = (bf16[512,3072]{1,0:T(8,128)(2,1)}, bf16[512,3072]{1,0:T(8,128)(2,1)}, u32[]{:S(2)}, u32[]{:S(2)}) collective-permute-start(bf16[512,3072]{1,0:T(8,128)(2,1)} %fusion.20), channel_id=1, source_target_pairs={{1,0},{2,1},{3,2},{5,4},{6,5},{7,6},{9,8},{10,9},{11,10},{13,12},{... | collective-permute-start | bytes 9437192 | tf_op jit(solution)/shard_map/ppermute | solution.py:55
  114.2 20.2 %collective-permute-start.2 = (bf16[512,3072]{1,0:T(8,128)(2,1)}, bf16[512,3072]{1,0:T(8,128)(2,1)}, u32[]{:S(2)}, u32[]{:S(2)}) collective-permute-start(bf16[512,3072]{1,0:T(8,128)(2,1)} %collective-permute-done), channel_id=1, source_target_pairs={{1,2},{2,3},{5,6},{6,7},{9,10},{10,11},{13,14},{14,15},{17,18},{18... | collective-permute-start | bytes 9437192 | tf_op jit(solution)/shard_map/ppermute | solution.py:55
  116.6 68.1 %collective-permute-start.3 = (bf16[512,3072]{1,0:T(8,128)(2,1)}, bf16[512,3072]{1,0:T(8,128)(2,1)}, u32[]{:S(2)}, u32[]{:S(2)}) collective-permute-start(bf16[512,3072]{1,0:T(8,128)(2,1)} %collective-permute-done.1), channel_id=1, source_target_pairs={{1,0},{2,1},{5,4},{6,5},{9,8},{10,9},{13,12},{14,13},{17,16},{18,1... | collective-permute-start | bytes 9437192 | tf_op jit(solution)/shard_map/ppermute | solution.py:55
  117.8 68.0 %collective-permute-start.4 = (bf16[512,3072]{1,0:T(8,128)(2,1)}, bf16[512,3072]{1,0:T(8,128)(2,1)}, u32[]{:S(2)}, u32[]{:S(2)}) collective-permute-start(bf16[512,3072]{1,0:T(8,128)(2,1)} %multiply_convert_fusion.5), channel_id=1, source_target_pairs={{0,1},{3,2},{4,5},{7,6},{8,9},{11,10},{12,13},{15,14},{16,17},{19,... | collective-permute-start | bytes 9437192 | tf_op jit(solution)/shard_map/ppermute | solution.py:55
  185.9 24.2 %collective-permute-start.5 = (bf16[512,3072]{1,0:T(8,128)(2,1)}, bf16[512,3072]{1,0:T(8,128)(2,1)S(1)}, u32[]{:S(2)}, u32[]{:S(2)}) collective-permute-start(bf16[512,3072]{1,0:T(8,128)(2,1)} %collective-permute-done.2), channel_id=1, source_target_pairs={{2,3},{6,7},{10,11},{14,15},{18,19},{22,23},{26,27},{30,31}} | collective-permute-start | bytes 9437192 | tf_op jit(solution)/shard_map/ppermute | solution.py:55
  186.7 66.8 %collective-permute-start.6 = (bf16[512,3072]{1,0:T(8,128)(2,1)}, bf16[512,3072]{1,0:T(8,128)(2,1)S(1)}, u32[]{:S(2)}, u32[]{:S(2)}) collective-permute-start(bf16[512,3072]{1,0:T(8,128)(2,1)} %collective-permute-done.3), channel_id=1, source_target_pairs={{1,0},{5,4},{9,8},{13,12},{17,16},{21,20},{25,24},{29,28}} | collective-permute-start | bytes 9437192 | tf_op jit(solution)/shard_map/ppermute | solution.py:55
  188.0 69.5 %collective-permute-start.7 = (bf16[384,4096]{1,0:T(8,128)(2,1)}, bf16[384,4096]{1,0:T(8,128)(2,1)}, u32[]{:S(2)}, u32[]{:S(2)}) collective-permute-start(bf16[384,4096]{1,0:T(8,128)(2,1)} %constant_dynamic-update-slice_fusion), channel_id=1, source_target_pairs={{3,1},{0,2},{7,5},{4,6},{11,9},{8,10},{15,13},{12,14},{19,17},{16,... | collective-permute-start | bytes 9437192 | tf_op jit(solution)/shard_map/ppermute | solution.py:55
  268.2 66.9 %collective-permute-start.8 = (bf16[384,2048]{1,0:T(8,128)(2,1)}, bf16[384,2048]{1,0:T(8,128)(2,1)}, u32[]{:S(2)}, u32[]{:S(2)}) collective-permute-start(bf16[384,2048]{1,0:T(8,128)(2,1)} %bitcast.61), channel_id=1, source_target_pairs={{3,1},{0,2},{2,0},{1,3},{7,5},{4,6},{6,4},{5,7},{11,9},{8,10},{10,... | collective-permute-start | bytes 4718600 | tf_op jit(solution)/shard_map/ppermute | solution.py:55
  335.1 291.5 %all-gather.17.cloned.1.call-start = ((), (), s32[]{:S(2)}) async-start(), calls=%async_computation.12 | async-start | bytes 28311552 | tf_op jit(solution)/shard_map/all_gather | solution.py:495
  340.3 18.1 %copy-start.29 = (bf16[512,3072]{1,0:T(8,128)(2,1)}, bf16[512,3072]{1,0:T(8,128)(2,1)S(1)}, u32[]{:S(2)}) copy-start(bf16[512,3072]{1,0:T(8,128)(2,1)S(1)} %convolution_convert_fusion.9) | copy-start | bytes 9437188
  340.3 18.1 %collective-permute-start.10 = (bf16[512,3072]{1,0:T(8,128)(2,1)S(1)}, bf16[512,3072]{1,0:T(8,128)(2,1)S(1)}, u32[]{:S(2)}, u32[]{:S(2)}) collective-permute-start(bf16[512,3072]{1,0:T(8,128)(2,1)S(1)} %convolution_convert_fusion.9), channel_id=1, source_target_pairs={{3,2},{7,6},{11,10},{15,14},{19,18},{23,22},{27,26},{31,30}} | collective-permute-start | bytes 9437192 | tf_op jit(solution)/shard_map/ppermute | solution.py:55
  341.6 72.7 %collective-permute-start.11 = (bf16[384,4096]{1,0:T(8,128)(2,1)}, bf16[384,4096]{1,0:T(8,128)(2,1)}, u32[]{:S(2)}, u32[]{:S(2)}) collective-permute-start(bf16[384,4096]{1,0:T(8,128)(2,1)} %constant_dynamic-update-slice_fusion), channel_id=1, source_target_pairs={{2,0},{1,3},{6,4},{5,7},{10,8},{9,11},{14,12},{13,15},{18,16},{17,... | collective-permute-start | bytes 9437192 | tf_op jit(solution)/shard_map/ppermute | solution.py:55
  342.9 73.5 %collective-permute-start.9 = (bf16[512,3072]{1,0:T(8,128)(2,1)S(1)}, bf16[512,3072]{1,0:T(8,128)(2,1)}, u32[]{:S(2)}, u32[]{:S(2)}) collective-permute-start(bf16[512,3072]{1,0:T(8,128)(2,1)S(1)} %convolution_convert_fusion.9), channel_id=1, source_target_pairs={{0,1},{4,5},{8,9},{12,13},{16,17},{20,21},{24,25},{28,29}} | collective-permute-start | bytes 9437192 | tf_op jit(solution)/shard_map/ppermute | solution.py:55
  424.4 70.4 %collective-permute-start.12 = (bf16[512,3072]{1,0:T(8,128)(2,1)}, bf16[512,3072]{1,0:T(8,128)(2,1)}, u32[]{:S(2)}, u32[]{:S(2)}) collective-permute-start(bf16[512,3072]{1,0:T(8,128)(2,1)} %add_convert_fusion.5), channel_id=1, source_target_pairs={{0,1},{1,2},{4,5},{5,6},{8,9},{9,10},{12,13},{13,14},{16,17},{17,1... | collective-permute-start | bytes 9437192 | tf_op jit(solution)/shard_map/ppermute | solution.py:55
  430.6 64.3 %collective-permute-start.13 = (bf16[512,3072]{1,0:T(8,128)(2,1)}, bf16[512,3072]{1,0:T(8,128)(2,1)}, u32[]{:S(2)}, u32[]{:S(2)}) collective-permute-start(bf16[512,3072]{1,0:T(8,128)(2,1)} %add_convert_fusion.5), channel_id=1, source_target_pairs={{3,2},{2,1},{7,6},{6,5},{11,10},{10,9},{15,14},{14,13},{19,18},{18... | collective-permute-start | bytes 9437192 | tf_op jit(solution)/shard_map/ppermute | solution.py:55
  432.9 70.0 %collective-permute-start.14 = (bf16[512,3072]{1,0:T(8,128)(2,1)}, bf16[512,3072]{1,0:T(8,128)(2,1)}, u32[]{:S(2)}, u32[]{:S(2)}) collective-permute-start(bf16[512,3072]{1,0:T(8,128)(2,1)} %multiply_convert_fusion.5), channel_id=1, source_target_pairs={{1,0},{2,3},{5,4},{6,7},{9,8},{10,11},{13,12},{14,15},{17,16},{18,... | collective-permute-start | bytes 9437192 | tf_op jit(solution)/shard_map/ppermute | solution.py:55
  502.9 491.3 %reduce-scatter.10.cloned.1.call-start = ((), (), s32[]{:S(2)}) async-start(), calls=%async_computation.14 | async-start | bytes 14155776 | tf_op jit(solution)/shard_map/reduce_scatter | solution.py:655
  510.2 17.6 %slice-start.2 = ((s8[12582912]{0:T(1024)(128)(4,1)}), s8[4194304]{0:T(1024)(128)(4,1)S(1)}, s32[]{:S(2)}) async-start(s8[12582912]{0:T(1024)(128)(4,1)} %bitcast.58), calls=%async_computation.22 | async-start | bytes 8388608
  510.2 17.6 %slice-start.3 = ((s8[12582912]{0:T(1024)(128)(4,1)}), s8[4194304]{0:T(1024)(128)(4,1)S(1)}, s32[]{:S(2)}) async-start(s8[12582912]{0:T(1024)(128)(4,1)} %bitcast.58), calls=%async_computation.23 | async-start | bytes 8388608
  516.9 66.8 %collective-permute-start.15 = (bf16[512,3072]{1,0:T(8,128)(2,1)}, bf16[512,3072]{1,0:T(8,128)(2,1)}, u32[]{:S(2)}, u32[]{:S(2)}) collective-permute-start(bf16[512,3072]{1,0:T(8,128)(2,1)} %get-tuple-element.201), channel_id=1, source_target_pairs={{0,1},{1,2},{2,3},{4,5},{5,6},{6,7},{8,9},{9,10},{10,11},{12,13},{... | collective-permute-start | bytes 9437192 | tf_op jit(solution)/shard_map/ppermute | solution.py:55
  520.6 69.0 %collective-permute-start.16 = (bf16[512,3072]{1,0:T(8,128)(2,1)}, bf16[512,3072]{1,0:T(8,128)(2,1)}, u32[]{:S(2)}, u32[]{:S(2)}) collective-permute-start(bf16[512,3072]{1,0:T(8,128)(2,1)} %get-tuple-element.202), channel_id=1, source_target_pairs={{3,2},{2,1},{1,0},{7,6},{6,5},{5,4},{11,10},{10,9},{9,8},{15,14},{... | collective-permute-start | bytes 9437192 | tf_op jit(solution)/shard_map/ppermute | solution.py:55
  545.2 44.5 %copy-start.18 = (bf16[512,3072]{1,0:T(8,128)(2,1)S(1)}, bf16[512,3072]{1,0:T(8,128)(2,1)}, u32[]{:S(2)}) copy-start(bf16[512,3072]{1,0:T(8,128)(2,1)} %convolution_convert_fusion.6) | copy-start | bytes 9437188
  598.4 83.8 %collective-permute-start.17 = (bf16[512,3072]{1,0:T(8,128)(2,1)}, bf16[512,3072]{1,0:T(8,128)(2,1)}, u32[]{:S(2)}, u32[]{:S(2)}) collective-permute-start(bf16[512,3072]{1,0:T(8,128)(2,1)} %multiply_convert_fusion.1.x_ref), channel_id=1, source_target_pairs={{0,1},{3,2},{1,0},{2,3},{4,5},{7,6},{5,4},{6,7},{8,9},{11,10},{9,8... | collective-permute-start | bytes 9437192 | tf_op jit(solution)/shard_map/ppermute | solution.py:55
  682.2 21.1 %copy-start.24 = (bf16[512,3072]{1,0:T(8,128)(2,1)S(1)}, bf16[512,3072]{1,0:T(8,128)(2,1)}, u32[]{:S(2)}) copy-start(bf16[512,3072]{1,0:T(8,128)(2,1)} %copy-done.23) | copy-start | bytes 9437188
  722.7 271.6 %reduce-scatter.12.cloned.1.call-start = ((), (), s32[]{:S(2)}) async-start(), calls=%async_computation.15 | async-start | bytes 14155776 | tf_op jit(solution)/shard_map/reduce_scatter | solution.py:655
  766.8 22.6 %copy-start.8 = (bf16[1024,2048]{1,0:T(8,128)(2,1)S(1)}, bf16[1024,2048]{1,0:T(8,128)(2,1)}, u32[]{:S(2)}) copy-start(bf16[1024,2048]{1,0:T(8,128)(2,1)} %get-tuple-element.232.refs_3_) | copy-start | bytes 12582916
  766.8 41.2 %collective-permute-start.18 = (bf16[512,1536]{1,0:T(8,128)(2,1)}, bf16[512,1536]{1,0:T(8,128)(2,1)}, u32[]{:S(2)}, u32[]{:S(2)}) collective-permute-start(bf16[512,1536]{1,0:T(8,128)(2,1)} %shard_map.236), channel_id=1, source_target_pairs={{0,1},{3,2},{1,0},{2,3},{4,5},{7,6},{5,4},{6,7},{8,9},{11,10},{9,8... | collective-permute-start | bytes 4718600 | tf_op jit(solution)/shard_map/ppermute | solution.py:55
  808.0 292.2 %reduce-scatter.8.cloned.1.call-start = ((), (), s32[]{:S(2)}) async-start(), calls=%async_computation.13 | async-start | bytes 14155776 | tf_op jit(solution)/shard_map/reduce_scatter | solution.py:655
  808.0 36.7 %collective-permute-start.19 = (bf16[512,1536]{1,0:T(8,128)(2,1)}, bf16[512,1536]{1,0:T(8,128)(2,1)}, u32[]{:S(2)}, u32[]{:S(2)}) collective-permute-start(bf16[512,1536]{1,0:T(8,128)(2,1)} %copy-done.4), channel_id=1, source_target_pairs={{0,1},{3,2},{1,0},{2,3},{4,5},{7,6},{5,4},{6,7},{8,9},{11,10},{9,8... | collective-permute-start | bytes 4718600 | tf_op jit(solution)/shard_map/ppermute | solution.py:55
  844.8 322.2 %reduce-scatter.14.cloned.1.call-start = ((), (), s32[]{:S(2)}) async-start(), calls=%async_computation.16 | async-start | bytes 14155776 | tf_op jit(solution)/shard_map/reduce_scatter | solution.py:655
  859.8 68.6 %collective-permute-start.20 = (bf16[512,3072]{1,0:T(8,128)(2,1)}, bf16[512,3072]{1,0:T(8,128)(2,1)}, u32[]{:S(2)}, u32[]{:S(2)}) collective-permute-start(bf16[512,3072]{1,0:T(8,128)(2,1)} %get-tuple-element.242), channel_id=1, source_target_pairs={{0,1},{1,2},{2,3},{4,5},{5,6},{6,7},{8,9},{9,10},{10,11},{12,13},{... | collective-permute-start | bytes 9437192 | tf_op jit(solution)/shard_map/ppermute | solution.py:55
  863.7 70.4 %collective-permute-start.21 = (bf16[512,3072]{1,0:T(8,128)(2,1)}, bf16[512,3072]{1,0:T(8,128)(2,1)}, u32[]{:S(2)}, u32[]{:S(2)}) collective-permute-start(bf16[512,3072]{1,0:T(8,128)(2,1)} %get-tuple-element.242), channel_id=1, source_target_pairs={{1,0},{2,1},{3,2},{5,4},{6,5},{7,6},{9,8},{10,9},{11,10},{13,12},{... | collective-permute-start | bytes 9437192 | tf_op jit(solution)/shard_map/ppermute | solution.py:55
  934.2 321.0 %reduce-scatter.16.cloned.1.call-start = ((), (), s32[]{:S(2)}) async-start(), calls=%async_computation.17 | async-start | bytes 14155776 | tf_op jit(solution)/shard_map/reduce_scatter | solution.py:655
  934.2 63.9 %collective-permute-start.22 = (bf16[512,3072]{1,0:T(8,128)(2,1)}, bf16[512,3072]{1,0:T(8,128)(2,1)}, u32[]{:S(2)}, u32[]{:S(2)}) collective-permute-start(bf16[512,3072]{1,0:T(8,128)(2,1)} %collective-permute-done.20), channel_id=1, source_target_pairs={{1,2},{2,3},{5,6},{6,7},{9,10},{10,11},{13,14},{14,15},{17,18},{18... | collective-permute-start | bytes 9437192 | tf_op jit(solution)/shard_map/ppermute | solution.py:55
  938.8 70.8 %collective-permute-start.23 = (bf16[512,3072]{1,0:T(8,128)(2,1)}, bf16[512,3072]{1,0:T(8,128)(2,1)}, u32[]{:S(2)}, u32[]{:S(2)}) collective-permute-start(bf16[512,3072]{1,0:T(8,128)(2,1)} %collective-permute-done.21), channel_id=1, source_target_pairs={{1,0},{2,1},{5,4},{6,5},{9,8},{10,9},{13,12},{14,13},{17,16},{18,1... | collective-permute-start | bytes 9437192 | tf_op jit(solution)/shard_map/ppermute | solution.py:55
  940.1 70.7 %collective-permute-start.24 = (bf16[512,3072]{1,0:T(8,128)(2,1)}, bf16[512,3072]{1,0:T(8,128)(2,1)}, u32[]{:S(2)}, u32[]{:S(2)}) collective-permute-start(bf16[512,3072]{1,0:T(8,128)(2,1)} %shard_map.239), channel_id=1, source_target_pairs={{0,1},{3,2},{4,5},{7,6},{8,9},{11,10},{12,13},{15,14},{16,17},{19,... | collective-permute-start | bytes 9437192 | tf_op jit(solution)/shard_map/ppermute | solution.py:55
  952.9 22.6 %copy-start.7 = (bf16[1024,2048]{1,0:T(8,128)(2,1)S(1)}, bf16[1024,2048]{1,0:T(8,128)(2,1)}, u32[]{:S(2)}) copy-start(bf16[1024,2048]{1,0:T(8,128)(2,1)} %get-tuple-element.253.refs_2_) | copy-start | bytes 12582916
  1010.8 283.9 %reduce-scatter.18.cloned.1.call-start = ((), (), s32[]{:S(2)}) async-start(), calls=%async_computation.18 | async-start | bytes 14155776 | tf_op jit(solution)/shard_map/reduce_scatter | solution.py:655
  1010.8 42.5 %collective-permute-start.25 = (bf16[512,3072]{1,0:T(8,128)(2,1)}, bf16[512,3072]{1,0:T(8,128)(2,1)}, u32[]{:S(2)}, u32[]{:S(2)}) collective-permute-start(bf16[512,3072]{1,0:T(8,128)(2,1)} %collective-permute-done.22), channel_id=1, source_target_pairs={{2,3},{6,7},{10,11},{14,15},{18,19},{22,23},{26,27},{30,31}} | collective-permute-start | bytes 9437192 | tf_op jit(solution)/shard_map/ppermute | solution.py:55
  1015.5 13.0 copy-start.27
  1015.5 19.1 %copy-start.6 = (bf16[1024,2048]{1,0:T(8,128)(2,1)S(1)}, bf16[1024,2048]{1,0:T(8,128)(2,1)}, u32[]{:S(2)}) copy-start(bf16[1024,2048]{1,0:T(8,128)(2,1)} %get-tuple-element.262.refs_0_) | copy-start | bytes 12582916
  1015.5 69.2 %collective-permute-start.26 = (bf16[512,3072]{1,0:T(8,128)(2,1)}, bf16[512,3072]{1,0:T(8,128)(2,1)}, u32[]{:S(2)}, u32[]{:S(2)}) collective-permute-start(bf16[512,3072]{1,0:T(8,128)(2,1)} %collective-permute-done.23), channel_id=1, source_target_pairs={{1,0},{5,4},{9,8},{13,12},{17,16},{21,20},{25,24},{29,28}} | collective-permute-start | bytes 9437192 | tf_op jit(solution)/shard_map/ppermute | solution.py:55
  1017.1 72.9 %collective-permute-start.27 = (bf16[384,4096]{1,0:T(8,128)(2,1)}, bf16[384,4096]{1,0:T(8,128)(2,1)}, u32[]{:S(2)}, u32[]{:S(2)}) collective-permute-start(bf16[384,4096]{1,0:T(8,128)(2,1)} %pad_maximum_fusion.3), channel_id=1, source_target_pairs={{0,2},{3,1},{4,6},{7,5},{8,10},{11,9},{12,14},{15,13},{16,18},{19,... | collective-permute-start | bytes 9437192 | tf_op jit(solution)/shard_map/ppermute | solution.py:55
  1090.0 343.5 %reduce-scatter.20.cloned.1.call-start = ((), (), s32[]{:S(2)}) async-start(), calls=%async_computation.19 | async-start | bytes 14155776 | tf_op jit(solution)/shard_map/reduce_scatter | solution.py:655
  1100.2 66.8 %collective-permute-start.28 = (bf16[384,2048]{1,0:T(8,128)(2,1)}, bf16[384,2048]{1,0:T(8,128)(2,1)}, u32[]{:S(2)}, u32[]{:S(2)}) collective-permute-start(bf16[384,2048]{1,0:T(8,128)(2,1)} %reduce-scatter.8.cloned.1.call-done), channel_id=1, source_target_pairs={{0,2},{3,1},{1,3},{2,0},{4,6},{7,5},{5,7},{6,4},{8,10},{11,9},{9,1... | collective-permute-start | bytes 4718600 | tf_op jit(solution)/shard_map/ppermute | solution.py:55
  1167.0 16.8 %copy-start.17 = (bf16[512,3072]{1,0:T(8,128)(2,1)S(1)}, bf16[512,3072]{1,0:T(8,128)(2,1)}, u32[]{:S(2)}) copy-start(bf16[512,3072]{1,0:T(8,128)(2,1)} %copy-done.16) | copy-start | bytes 9437188
  1167.0 16.8 %copy-start.19 = (bf16[512,3072]{1,0:T(8,128)(2,1)S(1)}, bf16[512,3072]{1,0:T(8,128)(2,1)}, u32[]{:S(2)}) copy-start(bf16[512,3072]{1,0:T(8,128)(2,1)} %multiply_convert_fusion.6) | copy-start | bytes 9437188
  1167.0 16.8 %copy-start.21 = (bf16[512,3072]{1,0:T(8,128)(2,1)S(1)}, bf16[512,3072]{1,0:T(8,128)(2,1)}, u32[]{:S(2)}) copy-start(bf16[512,3072]{1,0:T(8,128)(2,1)} %copy-done.20) | copy-start | bytes 9437188
  1176.9 69.4 %collective-permute-start.29 = (bf16[512,3072]{1,0:T(8,128)(2,1)}, bf16[512,3072]{1,0:T(8,128)(2,1)}, u32[]{:S(2)}, u32[]{:S(2)}) collective-permute-start(bf16[512,3072]{1,0:T(8,128)(2,1)} %convolution_convert_fusion.13), channel_id=1, source_target_pairs={{0,1},{4,5},{8,9},{12,13},{16,17},{20,21},{24,25},{28,29}} | collective-permute-start | bytes 9437192 | tf_op jit(solution)/shard_map/ppermute | solution.py:55
  1179.8 66.5 %collective-permute-start.30 = (bf16[512,3072]{1,0:T(8,128)(2,1)}, bf16[512,3072]{1,0:T(8,128)(2,1)}, u32[]{:S(2)}, u32[]{:S(2)}) collective-permute-start(bf16[512,3072]{1,0:T(8,128)(2,1)} %convolution_convert_fusion.13), channel_id=1, source_target_pairs={{3,2},{7,6},{11,10},{15,14},{19,18},{23,22},{27,26},{31,30}} | collective-permute-start | bytes 9437192 | tf_op jit(solution)/shard_map/ppermute | solution.py:55
  1182.1 73.1 %collective-permute-start.31 = (bf16[384,4096]{1,0:T(8,128)(2,1)}, bf16[384,4096]{1,0:T(8,128)(2,1)}, u32[]{:S(2)}, u32[]{:S(2)}) collective-permute-start(bf16[384,4096]{1,0:T(8,128)(2,1)} %pad_maximum_fusion.3), channel_id=1, source_target_pairs={{1,3},{2,0},{5,7},{6,4},{9,11},{10,8},{13,15},{14,12},{17,19},{18,... | collective-permute-start | bytes 9437192 | tf_op jit(solution)/shard_map/ppermute | solution.py:55
  1263.4 68.6 %collective-permute-start.32 = (bf16[512,3072]{1,0:T(8,128)(2,1)}, bf16[512,3072]{1,0:T(8,128)(2,1)}, u32[]{:S(2)}, u32[]{:S(2)}) collective-permute-start(bf16[512,3072]{1,0:T(8,128)(2,1)} %add_convert_fusion.2), channel_id=1, source_target_pairs={{0,1},{1,2},{4,5},{5,6},{8,9},{9,10},{12,13},{13,14},{16,17},{17,1... | collective-permute-start | bytes 9437192 | tf_op jit(solution)/shard_map/ppermute | solution.py:55
  1266.3 65.7 %collective-permute-start.33 = (bf16[512,3072]{1,0:T(8,128)(2,1)}, bf16[512,3072]{1,0:T(8,128)(2,1)}, u32[]{:S(2)}, u32[]{:S(2)}) collective-permute-start(bf16[512,3072]{1,0:T(8,128)(2,1)} %add_convert_fusion.2), channel_id=1, source_target_pairs={{3,2},{2,1},{7,6},{6,5},{11,10},{10,9},{15,14},{14,13},{19,18},{18... | collective-permute-start | bytes 9437192 | tf_op jit(solution)/shard_map/ppermute | solution.py:55
  1268.6 71.4 %collective-permute-start.34 = (bf16[512,3072]{1,0:T(8,128)(2,1)}, bf16[512,3072]{1,0:T(8,128)(2,1)}, u32[]{:S(2)}, u32[]{:S(2)}) collective-permute-start(bf16[512,3072]{1,0:T(8,128)(2,1)} %shard_map.239), channel_id=1, source_target_pairs={{1,0},{2,3},{5,4},{6,7},{9,8},{10,11},{13,12},{14,15},{17,16},{18,... | collective-permute-start | bytes 9437192 | tf_op jit(solution)/shard_map/ppermute | solution.py:55
  1348.4 68.5 %collective-permute-start.35 = (bf16[512,3072]{1,0:T(8,128)(2,1)}, bf16[512,3072]{1,0:T(8,128)(2,1)}, u32[]{:S(2)}, u32[]{:S(2)}) collective-permute-start(bf16[512,3072]{1,0:T(8,128)(2,1)} %get-tuple-element.290), channel_id=1, source_target_pairs={{0,1},{1,2},{2,3},{4,5},{5,6},{6,7},{8,9},{9,10},{10,11},{12,13},{... | collective-permute-start | bytes 9437192 | tf_op jit(solution)/shard_map/ppermute | solution.py:55
  1352.5 70.1 %collective-permute-start.36 = (bf16[512,3072]{1,0:T(8,128)(2,1)}, bf16[512,3072]{1,0:T(8,128)(2,1)}, u32[]{:S(2)}, u32[]{:S(2)}) collective-permute-start(bf16[512,3072]{1,0:T(8,128)(2,1)} %get-tuple-element.291), channel_id=1, source_target_pairs={{3,2},{2,1},{1,0},{7,6},{6,5},{5,4},{11,10},{10,9},{9,8},{15,14},{... | collective-permute-start | bytes 9437192 | tf_op jit(solution)/shard_map/ppermute | solution.py:55
  1386.0 36.6 %copy-start.3 = (bf16[512,3072]{1,0:T(8,128)(2,1)S(1)}, bf16[512,3072]{1,0:T(8,128)(2,1)}, u32[]{:S(2)}) copy-start(bf16[512,3072]{1,0:T(8,128)(2,1)} %convolution_convert_fusion.10.refs_0_) | copy-start | bytes 9437188
  (36 other events, 182.0 us)
Sparse Core Ops, SparseCore 0:
  14.0 54.9 all-gather.6
  70.8 39.7 all-gather.8
  112.5 72.1 all-gather.10
  186.4 125.3 all-gather.12
  335.2 70.4 all-gather.14
  503.0 123.5 all-gather.16
  722.8 92.4 reduce-scatter.9
  818.8 92.3 reduce-scatter.11
  914.7 92.3 reduce-scatter.7
  1010.5 92.3 reduce-scatter.13
  1106.4 92.4 reduce-scatter.15
  1202.2 92.3 reduce-scatter.17
  1298.2 92.3 reduce-scatter.19

commit v5 on v3

--- a/solution.py
+++ b/solution.py
@@ -492,24 +492,6 @@
     def gather(shard):
         return lax.all_gather(shard, "dp", axis=0, tiled=True)
 
-    own_qkv = jnp.concatenate(
-        [
-            part
-            for g in range(heads_kv)
-            for part in (
-                query_weight[:, g * qw : (g + 1) * qw],
-                key_projection_weight[:, g * hd : (g + 1) * hd],
-                value_projection_weight[:, g * hd : (g + 1) * hd],
-            )
-        ],
-        axis=1,
-    )
-    w_qkv = gather(own_qkv)
-    w_out = gather(out_weight.T)
-    gains = lax.all_gather(jnp.stack([attn_gain, mlp_gain]), "dp", axis=1, tiled=True).astype(F32)
-    gain_one, gain_two = gains[0], gains[1]
-    down_t = down_weight.T
-
     partners = halves(n, [(i, i ^ 1) for i in range(n)])
     outward = [halves(n, [((i + 2 * k) % n, i) for i in range(n)]) for k in range(1, slices)]
     homeward = [halves(n, [(i, (i + 2 * k) % n) for i in range(n)]) for k in range(1, slices)]
@@ -519,10 +501,6 @@
 
     def to_owners(sums, half):
         return [(one, pairs[half]) for one, pairs in zip(sums, homeward)]
-
-    w_down = [gather(down_t)]
-    both_weight = jnp.concatenate([gate_weight, up_weight], axis=1)
-    w_both = [gather(both_weight)]
 
     live_count = counts[0]
     own_index = place * rows + jnp.arange(rows, dtype=jnp.int32)
@@ -543,25 +521,59 @@
     attend, attend_back = attention_calls(n, rows, heads_q, heads_kv)
     tables = (cos, sin, query_seg, key_seg)
 
+    gains = lax.all_gather(jnp.stack([attn_gain, mlp_gain]), "dp", axis=1, tiled=True).astype(F32)
+    gain_one, gain_two = gains[0], gains[1]
+
     source = tokens.astype(F32)
     inv_one = norm_inverse(source)
     normed_one = (source * inv_one * gain_one).astype(BF16)
-    grad_result = cotangent.astype(F32) * live
-    grad_low = grad_result.astype(BF16)
+
+    def attention_weights(gate):
+        query, key, value = lax.optimization_barrier((query_weight, key_projection_weight, value_projection_weight, gate))[:3]
+        return jnp.concatenate(
+            [
+                part
+                for g in range(heads_kv)
+                for part in (
+                    query[:, g * qw : (g + 1) * qw],
+                    key[:, g * hd : (g + 1) * hd],
+                    value[:, g * hd : (g + 1) * hd],
+                )
+            ],
+            axis=1,
+        )
+
+    own_qkv = attention_weights(normed_one)
+    w_qkv = gather(own_qkv)
+    shards_here, early = [], []
+
+    def shard_layouts(step, gate):
+        if step != 1:
+            return ()
+        both = jnp.concatenate([after(gate_weight, gate), up_weight], axis=1)
+        masked = (after(cotangent, gate).astype(F32) * live).astype(BF16)
+        return (after(out_weight, gate).T, after(down_weight, gate).T, both, masked, *tables)
+
+    def took_rows(step, arrived, filled):
+        early.extend(arrived)
+        if step == 1:
+            shards_here.extend(filled[:4])
+
     more = slices - 1
-    early = []
     slots_one, projected = line_gather(
         after(normed_one, labels),
         n,
         lambda s, shard: dot(shard, w_qkv, NN),
-        lambda step, gate: tables if step == 1 else (),
+        shard_layouts,
         lambda step: {
-            n - 2: [(grad_low, partners[0])],
-            n - 1: to_others(both_weight, 0),
+            n - 2: [(shards_here[3], partners[0])] if shards_here else (),
+            n - 1: to_others(shards_here[2], 0) if shards_here else (),
         }.get(step, ()),
-        lambda step, arrived, filled: early.extend(arrived),
+        took_rows,
     )
     low_ends, both_ends = early[0], early[1:]
+    out_t, down_t, both_weight, grad_low = shards_here
+    w_out, w_down, w_both = gather(out_t), [gather(down_t)], [gather(both_weight)]
     projected[n - 1] = after(projected[n - 1], w_out, w_down[0])
 
     def attention(gate):
@@ -607,11 +619,11 @@
 
     def own_rows(gate):
         made = [one for w, gm in zip(w_both, grad_mixed) for one in gated(gate, w, gm, 0)]
-        return [spread(made[1::3] + made[2::3], weights, 0, F32), *made]
+        return [spread(made[1::3] + made[2::3], weights, 0, F32, HIDES, 0, 2), *made]
 
     swap = partners[0] + partners[1]
     weights = [(w, 0) for w in w_both] + [(w, 1) for w in w_both]
-    (two_theirs,), (ours, *mine) = travel([(normed_two, swap)], own_rows)
+    (two_theirs,), (ours_first, *mine) = travel([(normed_two, swap)], own_rows)
     two = jnp.concatenate([normed_two, two_theirs], axis=0)
     mixed, grad_gate, grad_up, d_down = [None] * slices, [None] * slices, [None] * slices, [None] * slices
     rows_in = two_theirs
@@ -630,13 +642,16 @@
         )
 
     def gate_weights(gate):
-        return tuple(dot(two, after(g, gate), TN, BF16) for g in grad_gate[1:])
+        return (
+            spread([after(grads[0], gate)] + grads[1:], weights, 0, F32, HIDES, 1, 2),
+            *(dot(two, after(g, gate), TN, BF16) for g in grad_gate[1:]),
+        )
 
     theirs = spread(grads, weights, 1, BF16, HIDES, 0, 2)
     (from_first,), (theirs, *d_up[1:]) = travel([(theirs, swap)], second_half)
-    (from_second,), d_gate[1:] = travel([(theirs, swap)], gate_weights)
+    (from_second,), (ours_second, *d_gate[1:]) = travel([(theirs, swap)], gate_weights)
     grad_hidden, grad_hidden_low = norm_back(
-        [(ours, 0, 2), (from_first, 0, 1), (from_second, 1, 1)], hidden, gain_two, cotangent, live, True
+        [(ours_first, 0, 1), (ours_second, 1, 1), (from_first, 0, 1), (from_second, 1, 1)], hidden, gain_two, cotangent, live, True
     )
 
     def owner_sum(partial):
@@ -705,6 +720,13 @@
         [(one, a + b) for one, (a, b) in zip(leaving, homeward)], attention_back
     )
     back_down, back_up, outputs, d_attention = [], [], [], []
+    all_heads = own_qkv.shape[1]
+
+    def columns(array, offset, size):
+        return jnp.concatenate(
+            [array[:, g * wide + offset : g * wide + offset + size] for g in range(heads_kv)], axis=1
+        ).astype(F32)
+
 
     def while_reduce(step, gate):
         if step == 1:
@@ -715,7 +737,13 @@
         if step == n - 1:
             from_partner = joined(result_ends, outputs[0])
             result = hidden + (results[1] + after(from_partner, gate).astype(F32))
-            return ((result * live).astype(BF16),)
+            sum_attention = owner_sum(d_attention[0])
+            return (
+                (result * live).astype(BF16),
+                turned(sum_attention, all_heads, out_weight.shape[0]),
+                *(columns(sum_attention, *place) for place in ((0, qw), (qw, hd), (qw + hd, hd))),
+                sum_attention,
+            )
         return ()
 
     def along_reduce(step):
@@ -735,7 +763,7 @@
         elif step == 2:
             outputs.extend(arrived)
         elif step == n - 1:
-            outputs.append(filled[0])
+            outputs.extend(filled)
 
     grad_normed_one = line_reduce(
         lambda s: dot(grad_qkv[s * rows : (s + 1) * rows], w_qkv, NT, BF16),
@@ -744,20 +772,15 @@
         along_reduce,
         took_reduce,
     )
-    output = outputs[1]
+    _, output, grad_out_w, grad_query_w, grad_key_w, grad_value_w, sum_attention = outputs
 
     def whole(first, back):
         return sum((one.astype(F32) for one in back), first.astype(F32))
 
-    all_heads = own_qkv.shape[1]
     grad_down_w = whole(sum_down, back_down).T
     grad_gate_w = whole(sum_gate, back_gate)
     grad_up_w = whole(sum_up, back_up)
-    sum_attention = owner_sum(d_attention[0])
     grad_qkv_w = sum_attention[:, :all_heads].astype(F32)
-    grad_out_w = turned(sum_attention, all_heads, out_weight.shape[0])
-    grad_tokens = norm_back([(term, 0, 2) for term in grad_normed_one], tokens, gain_one, grad_hidden, None, False)
-
     def along_row(weight, grad):
         return jnp.sum(weight.astype(F32) * grad, axis=1)
 
@@ -769,17 +792,14 @@
     )
     gain_own = lax.psum(gain_parts, "tensor") / jnp.stack([attn_gain, mlp_gain]).astype(F32)
 
-    def columns(offset, size):
-        return jnp.concatenate(
-            [grad_qkv_w[:, g * wide + offset : g * wide + offset + size] for g in range(heads_kv)], axis=1
-        )
+    grad_tokens = norm_back([(term, 0, 2) for term in grad_normed_one], tokens, gain_one, grad_hidden, None, False)
 
     return (
         output,
         grad_tokens,
-        columns(0, qw),
-        columns(qw, hd),
-        columns(qw + hd, hd),
+        grad_query_w,
+        grad_key_w,
+        grad_value_w,
         grad_out_w,
         gain_own[0],
         grad_gate_w,

time: 1440 us -> 1420 us (0.986)
  waiting for transfers between devices: 474 us -> 443 us
    ppermute x37, waiting for transfers between devices: 449 us -> 410 us  [travel(): lax.ppermute(array, 'tensor', pairs)]
    pallas_call x5 -> x6, Pallas kernels: 120 us -> 127 us  [spread(): pl.pallas_call(functools.partial(spread_kernel, count), grid=(tiles,), in...]
  transfers between devices with their start and end apart: 50 -> 50, of which waited for: 27 -> 28; matrix products, arithmetic and copies ran while one was open for 29% -> 30% of each run, Pallas kernels for 21% -> 22%
where the time goes in v5:
time: 1420 us; the launch traced here: 1410 us
  waiting for transfers between devices  443 us (31%)
  Pallas kernels  342 us (24%)
  matrix products  311 us (22%)
  other arithmetic  119 us (8%)
  starting transfers between devices  113 us (8%)
  local copies, waits for them, and re-layouts  37.4 us (3%)
  blocking collectives  32.2 us (2%)
  between operations  15.6 us (1%)
    ppermute x37, waiting for transfers between devices, travel(): lax.ppermute(array, 'tensor', pairs)  410 us
    dot_general x26, matrix products, dot(): return lax.dot_general(a, b, dims, preferred_element_type=F32).astype(out)  311 us
    pallas_call x6, Pallas kernels, spread(): pl.pallas_call(functools.partial(spread_kernel, count), grid=(tiles,), in...  127 us
    ppermute x37, starting transfers between devices, travel(): lax.ppermute(array, 'tensor', pairs)  112 us
    pallas_call x4, Pallas kernels, gated(): pl.pallas_call(gated_kernel, grid=(tiles,), in_specs=[pl.BlockSpec((rows,...  88 us
    pallas_call x1, Pallas kernels, attention_back(): attend_back(after(slot_table, gate), *grad_attended, rotated, attended, l...  55.6 us
    pallas_call x1, Pallas kernels, attention(): return attend(slot_table, *projected, *tables)  44.1 us
  transfers between devices with their start and end apart: 50, of which 28 were waited for; matrix products, arithmetic and copies ran while one was open for 30% of the time, Pallas kernels for 22%

profile of v5, /device:TPU:0, one launch (start us, length us, event | category | flops | bytes accessed | tf_op | source)
XLA Modules:
  0.0 1413.9 jit_solution(12329922663875216116)
XLA Ops:
  9.4 10.4 all_gather.24
  30.2 13.4 all_gather.25
  71.9 10.8 all-gather.7.cloned.1.call-done
  82.8 9.9 fusion.44.refs_0_
  92.7 19.6 %collective-permute-done = bf16[512,3072]{1,0:T(8,128)(2,1)} collective-permute-done((bf16[512,3072]{1,0:T(8,128)(2,1)}, bf16[512,3072]{1,0:T(8,128)(2,1)}, u32[]{:S(2)}, u32[]{:S(2)}) %collective-permute-start) | collective-permute-done | bytes 3145760 | tf_op jit(solution)/shard_map/ppermute | solution.py:55
  123.1 7.1 collective-permute-start.4
  132.4 9.2 fusion.45.refs_1_
  141.6 49.1 %collective-permute-done.3 = bf16[512,3072]{1,0:T(8,128)(2,1)} collective-permute-done((bf16[512,3072]{1,0:T(8,128)(2,1)}, bf16[512,3072]{1,0:T(8,128)(2,1)}, u32[]{:S(2)}, u32[]{:S(2)}) %collective-permute-start.3) | collective-permute-done | bytes 3145760 | tf_op jit(solution)/shard_map/ppermute | solution.py:55
  194.1 9.3 collective-permute-start.7
  205.7 9.2 fusion.46.refs_2_
  214.9 45.2 %collective-permute-done.6 = bf16[512,3072]{1,0:T(8,128)(2,1)S(1)} collective-permute-done((bf16[512,3072]{1,0:T(8,128)(2,1)}, bf16[512,3072]{1,0:T(8,128)(2,1)S(1)}, u32[]{:S(2)}, u32[]{:S(2)}) %collective-permute-start.6) | collective-permute-done | bytes 3145760 | tf_op jit(solution)/shard_map/ppermute | solution.py:55
  266.2 8.0 fusion.47.refs_3_
  280.7 44.1 %shard_map.230 = (bf16[2048,768]{1,0:T(8,128)(2,1)}, bf16[2048,1280]{1,0:T(8,128)(2,1)}, f32[2,8,2048]{2,1,0:T(8,128)}) custom-call(s32[8]{0:T(128)} %dynamic-slice_bitcast_fusion.place_ref, f32[512,1280]{1,0:T(8,128)} %fusion.44.refs_0_, f32[512,1280]{1,0:T(8,128)} %fusion.45.refs_1_, f32[512,1280]{1,0:T(8,128)} %fusion.46.refs_2_, ...), custom_call_target="tpu_custom_call" | custom-call | flops 1 | bytes 1 | tf_op jit(solution)/shard_map/pallas_call | solution.py:580
  324.8 16.8 %collective-permute-done.8 = bf16[384,2048]{1,0:T(8,128)(2,1)} collective-permute-done((bf16[384,2048]{1,0:T(8,128)(2,1)}, bf16[384,2048]{1,0:T(8,128)(2,1)}, u32[]{:S(2)}, u32[]{:S(2)}) %collective-permute-start.8) | collective-permute-done | bytes 1572896 | tf_op jit(solution)/shard_map/ppermute | solution.py:55
  349.5 7.2 collective-permute-start.9
  356.6 6.9 convolution_convert_fusion.8
  363.5 57.5 %collective-permute-done.11 = bf16[384,4096]{1,0:T(8,128)(2,1)S(1)} collective-permute-done((bf16[384,4096]{1,0:T(8,128)(2,1)S(1)}, bf16[384,4096]{1,0:T(8,128)(2,1)S(1)}, u32[]{:S(2)}, u32[]{:S(2)}) %collective-permute-start.11) | collective-permute-done | bytes 3145760 | tf_op jit(solution)/shard_map/ppermute | solution.py:55
  428.6 6.7 add_convert_fusion.5
  447.3 7.0 convolution_convert_fusion.6
  454.3 50.9 %collective-permute-done.12 = bf16[512,3072]{1,0:T(8,128)(2,1)S(1)} collective-permute-done((bf16[512,3072]{1,0:T(8,128)(2,1)S(1)}, bf16[512,3072]{1,0:T(8,128)(2,1)S(1)}, u32[]{:S(2)}, u32[]{:S(2)}) %collective-permute-start.12) | collective-permute-done | bytes 3145760 | tf_op jit(solution)/shard_map/ppermute | solution.py:55
  524.7 16.9 %fusion.40.gm_ref = f32[1024,2048]{1,0:T(8,128)} fusion(bf16[3072,2048]{1,0:T(8,128)(2,1)S(1)} %bitcast.56, bf16[512,3072]{1,0:T(8,128)(2,1)S(1)} %add.134, bf16[512,3072]{1,0:T(8,128)(2,1)S(1)} %copy-done.25), kind=kOutput, calls=%fused_computation.112 | convolution fusion | flops 12897484800 | bytes 27262976 | tf_op jit(solution)/shard_map/dot_general | solution.py:25
  541.6 19.0 %fusion.39.gm_ref = f32[1024,2048]{1,0:T(8,128)} fusion(bf16[3072,2048]{1,0:T(8,128)(2,1)} %all-gather.15.cloned.1.call-done.refs_3_, bf16[512,3072]{1,0:T(8,128)(2,1)} %copy-done.31, bf16[512,3072]{1,0:T(8,128)(2,1)} %multiply_convert_fusion.2), kind=kOutput, calls=%fused_computation.111 | convolution fusion | flops 12897484800 | bytes 27262976 | tf_op jit(solution)/shard_map/dot_general | solution.py:25
  560.6 21.4 %collective-permute-done.15 = bf16[512,3072]{1,0:T(8,128)(2,1)} collective-permute-done((bf16[512,3072]{1,0:T(8,128)(2,1)}, bf16[512,3072]{1,0:T(8,128)(2,1)}, u32[]{:S(2)}, u32[]{:S(2)}) %collective-permute-start.15) | collective-permute-done | bytes 3145760 | tf_op jit(solution)/shard_map/ppermute | solution.py:55
  596.2 21.2 %shard_map.231 = (bf16[1024,2048]{1,0:T(8,128)(2,1)}, bf16[1024,2048]{1,0:T(8,128)(2,1)}, bf16[1024,2048]{1,0:T(8,128)(2,1)}) custom-call(bf16[512,3072]{1,0:T(8,128)(2,1)} %multiply_convert_fusion.1.x_ref, bf16[3072,4096]{1,0:T(8,128)(2,1)} %all-gather.13.cloned.1.call-done.gate_ref.up_ref.refs_4_.refs_6_, ...), custom_call_target="tpu_custom_call" | custom-call | flops 1 | bytes 1 | tf_op jit(solution)/shard_map/pallas_call | solution.py:355
  617.5 21.0 %shard_map.232 = (bf16[1024,2048]{1,0:T(8,128)(2,1)}, bf16[1024,2048]{1,0:T(8,128)(2,1)}, bf16[1024,2048]{1,0:T(8,128)(2,1)}) custom-call(bf16[512,3072]{1,0:T(8,128)(2,1)} %multiply_convert_fusion.1.x_ref, bf16[3072,4096]{1,0:T(8,128)(2,1)} %all-gather.17.cloned.1.call-done.gate_ref.up_ref.refs_5_.refs_7_, ...), custom_call_target="tpu_custom_call" | custom-call | flops 1 | bytes 1 | tf_op jit(solution)/shard_map/pallas_call | solution.py:355
  638.5 19.5 %shard_map.233.refs_0_ = f32[512,1536]{1,0:T(8,128)S(1)} custom-call(bf16[1024,2048]{1,0:T(8,128)(2,1)} %get-tuple-element.246.refs_0_.refs_1_, bf16[1024,2048]{1,0:T(8,128)(2,1)} %get-tuple-element.241.refs_1_, bf16[1024,2048]{1,0:T(8,128)(2,1)} %get-tuple-element.247.refs_2_, bf16[1024,2048]{1,0:T(8,128)(2,1)} %get-tuple-element.242.refs_3_.refs_2_, ...), custom_call_target="tpu_custom_call" | custom-call | flops 1 | bytes 1 | tf_op jit(solution)/shard_map/pallas_call | solution.py:386
  662.9 21.2 %shard_map.234 = (bf16[1024,2048]{1,0:T(8,128)(2,1)}, bf16[1024,2048]{1,0:T(8,128)(2,1)}, bf16[1024,2048]{1,0:T(8,128)(2,1)}) custom-call(bf16[512,3072]{1,0:T(8,128)(2,1)} %collective-permute-done.17.x_ref, ...), custom_call_target="tpu_custom_call", output_to_operand_aliasing={{0}: (4, {}), {1}: (5, {}), {2}: (6, {})} | custom-call | flops 1 | bytes 1 | tf_op jit(solution)/shard_map/pallas_call | solution.py:355
  684.1 18.0 %convolution_convert_fusion.5 = bf16[3072,2048]{1,0:T(8,128)(2,1)} fusion(bf16[1024,2048]{1,0:T(8,128)(2,1)} %get-tuple-element.243.refs_1_, bf16[512,3072]{1,0:T(8,128)(2,1)S(1)} %copy-done.32, bf16[512,3072]{1,0:T(8,128)(2,1)S(1)} %copy-done.26), kind=kOutput, calls=%fused_computation.23 | convolution fusion | flops 12903776256 | bytes 23068672 | tf_op jit(solution)/shard_map/dot_general | solution.py:25
  702.2 24.6 %shard_map.235 = (bf16[1024,2048]{1,0:T(8,128)(2,1)}, bf16[1024,2048]{1,0:T(8,128)(2,1)}, bf16[1024,2048]{1,0:T(8,128)(2,1)}) custom-call(bf16[512,3072]{1,0:T(8,128)(2,1)} %collective-permute-done.17.x_ref, ...), custom_call_target="tpu_custom_call", output_to_operand_aliasing={{0}: (4, {}), {1}: (5, {}), {2}: (6, {})} | custom-call | flops 1 | bytes 1 | tf_op jit(solution)/shard_map/pallas_call | solution.py:355
  726.8 21.4 %shard_map.236 = bf16[512,1536]{1,0:T(8,128)(2,1)} custom-call(bf16[1024,2048]{1,0:T(8,128)(2,1)} %get-tuple-element.284.refs_0_, bf16[1024,2048]{1,0:T(8,128)(2,1)} %get-tuple-element.256.refs_1_, bf16[1024,2048]{1,0:T(8,128)(2,1)} %get-tuple-element.275.refs_2_, bf16[1024,2048]{1,0:T(8,128)(2,1)} %get-tuple-element.253.refs_3_, ...), custom_call_target="tpu_custom_call" | custom-call | flops 1 | bytes 1 | tf_op jit(solution)/shard_map/pallas_call | solution.py:386
  748.3 19.9 %shard_map.237 = bf16[512,1536]{1,0:T(8,128)(2,1)S(1)} custom-call(bf16[1024,2048]{1,0:T(8,128)(2,1)} %get-tuple-element.284.refs_0_, bf16[1024,2048]{1,0:T(8,128)(2,1)} %get-tuple-element.256.refs_1_, bf16[1024,2048]{1,0:T(8,128)(2,1)} %get-tuple-element.275.refs_2_, bf16[1024,2048]{1,0:T(8,128)(2,1)} %get-tuple-element.253.refs_3_, ...), custom_call_target="tpu_custom_call" | custom-call | flops 1 | bytes 1 | tf_op jit(solution)/shard_map/pallas_call | solution.py:386
  769.4 18.9 %convolution_convert_fusion.4 = bf16[3072,2048]{1,0:T(8,128)(2,1)} fusion(bf16[1024,2048]{1,0:T(8,128)(2,1)S(1)} %copy-done.14, bf16[512,3072]{1,0:T(8,128)(2,1)} %collective-permute-done.17.x_ref, bf16[512,3072]{1,0:T(8,128)(2,1)} %multiply_convert_fusion.1.x_ref), kind=kOutput, calls=%fused_computation.22 | convolution fusion | flops 12903776256 | bytes 23068672 | tf_op jit(solution)/shard_map/dot_general | solution.py:25
  790.4 21.6 %shard_map.238.refs_1_ = f32[512,1536]{1,0:T(8,128)S(1)} custom-call(bf16[1024,2048]{1,0:T(8,128)(2,1)} %get-tuple-element.284.refs_0_, bf16[1024,2048]{1,0:T(8,128)(2,1)} %get-tuple-element.256.refs_1_, bf16[1024,2048]{1,0:T(8,128)(2,1)} %get-tuple-element.275.refs_2_, bf16[1024,2048]{1,0:T(8,128)(2,1)} %get-tuple-element.253.refs_3_, ...), custom_call_target="tpu_custom_call" | custom-call | flops 1 | bytes 1 | tf_op jit(solution)/shard_map/pallas_call | solution.py:386
  813.8 19.0 %convolution_convert_fusion.3 = bf16[3072,2048]{1,0:T(8,128)(2,1)} fusion(bf16[1024,2048]{1,0:T(8,128)(2,1)S(1)} %copy-done.13, bf16[512,3072]{1,0:T(8,128)(2,1)} %collective-permute-done.17.x_ref, bf16[512,3072]{1,0:T(8,128)(2,1)} %multiply_convert_fusion.1.x_ref), kind=kOutput, calls=%fused_computation.21 | convolution fusion | flops 12903776256 | bytes 23068672 | tf_op jit(solution)/shard_map/dot_general | solution.py:25
  837.3 11.9 shard_map.239
  855.1 21.9 %shard_map.240 = bf16[512,3072]{1,0:T(8,128)(2,1)} custom-call(bf16[1024,2048]{1,0:T(8,128)(2,1)} %get-tuple-element.274.refs_0_, bf16[1024,2048]{1,0:T(8,128)(2,1)} %get-tuple-element.243.refs_1_, bf16[3072,2048]{1,0:T(8,128)(2,1)} %all-gather.11.cloned.1.call-done.refs_2_, bf16[3072,2048]{1,0:T(8,128)(2,1)} %all-gather.15.cloned.1.call-done.refs_3_), custom_call_target="tpu_custom_call" | custom-call | flops 12884901888 | bytes 25165824 | tf_op jit(solution)/shard_map/pallas_call | solution.py:386
  877.0 7.0 convolution_convert_fusion.17.refs_0_
  884.0 17.9 %convolution_convert_fusion.2 = bf16[3072,2048]{1,0:T(8,128)(2,1)} fusion(bf16[1024,2048]{1,0:T(8,128)(2,1)S(1)} %copy-done.16, bf16[512,3072]{1,0:T(8,128)(2,1)} %copy-done.31, bf16[512,3072]{1,0:T(8,128)(2,1)S(1)} %copy-done.27), kind=kOutput, calls=%fused_computation.20 | convolution fusion | flops 12903776256 | bytes 23068672 | tf_op jit(solution)/shard_map/dot_general | solution.py:25
  901.8 10.8 collective-permute-done.20
  937.2 22.4 %shard_map.241 = f32[512,3072]{1,0:T(8,128)} custom-call(bf16[1024,2048]{1,0:T(8,128)(2,1)} %get-tuple-element.274.refs_0_, bf16[1024,2048]{1,0:T(8,128)(2,1)} %get-tuple-element.243.refs_1_, bf16[3072,2048]{1,0:T(8,128)(2,1)} %all-gather.11.cloned.1.call-done.refs_2_, bf16[3072,2048]{1,0:T(8,128)(2,1)} %all-gather.15.cloned.1.call-done.refs_3_), custom_call_target="tpu_custom_call" | custom-call | flops 1 | bytes 1 | tf_op jit(solution)/shard_map/pallas_call | solution.py:386
  959.6 18.6 %convolution_convert_fusion.1 = bf16[3072,2048]{1,0:T(8,128)(2,1)} fusion(bf16[1024,2048]{1,0:T(8,128)(2,1)S(1)} %copy-done.12, bf16[512,3072]{1,0:T(8,128)(2,1)} %collective-permute-done.17.x_ref, bf16[512,3072]{1,0:T(8,128)(2,1)} %multiply_convert_fusion.1.x_ref), kind=kOutput, calls=%fused_computation.19 | convolution fusion | flops 12903776256 | bytes 23068672 | tf_op jit(solution)/shard_map/dot_general | solution.py:25
  982.2 7.9 collective-permute-done.23
  997.9 11.7 collective-permute-start.27
  1015.5 19.6 %convolution_convert_fusion = bf16[3072,2048]{1,0:T(8,128)(2,1)} fusion(bf16[1024,2048]{1,0:T(8,128)(2,1)S(1)} %copy-done.11, bf16[512,3072]{1,0:T(8,128)(2,1)} %collective-permute-done.17.x_ref, bf16[512,3072]{1,0:T(8,128)(2,1)} %multiply_convert_fusion.1.x_ref), kind=kOutput, calls=%fused_computation.18 | convolution fusion | flops 12903776256 | bytes 23068672 | tf_op jit(solution)/shard_map/dot_general | solution.py:25
  1035.1 26.6 %collective-permute-done.26 = bf16[512,3072]{1,0:T(8,128)(2,1)} collective-permute-done((bf16[512,3072]{1,0:T(8,128)(2,1)}, bf16[512,3072]{1,0:T(8,128)(2,1)}, u32[]{:S(2)}, u32[]{:S(2)}) %collective-permute-start.26) | collective-permute-done | bytes 3145760 | tf_op jit(solution)/shard_map/ppermute | solution.py:55
  1082.5 55.6 %shard_map.242 = bf16[2048,1280]{1,0:T(8,128)(2,1)} custom-call(s32[8]{0:T(128)} %dynamic-slice_bitcast_fusion.place_ref, bf16[512,768]{1,0:T(8,128)(2,1)} %convolution_convert_fusion.17.refs_0_, bf16[512,768]{1,0:T(8,128)(2,1)} %convolution_convert_fusion.16.refs_1_, bf16[512,768]{1,0:T(8,128)(2,1)} %convolution_convert_fusion.15.refs_2_, ...), custom_call_target="tpu_custom_call" | custom-call | flops 32212254720 | bytes 26214400 | tf_op jit(solution)/shard_map/pallas_call | solution.py:711
  1138.1 15.7 %fusion.22 = bf16[3072,768]{1,0:T(8,128)(2,1)} fusion(bf16[2048,768]{1,0:T(8,128)(2,1)} %get-tuple-element.294.refs_5_, bf16[512,3072]{1,0:T(8,128)(2,1)} %copy-done.37, bf16[512,3072]{1,0:T(8,128)(2,1)} %copy-done.34, bf16[512,3072]{1,0:T(8,128)(2,1)} %copy-done.33, bf16[512,3072]{1,0:T(8,128)(2,1)} %get-tuple-element.264), kind=kOutput, calls=%fused_computation.42 | convolution fusion | flops 9716367360 | bytes 20447232 | tf_op jit(solution)/shard_map/dot_general | solution.py:25
  1153.9 10.7 convolution_convert_fusion.13
  1171.3 20.8 %fusion.16 = bf16[3072,1280]{1,0:T(8,128)(2,1)S(1)} fusion(bf16[2048,1280]{1,0:T(8,128)(2,1)} %shard_map.242, bf16[512,3072]{1,0:T(8,128)(2,1)} %copy-done.30, bf16[512,3072]{1,0:T(8,128)(2,1)} %copy-done.29, bf16[512,3072]{1,0:T(8,128)(2,1)} %copy-done.28, bf16[512,3072]{1,0:T(8,128)(2,1)S(1)} %copy-done.24), kind=kOutput, calls=%fused_computation.17 | convolution fusion | flops 16160391168 | bytes 25690112 | tf_op jit(solution)/shard_map/dot_general | solution.py:25
  1192.1 8.7 pad_maximum_fusion
  1200.8 9.6 convolution_convert_fusion.12
  1210.4 13.7 collective-permute-done.29
  1224.0 9.1 collective-permute-done.31
  1233.2 8.0 add_convert_fusion.2
  1248.4 10.4 convolution_convert_fusion.11
  1258.8 13.2 reduce-scatter.18.cloned.1.call-done
  1272.0 29.4 %collective-permute-done.32 = bf16[512,3072]{1,0:T(8,128)(2,1)} collective-permute-done((bf16[512,3072]{1,0:T(8,128)(2,1)}, bf16[512,3072]{1,0:T(8,128)(2,1)}, u32[]{:S(2)}, u32[]{:S(2)}) %collective-permute-start.32) | collective-permute-done | bytes 3145760 | tf_op jit(solution)/shard_map/ppermute | solution.py:55
  1301.5 8.1 collective-permute-done.34
  1309.6 8.2 add_convert_fusion
  1323.6 10.0 convolution_convert_fusion.10.refs_0_
  1353.9 6.5 multiply_convert_fusion
  1360.4 7.5 reduce-scatter.20.cloned.1.call-done.x_ref
  1385.3 8.5 psum.7
  1396.3 10.8 shard_map.244
  (270 shorter events, 275.9 us)
Async XLA Ops:
  7.2 75.6 %all-gather.7.cloned.1.call-start = ((), (), s32[]{:S(2)}) async-start(), calls=%async_computation.7 | async-start | bytes 8847360 | tf_op jit(solution)/shard_map/all_gather | solution.py:493
  30.1 244.0 %all-gather.9.cloned.1.call-start = ((), (), s32[]{:S(2)}) async-start(), calls=%async_computation.8 | async-start | bytes 5308416 | tf_op jit(solution)/shard_map/all_gather | solution.py:493
  43.6 68.7 %collective-permute-start = (bf16[512,3072]{1,0:T(8,128)(2,1)}, bf16[512,3072]{1,0:T(8,128)(2,1)}, u32[]{:S(2)}, u32[]{:S(2)}) collective-permute-start(bf16[512,3072]{1,0:T(8,128)(2,1)} %fusion.21), channel_id=1, source_target_pairs={{0,1},{1,2},{2,3},{4,5},{5,6},{6,7},{8,9},{9,10},{10,11},{12,13},{... | collective-permute-start | bytes 9437192 | tf_op jit(solution)/shard_map/ppermute | solution.py:55
  48.7 69.4 %collective-permute-start.1 = (bf16[512,3072]{1,0:T(8,128)(2,1)}, bf16[512,3072]{1,0:T(8,128)(2,1)}, u32[]{:S(2)}, u32[]{:S(2)}) collective-permute-start(bf16[512,3072]{1,0:T(8,128)(2,1)} %fusion.21), channel_id=1, source_target_pairs={{1,0},{2,1},{3,2},{5,4},{6,5},{7,6},{9,8},{10,9},{11,10},{13,12},{... | collective-permute-start | bytes 9437192 | tf_op jit(solution)/shard_map/ppermute | solution.py:55
  118.1 156.1 %all-gather.11.cloned.1.call-start = ((), (), s32[]{:S(2)}) async-start(), calls=%async_computation.9 | async-start | bytes 14155776 | tf_op jit(solution)/shard_map/all_gather | solution.py:493
  118.8 303.8 %all-gather.13.cloned.1.call-start = ((), (), s32[]{:S(2)}) async-start(), calls=%async_computation.10 | async-start | bytes 28311552 | tf_op jit(solution)/shard_map/all_gather | solution.py:493
  119.4 422.2 %all-gather.15.cloned.1.call-start = ((), (), s32[]{:S(2)}) async-start(), calls=%async_computation.11 | async-start | bytes 14155776 | tf_op jit(solution)/shard_map/all_gather | solution.py:493
  119.5 22.2 %collective-permute-start.2 = (bf16[512,3072]{1,0:T(8,128)(2,1)}, bf16[512,3072]{1,0:T(8,128)(2,1)}, u32[]{:S(2)}, u32[]{:S(2)}) collective-permute-start(bf16[512,3072]{1,0:T(8,128)(2,1)} %collective-permute-done), channel_id=1, source_target_pairs={{1,2},{2,3},{5,6},{6,7},{9,10},{10,11},{13,14},{14,15},{17,18},{18... | collective-permute-start | bytes 9437192 | tf_op jit(solution)/shard_map/ppermute | solution.py:55
  121.8 68.9 %collective-permute-start.3 = (bf16[512,3072]{1,0:T(8,128)(2,1)}, bf16[512,3072]{1,0:T(8,128)(2,1)}, u32[]{:S(2)}, u32[]{:S(2)}) collective-permute-start(bf16[512,3072]{1,0:T(8,128)(2,1)} %collective-permute-done.1), channel_id=1, source_target_pairs={{1,0},{2,1},{5,4},{6,5},{9,8},{10,9},{13,12},{14,13},{17,16},{18,1... | collective-permute-start | bytes 9437192 | tf_op jit(solution)/shard_map/ppermute | solution.py:55
  123.1 68.8 %collective-permute-start.4 = (bf16[512,3072]{1,0:T(8,128)(2,1)}, bf16[512,3072]{1,0:T(8,128)(2,1)}, u32[]{:S(2)}, u32[]{:S(2)}) collective-permute-start(bf16[512,3072]{1,0:T(8,128)(2,1)} %multiply_convert_fusion.2), channel_id=1, source_target_pairs={{0,1},{3,2},{4,5},{7,6},{8,9},{11,10},{12,13},{15,14},{16,17},{19,... | collective-permute-start | bytes 9437192 | tf_op jit(solution)/shard_map/ppermute | solution.py:55
  132.4 61.7 %copy-start.17 = (bf16[384,4096]{1,0:T(8,128)(2,1)S(1)}, bf16[384,4096]{1,0:T(8,128)(2,1)}, u32[]{:S(2)}) copy-start(bf16[384,4096]{1,0:T(8,128)(2,1)} %pad_maximum_fusion.3) | copy-start | bytes 9437188
  191.9 23.0 %collective-permute-start.5 = (bf16[512,3072]{1,0:T(8,128)(2,1)}, bf16[512,3072]{1,0:T(8,128)(2,1)S(1)}, u32[]{:S(2)}, u32[]{:S(2)}) collective-permute-start(bf16[512,3072]{1,0:T(8,128)(2,1)} %collective-permute-done.2), channel_id=1, source_target_pairs={{2,3},{6,7},{10,11},{14,15},{18,19},{22,23},{26,27},{30,31}} | collective-permute-start | bytes 9437192 | tf_op jit(solution)/shard_map/ppermute | solution.py:55
  192.8 67.3 %collective-permute-start.6 = (bf16[512,3072]{1,0:T(8,128)(2,1)}, bf16[512,3072]{1,0:T(8,128)(2,1)S(1)}, u32[]{:S(2)}, u32[]{:S(2)}) collective-permute-start(bf16[512,3072]{1,0:T(8,128)(2,1)} %collective-permute-done.3), channel_id=1, source_target_pairs={{1,0},{5,4},{9,8},{13,12},{17,16},{21,20},{25,24},{29,28}} | collective-permute-start | bytes 9437192 | tf_op jit(solution)/shard_map/ppermute | solution.py:55
  194.1 69.6 %collective-permute-start.7 = (bf16[384,4096]{1,0:T(8,128)(2,1)S(1)}, bf16[384,4096]{1,0:T(8,128)(2,1)}, u32[]{:S(2)}, u32[]{:S(2)}) collective-permute-start(bf16[384,4096]{1,0:T(8,128)(2,1)S(1)} %copy-done.17), channel_id=1, source_target_pairs={{3,1},{0,2},{7,5},{4,6},{11,9},{8,10},{15,13},{12,14},{19,17},{16,... | collective-permute-start | bytes 9437192 | tf_op jit(solution)/shard_map/ppermute | solution.py:55
  274.2 67.5 %collective-permute-start.8 = (bf16[384,2048]{1,0:T(8,128)(2,1)}, bf16[384,2048]{1,0:T(8,128)(2,1)}, u32[]{:S(2)}, u32[]{:S(2)}) collective-permute-start(bf16[384,2048]{1,0:T(8,128)(2,1)} %bitcast.58), channel_id=1, source_target_pairs={{3,1},{0,2},{2,0},{1,3},{7,5},{4,6},{6,4},{5,7},{11,9},{8,10},{10,... | collective-permute-start | bytes 4718600 | tf_op jit(solution)/shard_map/ppermute | solution.py:55
  341.7 275.8 %all-gather.17.cloned.1.call-start = ((), (), s32[]{:S(2)}) async-start(), calls=%async_computation.12 | async-start | bytes 28311552 | tf_op jit(solution)/shard_map/all_gather | solution.py:493
  347.3 16.2 %collective-permute-start.10 = (bf16[512,3072]{1,0:T(8,128)(2,1)S(1)}, bf16[512,3072]{1,0:T(8,128)(2,1)S(1)}, u32[]{:S(2)}, u32[]{:S(2)}) collective-permute-start(bf16[512,3072]{1,0:T(8,128)(2,1)S(1)} %convolution_convert_fusion.9), channel_id=1, source_target_pairs={{3,2},{7,6},{11,10},{15,14},{19,18},{23,22},{27,26},{31,30}} | collective-permute-start | bytes 9437192 | tf_op jit(solution)/shard_map/ppermute | solution.py:55
  348.2 72.8 %collective-permute-start.11 = (bf16[384,4096]{1,0:T(8,128)(2,1)S(1)}, bf16[384,4096]{1,0:T(8,128)(2,1)S(1)}, u32[]{:S(2)}, u32[]{:S(2)}) collective-permute-start(bf16[384,4096]{1,0:T(8,128)(2,1)S(1)} %copy-done.18), channel_id=1, source_target_pairs={{2,0},{1,3},{6,4},{5,7},{10,8},{9,11},{14,12},{13,15},{18,16},{17,... | collective-permute-start | bytes 9437192 | tf_op jit(solution)/shard_map/ppermute | solution.py:55
  349.5 73.2 %collective-permute-start.9 = (bf16[512,3072]{1,0:T(8,128)(2,1)S(1)}, bf16[512,3072]{1,0:T(8,128)(2,1)}, u32[]{:S(2)}, u32[]{:S(2)}) collective-permute-start(bf16[512,3072]{1,0:T(8,128)(2,1)S(1)} %convolution_convert_fusion.9), channel_id=1, source_target_pairs={{0,1},{4,5},{8,9},{12,13},{16,17},{20,21},{24,25},{28,29}} | collective-permute-start | bytes 9437192 | tf_op jit(solution)/shard_map/ppermute | solution.py:55
  363.5 57.5 %copy-start.36 = (bf16[512,3072]{1,0:T(8,128)(2,1)}, bf16[512,3072]{1,0:T(8,128)(2,1)S(1)}, u32[]{:S(2)}) copy-start(bf16[512,3072]{1,0:T(8,128)(2,1)S(1)} %collective-permute-done.10) | copy-start | bytes 9437188
  428.5 549.7 %reduce-scatter.10.cloned.1.call-start = ((), (), s32[]{:S(2)}) async-start(), calls=%async_computation.14 | async-start | bytes 14155776 | tf_op jit(solution)/shard_map/reduce_scatter | solution.py:658
  435.2 69.9 %collective-permute-start.12 = (bf16[512,3072]{1,0:T(8,128)(2,1)S(1)}, bf16[512,3072]{1,0:T(8,128)(2,1)S(1)}, u32[]{:S(2)}, u32[]{:S(2)}) collective-permute-start(bf16[512,3072]{1,0:T(8,128)(2,1)S(1)} %add_convert_fusion.5), channel_id=1, source_target_pairs={{0,1},{1,2},{4,5},{5,6},{8,9},{9,10},{12,13},{13,14},{16,17},{17,1... | collective-permute-start | bytes 9437192 | tf_op jit(solution)/shard_map/ppermute | solution.py:55
  439.1 66.0 %collective-permute-start.13 = (bf16[512,3072]{1,0:T(8,128)(2,1)S(1)}, bf16[512,3072]{1,0:T(8,128)(2,1)S(1)}, u32[]{:S(2)}, u32[]{:S(2)}) collective-permute-start(bf16[512,3072]{1,0:T(8,128)(2,1)S(1)} %add_convert_fusion.5), channel_id=1, source_target_pairs={{3,2},{2,1},{7,6},{6,5},{11,10},{10,9},{15,14},{14,13},{19,18},{18... | collective-permute-start | bytes 9437192 | tf_op jit(solution)/shard_map/ppermute | solution.py:55
  440.0 70.3 %collective-permute-start.14 = (bf16[512,3072]{1,0:T(8,128)(2,1)S(1)}, bf16[512,3072]{1,0:T(8,128)(2,1)S(1)}, u32[]{:S(2)}, u32[]{:S(2)}) collective-permute-start(bf16[512,3072]{1,0:T(8,128)(2,1)S(1)} %copy-done.25), channel_id=1, source_target_pairs={{1,0},{2,3},{5,4},{6,7},{9,8},{10,11},{13,12},{14,15},{17,16},{18,... | collective-permute-start | bytes 9437192 | tf_op jit(solution)/shard_map/ppermute | solution.py:55
  447.3 63.1 %copy-start.19 = (bf16[512,3072]{1,0:T(8,128)(2,1)S(1)}, bf16[512,3072]{1,0:T(8,128)(2,1)}, u32[]{:S(2)}) copy-start(bf16[512,3072]{1,0:T(8,128)(2,1)} %convolution_convert_fusion.8) | copy-start | bytes 9437188
  514.7 67.2 %collective-permute-start.15 = (bf16[512,3072]{1,0:T(8,128)(2,1)}, bf16[512,3072]{1,0:T(8,128)(2,1)}, u32[]{:S(2)}, u32[]{:S(2)}) collective-permute-start(bf16[512,3072]{1,0:T(8,128)(2,1)} %get-tuple-element.221), channel_id=1, source_target_pairs={{0,1},{1,2},{2,3},{4,5},{5,6},{6,7},{8,9},{9,10},{10,11},{12,13},{... | collective-permute-start | bytes 9437192 | tf_op jit(solution)/shard_map/ppermute | solution.py:55
  518.2 69.5 %collective-permute-start.16 = (bf16[512,3072]{1,0:T(8,128)(2,1)}, bf16[512,3072]{1,0:T(8,128)(2,1)}, u32[]{:S(2)}, u32[]{:S(2)}) collective-permute-start(bf16[512,3072]{1,0:T(8,128)(2,1)} %get-tuple-element.222), channel_id=1, source_target_pairs={{3,2},{2,1},{1,0},{7,6},{6,5},{5,4},{11,10},{10,9},{9,8},{15,14},{... | collective-permute-start | bytes 9437192 | tf_op jit(solution)/shard_map/ppermute | solution.py:55
  541.6 46.1 %copy-start.23 = (bf16[512,3072]{1,0:T(8,128)(2,1)S(1)}, bf16[512,3072]{1,0:T(8,128)(2,1)}, u32[]{:S(2)}) copy-start(bf16[512,3072]{1,0:T(8,128)(2,1)} %convolution_convert_fusion.6) | copy-start | bytes 9437188
  560.6 32.0 %copy-start.9 = (f32[1,3072]{1,0:T(1,128)S(1)}, f32[1,3072]{1,0:T(1,128)}, u32[]{:S(2)}) copy-start(f32[1,3072]{1,0:T(1,128)} %get-tuple-element.388.gain_ref) | copy-start | bytes 36868
  596.2 66.7 %collective-permute-start.17 = (bf16[512,3072]{1,0:T(8,128)(2,1)}, bf16[512,3072]{1,0:T(8,128)(2,1)}, u32[]{:S(2)}, u32[]{:S(2)}) collective-permute-start(bf16[512,3072]{1,0:T(8,128)(2,1)} %multiply_convert_fusion.1.x_ref), channel_id=1, source_target_pairs={{0,1},{3,2},{1,0},{2,3},{4,5},{7,6},{5,4},{6,7},{8,9},{11,10},{9,8... | collective-permute-start | bytes 9437192 | tf_op jit(solution)/shard_map/ppermute | solution.py:55
  662.9 21.2 %copy-start.26 = (bf16[512,3072]{1,0:T(8,128)(2,1)S(1)}, bf16[512,3072]{1,0:T(8,128)(2,1)}, u32[]{:S(2)}) copy-start(bf16[512,3072]{1,0:T(8,128)(2,1)} %multiply_convert_fusion.2) | copy-start | bytes 9437188
  662.9 21.2 %copy-start.32 = (bf16[512,3072]{1,0:T(8,128)(2,1)S(1)}, bf16[512,3072]{1,0:T(8,128)(2,1)}, u32[]{:S(2)}) copy-start(bf16[512,3072]{1,0:T(8,128)(2,1)} %copy-done.31) | copy-start | bytes 9437188
  702.2 276.1 %reduce-scatter.12.cloned.1.call-start = ((), (), s32[]{:S(2)}) async-start(), calls=%async_computation.15 | async-start | bytes 14155776 | tf_op jit(solution)/shard_map/reduce_scatter | solution.py:658
  748.2 21.1 %copy-start.14 = (bf16[1024,2048]{1,0:T(8,128)(2,1)S(1)}, bf16[1024,2048]{1,0:T(8,128)(2,1)}, u32[]{:S(2)}) copy-start(bf16[1024,2048]{1,0:T(8,128)(2,1)} %get-tuple-element.253.refs_3_) | copy-start | bytes 12582916
  748.2 40.0 %collective-permute-start.18 = (bf16[512,1536]{1,0:T(8,128)(2,1)}, bf16[512,1536]{1,0:T(8,128)(2,1)}, u32[]{:S(2)}, u32[]{:S(2)}) collective-permute-start(bf16[512,1536]{1,0:T(8,128)(2,1)} %shard_map.236), channel_id=1, source_target_pairs={{0,1},{3,2},{1,0},{2,3},{4,5},{7,6},{5,4},{6,7},{8,9},{11,10},{9,8... | collective-permute-start | bytes 4718600 | tf_op jit(solution)/shard_map/ppermute | solution.py:55
  788.3 289.8 %reduce-scatter.8.cloned.1.call-start = ((), (), s32[]{:S(2)}) async-start(), calls=%async_computation.13 | async-start | bytes 14155776 | tf_op jit(solution)/shard_map/reduce_scatter | solution.py:658
  788.4 25.4 %copy-start.13 = (bf16[1024,2048]{1,0:T(8,128)(2,1)S(1)}, bf16[1024,2048]{1,0:T(8,128)(2,1)}, u32[]{:S(2)}) copy-start(bf16[1024,2048]{1,0:T(8,128)(2,1)} %get-tuple-element.256.refs_1_) | copy-start | bytes 12582916
  788.4 44.4 %collective-permute-start.19 = (bf16[512,1536]{1,0:T(8,128)(2,1)}, bf16[512,1536]{1,0:T(8,128)(2,1)}, u32[]{:S(2)}, u32[]{:S(2)}) collective-permute-start(bf16[512,1536]{1,0:T(8,128)(2,1)} %copy-done.6), channel_id=1, source_target_pairs={{0,1},{3,2},{1,0},{2,3},{4,5},{7,6},{5,4},{6,7},{8,9},{11,10},{9,8... | collective-permute-start | bytes 4718600 | tf_op jit(solution)/shard_map/ppermute | solution.py:55
  832.8 321.0 %reduce-scatter.14.cloned.1.call-start = ((), (), s32[]{:S(2)}) async-start(), calls=%async_computation.16 | async-start | bytes 14155776 | tf_op jit(solution)/shard_map/reduce_scatter | solution.py:658
  849.2 63.4 %collective-permute-start.20 = (bf16[512,3072]{1,0:T(8,128)(2,1)}, bf16[512,3072]{1,0:T(8,128)(2,1)}, u32[]{:S(2)}, u32[]{:S(2)}) collective-permute-start(bf16[512,3072]{1,0:T(8,128)(2,1)} %get-tuple-element.264), channel_id=1, source_target_pairs={{0,1},{1,2},{2,3},{4,5},{5,6},{6,7},{8,9},{9,10},{10,11},{12,13},{... | collective-permute-start | bytes 9437192 | tf_op jit(solution)/shard_map/ppermute | solution.py:55
  853.8 64.6 %collective-permute-start.21 = (bf16[512,3072]{1,0:T(8,128)(2,1)}, bf16[512,3072]{1,0:T(8,128)(2,1)}, u32[]{:S(2)}, u32[]{:S(2)}) collective-permute-start(bf16[512,3072]{1,0:T(8,128)(2,1)} %get-tuple-element.264), channel_id=1, source_target_pairs={{1,0},{2,1},{3,2},{5,4},{6,5},{7,6},{9,8},{10,9},{11,10},{13,12},{... | collective-permute-start | bytes 9437192 | tf_op jit(solution)/shard_map/ppermute | solution.py:55
  918.4 314.7 %reduce-scatter.16.cloned.1.call-start = ((), (), s32[]{:S(2)}) async-start(), calls=%async_computation.17 | async-start | bytes 14155776 | tf_op jit(solution)/shard_map/reduce_scatter | solution.py:658
  918.5 63.7 %collective-permute-start.22 = (bf16[512,3072]{1,0:T(8,128)(2,1)}, bf16[512,3072]{1,0:T(8,128)(2,1)}, u32[]{:S(2)}, u32[]{:S(2)}) collective-permute-start(bf16[512,3072]{1,0:T(8,128)(2,1)} %collective-permute-done.20), channel_id=1, source_target_pairs={{1,2},{2,3},{5,6},{6,7},{9,10},{10,11},{13,14},{14,15},{17,18},{18... | collective-permute-start | bytes 9437192 | tf_op jit(solution)/shard_map/ppermute | solution.py:55
  923.5 66.6 %collective-permute-start.23 = (bf16[512,3072]{1,0:T(8,128)(2,1)}, bf16[512,3072]{1,0:T(8,128)(2,1)}, u32[]{:S(2)}, u32[]{:S(2)}) collective-permute-start(bf16[512,3072]{1,0:T(8,128)(2,1)} %collective-permute-done.21), channel_id=1, source_target_pairs={{1,0},{2,1},{5,4},{6,5},{9,8},{10,9},{13,12},{14,13},{17,16},{18,1... | collective-permute-start | bytes 9437192 | tf_op jit(solution)/shard_map/ppermute | solution.py:55
  924.8 66.5 %collective-permute-start.24 = (bf16[512,3072]{1,0:T(8,128)(2,1)}, bf16[512,3072]{1,0:T(8,128)(2,1)}, u32[]{:S(2)}, u32[]{:S(2)}) collective-permute-start(bf16[512,3072]{1,0:T(8,128)(2,1)} %shard_map.240), channel_id=1, source_target_pairs={{0,1},{3,2},{4,5},{7,6},{8,9},{11,10},{12,13},{15,14},{16,17},{19,... | collective-permute-start | bytes 9437192 | tf_op jit(solution)/shard_map/ppermute | solution.py:55
  937.2 22.4 %copy-start.12 = (bf16[1024,2048]{1,0:T(8,128)(2,1)S(1)}, bf16[1024,2048]{1,0:T(8,128)(2,1)}, u32[]{:S(2)}) copy-start(bf16[1024,2048]{1,0:T(8,128)(2,1)} %get-tuple-element.275.refs_2_) | copy-start | bytes 12582916
  991.3 280.8 %reduce-scatter.18.cloned.1.call-start = ((), (), s32[]{:S(2)}) async-start(), calls=%async_computation.18 | async-start | bytes 14155776 | tf_op jit(solution)/shard_map/reduce_scatter | solution.py:658
  991.3 43.8 %collective-permute-start.25 = (bf16[512,3072]{1,0:T(8,128)(2,1)}, bf16[512,3072]{1,0:T(8,128)(2,1)}, u32[]{:S(2)}, u32[]{:S(2)}) collective-permute-start(bf16[512,3072]{1,0:T(8,128)(2,1)} %collective-permute-done.22), channel_id=1, source_target_pairs={{2,3},{6,7},{10,11},{14,15},{18,19},{22,23},{26,27},{30,31}} | collective-permute-start | bytes 9437192 | tf_op jit(solution)/shard_map/ppermute | solution.py:55
  996.4 19.1 %copy-start.11 = (bf16[1024,2048]{1,0:T(8,128)(2,1)S(1)}, bf16[1024,2048]{1,0:T(8,128)(2,1)}, u32[]{:S(2)}) copy-start(bf16[1024,2048]{1,0:T(8,128)(2,1)} %get-tuple-element.284.refs_0_) | copy-start | bytes 12582916
  996.4 65.2 %collective-permute-start.26 = (bf16[512,3072]{1,0:T(8,128)(2,1)}, bf16[512,3072]{1,0:T(8,128)(2,1)}, u32[]{:S(2)}, u32[]{:S(2)}) collective-permute-start(bf16[512,3072]{1,0:T(8,128)(2,1)} %collective-permute-done.23), channel_id=1, source_target_pairs={{1,0},{5,4},{9,8},{13,12},{17,16},{21,20},{25,24},{29,28}} | collective-permute-start | bytes 9437192 | tf_op jit(solution)/shard_map/ppermute | solution.py:55
  997.9 69.7 %collective-permute-start.27 = (bf16[384,4096]{1,0:T(8,128)(2,1)}, bf16[384,4096]{1,0:T(8,128)(2,1)}, u32[]{:S(2)}, u32[]{:S(2)}) collective-permute-start(bf16[384,4096]{1,0:T(8,128)(2,1)} %pad_maximum_fusion.4), channel_id=1, source_target_pairs={{0,2},{3,1},{4,6},{7,5},{8,10},{11,9},{12,14},{15,13},{16,18},{19,... | collective-permute-start | bytes 9437192 | tf_op jit(solution)/shard_map/ppermute | solution.py:55
  1067.6 300.3 %reduce-scatter.20.cloned.1.call-start = ((), (), s32[]{:S(2)}) async-start(), calls=%async_computation.19 | async-start | bytes 14155776 | tf_op jit(solution)/shard_map/reduce_scatter | solution.py:658
  1078.1 75.7 %collective-permute-start.28 = (bf16[384,2048]{1,0:T(8,128)(2,1)}, bf16[384,2048]{1,0:T(8,128)(2,1)}, u32[]{:S(2)}, u32[]{:S(2)}) collective-permute-start(bf16[384,2048]{1,0:T(8,128)(2,1)} %reduce-scatter.8.cloned.1.call-done), channel_id=1, source_target_pairs={{0,2},{3,1},{1,3},{2,0},{4,6},{7,5},{5,7},{6,4},{8,10},{11,9},{9,1... | collective-permute-start | bytes 4718600 | tf_op jit(solution)/shard_map/ppermute | solution.py:55
  1164.6 59.4 %collective-permute-start.29 = (bf16[512,3072]{1,0:T(8,128)(2,1)}, bf16[512,3072]{1,0:T(8,128)(2,1)}, u32[]{:S(2)}, u32[]{:S(2)}) collective-permute-start(bf16[512,3072]{1,0:T(8,128)(2,1)} %convolution_convert_fusion.13), channel_id=1, source_target_pairs={{0,1},{4,5},{8,9},{12,13},{16,17},{20,21},{24,25},{28,29}} | collective-permute-start | bytes 9437192 | tf_op jit(solution)/shard_map/ppermute | solution.py:55
  1167.7 56.4 %collective-permute-start.30 = (bf16[512,3072]{1,0:T(8,128)(2,1)}, bf16[512,3072]{1,0:T(8,128)(2,1)}, u32[]{:S(2)}, u32[]{:S(2)}) collective-permute-start(bf16[512,3072]{1,0:T(8,128)(2,1)} %convolution_convert_fusion.13), channel_id=1, source_target_pairs={{3,2},{7,6},{11,10},{15,14},{19,18},{23,22},{27,26},{31,30}} | collective-permute-start | bytes 9437192 | tf_op jit(solution)/shard_map/ppermute | solution.py:55
  1170.0 63.1 %collective-permute-start.31 = (bf16[384,4096]{1,0:T(8,128)(2,1)}, bf16[384,4096]{1,0:T(8,128)(2,1)}, u32[]{:S(2)}, u32[]{:S(2)}) collective-permute-start(bf16[384,4096]{1,0:T(8,128)(2,1)} %pad_maximum_fusion.4), channel_id=1, source_target_pairs={{1,3},{2,0},{5,7},{6,4},{9,11},{10,8},{13,15},{14,12},{17,19},{18,... | collective-permute-start | bytes 9437192 | tf_op jit(solution)/shard_map/ppermute | solution.py:55
  1241.2 60.2 %collective-permute-start.32 = (bf16[512,3072]{1,0:T(8,128)(2,1)}, bf16[512,3072]{1,0:T(8,128)(2,1)}, u32[]{:S(2)}, u32[]{:S(2)}) collective-permute-start(bf16[512,3072]{1,0:T(8,128)(2,1)} %add_convert_fusion.2), channel_id=1, source_target_pairs={{0,1},{1,2},{4,5},{5,6},{8,9},{9,10},{12,13},{13,14},{16,17},{17,1... | collective-permute-start | bytes 9437192 | tf_op jit(solution)/shard_map/ppermute | solution.py:55
  1244.6 56.9 %collective-permute-start.33 = (bf16[512,3072]{1,0:T(8,128)(2,1)}, bf16[512,3072]{1,0:T(8,128)(2,1)}, u32[]{:S(2)}, u32[]{:S(2)}) collective-permute-start(bf16[512,3072]{1,0:T(8,128)(2,1)} %add_convert_fusion.2), channel_id=1, source_target_pairs={{3,2},{2,1},{7,6},{6,5},{11,10},{10,9},{15,14},{14,13},{19,18},{18... | collective-permute-start | bytes 9437192 | tf_op jit(solution)/shard_map/ppermute | solution.py:55
  1246.9 62.6 %collective-permute-start.34 = (bf16[512,3072]{1,0:T(8,128)(2,1)}, bf16[512,3072]{1,0:T(8,128)(2,1)}, u32[]{:S(2)}, u32[]{:S(2)}) collective-permute-start(bf16[512,3072]{1,0:T(8,128)(2,1)} %shard_map.240), channel_id=1, source_target_pairs={{1,0},{2,3},{5,4},{6,7},{9,8},{10,11},{13,12},{14,15},{17,16},{18,... | collective-permute-start | bytes 9437192 | tf_op jit(solution)/shard_map/ppermute | solution.py:55
  1317.8 60.1 %collective-permute-start.35 = (bf16[512,3072]{1,0:T(8,128)(2,1)}, bf16[512,3072]{1,0:T(8,128)(2,1)}, u32[]{:S(2)}, u32[]{:S(2)}) collective-permute-start(bf16[512,3072]{1,0:T(8,128)(2,1)} %get-tuple-element.313), channel_id=1, source_target_pairs={{0,1},{1,2},{2,3},{4,5},{5,6},{6,7},{8,9},{9,10},{10,11},{12,13},{... | collective-permute-start | bytes 9437192 | tf_op jit(solution)/shard_map/ppermute | solution.py:55
  1322.3 61.4 %collective-permute-start.36 = (bf16[512,3072]{1,0:T(8,128)(2,1)}, bf16[512,3072]{1,0:T(8,128)(2,1)}, u32[]{:S(2)}, u32[]{:S(2)}) collective-permute-start(bf16[512,3072]{1,0:T(8,128)(2,1)} %get-tuple-element.314), channel_id=1, source_target_pairs={{3,2},{2,1},{1,0},{7,6},{6,5},{5,4},{11,10},{10,9},{9,8},{15,14},{... | collective-permute-start | bytes 9437192 | tf_op jit(solution)/shard_map/ppermute | solution.py:55
  1373.6 20.2 %copy-start.47 = (bf16[1,384]{1,0:T(2,128)(2,1)S(1)}, bf16[1,384]{1,0:T(2,128)(2,1)}, u32[]{:S(2)}) copy-start(bf16[1,384]{1,0:T(2,128)(2,1)} %copy-done.46) | copy-start | bytes 2308
  1373.6 20.2 %copy-start.49 = (bf16[1,384]{1,0:T(2,128)(2,1)S(1)}, bf16[1,384]{1,0:T(2,128)(2,1)}, u32[]{:S(2)}) copy-start(bf16[1,384]{1,0:T(2,128)(2,1)} %copy-done.48) | copy-start | bytes 2308
  1373.6 20.8 %copy-start.8 = (f32[1,3072]{1,0:T(1,128)S(1)}, f32[1,3072]{1,0:T(1,128)}, u32[]{:S(2)}) copy-start(f32[1,3072]{1,0:T(1,128)} %copy-done.7) | copy-start | bytes 36868
  (43 other events, 262.4 us)
Sparse Core Ops, SparseCore 0:
  30.2 52.4 all-gather.6
  118.2 37.3 all-gather.8
  157.5 72.1 all-gather.10
  231.4 125.3 all-gather.12
  358.5 72.1 all-gather.14
  432.4 125.3 all-gather.16
  702.3 90.2 reduce-scatter.9
  796.1 92.3 reduce-scatter.11
  892.1 92.4 reduce-scatter.7
  987.9 92.3 reduce-scatter.13
  1083.8 92.4 reduce-scatter.15
  1179.6 92.3 reduce-scatter.17
  1275.5 92.3 reduce-scatter.19

commit v6 on v5

--- a/solution.py
+++ b/solution.py
@@ -93,6 +93,44 @@
     return slots, used
 
 
+def choose_kernel(count, which_ref, *refs):
+    value = refs[0][...]
+    for c in range(1, count):
+        value = jnp.where(which_ref[0] == c, refs[c][...], value)
+    total = value.astype(F32)
+    for ref in refs[count:-1]:
+        total = total + ref[...].astype(F32)
+    refs[-1][...] = total.astype(BF16)
+
+
+def chosen_sum(place, choices, sums):
+    distinct = []
+    for value in choices:
+        if not any(value is other for other in distinct):
+            distinct.append(value)
+    table = [next(d for d, other in enumerate(distinct) if value is other) for value in choices]
+    which = jnp.asarray(table, jnp.int32)[place][None]
+    rows, width = choices[0].shape
+    tile = 64 if rows % 64 == 0 else rows
+
+    def candidate(c):
+        return pl.BlockSpec((tile, width), lambda i, which: (jnp.where(which[0] == c, i, 0), 0))
+
+    plain = pl.BlockSpec((tile, width), lambda i, which: (i, 0))
+    return pl.pallas_call(
+        functools.partial(choose_kernel, len(distinct)),
+        grid_spec=pltpu.PrefetchScalarGridSpec(
+            num_scalar_prefetch=1,
+            grid=(rows // tile,),
+            in_specs=[candidate(c) for c in range(len(distinct))] + [plain] * len(sums),
+            out_specs=plain,
+        ),
+        out_shape=jax.ShapeDtypeStruct((rows, width), BF16),
+        compiler_params=pltpu.CompilerParams(vmem_limit_bytes=30 << 20),
+        cost_estimate=HIDES,
+    )(which, *distinct, *sums)
+
+
 def line_reduce(part, n, fill=lambda step, gate: (), along=lambda step: (), took=lambda step, arrived, filled: None):
     place = lax.axis_index("tensor")
     parts = [None] * n
@@ -114,7 +152,7 @@
         leftward = [parts[order[i].index(i - n + k)] if i >= n - k else parts[n - k] for i in range(n)]
         if 2 * k <= n:
             choice = [r if i < k else l for i, (r, l) in enumerate(zip(rightward, leftward))]
-            to_right = to_left = add(pick(place, choice), right, left)
+            to_right = to_left = pick(place, choice) if right is None else chosen_sum(place, choice, (right, left))
         else:
             to_right, to_left = add(pick(place, rightward), right), add(pick(place, leftward), left)
 
@@ -373,8 +411,8 @@
     refs[-1][...] = total.astype(refs[-1].dtype)
 
 
-def spread(acts, weights, part, out, cost=HIDES, piece=0, pieces=1):
-    rows, hidden = acts[0].shape[0] // 2, acts[0].shape[1]
+def spread(acts, weights, part, out, cost=HIDES, piece=0, pieces=1, parts=2):
+    rows, hidden = acts[0].shape[0] // parts, acts[0].shape[1]
     width = weights[0][0].shape[0] // pieces
     tile = 256 if width % 256 == 0 else width
     tiles = width // tile
@@ -641,15 +679,12 @@
             *(dot(two, after(g, gate), TN, BF16) for g in grad_up[1:]),
         )
 
-    def gate_weights(gate):
-        return (
-            spread([after(grads[0], gate)] + grads[1:], weights, 0, F32, HIDES, 1, 2),
-            *(dot(two, after(g, gate), TN, BF16) for g in grad_gate[1:]),
-        )
+    def own_half(gate):
+        return (spread([after(grads[0], gate)] + grads[1:], weights, 0, F32, HIDES, 1, 2),)
 
     theirs = spread(grads, weights, 1, BF16, HIDES, 0, 2)
     (from_first,), (theirs, *d_up[1:]) = travel([(theirs, swap)], second_half)
-    (from_second,), (ours_second, *d_gate[1:]) = travel([(theirs, swap)], gate_weights)
+    (from_second,), (ours_second,) = travel([(theirs, swap)], own_half)
     grad_hidden, grad_hidden_low = norm_back(
         [(ours_first, 0, 1), (ours_second, 1, 1), (from_first, 0, 1), (from_second, 1, 1)], hidden, gain_two, cotangent, live, True
     )
@@ -669,24 +704,24 @@
         if step == 1:
             flops = 2 * rows * width * slices * gate_weight.shape[1]
             cost = pl.CostEstimate(flops=flops, transcendentals=0, bytes_accessed=flops // rows)
-            return (result_rows(1, BF16, gate, cost), d_of(grad_two, mixed[0], gate))
+            return (result_rows(1, BF16, gate, cost), *(d_of(two, g, gate) for g in grad_gate[1:]))
         if step == 2:
             return (result_rows(0, F32, gate), d_of(two, grad_up[0], gate), *joined_sums())
         if step == n - 1:
-            return (d_of(two, grad_gate[0], gate),)
+            return (d_of(grad_two, mixed[0], gate), d_of(two, grad_gate[0], gate))
         return ()
 
     def took_gather(step, arrived, filled):
         early.extend(arrived)
         if step == 1:
             results.append(filled[0])
-            d_down[0] = filled[1]
+            d_gate[1:] = filled[1:]
         elif step == 2:
             results.append(filled[0])
             d_up[0] = filled[1]
             sums.extend(filled[2:])
         elif step == n - 1:
-            d_gate[0] = filled[0]
+            d_down[0], d_gate[0] = filled
 
     sums = []
 
@@ -710,7 +745,7 @@
         return (
             attend_back(after(slot_table, gate), *grad_attended, rotated, attended, lse, *tables),
             d_of(jnp.concatenate(slots_back, axis=0), attended, gate),
-            sum_down,
+            sum_up,
         )
 
     sums_gate = [owner_sum(d) for d in d_gate[1:]]
@@ -731,7 +766,7 @@
     def while_reduce(step, gate):
         if step == 1:
             d_qkv = d_of(jnp.concatenate(slots_one, axis=0), grad_qkv, gate)
-            return (jnp.concatenate([d_qkv, d_out], axis=1), sum_up)
+            return (jnp.concatenate([d_qkv, d_out], axis=1), sum_down)
         if step == 2:
             return (sum_gate,)
         if step == n - 1:
@@ -765,8 +800,13 @@
         elif step == n - 1:
             outputs.extend(filled)
 
+    def rows_part(s):
+        if s == n - 1:
+            return spread([grad_qkv], [(w_qkv, 0)], s, BF16, parts=n)
+        return dot(grad_qkv[s * rows : (s + 1) * rows], w_qkv, NT, BF16)
+
     grad_normed_one = line_reduce(
-        lambda s: dot(grad_qkv[s * rows : (s + 1) * rows], w_qkv, NT, BF16),
+        rows_part,
         n,
         while_reduce,
         along_reduce,

time: 1420 us -> 1430 us (level)
  Pallas kernels: 342 us -> 364 us
  matrix products: 311 us -> 295 us
    reduce_scatter x7, waiting for transfers between devices: 20.8 us -> 62.9 us  [owner_sum(): return lax.psum_scatter(partial, 'dp', scatter_dimension=0, tiled=True)]
    ppermute x37, waiting for transfers between devices: 410 us -> 371 us  [travel(): lax.ppermute(array, 'tensor', pairs)]
    dot_general x26 -> x25, matrix products: 311 us -> 295 us  [dot(): return lax.dot_general(a, b, dims, preferred_element_type=F32).astype(out)]
    pallas_call x6 -> x7, Pallas kernels: 127 us -> 139 us  [spread(): pl.pallas_call(functools.partial(spread_kernel, count), grid=(tiles,), in...]
    unnamed x120 -> x140, local copies, waits for them, and re-layouts: 25.9 us -> 37 us
  transfers between devices with their start and end apart: 50 -> 50, of which waited for: 28 -> 28; matrix products, arithmetic and copies ran while one was open for 30% -> 28% of each run, Pallas kernels for 22% -> 23%
where the time goes in v6:
time: 1430 us; the launch traced here: 1420 us
  waiting for transfers between devices  447 us (31%)
  Pallas kernels  364 us (25%)
  matrix products  295 us (21%)
  other arithmetic  113 us (8%)
  starting transfers between devices  103 us (7%)
  local copies, waits for them, and re-layouts  48.6 us (3%)
  blocking collectives  35.4 us (2%)
  between operations  15.6 us (1%)
    ppermute x37, waiting for transfers between devices, travel(): lax.ppermute(array, 'tensor', pairs)  371 us
    dot_general x25, matrix products, dot(): return lax.dot_general(a, b, dims, preferred_element_type=F32).astype(out)  295 us
    pallas_call x7, Pallas kernels, spread(): pl.pallas_call(functools.partial(spread_kernel, count), grid=(tiles,), in...  139 us
    ppermute x37, starting transfers between devices, travel(): lax.ppermute(array, 'tensor', pairs)  103 us
    pallas_call x4, Pallas kernels, gated(): pl.pallas_call(gated_kernel, grid=(tiles,), in_specs=[pl.BlockSpec((rows,...  87.9 us
    reduce_scatter x7, waiting for transfers between devices, owner_sum(): return lax.psum_scatter(partial, 'dp', scatter_dimension=0, tiled=True)  62.9 us
    pallas_call x1, Pallas kernels, attention_back(): attend_back(after(slot_table, gate), *grad_attended, rotated, attended, l...  56.1 us
    pallas_call x1, Pallas kernels, attention(): return attend(slot_table, *projected, *tables)  43.1 us
  transfers between devices with their start and end apart: 50, of which 28 were waited for; matrix products, arithmetic and copies ran while one was open for 28% of the time, Pallas kernels for 23%

profile of v6, /device:TPU:0, one launch (start us, length us, event | category | flops | bytes accessed | tf_op | source)
XLA Modules:
  0.0 1422.2 jit_solution(12553190780807361482)
XLA Ops:
  9.4 10.4 all_gather.24
  30.3 13.4 all_gather.25
  71.5 11.4 all-gather.7.cloned.1.call-done.refs_1_
  82.8 9.9 fusion.43.refs_0_
  92.7 19.6 %collective-permute-done = bf16[512,3072]{1,0:T(8,128)(2,1)} collective-permute-done((bf16[512,3072]{1,0:T(8,128)(2,1)}, bf16[512,3072]{1,0:T(8,128)(2,1)}, u32[]{:S(2)}, u32[]{:S(2)}) %collective-permute-start) | collective-permute-done | bytes 3145760 | tf_op jit(solution)/shard_map/ppermute | solution.py:55
  123.1 7.1 collective-permute-start.4
  132.6 9.2 fusion.44.refs_1_
  141.8 48.9 %collective-permute-done.3 = bf16[512,3072]{1,0:T(8,128)(2,1)} collective-permute-done((bf16[512,3072]{1,0:T(8,128)(2,1)}, bf16[512,3072]{1,0:T(8,128)(2,1)}, u32[]{:S(2)}, u32[]{:S(2)}) %collective-permute-start.3) | collective-permute-done | bytes 3145760 | tf_op jit(solution)/shard_map/ppermute | solution.py:55
  194.1 9.2 collective-permute-start.7
  211.4 48.6 %collective-permute-done.6 = bf16[512,3072]{1,0:T(8,128)(2,1)S(1)} collective-permute-done((bf16[512,3072]{1,0:T(8,128)(2,1)}, bf16[512,3072]{1,0:T(8,128)(2,1)S(1)}, u32[]{:S(2)}, u32[]{:S(2)}) %collective-permute-start.6) | collective-permute-done | bytes 3145760 | tf_op jit(solution)/shard_map/ppermute | solution.py:55
  279.7 43.1 %shard_map.248 = (bf16[2048,768]{1,0:T(8,128)(2,1)}, bf16[2048,1280]{1,0:T(8,128)(2,1)}, f32[2,8,2048]{2,1,0:T(8,128)}) custom-call(s32[8]{0:T(128)} %dynamic-slice_bitcast_fusion.place_ref, f32[512,1280]{1,0:T(8,128)} %fusion.43.refs_0_, f32[512,1280]{1,0:T(8,128)} %fusion.44.refs_1_, f32[512,1280]{1,0:T(8,128)} %fusion.45.refs_2_, ...), custom_call_target="tpu_custom_call" | custom-call | flops 1 | bytes 1 | tf_op jit(solution)/shard_map/pallas_call | solution.py:618
  322.8 16.8 %collective-permute-done.8 = bf16[384,2048]{1,0:T(8,128)(2,1)} collective-permute-done((bf16[384,2048]{1,0:T(8,128)(2,1)}, bf16[384,2048]{1,0:T(8,128)(2,1)}, u32[]{:S(2)}, u32[]{:S(2)}) %collective-permute-start.8) | collective-permute-done | bytes 1572896 | tf_op jit(solution)/shard_map/ppermute | solution.py:55
  348.8 6.9 convolution_convert_fusion.8.refs_0_
  355.7 58.5 %collective-permute-done.9.refs_2_ = bf16[512,3072]{1,0:T(8,128)(2,1)S(1)} collective-permute-done((bf16[512,3072]{1,0:T(8,128)(2,1)S(1)}, bf16[512,3072]{1,0:T(8,128)(2,1)S(1)}, u32[]{:S(2)}, u32[]{:S(2)}) %collective-permute-start.9) | collective-permute-done | bytes 3145760 | tf_op jit(solution)/shard_map/ppermute | solution.py:55
  420.5 6.0 add.127
  441.2 6.0 convolution_convert_fusion.7
  447.2 7.0 convolution_convert_fusion.6
  454.2 51.7 %collective-permute-done.12 = bf16[512,3072]{1,0:T(8,128)(2,1)S(1)} collective-permute-done((bf16[512,3072]{1,0:T(8,128)(2,1)S(1)}, bf16[512,3072]{1,0:T(8,128)(2,1)S(1)}, u32[]{:S(2)}, u32[]{:S(2)}) %collective-permute-start.12) | collective-permute-done | bytes 3145760 | tf_op jit(solution)/shard_map/ppermute | solution.py:55
  525.5 16.8 %fusion.39.gm_ref = f32[1024,2048]{1,0:T(8,128)} fusion(bf16[3072,2048]{1,0:T(8,128)(2,1)S(1)} %bitcast.53, bf16[512,3072]{1,0:T(8,128)(2,1)S(1)} %add.122, bf16[512,3072]{1,0:T(8,128)(2,1)S(1)} %copy-done.34), kind=kOutput, calls=%fused_computation.108 | convolution fusion | flops 12897484800 | bytes 27262976 | tf_op jit(solution)/shard_map/dot_general | solution.py:25
  542.3 19.0 %fusion.38.gm_ref = f32[1024,2048]{1,0:T(8,128)} fusion(bf16[3072,2048]{1,0:T(8,128)(2,1)} %all-gather.15.cloned.1.call-done.refs_3_, bf16[512,3072]{1,0:T(8,128)(2,1)} %copy-done.40, bf16[512,3072]{1,0:T(8,128)(2,1)} %multiply_convert_fusion.2), kind=kOutput, calls=%fused_computation.107 | convolution fusion | flops 12897484800 | bytes 27262976 | tf_op jit(solution)/shard_map/dot_general | solution.py:25
  561.3 22.3 %collective-permute-done.15 = bf16[512,3072]{1,0:T(8,128)(2,1)} collective-permute-done((bf16[512,3072]{1,0:T(8,128)(2,1)}, bf16[512,3072]{1,0:T(8,128)(2,1)}, u32[]{:S(2)}, u32[]{:S(2)}) %collective-permute-start.15) | collective-permute-done | bytes 3145760 | tf_op jit(solution)/shard_map/ppermute | solution.py:55
  598.0 21.2 %shard_map.250 = (bf16[1024,2048]{1,0:T(8,128)(2,1)}, bf16[1024,2048]{1,0:T(8,128)(2,1)}, bf16[1024,2048]{1,0:T(8,128)(2,1)}) custom-call(bf16[512,3072]{1,0:T(8,128)(2,1)} %multiply_convert_fusion.1.x_ref, bf16[3072,4096]{1,0:T(8,128)(2,1)} %all-gather.13.cloned.1.call-done.gate_ref.up_ref.refs_4_.refs_6_, ...), custom_call_target="tpu_custom_call" | custom-call | flops 1 | bytes 1 | tf_op jit(solution)/shard_map/pallas_call | solution.py:393
  619.1 21.1 %shard_map.251 = (bf16[1024,2048]{1,0:T(8,128)(2,1)}, bf16[1024,2048]{1,0:T(8,128)(2,1)}, bf16[1024,2048]{1,0:T(8,128)(2,1)}) custom-call(bf16[512,3072]{1,0:T(8,128)(2,1)} %multiply_convert_fusion.1.x_ref, bf16[3072,4096]{1,0:T(8,128)(2,1)} %all-gather.17.cloned.1.call-done.gate_ref.up_ref.refs_5_.refs_7_, ...), custom_call_target="tpu_custom_call" | custom-call | flops 1 | bytes 1 | tf_op jit(solution)/shard_map/pallas_call | solution.py:393
  640.2 19.5 %shard_map.252.refs_0_ = f32[512,1536]{1,0:T(8,128)S(1)} custom-call(bf16[1024,2048]{1,0:T(8,128)(2,1)} %get-tuple-element.248.refs_0_.refs_1_, bf16[1024,2048]{1,0:T(8,128)(2,1)} %get-tuple-element.243.refs_1_, bf16[1024,2048]{1,0:T(8,128)(2,1)} %get-tuple-element.249.refs_2_, bf16[1024,2048]{1,0:T(8,128)(2,1)} %get-tuple-element.244.refs_3_.refs_2_, ...), custom_call_target="tpu_custom_call" | custom-call | flops 1 | bytes 1 | tf_op jit(solution)/shard_map/pallas_call | solution.py:424
  665.6 21.1 %shard_map.253 = (bf16[1024,2048]{1,0:T(8,128)(2,1)}, bf16[1024,2048]{1,0:T(8,128)(2,1)}, bf16[1024,2048]{1,0:T(8,128)(2,1)}) custom-call(bf16[512,3072]{1,0:T(8,128)(2,1)} %collective-permute-done.17.x_ref, ...), custom_call_target="tpu_custom_call", output_to_operand_aliasing={{0}: (4, {}), {1}: (5, {}), {2}: (6, {})} | custom-call | flops 1 | bytes 1 | tf_op jit(solution)/shard_map/pallas_call | solution.py:393
  686.7 17.9 %convolution_convert_fusion.5 = bf16[3072,2048]{1,0:T(8,128)(2,1)} fusion(bf16[1024,2048]{1,0:T(8,128)(2,1)} %get-tuple-element.245.refs_1_, bf16[512,3072]{1,0:T(8,128)(2,1)S(1)} %copy-done.41, bf16[512,3072]{1,0:T(8,128)(2,1)S(1)} %copy-done.35), kind=kOutput, calls=%fused_computation.23 | convolution fusion | flops 12903776256 | bytes 23068672 | tf_op jit(solution)/shard_map/dot_general | solution.py:25
  704.7 24.5 %shard_map.254 = (bf16[1024,2048]{1,0:T(8,128)(2,1)}, bf16[1024,2048]{1,0:T(8,128)(2,1)}, bf16[1024,2048]{1,0:T(8,128)(2,1)}) custom-call(bf16[512,3072]{1,0:T(8,128)(2,1)} %collective-permute-done.17.x_ref, ...), custom_call_target="tpu_custom_call", output_to_operand_aliasing={{0}: (4, {}), {1}: (5, {}), {2}: (6, {})} | custom-call | flops 1 | bytes 1 | tf_op jit(solution)/shard_map/pallas_call | solution.py:393
  729.3 21.4 %shard_map.255 = bf16[512,1536]{1,0:T(8,128)(2,1)} custom-call(bf16[1024,2048]{1,0:T(8,128)(2,1)} %get-tuple-element.286.refs_0_, bf16[1024,2048]{1,0:T(8,128)(2,1)} %get-tuple-element.266.refs_1_, bf16[1024,2048]{1,0:T(8,128)(2,1)} %get-tuple-element.276.refs_2_, bf16[1024,2048]{1,0:T(8,128)(2,1)} %get-tuple-element.255.refs_3_, ...), custom_call_target="tpu_custom_call" | custom-call | flops 1 | bytes 1 | tf_op jit(solution)/shard_map/pallas_call | solution.py:424
  750.7 19.9 %shard_map.256 = bf16[512,1536]{1,0:T(8,128)(2,1)S(1)} custom-call(bf16[1024,2048]{1,0:T(8,128)(2,1)} %get-tuple-element.286.refs_0_, bf16[1024,2048]{1,0:T(8,128)(2,1)} %get-tuple-element.266.refs_1_, bf16[1024,2048]{1,0:T(8,128)(2,1)} %get-tuple-element.276.refs_2_, bf16[1024,2048]{1,0:T(8,128)(2,1)} %get-tuple-element.255.refs_3_, ...), custom_call_target="tpu_custom_call" | custom-call | flops 1 | bytes 1 | tf_op jit(solution)/shard_map/pallas_call | solution.py:424
  771.8 18.9 %convolution_convert_fusion.4 = bf16[3072,2048]{1,0:T(8,128)(2,1)} fusion(bf16[1024,2048]{1,0:T(8,128)(2,1)S(1)} %copy-done.23, bf16[512,3072]{1,0:T(8,128)(2,1)} %collective-permute-done.17.x_ref, bf16[512,3072]{1,0:T(8,128)(2,1)} %multiply_convert_fusion.1.x_ref), kind=kOutput, calls=%fused_computation.22 | convolution fusion | flops 12903776256 | bytes 23068672 | tf_op jit(solution)/shard_map/dot_general | solution.py:25
  792.9 21.6 %shard_map.257.refs_1_ = f32[512,1536]{1,0:T(8,128)S(1)} custom-call(bf16[1024,2048]{1,0:T(8,128)(2,1)} %get-tuple-element.286.refs_0_, bf16[1024,2048]{1,0:T(8,128)(2,1)} %get-tuple-element.266.refs_1_, bf16[1024,2048]{1,0:T(8,128)(2,1)} %get-tuple-element.276.refs_2_, bf16[1024,2048]{1,0:T(8,128)(2,1)} %get-tuple-element.255.refs_3_, ...), custom_call_target="tpu_custom_call" | custom-call | flops 1 | bytes 1 | tf_op jit(solution)/shard_map/pallas_call | solution.py:424
  816.4 6.1 collective-permute-done.19.refs_3_
  822.5 11.8 shard_map.258
  840.0 21.6 %shard_map.259 = bf16[512,3072]{1,0:T(8,128)(2,1)} custom-call(bf16[1024,2048]{1,0:T(8,128)(2,1)} %get-tuple-element.285.refs_0_, bf16[1024,2048]{1,0:T(8,128)(2,1)} %get-tuple-element.245.refs_1_, bf16[3072,2048]{1,0:T(8,128)(2,1)} %all-gather.11.cloned.1.call-done.refs_2_, bf16[3072,2048]{1,0:T(8,128)(2,1)} %all-gather.15.cloned.1.call-done.refs_3_), custom_call_target="tpu_custom_call" | custom-call | flops 12884901888 | bytes 25165824 | tf_op jit(solution)/shard_map/pallas_call | solution.py:424
  867.2 18.5 %convolution_convert_fusion.3 = bf16[3072,2048]{1,0:T(8,128)(2,1)} fusion(bf16[1024,2048]{1,0:T(8,128)(2,1)S(1)} %copy-done.22, bf16[512,3072]{1,0:T(8,128)(2,1)} %collective-permute-done.17.x_ref, bf16[512,3072]{1,0:T(8,128)(2,1)} %multiply_convert_fusion.1.x_ref), kind=kOutput, calls=%fused_computation.21 | convolution fusion | flops 12903776256 | bytes 23068672 | tf_op jit(solution)/shard_map/dot_general | solution.py:25
  885.7 12.4 collective-permute-done.20
  907.7 6.5 collective-permute-start.24
  919.1 6.9 convolution_convert_fusion.15.refs_1_
  926.0 22.7 %shard_map.260 = f32[512,3072]{1,0:T(8,128)} custom-call(bf16[1024,2048]{1,0:T(8,128)(2,1)} %get-tuple-element.285.refs_0_, bf16[1024,2048]{1,0:T(8,128)(2,1)} %get-tuple-element.245.refs_1_, bf16[3072,2048]{1,0:T(8,128)(2,1)} %all-gather.11.cloned.1.call-done.refs_2_, bf16[3072,2048]{1,0:T(8,128)(2,1)} %all-gather.15.cloned.1.call-done.refs_3_), custom_call_target="tpu_custom_call" | custom-call | flops 1 | bytes 1 | tf_op jit(solution)/shard_map/pallas_call | solution.py:424
  948.6 18.7 %convolution_convert_fusion.2 = bf16[3072,2048]{1,0:T(8,128)(2,1)} fusion(bf16[1024,2048]{1,0:T(8,128)(2,1)S(1)} %copy-done.21, bf16[512,3072]{1,0:T(8,128)(2,1)} %collective-permute-done.17.x_ref, bf16[512,3072]{1,0:T(8,128)(2,1)} %multiply_convert_fusion.1.x_ref), kind=kOutput, calls=%fused_computation.20 | convolution fusion | flops 12903776256 | bytes 23068672 | tf_op jit(solution)/shard_map/dot_general | solution.py:25
  978.0 10.7 collective-permute-start.27
  992.6 17.9 %convolution_convert_fusion.1 = bf16[3072,2048]{1,0:T(8,128)(2,1)} fusion(bf16[1024,2048]{1,0:T(8,128)(2,1)S(1)} %copy-done.25, bf16[512,3072]{1,0:T(8,128)(2,1)} %copy-done.40, bf16[512,3072]{1,0:T(8,128)(2,1)S(1)} %copy-done.36), kind=kOutput, calls=%fused_computation.19 | convolution fusion | flops 12903776256 | bytes 23068672 | tf_op jit(solution)/shard_map/dot_general | solution.py:25
  1010.5 8.8 convolution_convert_fusion.14.refs_2_
  1019.3 18.7 %convolution_convert_fusion = bf16[3072,2048]{1,0:T(8,128)(2,1)} fusion(bf16[1024,2048]{1,0:T(8,128)(2,1)S(1)} %copy-done.20, bf16[512,3072]{1,0:T(8,128)(2,1)} %collective-permute-done.17.x_ref, bf16[512,3072]{1,0:T(8,128)(2,1)} %multiply_convert_fusion.1.x_ref), kind=kOutput, calls=%fused_computation.18 | convolution fusion | flops 12903776256 | bytes 23068672 | tf_op jit(solution)/shard_map/dot_general | solution.py:25
  1052.5 6.0 convolution_convert_fusion.13.refs_3_
  1062.4 56.1 %shard_map.261.refs_0_ = bf16[2048,1280]{1,0:T(8,128)(2,1)} custom-call(s32[8]{0:T(128)} %dynamic-slice_bitcast_fusion.place_ref, bf16[512,768]{1,0:T(8,128)(2,1)} %convolution_convert_fusion.16.refs_0_, bf16[512,768]{1,0:T(8,128)(2,1)} %convolution_convert_fusion.15.refs_1_, bf16[512,768]{1,0:T(8,128)(2,1)} %convolution_convert_fusion.14.refs_2_, ...), custom_call_target="tpu_custom_call" | custom-call | flops 32212254720 | bytes 26214400 | tf_op jit(solution)/shard_map/pallas_call | solution.py:746
  1118.5 15.7 %fusion.22 = bf16[3072,768]{1,0:T(8,128)(2,1)} fusion(bf16[2048,768]{1,0:T(8,128)(2,1)} %get-tuple-element.296.refs_5_, bf16[512,3072]{1,0:T(8,128)(2,1)} %copy-done.43, bf16[512,3072]{1,0:T(8,128)(2,1)} %select_select_fusion.1, bf16[512,3072]{1,0:T(8,128)(2,1)} %copy-done.42, bf16[512,3072]{1,0:T(8,128)(2,1)} %get-tuple-element.263), kind=kOutput, calls=%fused_computation.40 | convolution fusion | flops 9716367360 | bytes 20447232 | tf_op jit(solution)/shard_map/dot_general | solution.py:25
  1134.2 12.6 shard_map.262.refs_1_
  1153.5 20.9 %fusion.16 = bf16[3072,1280]{1,0:T(8,128)(2,1)S(1)} fusion(bf16[2048,1280]{1,0:T(8,128)(2,1)} %shard_map.261.refs_0_, bf16[512,3072]{1,0:T(8,128)(2,1)} %copy-done.39, bf16[512,3072]{1,0:T(8,128)(2,1)} %copy-done.38, bf16[512,3072]{1,0:T(8,128)(2,1)} %copy-done.37, bf16[512,3072]{1,0:T(8,128)(2,1)S(1)} %copy-done.33), kind=kOutput, calls=%fused_computation.17 | convolution fusion | flops 16160391168 | bytes 25690112 | tf_op jit(solution)/shard_map/dot_general | solution.py:25
  1174.4 8.3 pad_maximum_fusion
  1182.7 9.7 convolution_convert_fusion.12.refs_0_
  1192.4 16.7 %collective-permute-done.29.refs_2_ = bf16[512,3072]{1,0:T(8,128)(2,1)} collective-permute-done((bf16[512,3072]{1,0:T(8,128)(2,1)}, bf16[512,3072]{1,0:T(8,128)(2,1)}, u32[]{:S(2)}, u32[]{:S(2)}) %collective-permute-start.29) | collective-permute-done | bytes 3145760 | tf_op jit(solution)/shard_map/ppermute | solution.py:55
  1209.1 9.1 collective-permute-done.31
  1220.5 7.9 shard_map.263
  1235.9 9.8 convolution_convert_fusion.11
  1245.7 37.8 %reduce-scatter.18.cloned.1.call-done = bf16[384,2048]{1,0:T(8,128)(2,1)} async-done(((bf16[3072,2048]{1,0:T(8,128)(2,1)}), bf16[384,2048]{1,0:T(8,128)(2,1)}) %reduce-scatter.18.cloned.1.call-update) | async-done | bytes 1572880 | tf_op jit(solution)/shard_map/reduce_scatter | solution.py:693
  1283.5 7.3 collective-permute-done.32
  1290.8 8.2 collective-permute-done.34
  1299.0 11.3 add_convert_fusion
  1316.7 9.7 convolution_convert_fusion.10.refs_0_
  1346.0 8.3 multiply_convert_fusion
  1354.3 25.1 %reduce-scatter.20.cloned.1.call-done.x_ref = bf16[384,2048]{1,0:T(8,128)(2,1)} async-done(((bf16[3072,2048]{1,0:T(8,128)(2,1)}), bf16[384,2048]{1,0:T(8,128)(2,1)}) %reduce-scatter.20.cloned.1.call-update) | async-done | bytes 1572880 | tf_op jit(solution)/shard_map/reduce_scatter | solution.py:693
  1390.4 11.7 psum.7
  1404.6 10.8 shard_map.265
  (292 shorter events, 273.3 us)
Async XLA Ops:
  7.2 75.7 %all-gather.7.cloned.1.call-start = ((), (), s32[]{:S(2)}) async-start(), calls=%async_computation.7 | async-start | bytes 8847360 | tf_op jit(solution)/shard_map/all_gather | solution.py:531
  30.2 243.8 %all-gather.9.cloned.1.call-start = ((), (), s32[]{:S(2)}) async-start(), calls=%async_computation.8 | async-start | bytes 5308416 | tf_op jit(solution)/shard_map/all_gather | solution.py:531
  43.6 68.7 %collective-permute-start = (bf16[512,3072]{1,0:T(8,128)(2,1)}, bf16[512,3072]{1,0:T(8,128)(2,1)}, u32[]{:S(2)}, u32[]{:S(2)}) collective-permute-start(bf16[512,3072]{1,0:T(8,128)(2,1)} %fusion.21), channel_id=1, source_target_pairs={{0,1},{1,2},{2,3},{4,5},{5,6},{6,7},{8,9},{9,10},{10,11},{12,13},{... | collective-permute-start | bytes 9437192 | tf_op jit(solution)/shard_map/ppermute | solution.py:55
  48.7 69.4 %collective-permute-start.1 = (bf16[512,3072]{1,0:T(8,128)(2,1)}, bf16[512,3072]{1,0:T(8,128)(2,1)}, u32[]{:S(2)}, u32[]{:S(2)}) collective-permute-start(bf16[512,3072]{1,0:T(8,128)(2,1)} %fusion.21), channel_id=1, source_target_pairs={{1,0},{2,1},{3,2},{5,4},{6,5},{7,6},{9,8},{10,9},{11,10},{13,12},{... | collective-permute-start | bytes 9437192 | tf_op jit(solution)/shard_map/ppermute | solution.py:55
  118.1 155.9 %all-gather.11.cloned.1.call-start = ((), (), s32[]{:S(2)}) async-start(), calls=%async_computation.9 | async-start | bytes 14155776 | tf_op jit(solution)/shard_map/all_gather | solution.py:531
  118.8 301.6 %all-gather.13.cloned.1.call-start = ((), (), s32[]{:S(2)}) async-start(), calls=%async_computation.10 | async-start | bytes 28311552 | tf_op jit(solution)/shard_map/all_gather | solution.py:531
  119.4 422.9 %all-gather.15.cloned.1.call-start = ((), (), s32[]{:S(2)}) async-start(), calls=%async_computation.11 | async-start | bytes 14155776 | tf_op jit(solution)/shard_map/all_gather | solution.py:531
  119.5 22.4 %collective-permute-start.2 = (bf16[512,3072]{1,0:T(8,128)(2,1)}, bf16[512,3072]{1,0:T(8,128)(2,1)}, u32[]{:S(2)}, u32[]{:S(2)}) collective-permute-start(bf16[512,3072]{1,0:T(8,128)(2,1)} %collective-permute-done), channel_id=1, source_target_pairs={{1,2},{2,3},{5,6},{6,7},{9,10},{10,11},{13,14},{14,15},{17,18},{18... | collective-permute-start | bytes 9437192 | tf_op jit(solution)/shard_map/ppermute | solution.py:55
  121.8 69.0 %collective-permute-start.3 = (bf16[512,3072]{1,0:T(8,128)(2,1)}, bf16[512,3072]{1,0:T(8,128)(2,1)}, u32[]{:S(2)}, u32[]{:S(2)}) collective-permute-start(bf16[512,3072]{1,0:T(8,128)(2,1)} %collective-permute-done.1), channel_id=1, source_target_pairs={{1,0},{2,1},{5,4},{6,5},{9,8},{10,9},{13,12},{14,13},{17,16},{18,1... | collective-permute-start | bytes 9437192 | tf_op jit(solution)/shard_map/ppermute | solution.py:55
  123.1 68.9 %collective-permute-start.4 = (bf16[512,3072]{1,0:T(8,128)(2,1)}, bf16[512,3072]{1,0:T(8,128)(2,1)}, u32[]{:S(2)}, u32[]{:S(2)}) collective-permute-start(bf16[512,3072]{1,0:T(8,128)(2,1)} %multiply_convert_fusion.2), channel_id=1, source_target_pairs={{0,1},{3,2},{4,5},{7,6},{8,9},{11,10},{12,13},{15,14},{16,17},{19,... | collective-permute-start | bytes 9437192 | tf_op jit(solution)/shard_map/ppermute | solution.py:55
  130.2 75.4 %slice-start.3 = ((s8[7864320]{0:T(1024)(128)(4,1)}), s8[4194304]{0:T(1024)(128)(4,1)S(1)}, s32[]{:S(2)}) async-start(s8[7864320]{0:T(1024)(128)(4,1)} %bitcast.54), calls=%async_computation.23 | async-start | bytes 8388608
  132.6 61.5 %copy-start.26 = (bf16[384,4096]{1,0:T(8,128)(2,1)S(1)}, bf16[384,4096]{1,0:T(8,128)(2,1)}, u32[]{:S(2)}) copy-start(bf16[384,4096]{1,0:T(8,128)(2,1)} %pad_maximum_fusion.3) | copy-start | bytes 9437188
  132.6 73.0 %slice-start.4 = ((s8[7864320]{0:T(1024)(128)(4,1)}), s8[3670016]{0:T(1024)(128)(4,1)S(1)}, s32[]{:S(2)}) async-start(s8[7864320]{0:T(1024)(128)(4,1)} %bitcast.54), calls=%async_computation.24 | async-start | bytes 7340032
  191.9 19.5 %collective-permute-start.5 = (bf16[512,3072]{1,0:T(8,128)(2,1)}, bf16[512,3072]{1,0:T(8,128)(2,1)S(1)}, u32[]{:S(2)}, u32[]{:S(2)}) collective-permute-start(bf16[512,3072]{1,0:T(8,128)(2,1)} %collective-permute-done.2), channel_id=1, source_target_pairs={{2,3},{6,7},{10,11},{14,15},{18,19},{22,23},{26,27},{30,31}} | collective-permute-start | bytes 9437192 | tf_op jit(solution)/shard_map/ppermute | solution.py:55
  192.8 67.3 %collective-permute-start.6 = (bf16[512,3072]{1,0:T(8,128)(2,1)}, bf16[512,3072]{1,0:T(8,128)(2,1)S(1)}, u32[]{:S(2)}, u32[]{:S(2)}) collective-permute-start(bf16[512,3072]{1,0:T(8,128)(2,1)} %collective-permute-done.3), channel_id=1, source_target_pairs={{1,0},{5,4},{9,8},{13,12},{17,16},{21,20},{25,24},{29,28}} | collective-permute-start | bytes 9437192 | tf_op jit(solution)/shard_map/ppermute | solution.py:55
  194.1 69.6 %collective-permute-start.7 = (bf16[384,4096]{1,0:T(8,128)(2,1)S(1)}, bf16[384,4096]{1,0:T(8,128)(2,1)}, u32[]{:S(2)}, u32[]{:S(2)}) collective-permute-start(bf16[384,4096]{1,0:T(8,128)(2,1)S(1)} %copy-done.26), channel_id=1, source_target_pairs={{3,1},{0,2},{7,5},{4,6},{11,9},{8,10},{15,13},{12,14},{19,17},{16,... | collective-permute-start | bytes 9437192 | tf_op jit(solution)/shard_map/ppermute | solution.py:55
  274.0 65.6 %collective-permute-start.8 = (bf16[384,2048]{1,0:T(8,128)(2,1)}, bf16[384,2048]{1,0:T(8,128)(2,1)}, u32[]{:S(2)}, u32[]{:S(2)}) collective-permute-start(bf16[384,2048]{1,0:T(8,128)(2,1)} %bitcast.57), channel_id=1, source_target_pairs={{3,1},{0,2},{2,0},{1,3},{7,5},{4,6},{6,4},{5,7},{11,9},{8,10},{10,... | collective-permute-start | bytes 4718600 | tf_op jit(solution)/shard_map/ppermute | solution.py:55
  339.6 279.6 %all-gather.17.cloned.1.call-start = ((), (), s32[]{:S(2)}) async-start(), calls=%async_computation.12 | async-start | bytes 28311552 | tf_op jit(solution)/shard_map/all_gather | solution.py:531
  345.2 69.1 %collective-permute-start.9 = (bf16[512,3072]{1,0:T(8,128)(2,1)S(1)}, bf16[512,3072]{1,0:T(8,128)(2,1)S(1)}, u32[]{:S(2)}, u32[]{:S(2)}) collective-permute-start(bf16[512,3072]{1,0:T(8,128)(2,1)S(1)} %convolution_convert_fusion.9.refs_1_), channel_id=1, source_target_pairs={{0,1},{4,5},{8,9},{12,13},{16,17},{20,21},{24,25},{28,29}} | collective-permute-start | bytes 9437192 | tf_op jit(solution)/shard_map/ppermute | solution.py:55
  346.7 69.3 %collective-permute-start.10 = (bf16[512,3072]{1,0:T(8,128)(2,1)S(1)}, bf16[512,3072]{1,0:T(8,128)(2,1)S(1)}, u32[]{:S(2)}, u32[]{:S(2)}) collective-permute-start(bf16[512,3072]{1,0:T(8,128)(2,1)S(1)} %convolution_convert_fusion.9.refs_1_), channel_id=1, source_target_pairs={{3,2},{7,6},{11,10},{15,14},{19,18},{23,22},{27,26},{31,30}} | collective-permute-start | bytes 9437192 | tf_op jit(solution)/shard_map/ppermute | solution.py:55
  347.5 72.9 %collective-permute-start.11 = (bf16[384,4096]{1,0:T(8,128)(2,1)S(1)}, bf16[384,4096]{1,0:T(8,128)(2,1)}, u32[]{:S(2)}, u32[]{:S(2)}) collective-permute-start(bf16[384,4096]{1,0:T(8,128)(2,1)S(1)} %copy-done.27), channel_id=1, source_target_pairs={{2,0},{1,3},{6,4},{5,7},{10,8},{9,11},{14,12},{13,15},{18,16},{17,... | collective-permute-start | bytes 9437192 | tf_op jit(solution)/shard_map/ppermute | solution.py:55
  426.5 540.8 %reduce-scatter.10.cloned.1.call-start = ((), (), s32[]{:S(2)}) async-start(), calls=%async_computation.14 | async-start | bytes 14155776 | tf_op jit(solution)/shard_map/reduce_scatter | solution.py:693
  437.5 68.4 %collective-permute-start.12 = (bf16[512,3072]{1,0:T(8,128)(2,1)S(1)}, bf16[512,3072]{1,0:T(8,128)(2,1)S(1)}, u32[]{:S(2)}, u32[]{:S(2)}) collective-permute-start(bf16[512,3072]{1,0:T(8,128)(2,1)S(1)} %shard_map.249), channel_id=1, source_target_pairs={{0,1},{1,2},{4,5},{5,6},{8,9},{9,10},{12,13},{13,14},{16,17},{17,1... | collective-permute-start | bytes 9437192 | tf_op jit(solution)/shard_map/ppermute | solution.py:55
  439.0 66.9 %collective-permute-start.13 = (bf16[512,3072]{1,0:T(8,128)(2,1)S(1)}, bf16[512,3072]{1,0:T(8,128)(2,1)S(1)}, u32[]{:S(2)}, u32[]{:S(2)}) collective-permute-start(bf16[512,3072]{1,0:T(8,128)(2,1)S(1)} %shard_map.249), channel_id=1, source_target_pairs={{3,2},{2,1},{7,6},{6,5},{11,10},{10,9},{15,14},{14,13},{19,18},{18... | collective-permute-start | bytes 9437192 | tf_op jit(solution)/shard_map/ppermute | solution.py:55
  439.9 71.2 %collective-permute-start.14 = (bf16[512,3072]{1,0:T(8,128)(2,1)S(1)}, bf16[512,3072]{1,0:T(8,128)(2,1)S(1)}, u32[]{:S(2)}, u32[]{:S(2)}) collective-permute-start(bf16[512,3072]{1,0:T(8,128)(2,1)S(1)} %copy-done.34), channel_id=1, source_target_pairs={{1,0},{2,3},{5,4},{6,7},{9,8},{10,11},{13,12},{14,15},{17,16},{18,... | collective-permute-start | bytes 9437192 | tf_op jit(solution)/shard_map/ppermute | solution.py:55
  447.1 63.9 %copy-start.3 = (bf16[512,3072]{1,0:T(8,128)(2,1)S(1)}, bf16[512,3072]{1,0:T(8,128)(2,1)}, u32[]{:S(2)}) copy-start(bf16[512,3072]{1,0:T(8,128)(2,1)} %convolution_convert_fusion.8.refs_0_) | copy-start | bytes 9437188
  515.4 68.1 %collective-permute-start.15 = (bf16[512,3072]{1,0:T(8,128)(2,1)}, bf16[512,3072]{1,0:T(8,128)(2,1)}, u32[]{:S(2)}, u32[]{:S(2)}) collective-permute-start(bf16[512,3072]{1,0:T(8,128)(2,1)} %get-tuple-element.222), channel_id=1, source_target_pairs={{0,1},{1,2},{2,3},{4,5},{5,6},{6,7},{8,9},{9,10},{10,11},{12,13},{... | collective-permute-start | bytes 9437192 | tf_op jit(solution)/shard_map/ppermute | solution.py:55
  519.0 70.4 %collective-permute-start.16 = (bf16[512,3072]{1,0:T(8,128)(2,1)}, bf16[512,3072]{1,0:T(8,128)(2,1)}, u32[]{:S(2)}, u32[]{:S(2)}) collective-permute-start(bf16[512,3072]{1,0:T(8,128)(2,1)} %get-tuple-element.223), channel_id=1, source_target_pairs={{3,2},{2,1},{1,0},{7,6},{6,5},{5,4},{11,10},{10,9},{9,8},{15,14},{... | collective-permute-start | bytes 9437192 | tf_op jit(solution)/shard_map/ppermute | solution.py:55
  542.3 47.1 %copy-start.32 = (bf16[512,3072]{1,0:T(8,128)(2,1)S(1)}, bf16[512,3072]{1,0:T(8,128)(2,1)}, u32[]{:S(2)}) copy-start(bf16[512,3072]{1,0:T(8,128)(2,1)} %convolution_convert_fusion.6) | copy-start | bytes 9437188
  561.3 33.0 %copy-start.18 = (f32[1,3072]{1,0:T(1,128)S(1)}, f32[1,3072]{1,0:T(1,128)}, u32[]{:S(2)}) copy-start(f32[1,3072]{1,0:T(1,128)} %get-tuple-element.391.gain_ref) | copy-start | bytes 36868
  598.0 67.6 %collective-permute-start.17 = (bf16[512,3072]{1,0:T(8,128)(2,1)}, bf16[512,3072]{1,0:T(8,128)(2,1)}, u32[]{:S(2)}, u32[]{:S(2)}) collective-permute-start(bf16[512,3072]{1,0:T(8,128)(2,1)} %multiply_convert_fusion.1.x_ref), channel_id=1, source_target_pairs={{0,1},{3,2},{1,0},{2,3},{4,5},{7,6},{5,4},{6,7},{8,9},{11,10},{9,8... | collective-permute-start | bytes 9437192 | tf_op jit(solution)/shard_map/ppermute | solution.py:55
  665.6 21.1 %copy-start.35 = (bf16[512,3072]{1,0:T(8,128)(2,1)S(1)}, bf16[512,3072]{1,0:T(8,128)(2,1)}, u32[]{:S(2)}) copy-start(bf16[512,3072]{1,0:T(8,128)(2,1)} %multiply_convert_fusion.2) | copy-start | bytes 9437188
  665.6 21.1 %copy-start.41 = (bf16[512,3072]{1,0:T(8,128)(2,1)S(1)}, bf16[512,3072]{1,0:T(8,128)(2,1)}, u32[]{:S(2)}) copy-start(bf16[512,3072]{1,0:T(8,128)(2,1)} %copy-done.40) | copy-start | bytes 9437188
  704.7 262.7 %reduce-scatter.12.cloned.1.call-start = ((), (), s32[]{:S(2)}) async-start(), calls=%async_computation.15 | async-start | bytes 14155776 | tf_op jit(solution)/shard_map/reduce_scatter | solution.py:693
  750.7 40.0 %collective-permute-start.18 = (bf16[512,1536]{1,0:T(8,128)(2,1)}, bf16[512,1536]{1,0:T(8,128)(2,1)}, u32[]{:S(2)}, u32[]{:S(2)}) collective-permute-start(bf16[512,1536]{1,0:T(8,128)(2,1)} %shard_map.255), channel_id=1, source_target_pairs={{0,1},{3,2},{1,0},{2,3},{4,5},{7,6},{5,4},{6,7},{8,9},{11,10},{9,8... | collective-permute-start | bytes 4718600 | tf_op jit(solution)/shard_map/ppermute | solution.py:55
  790.8 267.7 %reduce-scatter.8.cloned.1.call-start = ((), (), s32[]{:S(2)}) async-start(), calls=%async_computation.13 | async-start | bytes 14155776 | tf_op jit(solution)/shard_map/reduce_scatter | solution.py:693
  790.8 31.6 %collective-permute-start.19 = (bf16[512,1536]{1,0:T(8,128)(2,1)}, bf16[512,1536]{1,0:T(8,128)(2,1)S(1)}, u32[]{:S(2)}, u32[]{:S(2)}) collective-permute-start(bf16[512,1536]{1,0:T(8,128)(2,1)} %copy-done.15), channel_id=1, source_target_pairs={{0,1},{3,2},{1,0},{2,3},{4,5},{7,6},{5,4},{6,7},{8,9},{11,10},{9,8... | collective-permute-start | bytes 4718600 | tf_op jit(solution)/shard_map/ppermute | solution.py:55
  792.8 29.6 %copy-start.1 = (bf16[512,3072]{1,0:T(8,128)(2,1)S(1)}, bf16[512,3072]{1,0:T(8,128)(2,1)}, u32[]{:S(2)}) copy-start(bf16[512,3072]{1,0:T(8,128)(2,1)} %straight_ref.1) | copy-start | bytes 9437188
  792.8 29.6 %copy-start.6 = (f32[512,1536]{1,0:T(8,128)S(1)}, f32[512,1536]{1,0:T(8,128)}, u32[]{:S(2)}) copy-start(f32[512,1536]{1,0:T(8,128)} %copy-done.5) | copy-start | bytes 9437188
  792.9 29.6 %copy-start.19 = (f32[1,3072]{1,0:T(1,128)S(1)}, f32[1,3072]{1,0:T(1,128)}, u32[]{:S(2)}) copy-start(f32[1,3072]{1,0:T(1,128)} %get-tuple-element.391.gain_ref) | copy-start | bytes 36868
  822.4 39.1 %slice-start.5 = ((s8[4718592]{0:T(1024)(128)(4,1)}), s8[524288]{0:T(1024)(128)(4,1)S(1)}, s32[]{:S(2)}) async-start(s8[4718592]{0:T(1024)(128)(4,1)} %bitcast.62), calls=%async_computation.25 | async-start | bytes 1048576
  834.2 63.9 %collective-permute-start.20 = (bf16[512,3072]{1,0:T(8,128)(2,1)}, bf16[512,3072]{1,0:T(8,128)(2,1)}, u32[]{:S(2)}, u32[]{:S(2)}) collective-permute-start(bf16[512,3072]{1,0:T(8,128)(2,1)} %get-tuple-element.263), channel_id=1, source_target_pairs={{0,1},{1,2},{2,3},{4,5},{5,6},{6,7},{8,9},{9,10},{10,11},{12,13},{... | collective-permute-start | bytes 9437192 | tf_op jit(solution)/shard_map/ppermute | solution.py:55
  838.7 65.3 %collective-permute-start.21 = (bf16[512,3072]{1,0:T(8,128)(2,1)}, bf16[512,3072]{1,0:T(8,128)(2,1)}, u32[]{:S(2)}, u32[]{:S(2)}) collective-permute-start(bf16[512,3072]{1,0:T(8,128)(2,1)} %get-tuple-element.263), channel_id=1, source_target_pairs={{1,0},{2,1},{3,2},{5,4},{6,5},{7,6},{9,8},{10,9},{11,10},{13,12},{... | collective-permute-start | bytes 9437192 | tf_op jit(solution)/shard_map/ppermute | solution.py:55
  840.0 21.6 %slice-start.6 = ((s8[4718592]{0:T(1024)(128)(4,1)}), s8[4194304]{0:T(1024)(128)(4,1)S(1)}, s32[]{:S(2)}) async-start(s8[4718592]{0:T(1024)(128)(4,1)} %bitcast.62), calls=%async_computation.26 | async-start | bytes 8388608
  904.0 230.2 %reduce-scatter.14.cloned.1.call-start = ((), (), s32[]{:S(2)}) async-start(), calls=%async_computation.16 | async-start | bytes 14155776 | tf_op jit(solution)/shard_map/reduce_scatter | solution.py:693
  904.0 67.2 %collective-permute-start.22 = (bf16[512,3072]{1,0:T(8,128)(2,1)}, bf16[512,3072]{1,0:T(8,128)(2,1)}, u32[]{:S(2)}, u32[]{:S(2)}) collective-permute-start(bf16[512,3072]{1,0:T(8,128)(2,1)} %collective-permute-done.20), channel_id=1, source_target_pairs={{1,2},{2,3},{5,6},{6,7},{9,10},{10,11},{13,14},{14,15},{17,18},{18... | collective-permute-start | bytes 9437192 | tf_op jit(solution)/shard_map/ppermute | solution.py:55
  906.4 66.3 %collective-permute-start.23 = (bf16[512,3072]{1,0:T(8,128)(2,1)}, bf16[512,3072]{1,0:T(8,128)(2,1)}, u32[]{:S(2)}, u32[]{:S(2)}) collective-permute-start(bf16[512,3072]{1,0:T(8,128)(2,1)} %collective-permute-done.21), channel_id=1, source_target_pairs={{1,0},{2,1},{5,4},{6,5},{9,8},{10,9},{13,12},{14,13},{17,16},{18,1... | collective-permute-start | bytes 9437192 | tf_op jit(solution)/shard_map/ppermute | solution.py:55
  907.7 66.2 %collective-permute-start.24 = (bf16[512,3072]{1,0:T(8,128)(2,1)}, bf16[512,3072]{1,0:T(8,128)(2,1)}, u32[]{:S(2)}, u32[]{:S(2)}) collective-permute-start(bf16[512,3072]{1,0:T(8,128)(2,1)} %shard_map.259), channel_id=1, source_target_pairs={{0,1},{3,2},{4,5},{7,6},{8,9},{11,10},{12,13},{15,14},{16,17},{19,... | collective-permute-start | bytes 9437192 | tf_op jit(solution)/shard_map/ppermute | solution.py:55
  926.0 22.7 %copy-start.21 = (bf16[1024,2048]{1,0:T(8,128)(2,1)S(1)}, bf16[1024,2048]{1,0:T(8,128)(2,1)}, u32[]{:S(2)}) copy-start(bf16[1024,2048]{1,0:T(8,128)(2,1)} %get-tuple-element.276.refs_2_) | copy-start | bytes 12582916
  973.9 244.3 %reduce-scatter.16.cloned.1.call-start = ((), (), s32[]{:S(2)}) async-start(), calls=%async_computation.17 | async-start | bytes 14155776 | tf_op jit(solution)/shard_map/reduce_scatter | solution.py:693
  974.0 64.1 %collective-permute-start.25 = (bf16[512,3072]{1,0:T(8,128)(2,1)}, bf16[512,3072]{1,0:T(8,128)(2,1)}, u32[]{:S(2)}, u32[]{:S(2)}) collective-permute-start(bf16[512,3072]{1,0:T(8,128)(2,1)} %collective-permute-done.22), channel_id=1, source_target_pairs={{2,3},{6,7},{10,11},{14,15},{18,19},{22,23},{26,27},{30,31}} | collective-permute-start | bytes 9437192 | tf_op jit(solution)/shard_map/ppermute | solution.py:55
  976.4 65.5 %collective-permute-start.26 = (bf16[512,3072]{1,0:T(8,128)(2,1)}, bf16[512,3072]{1,0:T(8,128)(2,1)}, u32[]{:S(2)}, u32[]{:S(2)}) collective-permute-start(bf16[512,3072]{1,0:T(8,128)(2,1)} %collective-permute-done.23), channel_id=1, source_target_pairs={{1,0},{5,4},{9,8},{13,12},{17,16},{21,20},{25,24},{29,28}} | collective-permute-start | bytes 9437192 | tf_op jit(solution)/shard_map/ppermute | solution.py:55
  978.0 69.4 %collective-permute-start.27 = (bf16[384,4096]{1,0:T(8,128)(2,1)}, bf16[384,4096]{1,0:T(8,128)(2,1)}, u32[]{:S(2)}, u32[]{:S(2)}) collective-permute-start(bf16[384,4096]{1,0:T(8,128)(2,1)} %pad_maximum_fusion.4), channel_id=1, source_target_pairs={{0,2},{3,1},{4,6},{7,5},{8,10},{11,9},{12,14},{15,13},{16,18},{19,... | collective-permute-start | bytes 9437192 | tf_op jit(solution)/shard_map/ppermute | solution.py:55
  1047.4 236.1 %reduce-scatter.18.cloned.1.call-start = ((), (), s32[]{:S(2)}) async-start(), calls=%async_computation.18 | async-start | bytes 14155776 | tf_op jit(solution)/shard_map/reduce_scatter | solution.py:693
  1048.0 331.5 %reduce-scatter.20.cloned.1.call-start = ((), (), s32[]{:S(2)}) async-start(), calls=%async_computation.19 | async-start | bytes 14155776 | tf_op jit(solution)/shard_map/reduce_scatter | solution.py:693
  1058.5 75.7 %collective-permute-start.28 = (bf16[384,2048]{1,0:T(8,128)(2,1)}, bf16[384,2048]{1,0:T(8,128)(2,1)}, u32[]{:S(2)}, u32[]{:S(2)}) collective-permute-start(bf16[384,2048]{1,0:T(8,128)(2,1)} %reduce-scatter.8.cloned.1.call-done), channel_id=1, source_target_pairs={{0,2},{3,1},{1,3},{2,0},{4,6},{7,5},{5,7},{6,4},{8,10},{11,9},{9,1... | collective-permute-start | bytes 4718600 | tf_op jit(solution)/shard_map/ppermute | solution.py:55
  1146.9 62.2 %collective-permute-start.29 = (bf16[512,3072]{1,0:T(8,128)(2,1)}, bf16[512,3072]{1,0:T(8,128)(2,1)}, u32[]{:S(2)}, u32[]{:S(2)}) collective-permute-start(bf16[512,3072]{1,0:T(8,128)(2,1)} %shard_map.262.refs_1_), channel_id=1, source_target_pairs={{0,1},{4,5},{8,9},{12,13},{16,17},{20,21},{24,25},{28,29}} | collective-permute-start | bytes 9437192 | tf_op jit(solution)/shard_map/ppermute | solution.py:55
  1150.0 59.2 %collective-permute-start.30 = (bf16[512,3072]{1,0:T(8,128)(2,1)}, bf16[512,3072]{1,0:T(8,128)(2,1)}, u32[]{:S(2)}, u32[]{:S(2)}) collective-permute-start(bf16[512,3072]{1,0:T(8,128)(2,1)} %shard_map.262.refs_1_), channel_id=1, source_target_pairs={{3,2},{7,6},{11,10},{15,14},{19,18},{23,22},{27,26},{31,30}} | collective-permute-start | bytes 9437192 | tf_op jit(solution)/shard_map/ppermute | solution.py:55
  1152.2 66.0 %collective-permute-start.31 = (bf16[384,4096]{1,0:T(8,128)(2,1)}, bf16[384,4096]{1,0:T(8,128)(2,1)}, u32[]{:S(2)}, u32[]{:S(2)}) collective-permute-start(bf16[384,4096]{1,0:T(8,128)(2,1)} %pad_maximum_fusion.4), channel_id=1, source_target_pairs={{1,3},{2,0},{5,7},{6,4},{9,11},{10,8},{13,15},{14,12},{17,19},{18,... | collective-permute-start | bytes 9437192 | tf_op jit(solution)/shard_map/ppermute | solution.py:55
  1228.4 62.4 %collective-permute-start.32 = (bf16[512,3072]{1,0:T(8,128)(2,1)}, bf16[512,3072]{1,0:T(8,128)(2,1)}, u32[]{:S(2)}, u32[]{:S(2)}) collective-permute-start(bf16[512,3072]{1,0:T(8,128)(2,1)} %shard_map.263), channel_id=1, source_target_pairs={{0,1},{1,2},{4,5},{5,6},{8,9},{9,10},{12,13},{13,14},{16,17},{17,1... | collective-permute-start | bytes 9437192 | tf_op jit(solution)/shard_map/ppermute | solution.py:55
  1232.2 58.6 %collective-permute-start.33 = (bf16[512,3072]{1,0:T(8,128)(2,1)}, bf16[512,3072]{1,0:T(8,128)(2,1)}, u32[]{:S(2)}, u32[]{:S(2)}) collective-permute-start(bf16[512,3072]{1,0:T(8,128)(2,1)} %shard_map.263), channel_id=1, source_target_pairs={{3,2},{2,1},{7,6},{6,5},{11,10},{10,9},{15,14},{14,13},{19,18},{18... | collective-permute-start | bytes 9437192 | tf_op jit(solution)/shard_map/ppermute | solution.py:55
  1234.6 64.4 %collective-permute-start.34 = (bf16[512,3072]{1,0:T(8,128)(2,1)}, bf16[512,3072]{1,0:T(8,128)(2,1)}, u32[]{:S(2)}, u32[]{:S(2)}) collective-permute-start(bf16[512,3072]{1,0:T(8,128)(2,1)} %shard_map.259), channel_id=1, source_target_pairs={{1,0},{2,3},{5,4},{6,7},{9,8},{10,11},{13,12},{14,15},{17,16},{18,... | collective-permute-start | bytes 9437192 | tf_op jit(solution)/shard_map/ppermute | solution.py:55
  1310.3 78.5 %collective-permute-start.35 = (bf16[512,3072]{1,0:T(8,128)(2,1)}, bf16[512,3072]{1,0:T(8,128)(2,1)}, u32[]{:S(2)}, u32[]{:S(2)}) collective-permute-start(bf16[512,3072]{1,0:T(8,128)(2,1)} %get-tuple-element.315), channel_id=1, source_target_pairs={{0,1},{1,2},{2,3},{4,5},{5,6},{6,7},{8,9},{9,10},{10,11},{12,13},{... | collective-permute-start | bytes 9437192 | tf_op jit(solution)/shard_map/ppermute | solution.py:55
  1315.5 73.4 %collective-permute-start.36 = (bf16[512,3072]{1,0:T(8,128)(2,1)}, bf16[512,3072]{1,0:T(8,128)(2,1)}, u32[]{:S(2)}, u32[]{:S(2)}) collective-permute-start(bf16[512,3072]{1,0:T(8,128)(2,1)} %get-tuple-element.316), channel_id=1, source_target_pairs={{3,2},{2,1},{1,0},{7,6},{6,5},{5,4},{11,10},{10,9},{9,8},{15,14},{... | collective-permute-start | bytes 9437192 | tf_op jit(solution)/shard_map/ppermute | solution.py:55
  (53 other events, 339.8 us)
Sparse Core Ops, SparseCore 0:
  30.3 52.5 all-gather.6
  118.2 37.3 all-gather.8
  157.5 72.1 all-gather.10
  231.4 125.3 all-gather.12
  358.5 72.1 all-gather.14
  432.4 125.3 all-gather.16
  704.8 90.2 reduce-scatter.9
  798.6 92.3 reduce-scatter.11
  904.1 91.8 reduce-scatter.7
  999.3 92.3 reduce-scatter.13
  1095.3 92.3 reduce-scatter.15
  1191.0 92.3 reduce-scatter.17
  1287.0 92.4 reduce-scatter.19

commit v7 on v6

--- a/solution.py
+++ b/solution.py
@@ -411,8 +411,8 @@
     refs[-1][...] = total.astype(refs[-1].dtype)
 
 
-def spread(acts, weights, part, out, cost=HIDES, piece=0, pieces=1, parts=2):
-    rows, hidden = acts[0].shape[0] // parts, acts[0].shape[1]
+def spread(acts, weights, part, out, cost=HIDES, piece=0, pieces=1):
+    rows, hidden = acts[0].shape[0] // 2, acts[0].shape[1]
     width = weights[0][0].shape[0] // pieces
     tile = 256 if width % 256 == 0 else width
     tiles = width // tile
@@ -467,7 +467,7 @@
 
 def norm_back(grads, source, gain, straight, mask, low):
     rows, width = source.shape
-    tile = 64 if rows % 64 == 0 else rows
+    tile = 32 if rows % 32 == 0 else rows
     block = lambda wide: pl.BlockSpec((tile, wide), lambda i: (i, 0))
     masked = mask is not None
     out_shape = [jax.ShapeDtypeStruct((rows, width), F32)] + [jax.ShapeDtypeStruct((rows, width), BF16)] * low
@@ -640,7 +640,9 @@
 
     def took_out(step, arrived, filled):
         if step == 1:
-            w_both.extend(gather(joined(a, b)) for a, b in zip(both_ends, arrived))
+            for a, b, (by_ends, _) in zip(both_ends, arrived, outward):
+                choice = [a if any(i == to for _, to in by_ends) else b for i in range(n)]
+                w_both.append(gather(chosen_sum(place, choice, ())))
         elif step == n - 1:
             grad_mixed.extend(filled)
         else:
@@ -679,12 +681,15 @@
             *(dot(two, after(g, gate), TN, BF16) for g in grad_up[1:]),
         )
 
-    def own_half(gate):
-        return (spread([after(grads[0], gate)] + grads[1:], weights, 0, F32, HIDES, 1, 2),)
+    def gate_weights(gate):
+        return (
+            spread([after(grads[0], gate)] + grads[1:], weights, 0, F32, HIDES, 1, 2),
+            *(dot(two, after(g, gate), TN, BF16) for g in grad_gate[1:]),
+        )
 
     theirs = spread(grads, weights, 1, BF16, HIDES, 0, 2)
     (from_first,), (theirs, *d_up[1:]) = travel([(theirs, swap)], second_half)
-    (from_second,), (ours_second,) = travel([(theirs, swap)], own_half)
+    (from_second,), (ours_second, *d_gate[1:]) = travel([(theirs, swap)], gate_weights)
     grad_hidden, grad_hidden_low = norm_back(
         [(ours_first, 0, 1), (ours_second, 1, 1), (from_first, 0, 1), (from_second, 1, 1)], hidden, gain_two, cotangent, live, True
     )
@@ -704,24 +709,24 @@
         if step == 1:
             flops = 2 * rows * width * slices * gate_weight.shape[1]
             cost = pl.CostEstimate(flops=flops, transcendentals=0, bytes_accessed=flops // rows)
-            return (result_rows(1, BF16, gate, cost), *(d_of(two, g, gate) for g in grad_gate[1:]))
+            return (result_rows(1, BF16, gate, cost), d_of(grad_two, mixed[0], gate))
         if step == 2:
             return (result_rows(0, F32, gate), d_of(two, grad_up[0], gate), *joined_sums())
         if step == n - 1:
-            return (d_of(grad_two, mixed[0], gate), d_of(two, grad_gate[0], gate))
+            return (d_of(two, grad_gate[0], gate),)
         return ()
 
     def took_gather(step, arrived, filled):
         early.extend(arrived)
         if step == 1:
             results.append(filled[0])
-            d_gate[1:] = filled[1:]
+            d_down[0] = filled[1]
         elif step == 2:
             results.append(filled[0])
             d_up[0] = filled[1]
             sums.extend(filled[2:])
         elif step == n - 1:
-            d_down[0], d_gate[0] = filled
+            d_gate[0] = filled[0]
 
     sums = []
 
@@ -745,7 +750,7 @@
         return (
             attend_back(after(slot_table, gate), *grad_attended, rotated, attended, lse, *tables),
             d_of(jnp.concatenate(slots_back, axis=0), attended, gate),
-            sum_up,
+            sum_down,
         )
 
     sums_gate = [owner_sum(d) for d in d_gate[1:]]
@@ -766,7 +771,7 @@
     def while_reduce(step, gate):
         if step == 1:
             d_qkv = d_of(jnp.concatenate(slots_one, axis=0), grad_qkv, gate)
-            return (jnp.concatenate([d_qkv, d_out], axis=1), sum_down)
+            return (jnp.concatenate([d_qkv, d_out], axis=1), sum_up)
         if step == 2:
             return (sum_gate,)
         if step == n - 1:
@@ -800,13 +805,8 @@
         elif step == n - 1:
             outputs.extend(filled)
 
-    def rows_part(s):
-        if s == n - 1:
-            return spread([grad_qkv], [(w_qkv, 0)], s, BF16, parts=n)
-        return dot(grad_qkv[s * rows : (s + 1) * rows], w_qkv, NT, BF16)
-
     grad_normed_one = line_reduce(
-        rows_part,
+        lambda s: dot(grad_qkv[s * rows : (s + 1) * rows], w_qkv, NT, BF16),
         n,
         while_reduce,
         along_reduce,

time: 1430 us -> 1430 us (level)
  matrix products: 295 us -> 310 us
  waiting for transfers between devices: 447 us -> 432 us
    reduce_scatter x7, waiting for transfers between devices: 62.9 us -> 24.2 us  [owner_sum(): return lax.psum_scatter(partial, 'dp', scatter_dimension=0, tiled=True)]
    ppermute x37, waiting for transfers between devices: 371 us -> 395 us  [travel(): lax.ppermute(array, 'tensor', pairs)]
    dot_general x25 -> x26, matrix products: 295 us -> 310 us  [dot(): return lax.dot_general(a, b, dims, preferred_element_type=F32).astype(out)]
    pallas_call x7 -> x6, Pallas kernels: 139 us -> 126 us  [spread(): pl.pallas_call(functools.partial(spread_kernel, count), grid=(tiles,), in...]
    unnamed x140 -> x144, local copies, waits for them, and re-layouts: 37 us -> 47.1 us
  transfers between devices with their start and end apart: 50 -> 50, of which waited for: 28 -> 27; matrix products, arithmetic and copies ran while one was open for 28% -> 28% of each run, Pallas kernels for 23% -> 23%
where the time goes in v7:
time: 1430 us; the launch traced here: 1420 us
  waiting for transfers between devices  432 us (30%)
  Pallas kernels  361 us (25%)
  matrix products  310 us (22%)
  starting transfers between devices  111 us (8%)
  other arithmetic  99.1 us (7%)
  local copies, waits for them, and re-layouts  59.1 us (4%)
  blocking collectives  33.4 us (2%)
  between operations  15.6 us (1%)
    ppermute x37, waiting for transfers between devices, travel(): lax.ppermute(array, 'tensor', pairs)  395 us
    dot_general x26, matrix products, dot(): return lax.dot_general(a, b, dims, preferred_element_type=F32).astype(out)  310 us
    pallas_call x6, Pallas kernels, spread(): pl.pallas_call(functools.partial(spread_kernel, count), grid=(tiles,), in...  126 us
    ppermute x37, starting transfers between devices, travel(): lax.ppermute(array, 'tensor', pairs)  110 us
    pallas_call x4, Pallas kernels, gated(): pl.pallas_call(gated_kernel, grid=(tiles,), in_specs=[pl.BlockSpec((rows,...  88.2 us
    pallas_call x1, Pallas kernels, attention_back(): attend_back(after(slot_table, gate), *grad_attended, rotated, attended, l...  55.5 us
    unnamed x144, local copies, waits for them, and re-layouts  47.1 us
    pallas_call x1, Pallas kernels, attention(): return attend(slot_table, *projected, *tables)  45.8 us
  transfers between devices with their start and end apart: 50, of which 27 were waited for; matrix products, arithmetic and copies ran while one was open for 28% of the time, Pallas kernels for 23%

profile of v7, /device:TPU:0, one launch (start us, length us, event | category | flops | bytes accessed | tf_op | source)
XLA Modules:
  0.0 1420.5 jit_solution(4578933996246773407)
XLA Ops:
  9.4 10.4 all_gather.24
  30.2 13.4 all_gather.25
  71.8 11.0 all-gather.7.cloned.1.call-done
  82.8 9.9 fusion.44.refs_0_
  92.7 19.6 %collective-permute-done = bf16[512,3072]{1,0:T(8,128)(2,1)} collective-permute-done((bf16[512,3072]{1,0:T(8,128)(2,1)}, bf16[512,3072]{1,0:T(8,128)(2,1)}, u32[]{:S(2)}, u32[]{:S(2)}) %collective-permute-start) | collective-permute-done | bytes 3145760 | tf_op jit(solution)/shard_map/ppermute | solution.py:55
  123.0 6.9 collective-permute-start.4
  132.2 9.2 fusion.45.refs_1_
  141.5 49.3 %collective-permute-done.3 = bf16[512,3072]{1,0:T(8,128)(2,1)} collective-permute-done((bf16[512,3072]{1,0:T(8,128)(2,1)}, bf16[512,3072]{1,0:T(8,128)(2,1)}, u32[]{:S(2)}, u32[]{:S(2)}) %collective-permute-start.3) | collective-permute-done | bytes 3145760 | tf_op jit(solution)/shard_map/ppermute | solution.py:55
  194.1 7.8 collective-permute-start.7
  204.4 9.2 fusion.46.refs_2_
  213.6 46.5 %collective-permute-done.6 = bf16[512,3072]{1,0:T(8,128)(2,1)S(1)} collective-permute-done((bf16[512,3072]{1,0:T(8,128)(2,1)}, bf16[512,3072]{1,0:T(8,128)(2,1)S(1)}, u32[]{:S(2)}, u32[]{:S(2)}) %collective-permute-start.6) | collective-permute-done | bytes 3145760 | tf_op jit(solution)/shard_map/ppermute | solution.py:55
  267.9 8.0 fusion.47.refs_3_
  282.4 45.8 %shard_map.257 = (bf16[2048,768]{1,0:T(8,128)(2,1)}, bf16[2048,1280]{1,0:T(8,128)(2,1)}, f32[2,8,2048]{2,1,0:T(8,128)}) custom-call(s32[8]{0:T(128)} %dynamic-slice_bitcast_fusion.place_ref, f32[512,1280]{1,0:T(8,128)} %fusion.44.refs_0_, f32[512,1280]{1,0:T(8,128)} %fusion.45.refs_1_, f32[512,1280]{1,0:T(8,128)} %fusion.46.refs_2_, ...), custom_call_target="tpu_custom_call" | custom-call | flops 1 | bytes 1 | tf_op jit(solution)/shard_map/pallas_call | solution.py:618
  328.2 15.0 %collective-permute-done.8 = bf16[384,2048]{1,0:T(8,128)(2,1)} collective-permute-done((bf16[384,2048]{1,0:T(8,128)(2,1)}, bf16[384,2048]{1,0:T(8,128)(2,1)}, u32[]{:S(2)}, u32[]{:S(2)}) %collective-permute-start.8) | collective-permute-done | bytes 1572896 | tf_op jit(solution)/shard_map/ppermute | solution.py:55
  350.9 6.1 collective-permute-start.9
  357.6 6.9 convolution_convert_fusion.8.refs_0_
  366.3 56.1 %collective-permute-done.11.refs_0_ = bf16[384,4096]{1,0:T(8,128)(2,1)S(1)} collective-permute-done((bf16[384,4096]{1,0:T(8,128)(2,1)S(1)}, bf16[384,4096]{1,0:T(8,128)(2,1)S(1)}, u32[]{:S(2)}, u32[]{:S(2)}) %collective-permute-start.11) | collective-permute-done | bytes 3145760 | tf_op jit(solution)/shard_map/ppermute | solution.py:55
  459.9 52.4 %collective-permute-done.12 = bf16[512,3072]{1,0:T(8,128)(2,1)S(1)} collective-permute-done((bf16[512,3072]{1,0:T(8,128)(2,1)S(1)}, bf16[512,3072]{1,0:T(8,128)(2,1)S(1)}, u32[]{:S(2)}, u32[]{:S(2)}) %collective-permute-start.12) | collective-permute-done | bytes 3145760 | tf_op jit(solution)/shard_map/ppermute | solution.py:55
  531.6 16.9 %fusion.40.gm_ref = f32[1024,2048]{1,0:T(8,128)} fusion(bf16[3072,2048]{1,0:T(8,128)(2,1)S(1)} %bitcast.56, bf16[512,3072]{1,0:T(8,128)(2,1)S(1)} %add.120, bf16[512,3072]{1,0:T(8,128)(2,1)S(1)} %copy-done.38), kind=kOutput, calls=%fused_computation.110 | convolution fusion | flops 12897484800 | bytes 27262976 | tf_op jit(solution)/shard_map/dot_general | solution.py:25
  548.5 18.9 %fusion.39.gm_ref = f32[1024,2048]{1,0:T(8,128)} fusion(bf16[3072,2048]{1,0:T(8,128)(2,1)} %all-gather.15.cloned.1.call-done.refs_3_, bf16[512,3072]{1,0:T(8,128)(2,1)} %copy-done.44, bf16[512,3072]{1,0:T(8,128)(2,1)} %multiply_convert_fusion.2), kind=kOutput, calls=%fused_computation.109 | convolution fusion | flops 12897484800 | bytes 27262976 | tf_op jit(solution)/shard_map/dot_general | solution.py:25
  567.5 20.8 %collective-permute-done.15 = bf16[512,3072]{1,0:T(8,128)(2,1)} collective-permute-done((bf16[512,3072]{1,0:T(8,128)(2,1)}, bf16[512,3072]{1,0:T(8,128)(2,1)}, u32[]{:S(2)}, u32[]{:S(2)}) %collective-permute-start.15) | collective-permute-done | bytes 3145760 | tf_op jit(solution)/shard_map/ppermute | solution.py:55
  602.6 21.2 %shard_map.259 = (bf16[1024,2048]{1,0:T(8,128)(2,1)}, bf16[1024,2048]{1,0:T(8,128)(2,1)}, bf16[1024,2048]{1,0:T(8,128)(2,1)}) custom-call(bf16[512,3072]{1,0:T(8,128)(2,1)} %multiply_convert_fusion.1.x_ref, bf16[3072,4096]{1,0:T(8,128)(2,1)} %all-gather.13.cloned.1.call-done.gate_ref.up_ref.refs_4_.refs_6_, ...), custom_call_target="tpu_custom_call" | custom-call | flops 1 | bytes 1 | tf_op jit(solution)/shard_map/pallas_call | solution.py:393
  623.8 21.0 %shard_map.261 = (bf16[1024,2048]{1,0:T(8,128)(2,1)}, bf16[1024,2048]{1,0:T(8,128)(2,1)}, bf16[1024,2048]{1,0:T(8,128)(2,1)}) custom-call(bf16[512,3072]{1,0:T(8,128)(2,1)} %multiply_convert_fusion.1.x_ref, bf16[3072,4096]{1,0:T(8,128)(2,1)} %all-gather.17.cloned.1.call-done.gate_ref.up_ref.refs_5_.refs_7_, ...), custom_call_target="tpu_custom_call" | custom-call | flops 1 | bytes 1 | tf_op jit(solution)/shard_map/pallas_call | solution.py:393
  644.9 19.5 %shard_map.262.refs_0_ = f32[512,1536]{1,0:T(8,128)S(1)} custom-call(bf16[1024,2048]{1,0:T(8,128)(2,1)} %get-tuple-element.246.refs_0_.refs_1_, bf16[1024,2048]{1,0:T(8,128)(2,1)} %get-tuple-element.241.refs_1_, bf16[1024,2048]{1,0:T(8,128)(2,1)} %get-tuple-element.247.refs_2_, bf16[1024,2048]{1,0:T(8,128)(2,1)} %get-tuple-element.242.refs_3_.refs_2_, ...), custom_call_target="tpu_custom_call" | custom-call | flops 1 | bytes 1 | tf_op jit(solution)/shard_map/pallas_call | solution.py:424
  668.5 21.2 %shard_map.263 = (bf16[1024,2048]{1,0:T(8,128)(2,1)}, bf16[1024,2048]{1,0:T(8,128)(2,1)}, bf16[1024,2048]{1,0:T(8,128)(2,1)}) custom-call(bf16[512,3072]{1,0:T(8,128)(2,1)} %collective-permute-done.17.x_ref, ...), custom_call_target="tpu_custom_call", output_to_operand_aliasing={{0}: (4, {}), {1}: (5, {}), {2}: (6, {})} | custom-call | flops 1 | bytes 1 | tf_op jit(solution)/shard_map/pallas_call | solution.py:393
  689.7 18.0 %convolution_convert_fusion.5 = bf16[3072,2048]{1,0:T(8,128)(2,1)} fusion(bf16[1024,2048]{1,0:T(8,128)(2,1)} %get-tuple-element.243.refs_1_, bf16[512,3072]{1,0:T(8,128)(2,1)S(1)} %copy-done.45, bf16[512,3072]{1,0:T(8,128)(2,1)S(1)} %copy-done.39), kind=kOutput, calls=%fused_computation.23 | convolution fusion | flops 12903776256 | bytes 23068672 | tf_op jit(solution)/shard_map/dot_general | solution.py:25
  707.8 24.7 %shard_map.264 = (bf16[1024,2048]{1,0:T(8,128)(2,1)}, bf16[1024,2048]{1,0:T(8,128)(2,1)}, bf16[1024,2048]{1,0:T(8,128)(2,1)}) custom-call(bf16[512,3072]{1,0:T(8,128)(2,1)} %collective-permute-done.17.x_ref, ...), custom_call_target="tpu_custom_call", output_to_operand_aliasing={{0}: (4, {}), {1}: (5, {}), {2}: (6, {})} | custom-call | flops 1 | bytes 1 | tf_op jit(solution)/shard_map/pallas_call | solution.py:393
  732.5 21.2 %shard_map.265 = bf16[512,1536]{1,0:T(8,128)(2,1)} custom-call(bf16[1024,2048]{1,0:T(8,128)(2,1)} %get-tuple-element.284.refs_0_, bf16[1024,2048]{1,0:T(8,128)(2,1)} %get-tuple-element.256.refs_1_, bf16[1024,2048]{1,0:T(8,128)(2,1)} %get-tuple-element.275.refs_2_, bf16[1024,2048]{1,0:T(8,128)(2,1)} %get-tuple-element.253.refs_3_, ...), custom_call_target="tpu_custom_call" | custom-call | flops 1 | bytes 1 | tf_op jit(solution)/shard_map/pallas_call | solution.py:424
  753.7 19.9 %shard_map.266 = bf16[512,1536]{1,0:T(8,128)(2,1)S(1)} custom-call(bf16[1024,2048]{1,0:T(8,128)(2,1)} %get-tuple-element.284.refs_0_, bf16[1024,2048]{1,0:T(8,128)(2,1)} %get-tuple-element.256.refs_1_, bf16[1024,2048]{1,0:T(8,128)(2,1)} %get-tuple-element.275.refs_2_, bf16[1024,2048]{1,0:T(8,128)(2,1)} %get-tuple-element.253.refs_3_, ...), custom_call_target="tpu_custom_call" | custom-call | flops 1 | bytes 1 | tf_op jit(solution)/shard_map/pallas_call | solution.py:424
  774.9 18.6 %convolution_convert_fusion.4 = bf16[3072,2048]{1,0:T(8,128)(2,1)} fusion(bf16[1024,2048]{1,0:T(8,128)(2,1)S(1)} %copy-done.28, bf16[512,3072]{1,0:T(8,128)(2,1)} %collective-permute-done.17.x_ref, bf16[512,3072]{1,0:T(8,128)(2,1)} %multiply_convert_fusion.1.x_ref), kind=kOutput, calls=%fused_computation.22 | convolution fusion | flops 12903776256 | bytes 23068672 | tf_op jit(solution)/shard_map/dot_general | solution.py:25
  795.5 20.6 %shard_map.267.refs_1_ = f32[512,1536]{1,0:T(8,128)S(1)} custom-call(bf16[1024,2048]{1,0:T(8,128)(2,1)} %get-tuple-element.284.refs_0_, bf16[1024,2048]{1,0:T(8,128)(2,1)} %get-tuple-element.256.refs_1_, bf16[1024,2048]{1,0:T(8,128)(2,1)} %get-tuple-element.275.refs_2_, bf16[1024,2048]{1,0:T(8,128)(2,1)} %get-tuple-element.253.refs_3_, ...), custom_call_target="tpu_custom_call" | custom-call | flops 1 | bytes 1 | tf_op jit(solution)/shard_map/pallas_call | solution.py:424
  818.0 19.7 %convolution_convert_fusion.3 = bf16[3072,2048]{1,0:T(8,128)(2,1)} fusion(bf16[1024,2048]{1,0:T(8,128)(2,1)S(1)} %copy-done.27, bf16[512,3072]{1,0:T(8,128)(2,1)} %collective-permute-done.17.x_ref, bf16[512,3072]{1,0:T(8,128)(2,1)} %multiply_convert_fusion.1.x_ref), kind=kOutput, calls=%fused_computation.21 | convolution fusion | flops 12903776256 | bytes 23068672 | tf_op jit(solution)/shard_map/dot_general | solution.py:25
  842.6 15.6 %shard_map.268 = (f32[512,3072]{1,0:T(8,128)}, bf16[512,3072]{1,0:T(8,128)(2,1)}) custom-call(f32[1,3072]{1,0:T(1,128)S(1)} %copy-done.24, f32[512,3072]{1,0:T(8,128)} %copy-done.29, bf16[512,3072]{1,0:T(8,128)(2,1)S(1)} %copy-done.1, f32[512,1536]{1,0:T(8,128)S(1)} %copy-done.7, f32[512,1536]{1,0:T(8,128)} %copy-done.8, ...), custom_call_target="tpu_custom_call" | custom-call | flops 1 | bytes 1 | tf_op jit(solution)/shard_map/pallas_call | solution.py:474
  864.6 21.9 %shard_map.269 = bf16[512,3072]{1,0:T(8,128)(2,1)} custom-call(bf16[1024,2048]{1,0:T(8,128)(2,1)} %get-tuple-element.274.refs_0_, bf16[1024,2048]{1,0:T(8,128)(2,1)} %get-tuple-element.243.refs_1_, bf16[3072,2048]{1,0:T(8,128)(2,1)} %all-gather.11.cloned.1.call-done.refs_2_, bf16[3072,2048]{1,0:T(8,128)(2,1)} %all-gather.15.cloned.1.call-done.refs_3_), custom_call_target="tpu_custom_call" | custom-call | flops 12884901888 | bytes 25165824 | tf_op jit(solution)/shard_map/pallas_call | solution.py:424
  886.5 7.0 convolution_convert_fusion.17.refs_0_
  893.4 17.9 %convolution_convert_fusion.2 = bf16[3072,2048]{1,0:T(8,128)(2,1)} fusion(bf16[1024,2048]{1,0:T(8,128)(2,1)S(1)} %copy-done.30, bf16[512,3072]{1,0:T(8,128)(2,1)} %copy-done.44, bf16[512,3072]{1,0:T(8,128)(2,1)S(1)} %copy-done.40), kind=kOutput, calls=%fused_computation.20 | convolution fusion | flops 12903776256 | bytes 23068672 | tf_op jit(solution)/shard_map/dot_general | solution.py:25
  911.3 9.5 collective-permute-done.20
  932.5 6.9 collective-permute-start.24
  939.3 6.0 convolution_convert_fusion.16.refs_1_
  945.3 22.9 %shard_map.270 = f32[512,3072]{1,0:T(8,128)} custom-call(bf16[1024,2048]{1,0:T(8,128)(2,1)} %get-tuple-element.274.refs_0_, bf16[1024,2048]{1,0:T(8,128)(2,1)} %get-tuple-element.243.refs_1_, bf16[3072,2048]{1,0:T(8,128)(2,1)} %all-gather.11.cloned.1.call-done.refs_2_, bf16[3072,2048]{1,0:T(8,128)(2,1)} %all-gather.15.cloned.1.call-done.refs_3_), custom_call_target="tpu_custom_call" | custom-call | flops 1 | bytes 1 | tf_op jit(solution)/shard_map/pallas_call | solution.py:424
  968.2 19.7 %convolution_convert_fusion.1 = bf16[3072,2048]{1,0:T(8,128)(2,1)} fusion(bf16[1024,2048]{1,0:T(8,128)(2,1)S(1)} %copy-done.26, bf16[512,3072]{1,0:T(8,128)(2,1)} %collective-permute-done.17.x_ref, bf16[512,3072]{1,0:T(8,128)(2,1)} %multiply_convert_fusion.1.x_ref), kind=kOutput, calls=%fused_computation.19 | convolution fusion | flops 12903776256 | bytes 23068672 | tf_op jit(solution)/shard_map/dot_general | solution.py:25
  1004.8 11.6 collective-permute-start.27
  1022.2 19.4 %convolution_convert_fusion = bf16[3072,2048]{1,0:T(8,128)(2,1)} fusion(bf16[1024,2048]{1,0:T(8,128)(2,1)S(1)} %copy-done.25, bf16[512,3072]{1,0:T(8,128)(2,1)} %collective-permute-done.17.x_ref, bf16[512,3072]{1,0:T(8,128)(2,1)} %multiply_convert_fusion.1.x_ref), kind=kOutput, calls=%fused_computation.18 | convolution fusion | flops 12903776256 | bytes 23068672 | tf_op jit(solution)/shard_map/dot_general | solution.py:25
  1041.6 25.5 %collective-permute-done.26 = bf16[512,3072]{1,0:T(8,128)(2,1)} collective-permute-done((bf16[512,3072]{1,0:T(8,128)(2,1)}, bf16[512,3072]{1,0:T(8,128)(2,1)}, u32[]{:S(2)}, u32[]{:S(2)}) %collective-permute-start.26) | collective-permute-done | bytes 3145760 | tf_op jit(solution)/shard_map/ppermute | solution.py:55
  1077.4 6.0 convolution_convert_fusion.14.refs_3_
  1087.5 55.5 %shard_map.271 = bf16[2048,1280]{1,0:T(8,128)(2,1)} custom-call(s32[8]{0:T(128)} %dynamic-slice_bitcast_fusion.place_ref, bf16[512,768]{1,0:T(8,128)(2,1)} %convolution_convert_fusion.17.refs_0_, bf16[512,768]{1,0:T(8,128)(2,1)} %convolution_convert_fusion.16.refs_1_, bf16[512,768]{1,0:T(8,128)(2,1)} %convolution_convert_fusion.15.refs_2_, ...), custom_call_target="tpu_custom_call" | custom-call | flops 32212254720 | bytes 26214400 | tf_op jit(solution)/shard_map/pallas_call | solution.py:751
  1143.0 16.0 %fusion.22 = bf16[3072,768]{1,0:T(8,128)(2,1)} fusion(bf16[2048,768]{1,0:T(8,128)(2,1)} %get-tuple-element.294.refs_5_, bf16[512,3072]{1,0:T(8,128)(2,1)} %copy-done.48, bf16[512,3072]{1,0:T(8,128)(2,1)} %copy-done.47, bf16[512,3072]{1,0:T(8,128)(2,1)} %copy-done.46, bf16[512,3072]{1,0:T(8,128)(2,1)} %get-tuple-element.264), kind=kOutput, calls=%fused_computation.40 | convolution fusion | flops 9716367360 | bytes 20447232 | tf_op jit(solution)/shard_map/dot_general | solution.py:25
  1159.0 10.7 convolution_convert_fusion.13.refs_1_
  1176.4 20.8 %fusion.16 = bf16[3072,1280]{1,0:T(8,128)(2,1)S(1)} fusion(bf16[2048,1280]{1,0:T(8,128)(2,1)} %shard_map.271, bf16[512,3072]{1,0:T(8,128)(2,1)} %copy-done.43, bf16[512,3072]{1,0:T(8,128)(2,1)} %copy-done.42, bf16[512,3072]{1,0:T(8,128)(2,1)} %copy-done.41, bf16[512,3072]{1,0:T(8,128)(2,1)S(1)} %copy-done.37), kind=kOutput, calls=%fused_computation.17 | convolution fusion | flops 16160391168 | bytes 25690112 | tf_op jit(solution)/shard_map/dot_general | solution.py:25
  1197.3 8.9 pad_maximum_fusion
  1206.1 9.7 convolution_convert_fusion.12.refs_0_
  1215.9 12.0 collective-permute-done.29.refs_2_
  1227.9 9.1 collective-permute-done.31
  1238.9 8.0 shard_map.272
  1254.3 9.9 convolution_convert_fusion.11
  1264.1 14.2 reduce-scatter.18.cloned.1.call-done
  1278.3 27.2 %collective-permute-done.32 = bf16[512,3072]{1,0:T(8,128)(2,1)} collective-permute-done((bf16[512,3072]{1,0:T(8,128)(2,1)}, bf16[512,3072]{1,0:T(8,128)(2,1)}, u32[]{:S(2)}, u32[]{:S(2)}) %collective-permute-start.32) | collective-permute-done | bytes 3145760 | tf_op jit(solution)/shard_map/ppermute | solution.py:55
  1305.5 8.1 collective-permute-done.34
  1313.6 8.6 add_convert_fusion
  1327.7 9.6 convolution_convert_fusion.10.refs_0_
  1357.9 6.4 multiply_convert_fusion
  1364.2 10.0 reduce-scatter.20.cloned.1.call-done.x_ref
  1387.3 9.6 psum.7
  1399.5 14.3 %shard_map.274 = f32[512,3072]{1,0:T(8,128)} custom-call(f32[1,3072]{1,0:T(1,128)S(1)} %copy-done.22, bf16[512,3072]{1,0:T(8,128)(2,1)S(1)} %copy-done, f32[512,3072]{1,0:T(8,128)} %get-tuple-element.321.straight_ref, bf16[512,3072]{1,0:T(8,128)(2,1)S(1)} %copy-done.9, bf16[512,3072]{1,0:T(8,128)(2,1)} %collective-permute-done.35.refs_1_, ...), custom_call_target="tpu_custom_call" | custom-call | flops 1 | bytes 1 | tf_op jit(solution)/shard_map/pallas_call | solution.py:474
  (295 shorter events, 280.9 us)
Async XLA Ops:
  7.2 75.6 %all-gather.7.cloned.1.call-start = ((), (), s32[]{:S(2)}) async-start(), calls=%async_computation.7 | async-start | bytes 8847360 | tf_op jit(solution)/shard_map/all_gather | solution.py:531
  30.1 245.8 %all-gather.9.cloned.1.call-start = ((), (), s32[]{:S(2)}) async-start(), calls=%async_computation.8 | async-start | bytes 5308416 | tf_op jit(solution)/shard_map/all_gather | solution.py:531
  43.6 68.7 %collective-permute-start = (bf16[512,3072]{1,0:T(8,128)(2,1)}, bf16[512,3072]{1,0:T(8,128)(2,1)}, u32[]{:S(2)}, u32[]{:S(2)}) collective-permute-start(bf16[512,3072]{1,0:T(8,128)(2,1)} %fusion.21), channel_id=1, source_target_pairs={{0,1},{1,2},{2,3},{4,5},{5,6},{6,7},{8,9},{9,10},{10,11},{12,13},{... | collective-permute-start | bytes 9437192 | tf_op jit(solution)/shard_map/ppermute | solution.py:55
  48.7 69.4 %collective-permute-start.1 = (bf16[512,3072]{1,0:T(8,128)(2,1)}, bf16[512,3072]{1,0:T(8,128)(2,1)}, u32[]{:S(2)}, u32[]{:S(2)}) collective-permute-start(bf16[512,3072]{1,0:T(8,128)(2,1)} %fusion.21), channel_id=1, source_target_pairs={{1,0},{2,1},{3,2},{5,4},{6,5},{7,6},{9,8},{10,9},{11,10},{13,12},{... | collective-permute-start | bytes 9437192 | tf_op jit(solution)/shard_map/ppermute | solution.py:55
  118.1 157.8 %all-gather.11.cloned.1.call-start = ((), (), s32[]{:S(2)}) async-start(), calls=%async_computation.9 | async-start | bytes 14155776 | tf_op jit(solution)/shard_map/all_gather | solution.py:531
  118.8 306.9 %all-gather.13.cloned.1.call-start = ((), (), s32[]{:S(2)}) async-start(), calls=%async_computation.10 | async-start | bytes 28311552 | tf_op jit(solution)/shard_map/all_gather | solution.py:531
  119.4 429.1 %all-gather.15.cloned.1.call-start = ((), (), s32[]{:S(2)}) async-start(), calls=%async_computation.11 | async-start | bytes 14155776 | tf_op jit(solution)/shard_map/all_gather | solution.py:531
  119.4 22.0 %collective-permute-start.2 = (bf16[512,3072]{1,0:T(8,128)(2,1)}, bf16[512,3072]{1,0:T(8,128)(2,1)}, u32[]{:S(2)}, u32[]{:S(2)}) collective-permute-start(bf16[512,3072]{1,0:T(8,128)(2,1)} %collective-permute-done), channel_id=1, source_target_pairs={{1,2},{2,3},{5,6},{6,7},{9,10},{10,11},{13,14},{14,15},{17,18},{18... | collective-permute-start | bytes 9437192 | tf_op jit(solution)/shard_map/ppermute | solution.py:55
  121.8 69.0 %collective-permute-start.3 = (bf16[512,3072]{1,0:T(8,128)(2,1)}, bf16[512,3072]{1,0:T(8,128)(2,1)}, u32[]{:S(2)}, u32[]{:S(2)}) collective-permute-start(bf16[512,3072]{1,0:T(8,128)(2,1)} %collective-permute-done.1), channel_id=1, source_target_pairs={{1,0},{2,1},{5,4},{6,5},{9,8},{10,9},{13,12},{14,13},{17,16},{18,1... | collective-permute-start | bytes 9437192 | tf_op jit(solution)/shard_map/ppermute | solution.py:55
  123.0 68.9 %collective-permute-start.4 = (bf16[512,3072]{1,0:T(8,128)(2,1)}, bf16[512,3072]{1,0:T(8,128)(2,1)}, u32[]{:S(2)}, u32[]{:S(2)}) collective-permute-start(bf16[512,3072]{1,0:T(8,128)(2,1)} %multiply_convert_fusion.2), channel_id=1, source_target_pairs={{0,1},{3,2},{4,5},{7,6},{8,9},{11,10},{12,13},{15,14},{16,17},{19,... | collective-permute-start | bytes 9437192 | tf_op jit(solution)/shard_map/ppermute | solution.py:55
  132.2 61.9 %copy-start.31 = (bf16[384,4096]{1,0:T(8,128)(2,1)S(1)}, bf16[384,4096]{1,0:T(8,128)(2,1)}, u32[]{:S(2)}) copy-start(bf16[384,4096]{1,0:T(8,128)(2,1)} %pad_maximum_fusion.3) | copy-start | bytes 9437188
  191.9 21.6 %collective-permute-start.5 = (bf16[512,3072]{1,0:T(8,128)(2,1)}, bf16[512,3072]{1,0:T(8,128)(2,1)S(1)}, u32[]{:S(2)}, u32[]{:S(2)}) collective-permute-start(bf16[512,3072]{1,0:T(8,128)(2,1)} %collective-permute-done.2), channel_id=1, source_target_pairs={{2,3},{6,7},{10,11},{14,15},{18,19},{22,23},{26,27},{30,31}} | collective-permute-start | bytes 9437192 | tf_op jit(solution)/shard_map/ppermute | solution.py:55
  192.8 67.3 %collective-permute-start.6 = (bf16[512,3072]{1,0:T(8,128)(2,1)}, bf16[512,3072]{1,0:T(8,128)(2,1)S(1)}, u32[]{:S(2)}, u32[]{:S(2)}) collective-permute-start(bf16[512,3072]{1,0:T(8,128)(2,1)} %collective-permute-done.3), channel_id=1, source_target_pairs={{1,0},{5,4},{9,8},{13,12},{17,16},{21,20},{25,24},{29,28}} | collective-permute-start | bytes 9437192 | tf_op jit(solution)/shard_map/ppermute | solution.py:55
  194.1 69.7 %collective-permute-start.7 = (bf16[384,4096]{1,0:T(8,128)(2,1)S(1)}, bf16[384,4096]{1,0:T(8,128)(2,1)S(1)}, u32[]{:S(2)}, u32[]{:S(2)}) collective-permute-start(bf16[384,4096]{1,0:T(8,128)(2,1)S(1)} %copy-done.31), channel_id=1, source_target_pairs={{3,1},{0,2},{7,5},{4,6},{11,9},{8,10},{15,13},{12,14},{19,17},{16,... | collective-permute-start | bytes 9437192 | tf_op jit(solution)/shard_map/ppermute | solution.py:55
  275.9 67.3 %collective-permute-start.8 = (bf16[384,2048]{1,0:T(8,128)(2,1)}, bf16[384,2048]{1,0:T(8,128)(2,1)}, u32[]{:S(2)}, u32[]{:S(2)}) collective-permute-start(bf16[384,2048]{1,0:T(8,128)(2,1)} %bitcast.58), channel_id=1, source_target_pairs={{3,1},{0,2},{2,0},{1,3},{7,5},{4,6},{6,4},{5,7},{11,9},{8,10},{10,... | collective-permute-start | bytes 4718600 | tf_op jit(solution)/shard_map/ppermute | solution.py:55
  343.3 280.5 %all-gather.17.cloned.1.call-start = ((), (), s32[]{:S(2)}) async-start(), calls=%async_computation.12 | async-start | bytes 28311552 | tf_op jit(solution)/shard_map/all_gather | solution.py:531
  348.7 15.8 %collective-permute-start.10 = (bf16[512,3072]{1,0:T(8,128)(2,1)S(1)}, bf16[512,3072]{1,0:T(8,128)(2,1)S(1)}, u32[]{:S(2)}, u32[]{:S(2)}) collective-permute-start(bf16[512,3072]{1,0:T(8,128)(2,1)S(1)} %convolution_convert_fusion.9.refs_1_), channel_id=1, source_target_pairs={{3,2},{7,6},{11,10},{15,14},{19,18},{23,22},{27,26},{31,30}} | collective-permute-start | bytes 9437192 | tf_op jit(solution)/shard_map/ppermute | solution.py:55
  349.6 72.8 %collective-permute-start.11 = (bf16[384,4096]{1,0:T(8,128)(2,1)S(1)}, bf16[384,4096]{1,0:T(8,128)(2,1)S(1)}, u32[]{:S(2)}, u32[]{:S(2)}) collective-permute-start(bf16[384,4096]{1,0:T(8,128)(2,1)S(1)} %copy-done.32), channel_id=1, source_target_pairs={{2,0},{1,3},{6,4},{5,7},{10,8},{9,11},{14,12},{13,15},{18,16},{17,... | collective-permute-start | bytes 9437192 | tf_op jit(solution)/shard_map/ppermute | solution.py:55
  350.9 73.2 %collective-permute-start.9 = (bf16[512,3072]{1,0:T(8,128)(2,1)S(1)}, bf16[512,3072]{1,0:T(8,128)(2,1)S(1)}, u32[]{:S(2)}, u32[]{:S(2)}) collective-permute-start(bf16[512,3072]{1,0:T(8,128)(2,1)S(1)} %convolution_convert_fusion.9.refs_1_), channel_id=1, source_target_pairs={{0,1},{4,5},{8,9},{12,13},{16,17},{20,21},{24,25},{28,29}} | collective-permute-start | bytes 9437192 | tf_op jit(solution)/shard_map/ppermute | solution.py:55
  432.3 555.6 %reduce-scatter.10.cloned.1.call-start = ((), (), s32[]{:S(2)}) async-start(), calls=%async_computation.14 | async-start | bytes 14155776 | tf_op jit(solution)/shard_map/reduce_scatter | solution.py:698
  442.8 69.4 %collective-permute-start.12 = (bf16[512,3072]{1,0:T(8,128)(2,1)S(1)}, bf16[512,3072]{1,0:T(8,128)(2,1)S(1)}, u32[]{:S(2)}, u32[]{:S(2)}) collective-permute-start(bf16[512,3072]{1,0:T(8,128)(2,1)S(1)} %shard_map.258), channel_id=1, source_target_pairs={{0,1},{1,2},{4,5},{5,6},{8,9},{9,10},{12,13},{13,14},{16,17},{17,1... | collective-permute-start | bytes 9437192 | tf_op jit(solution)/shard_map/ppermute | solution.py:55
  447.2 65.1 %collective-permute-start.13 = (bf16[512,3072]{1,0:T(8,128)(2,1)S(1)}, bf16[512,3072]{1,0:T(8,128)(2,1)S(1)}, u32[]{:S(2)}, u32[]{:S(2)}) collective-permute-start(bf16[512,3072]{1,0:T(8,128)(2,1)S(1)} %shard_map.258), channel_id=1, source_target_pairs={{3,2},{2,1},{7,6},{6,5},{11,10},{10,9},{15,14},{14,13},{19,18},{18... | collective-permute-start | bytes 9437192 | tf_op jit(solution)/shard_map/ppermute | solution.py:55
  448.0 69.4 %collective-permute-start.14 = (bf16[512,3072]{1,0:T(8,128)(2,1)S(1)}, bf16[512,3072]{1,0:T(8,128)(2,1)S(1)}, u32[]{:S(2)}, u32[]{:S(2)}) collective-permute-start(bf16[512,3072]{1,0:T(8,128)(2,1)S(1)} %copy-done.38), channel_id=1, source_target_pairs={{1,0},{2,3},{5,4},{6,7},{9,8},{10,11},{13,12},{14,15},{17,16},{18,... | collective-permute-start | bytes 9437192 | tf_op jit(solution)/shard_map/ppermute | solution.py:55
  454.6 62.9 %copy-start.4 = (bf16[512,3072]{1,0:T(8,128)(2,1)S(1)}, bf16[512,3072]{1,0:T(8,128)(2,1)}, u32[]{:S(2)}) copy-start(bf16[512,3072]{1,0:T(8,128)(2,1)} %convolution_convert_fusion.8.refs_0_) | copy-start | bytes 9437188
  521.8 66.5 %collective-permute-start.15 = (bf16[512,3072]{1,0:T(8,128)(2,1)}, bf16[512,3072]{1,0:T(8,128)(2,1)}, u32[]{:S(2)}, u32[]{:S(2)}) collective-permute-start(bf16[512,3072]{1,0:T(8,128)(2,1)} %get-tuple-element.221), channel_id=1, source_target_pairs={{0,1},{1,2},{2,3},{4,5},{5,6},{6,7},{8,9},{9,10},{10,11},{12,13},{... | collective-permute-start | bytes 9437192 | tf_op jit(solution)/shard_map/ppermute | solution.py:55
  525.3 68.7 %collective-permute-start.16 = (bf16[512,3072]{1,0:T(8,128)(2,1)}, bf16[512,3072]{1,0:T(8,128)(2,1)}, u32[]{:S(2)}, u32[]{:S(2)}) collective-permute-start(bf16[512,3072]{1,0:T(8,128)(2,1)} %get-tuple-element.222), channel_id=1, source_target_pairs={{3,2},{2,1},{1,0},{7,6},{6,5},{5,4},{11,10},{10,9},{9,8},{15,14},{... | collective-permute-start | bytes 9437192 | tf_op jit(solution)/shard_map/ppermute | solution.py:55
  548.5 45.5 %copy-start.36 = (bf16[512,3072]{1,0:T(8,128)(2,1)S(1)}, bf16[512,3072]{1,0:T(8,128)(2,1)}, u32[]{:S(2)}) copy-start(bf16[512,3072]{1,0:T(8,128)(2,1)} %convolution_convert_fusion.6) | copy-start | bytes 9437188
  567.5 31.5 %copy-start.23 = (f32[1,3072]{1,0:T(1,128)S(1)}, f32[1,3072]{1,0:T(1,128)}, u32[]{:S(2)}) copy-start(f32[1,3072]{1,0:T(1,128)} %get-tuple-element.388.gain_ref) | copy-start | bytes 36868
  602.6 65.9 %collective-permute-start.17 = (bf16[512,3072]{1,0:T(8,128)(2,1)}, bf16[512,3072]{1,0:T(8,128)(2,1)}, u32[]{:S(2)}, u32[]{:S(2)}) collective-permute-start(bf16[512,3072]{1,0:T(8,128)(2,1)} %multiply_convert_fusion.1.x_ref), channel_id=1, source_target_pairs={{0,1},{3,2},{1,0},{2,3},{4,5},{7,6},{5,4},{6,7},{8,9},{11,10},{9,8... | collective-permute-start | bytes 9437192 | tf_op jit(solution)/shard_map/ppermute | solution.py:55
  668.5 21.2 %copy-start.39 = (bf16[512,3072]{1,0:T(8,128)(2,1)S(1)}, bf16[512,3072]{1,0:T(8,128)(2,1)}, u32[]{:S(2)}) copy-start(bf16[512,3072]{1,0:T(8,128)(2,1)} %multiply_convert_fusion.2) | copy-start | bytes 9437188
  668.5 21.2 %copy-start.45 = (bf16[512,3072]{1,0:T(8,128)(2,1)S(1)}, bf16[512,3072]{1,0:T(8,128)(2,1)}, u32[]{:S(2)}) copy-start(bf16[512,3072]{1,0:T(8,128)(2,1)} %copy-done.44) | copy-start | bytes 9437188
  707.7 280.2 %reduce-scatter.12.cloned.1.call-start = ((), (), s32[]{:S(2)}) async-start(), calls=%async_computation.15 | async-start | bytes 14155776 | tf_op jit(solution)/shard_map/reduce_scatter | solution.py:698
  753.7 21.1 %copy-start.28 = (bf16[1024,2048]{1,0:T(8,128)(2,1)S(1)}, bf16[1024,2048]{1,0:T(8,128)(2,1)}, u32[]{:S(2)}) copy-start(bf16[1024,2048]{1,0:T(8,128)(2,1)} %get-tuple-element.253.refs_3_) | copy-start | bytes 12582916
  753.7 39.7 %collective-permute-start.18 = (bf16[512,1536]{1,0:T(8,128)(2,1)}, bf16[512,1536]{1,0:T(8,128)(2,1)}, u32[]{:S(2)}, u32[]{:S(2)}) collective-permute-start(bf16[512,1536]{1,0:T(8,128)(2,1)} %shard_map.265), channel_id=1, source_target_pairs={{0,1},{3,2},{1,0},{2,3},{4,5},{7,6},{5,4},{6,7},{8,9},{11,10},{9,8... | collective-permute-start | bytes 4718600 | tf_op jit(solution)/shard_map/ppermute | solution.py:55
  793.5 289.9 %reduce-scatter.8.cloned.1.call-start = ((), (), s32[]{:S(2)}) async-start(), calls=%async_computation.13 | async-start | bytes 14155776 | tf_op jit(solution)/shard_map/reduce_scatter | solution.py:698
  793.5 24.4 %copy-start.27 = (bf16[1024,2048]{1,0:T(8,128)(2,1)S(1)}, bf16[1024,2048]{1,0:T(8,128)(2,1)}, u32[]{:S(2)}) copy-start(bf16[1024,2048]{1,0:T(8,128)(2,1)} %get-tuple-element.256.refs_1_) | copy-start | bytes 12582916
  793.5 44.2 %collective-permute-start.19 = (bf16[512,1536]{1,0:T(8,128)(2,1)}, bf16[512,1536]{1,0:T(8,128)(2,1)}, u32[]{:S(2)}, u32[]{:S(2)}) collective-permute-start(bf16[512,1536]{1,0:T(8,128)(2,1)} %copy-done.20), channel_id=1, source_target_pairs={{0,1},{3,2},{1,0},{2,3},{4,5},{7,6},{5,4},{6,7},{8,9},{11,10},{9,8... | collective-permute-start | bytes 4718600 | tf_op jit(solution)/shard_map/ppermute | solution.py:55
  837.7 321.3 %reduce-scatter.14.cloned.1.call-start = ((), (), s32[]{:S(2)}) async-start(), calls=%async_computation.16 | async-start | bytes 14155776 | tf_op jit(solution)/shard_map/reduce_scatter | solution.py:698
  858.2 62.7 %collective-permute-start.20 = (bf16[512,3072]{1,0:T(8,128)(2,1)}, bf16[512,3072]{1,0:T(8,128)(2,1)}, u32[]{:S(2)}, u32[]{:S(2)}) collective-permute-start(bf16[512,3072]{1,0:T(8,128)(2,1)} %get-tuple-element.264), channel_id=1, source_target_pairs={{0,1},{1,2},{2,3},{4,5},{5,6},{6,7},{8,9},{9,10},{10,11},{12,13},{... | collective-permute-start | bytes 9437192 | tf_op jit(solution)/shard_map/ppermute | solution.py:55
  863.3 63.3 %collective-permute-start.21 = (bf16[512,3072]{1,0:T(8,128)(2,1)}, bf16[512,3072]{1,0:T(8,128)(2,1)}, u32[]{:S(2)}, u32[]{:S(2)}) collective-permute-start(bf16[512,3072]{1,0:T(8,128)(2,1)} %get-tuple-element.264), channel_id=1, source_target_pairs={{1,0},{2,1},{3,2},{5,4},{6,5},{7,6},{9,8},{10,9},{11,10},{13,12},{... | collective-permute-start | bytes 9437192 | tf_op jit(solution)/shard_map/ppermute | solution.py:55
  926.6 310.4 %reduce-scatter.16.cloned.1.call-start = ((), (), s32[]{:S(2)}) async-start(), calls=%async_computation.17 | async-start | bytes 14155776 | tf_op jit(solution)/shard_map/reduce_scatter | solution.py:698
  926.6 65.2 %collective-permute-start.22 = (bf16[512,3072]{1,0:T(8,128)(2,1)}, bf16[512,3072]{1,0:T(8,128)(2,1)}, u32[]{:S(2)}, u32[]{:S(2)}) collective-permute-start(bf16[512,3072]{1,0:T(8,128)(2,1)} %collective-permute-done.20), channel_id=1, source_target_pairs={{1,2},{2,3},{5,6},{6,7},{9,10},{10,11},{13,14},{14,15},{17,18},{18... | collective-permute-start | bytes 9437192 | tf_op jit(solution)/shard_map/ppermute | solution.py:55
  931.2 65.7 %collective-permute-start.23 = (bf16[512,3072]{1,0:T(8,128)(2,1)}, bf16[512,3072]{1,0:T(8,128)(2,1)}, u32[]{:S(2)}, u32[]{:S(2)}) collective-permute-start(bf16[512,3072]{1,0:T(8,128)(2,1)} %collective-permute-done.21), channel_id=1, source_target_pairs={{1,0},{2,1},{5,4},{6,5},{9,8},{10,9},{13,12},{14,13},{17,16},{18,1... | collective-permute-start | bytes 9437192 | tf_op jit(solution)/shard_map/ppermute | solution.py:55
  932.5 65.6 %collective-permute-start.24 = (bf16[512,3072]{1,0:T(8,128)(2,1)}, bf16[512,3072]{1,0:T(8,128)(2,1)}, u32[]{:S(2)}, u32[]{:S(2)}) collective-permute-start(bf16[512,3072]{1,0:T(8,128)(2,1)} %shard_map.269), channel_id=1, source_target_pairs={{0,1},{3,2},{4,5},{7,6},{8,9},{11,10},{12,13},{15,14},{16,17},{19,... | collective-permute-start | bytes 9437192 | tf_op jit(solution)/shard_map/ppermute | solution.py:55
  945.3 22.9 %copy-start.26 = (bf16[1024,2048]{1,0:T(8,128)(2,1)S(1)}, bf16[1024,2048]{1,0:T(8,128)(2,1)}, u32[]{:S(2)}) copy-start(bf16[1024,2048]{1,0:T(8,128)(2,1)} %get-tuple-element.275.refs_2_) | copy-start | bytes 12582916
  998.0 280.3 %reduce-scatter.18.cloned.1.call-start = ((), (), s32[]{:S(2)}) async-start(), calls=%async_computation.18 | async-start | bytes 14155776 | tf_op jit(solution)/shard_map/reduce_scatter | solution.py:698
  998.1 43.6 %collective-permute-start.25 = (bf16[512,3072]{1,0:T(8,128)(2,1)}, bf16[512,3072]{1,0:T(8,128)(2,1)}, u32[]{:S(2)}, u32[]{:S(2)}) collective-permute-start(bf16[512,3072]{1,0:T(8,128)(2,1)} %collective-permute-done.22), channel_id=1, source_target_pairs={{2,3},{6,7},{10,11},{14,15},{18,19},{22,23},{26,27},{30,31}} | collective-permute-start | bytes 9437192 | tf_op jit(solution)/shard_map/ppermute | solution.py:55
  1003.2 19.0 %copy-start.25 = (bf16[1024,2048]{1,0:T(8,128)(2,1)S(1)}, bf16[1024,2048]{1,0:T(8,128)(2,1)}, u32[]{:S(2)}) copy-start(bf16[1024,2048]{1,0:T(8,128)(2,1)} %get-tuple-element.284.refs_0_) | copy-start | bytes 12582916
  1003.2 63.9 %collective-permute-start.26 = (bf16[512,3072]{1,0:T(8,128)(2,1)}, bf16[512,3072]{1,0:T(8,128)(2,1)}, u32[]{:S(2)}, u32[]{:S(2)}) collective-permute-start(bf16[512,3072]{1,0:T(8,128)(2,1)} %collective-permute-done.23), channel_id=1, source_target_pairs={{1,0},{5,4},{9,8},{13,12},{17,16},{21,20},{25,24},{29,28}} | collective-permute-start | bytes 9437192 | tf_op jit(solution)/shard_map/ppermute | solution.py:55
  1004.8 68.2 %collective-permute-start.27 = (bf16[384,4096]{1,0:T(8,128)(2,1)}, bf16[384,4096]{1,0:T(8,128)(2,1)}, u32[]{:S(2)}, u32[]{:S(2)}) collective-permute-start(bf16[384,4096]{1,0:T(8,128)(2,1)} %pad_maximum_fusion.4), channel_id=1, source_target_pairs={{0,2},{3,1},{4,6},{7,5},{8,10},{11,9},{12,14},{15,13},{16,18},{19,... | collective-permute-start | bytes 9437192 | tf_op jit(solution)/shard_map/ppermute | solution.py:55
  1073.0 301.3 %reduce-scatter.20.cloned.1.call-start = ((), (), s32[]{:S(2)}) async-start(), calls=%async_computation.19 | async-start | bytes 14155776 | tf_op jit(solution)/shard_map/reduce_scatter | solution.py:698
  1083.4 75.6 %collective-permute-start.28 = (bf16[384,2048]{1,0:T(8,128)(2,1)}, bf16[384,2048]{1,0:T(8,128)(2,1)}, u32[]{:S(2)}, u32[]{:S(2)}) collective-permute-start(bf16[384,2048]{1,0:T(8,128)(2,1)} %reduce-scatter.8.cloned.1.call-done), channel_id=1, source_target_pairs={{0,2},{3,1},{1,3},{2,0},{4,6},{7,5},{5,7},{6,4},{8,10},{11,9},{9,1... | collective-permute-start | bytes 4718600 | tf_op jit(solution)/shard_map/ppermute | solution.py:55
  1159.0 17.4 %copy-start.37 = (bf16[512,3072]{1,0:T(8,128)(2,1)S(1)}, bf16[512,3072]{1,0:T(8,128)(2,1)}, u32[]{:S(2)}) copy-start(bf16[512,3072]{1,0:T(8,128)(2,1)} %fusion.21) | copy-start | bytes 9437188
  1169.8 58.2 %collective-permute-start.29 = (bf16[512,3072]{1,0:T(8,128)(2,1)}, bf16[512,3072]{1,0:T(8,128)(2,1)}, u32[]{:S(2)}, u32[]{:S(2)}) collective-permute-start(bf16[512,3072]{1,0:T(8,128)(2,1)} %convolution_convert_fusion.13.refs_1_), channel_id=1, source_target_pairs={{0,1},{4,5},{8,9},{12,13},{16,17},{20,21},{24,25},{28,29}} | collective-permute-start | bytes 9437192 | tf_op jit(solution)/shard_map/ppermute | solution.py:55
  1172.8 55.1 %collective-permute-start.30 = (bf16[512,3072]{1,0:T(8,128)(2,1)}, bf16[512,3072]{1,0:T(8,128)(2,1)}, u32[]{:S(2)}, u32[]{:S(2)}) collective-permute-start(bf16[512,3072]{1,0:T(8,128)(2,1)} %convolution_convert_fusion.13.refs_1_), channel_id=1, source_target_pairs={{3,2},{7,6},{11,10},{15,14},{19,18},{23,22},{27,26},{31,30}} | collective-permute-start | bytes 9437192 | tf_op jit(solution)/shard_map/ppermute | solution.py:55
  1175.1 61.9 %collective-permute-start.31 = (bf16[384,4096]{1,0:T(8,128)(2,1)}, bf16[384,4096]{1,0:T(8,128)(2,1)}, u32[]{:S(2)}, u32[]{:S(2)}) collective-permute-start(bf16[384,4096]{1,0:T(8,128)(2,1)} %pad_maximum_fusion.4), channel_id=1, source_target_pairs={{1,3},{2,0},{5,7},{6,4},{9,11},{10,8},{13,15},{14,12},{17,19},{18,... | collective-permute-start | bytes 9437192 | tf_op jit(solution)/shard_map/ppermute | solution.py:55
  1246.9 58.6 %collective-permute-start.32 = (bf16[512,3072]{1,0:T(8,128)(2,1)}, bf16[512,3072]{1,0:T(8,128)(2,1)}, u32[]{:S(2)}, u32[]{:S(2)}) collective-permute-start(bf16[512,3072]{1,0:T(8,128)(2,1)} %shard_map.272), channel_id=1, source_target_pairs={{0,1},{1,2},{4,5},{5,6},{8,9},{9,10},{12,13},{13,14},{16,17},{17,1... | collective-permute-start | bytes 9437192 | tf_op jit(solution)/shard_map/ppermute | solution.py:55
  1250.6 54.9 %collective-permute-start.33 = (bf16[512,3072]{1,0:T(8,128)(2,1)}, bf16[512,3072]{1,0:T(8,128)(2,1)}, u32[]{:S(2)}, u32[]{:S(2)}) collective-permute-start(bf16[512,3072]{1,0:T(8,128)(2,1)} %shard_map.272), channel_id=1, source_target_pairs={{3,2},{2,1},{7,6},{6,5},{11,10},{10,9},{15,14},{14,13},{19,18},{18... | collective-permute-start | bytes 9437192 | tf_op jit(solution)/shard_map/ppermute | solution.py:55
  1253.0 60.6 %collective-permute-start.34 = (bf16[512,3072]{1,0:T(8,128)(2,1)}, bf16[512,3072]{1,0:T(8,128)(2,1)}, u32[]{:S(2)}, u32[]{:S(2)}) collective-permute-start(bf16[512,3072]{1,0:T(8,128)(2,1)} %shard_map.269), channel_id=1, source_target_pairs={{1,0},{2,3},{5,4},{6,7},{9,8},{10,11},{13,12},{14,15},{17,16},{18,... | collective-permute-start | bytes 9437192 | tf_op jit(solution)/shard_map/ppermute | solution.py:55
  1322.2 61.5 %collective-permute-start.35 = (bf16[512,3072]{1,0:T(8,128)(2,1)}, bf16[512,3072]{1,0:T(8,128)(2,1)}, u32[]{:S(2)}, u32[]{:S(2)}) collective-permute-start(bf16[512,3072]{1,0:T(8,128)(2,1)} %get-tuple-element.313), channel_id=1, source_target_pairs={{0,1},{1,2},{2,3},{4,5},{5,6},{6,7},{8,9},{9,10},{10,11},{12,13},{... | collective-permute-start | bytes 9437192 | tf_op jit(solution)/shard_map/ppermute | solution.py:55
  1326.3 59.5 %collective-permute-start.36 = (bf16[512,3072]{1,0:T(8,128)(2,1)}, bf16[512,3072]{1,0:T(8,128)(2,1)}, u32[]{:S(2)}, u32[]{:S(2)}) collective-permute-start(bf16[512,3072]{1,0:T(8,128)(2,1)} %get-tuple-element.314), channel_id=1, source_target_pairs={{3,2},{2,1},{1,0},{7,6},{6,5},{5,4},{11,10},{10,9},{9,8},{15,14},{... | collective-permute-start | bytes 9437192 | tf_op jit(solution)/shard_map/ppermute | solution.py:55
  1379.9 17.1 %copy-start.57 = (bf16[1,384]{1,0:T(2,128)(2,1)S(1)}, bf16[1,384]{1,0:T(2,128)(2,1)}, u32[]{:S(2)}) copy-start(bf16[1,384]{1,0:T(2,128)(2,1)} %copy-done.56) | copy-start | bytes 2308
  1379.9 17.0 %copy-start.59 = (bf16[1,384]{1,0:T(2,128)(2,1)S(1)}, bf16[1,384]{1,0:T(2,128)(2,1)}, u32[]{:S(2)}) copy-start(bf16[1,384]{1,0:T(2,128)(2,1)} %copy-done.58) | copy-start | bytes 2308
  1379.9 17.7 %copy-start.22 = (f32[1,3072]{1,0:T(1,128)S(1)}, f32[1,3072]{1,0:T(1,128)}, u32[]{:S(2)}) copy-start(f32[1,3072]{1,0:T(1,128)} %copy-done.21) | copy-start | bytes 36868
  (55 other events, 283.7 us)
Sparse Core Ops, SparseCore 0:
  30.2 52.4 all-gather.6
  118.2 37.3 all-gather.8
  157.4 72.1 all-gather.10
  231.3 125.3 all-gather.12
  358.4 72.1 all-gather.14
  432.5 125.1 all-gather.16
  707.9 90.9 reduce-scatter.9
  802.4 92.4 reduce-scatter.11
  898.3 92.4 reduce-scatter.7
  994.2 92.3 reduce-scatter.13
  1090.1 92.3 reduce-scatter.15
  1185.9 92.4 reduce-scatter.17
  1281.8 92.3 reduce-scatter.19

commit v8 on v5

--- a/solution.py
+++ b/solution.py
@@ -429,7 +429,7 @@
 
 def norm_back(grads, source, gain, straight, mask, low):
     rows, width = source.shape
-    tile = 64 if rows % 64 == 0 else rows
+    tile = 128 if rows % 128 == 0 else rows
     block = lambda wide: pl.BlockSpec((tile, wide), lambda i: (i, 0))
     masked = mask is not None
     out_shape = [jax.ShapeDtypeStruct((rows, width), F32)] + [jax.ShapeDtypeStruct((rows, width), BF16)] * low
@@ -709,18 +709,16 @@
     def attention_back(gate):
         return (
             attend_back(after(slot_table, gate), *grad_attended, rotated, attended, lse, *tables),
-            d_of(jnp.concatenate(slots_back, axis=0), attended, gate),
             sum_down,
         )
 
     sums_gate = [owner_sum(d) for d in d_gate[1:]]
     sum_down, sum_up, sum_gate = owner_sum(d_down[0]), owner_sum(d_up[0]), owner_sum(d_gate[0])
     leaving = [after(one, grad_attended[n - 1]) for one in sums_gate]
-    back_gate, (grad_qkv, d_out, _) = travel(
+    back_gate, (grad_qkv, _) = travel(
         [(one, a + b) for one, (a, b) in zip(leaving, homeward)], attention_back
     )
     back_down, back_up, outputs, d_attention = [], [], [], []
-    all_heads = own_qkv.shape[1]
 
     def columns(array, offset, size):
         return jnp.concatenate(
@@ -730,17 +728,15 @@
 
     def while_reduce(step, gate):
         if step == 1:
-            d_qkv = d_of(jnp.concatenate(slots_one, axis=0), grad_qkv, gate)
-            return (jnp.concatenate([d_qkv, d_out], axis=1), sum_up)
+            return (d_of(jnp.concatenate(slots_one, axis=0), grad_qkv, gate), sum_up)
         if step == 2:
-            return (sum_gate,)
+            return (d_of(jnp.concatenate(slots_back, axis=0), attended, gate), sum_gate)
         if step == n - 1:
             from_partner = joined(result_ends, outputs[0])
             result = hidden + (results[1] + after(from_partner, gate).astype(F32))
             sum_attention = owner_sum(d_attention[0])
             return (
                 (result * live).astype(BF16),
-                turned(sum_attention, all_heads, out_weight.shape[0]),
                 *(columns(sum_attention, *place) for place in ((0, qw), (qw, hd), (qw + hd, hd))),
                 sum_attention,
             )
@@ -762,6 +758,7 @@
             d_attention.append(filled[0])
         elif step == 2:
             outputs.extend(arrived)
+            d_attention.append(filled[0])
         elif step == n - 1:
             outputs.extend(filled)
 
@@ -772,7 +769,7 @@
         along_reduce,
         took_reduce,
     )
-    _, output, grad_out_w, grad_query_w, grad_key_w, grad_value_w, sum_attention = outputs
+    _, output, grad_query_w, grad_key_w, grad_value_w, sum_attention = outputs
 
     def whole(first, back):
         return sum((one.astype(F32) for one in back), first.astype(F32))
@@ -780,7 +777,7 @@
     grad_down_w = whole(sum_down, back_down).T
     grad_gate_w = whole(sum_gate, back_gate)
     grad_up_w = whole(sum_up, back_up)
-    grad_qkv_w = sum_attention[:, :all_heads].astype(F32)
+    grad_qkv_w = sum_attention.astype(F32)
     def along_row(weight, grad):
         return jnp.sum(weight.astype(F32) * grad, axis=1)
 
@@ -793,6 +790,7 @@
     gain_own = lax.psum(gain_parts, "tensor") / jnp.stack([attn_gain, mlp_gain]).astype(F32)
 
     grad_tokens = norm_back([(term, 0, 2) for term in grad_normed_one], tokens, gain_one, grad_hidden, None, False)
+    grad_out_w = turned(after(owner_sum(d_attention[1]), grad_tokens), 0, out_weight.shape[0])
 
     return (
         output,

time: 1420 us -> 1430 us (level)
  waiting for transfers between devices: 443 us -> 469 us
    ppermute x37, waiting for transfers between devices: 410 us -> 452 us  [travel(): lax.ppermute(array, 'tensor', pairs)]
    reduce_scatter x7 -> x8, waiting for transfers between devices: 20.8 us -> 4.26 us  [owner_sum(): return lax.psum_scatter(partial, 'dp', scatter_dimension=0, tiled=True)]
  transfers between devices with their start and end apart: 50 -> 51, of which waited for: 28 -> 28; matrix products, arithmetic and copies ran while one was open for 30% -> 29% of each run, Pallas kernels for 22% -> 22%
where the time goes in v8:
time: 1430 us
  waiting for transfers between devices  469 us (33%)
  Pallas kernels  339 us (24%)
  matrix products  309 us (22%)
  starting transfers between devices  113 us (8%)
  other arithmetic  112 us (8%)
  local copies, waits for them, and re-layouts  35.4 us (2%)
  blocking collectives  32.1 us (2%)
  between operations  15.6 us (1%)
    ppermute x37, waiting for transfers between devices, travel(): lax.ppermute(array, 'tensor', pairs)  452 us
    dot_general x26, matrix products, dot(): return lax.dot_general(a, b, dims, preferred_element_type=F32).astype(out)  309 us
    pallas_call x6, Pallas kernels, spread(): pl.pallas_call(functools.partial(spread_kernel, count), grid=(tiles,), in...  127 us
    ppermute x37, starting transfers between devices, travel(): lax.ppermute(array, 'tensor', pairs)  112 us
    pallas_call x4, Pallas kernels, gated(): pl.pallas_call(gated_kernel, grid=(tiles,), in_specs=[pl.BlockSpec((rows,...  88.1 us
    pallas_call x1, Pallas kernels, attention_back(): attend_back(after(slot_table, gate), *grad_attended, rotated, attended, l...  55.5 us
    pallas_call x1, Pallas kernels, attention(): return attend(slot_table, *projected, *tables)  44.3 us
  transfers between devices with their start and end apart: 51, of which 28 were waited for; matrix products, arithmetic and copies ran while one was open for 29% of the time, Pallas kernels for 22%

profile of v8, /device:TPU:0, one launch (start us, length us, event | category | flops | bytes accessed | tf_op | source)
XLA Modules:
  0.0 1426.6 jit_solution(13793216807114741797)
XLA Ops:
  9.4 10.4 all_gather.24
  30.3 13.4 all_gather.25
  71.8 11.0 all-gather.7.cloned.1.call-done
  82.8 9.9 fusion.44.refs_0_
  92.7 19.6 %collective-permute-done = bf16[512,3072]{1,0:T(8,128)(2,1)} collective-permute-done((bf16[512,3072]{1,0:T(8,128)(2,1)}, bf16[512,3072]{1,0:T(8,128)(2,1)}, u32[]{:S(2)}, u32[]{:S(2)}) %collective-permute-start) | collective-permute-done | bytes 3145760 | tf_op jit(solution)/shard_map/ppermute | solution.py:55
  123.1 7.1 collective-permute-start.4
  132.5 9.2 fusion.45.refs_1_
  141.7 49.1 %collective-permute-done.3 = bf16[512,3072]{1,0:T(8,128)(2,1)} collective-permute-done((bf16[512,3072]{1,0:T(8,128)(2,1)}, bf16[512,3072]{1,0:T(8,128)(2,1)}, u32[]{:S(2)}, u32[]{:S(2)}) %collective-permute-start.3) | collective-permute-done | bytes 3145760 | tf_op jit(solution)/shard_map/ppermute | solution.py:55
  194.1 9.3 collective-permute-start.7
  205.7 9.2 fusion.46.refs_2_
  214.9 45.1 %collective-permute-done.6 = bf16[512,3072]{1,0:T(8,128)(2,1)S(1)} collective-permute-done((bf16[512,3072]{1,0:T(8,128)(2,1)}, bf16[512,3072]{1,0:T(8,128)(2,1)S(1)}, u32[]{:S(2)}, u32[]{:S(2)}) %collective-permute-start.6) | collective-permute-done | bytes 3145760 | tf_op jit(solution)/shard_map/ppermute | solution.py:55
  266.3 8.1 fusion.47.refs_3_
  281.0 44.3 %shard_map.230 = (bf16[2048,768]{1,0:T(8,128)(2,1)}, bf16[2048,1280]{1,0:T(8,128)(2,1)}, f32[2,8,2048]{2,1,0:T(8,128)}) custom-call(s32[8]{0:T(128)} %dynamic-slice_bitcast_fusion.place_ref, f32[512,1280]{1,0:T(8,128)} %fusion.44.refs_0_, f32[512,1280]{1,0:T(8,128)} %fusion.45.refs_1_, f32[512,1280]{1,0:T(8,128)} %fusion.46.refs_2_, ...), custom_call_target="tpu_custom_call" | custom-call | flops 1 | bytes 1 | tf_op jit(solution)/shard_map/pallas_call | solution.py:580
  325.2 16.5 %collective-permute-done.8 = bf16[384,2048]{1,0:T(8,128)(2,1)} collective-permute-done((bf16[384,2048]{1,0:T(8,128)(2,1)}, bf16[384,2048]{1,0:T(8,128)(2,1)}, u32[]{:S(2)}, u32[]{:S(2)}) %collective-permute-start.8) | collective-permute-done | bytes 1572896 | tf_op jit(solution)/shard_map/ppermute | solution.py:55
  349.5 7.2 collective-permute-start.9
  356.8 6.9 convolution_convert_fusion.8
  363.6 57.4 %collective-permute-done.11 = bf16[384,4096]{1,0:T(8,128)(2,1)S(1)} collective-permute-done((bf16[384,4096]{1,0:T(8,128)(2,1)S(1)}, bf16[384,4096]{1,0:T(8,128)(2,1)S(1)}, u32[]{:S(2)}, u32[]{:S(2)}) %collective-permute-start.11) | collective-permute-done | bytes 3145760 | tf_op jit(solution)/shard_map/ppermute | solution.py:55
  428.6 6.7 add_convert_fusion.5
  447.4 7.0 convolution_convert_fusion.6
  454.4 50.9 %collective-permute-done.12 = bf16[512,3072]{1,0:T(8,128)(2,1)S(1)} collective-permute-done((bf16[512,3072]{1,0:T(8,128)(2,1)S(1)}, bf16[512,3072]{1,0:T(8,128)(2,1)S(1)}, u32[]{:S(2)}, u32[]{:S(2)}) %collective-permute-start.12) | collective-permute-done | bytes 3145760 | tf_op jit(solution)/shard_map/ppermute | solution.py:55
  524.7 16.8 %fusion.40.gm_ref = f32[1024,2048]{1,0:T(8,128)} fusion(bf16[3072,2048]{1,0:T(8,128)(2,1)S(1)} %bitcast.56, bf16[512,3072]{1,0:T(8,128)(2,1)S(1)} %add.136, bf16[512,3072]{1,0:T(8,128)(2,1)S(1)} %copy-done.25), kind=kOutput, calls=%fused_computation.111 | convolution fusion | flops 12897484800 | bytes 27262976 | tf_op jit(solution)/shard_map/dot_general | solution.py:25
  541.4 19.0 %fusion.39.gm_ref = f32[1024,2048]{1,0:T(8,128)} fusion(bf16[3072,2048]{1,0:T(8,128)(2,1)} %all-gather.15.cloned.1.call-done.refs_3_, bf16[512,3072]{1,0:T(8,128)(2,1)} %copy-done.34, bf16[512,3072]{1,0:T(8,128)(2,1)} %multiply_convert_fusion.2), kind=kOutput, calls=%fused_computation.110 | convolution fusion | flops 12897484800 | bytes 27262976 | tf_op jit(solution)/shard_map/dot_general | solution.py:25
  560.4 21.6 %collective-permute-done.15 = bf16[512,3072]{1,0:T(8,128)(2,1)} collective-permute-done((bf16[512,3072]{1,0:T(8,128)(2,1)}, bf16[512,3072]{1,0:T(8,128)(2,1)}, u32[]{:S(2)}, u32[]{:S(2)}) %collective-permute-start.15) | collective-permute-done | bytes 3145760 | tf_op jit(solution)/shard_map/ppermute | solution.py:55
  596.4 21.2 %shard_map.231 = (bf16[1024,2048]{1,0:T(8,128)(2,1)}, bf16[1024,2048]{1,0:T(8,128)(2,1)}, bf16[1024,2048]{1,0:T(8,128)(2,1)}) custom-call(bf16[512,3072]{1,0:T(8,128)(2,1)} %multiply_convert_fusion.1.x_ref, bf16[3072,4096]{1,0:T(8,128)(2,1)} %all-gather.13.cloned.1.call-done.gate_ref.up_ref.refs_4_.refs_6_, ...), custom_call_target="tpu_custom_call" | custom-call | flops 1 | bytes 1 | tf_op jit(solution)/shard_map/pallas_call | solution.py:355
  617.6 21.0 %shard_map.232 = (bf16[1024,2048]{1,0:T(8,128)(2,1)}, bf16[1024,2048]{1,0:T(8,128)(2,1)}, bf16[1024,2048]{1,0:T(8,128)(2,1)}) custom-call(bf16[512,3072]{1,0:T(8,128)(2,1)} %multiply_convert_fusion.1.x_ref, bf16[3072,4096]{1,0:T(8,128)(2,1)} %all-gather.17.cloned.1.call-done.gate_ref.up_ref.refs_5_.refs_7_, ...), custom_call_target="tpu_custom_call" | custom-call | flops 1 | bytes 1 | tf_op jit(solution)/shard_map/pallas_call | solution.py:355
  638.6 19.5 %shard_map.233.refs_0_ = f32[512,1536]{1,0:T(8,128)S(1)} custom-call(bf16[1024,2048]{1,0:T(8,128)(2,1)} %get-tuple-element.246.refs_0_.refs_1_, bf16[1024,2048]{1,0:T(8,128)(2,1)} %get-tuple-element.241.refs_1_, bf16[1024,2048]{1,0:T(8,128)(2,1)} %get-tuple-element.247.refs_2_, bf16[1024,2048]{1,0:T(8,128)(2,1)} %get-tuple-element.242.refs_3_.refs_2_, ...), custom_call_target="tpu_custom_call" | custom-call | flops 1 | bytes 1 | tf_op jit(solution)/shard_map/pallas_call | solution.py:386
  663.1 21.2 %shard_map.234 = (bf16[1024,2048]{1,0:T(8,128)(2,1)}, bf16[1024,2048]{1,0:T(8,128)(2,1)}, bf16[1024,2048]{1,0:T(8,128)(2,1)}) custom-call(bf16[512,3072]{1,0:T(8,128)(2,1)} %collective-permute-done.17.x_ref, ...), custom_call_target="tpu_custom_call", output_to_operand_aliasing={{0}: (4, {}), {1}: (5, {}), {2}: (6, {})} | custom-call | flops 1 | bytes 1 | tf_op jit(solution)/shard_map/pallas_call | solution.py:355
  684.3 17.9 %convolution_convert_fusion.5 = bf16[3072,2048]{1,0:T(8,128)(2,1)} fusion(bf16[1024,2048]{1,0:T(8,128)(2,1)} %get-tuple-element.243.refs_1_, bf16[512,3072]{1,0:T(8,128)(2,1)S(1)} %copy-done.35, bf16[512,3072]{1,0:T(8,128)(2,1)S(1)} %copy-done.26), kind=kOutput, calls=%fused_computation.22 | convolution fusion | flops 12903776256 | bytes 23068672 | tf_op jit(solution)/shard_map/dot_general | solution.py:25
  702.3 24.6 %shard_map.235 = (bf16[1024,2048]{1,0:T(8,128)(2,1)}, bf16[1024,2048]{1,0:T(8,128)(2,1)}, bf16[1024,2048]{1,0:T(8,128)(2,1)}) custom-call(bf16[512,3072]{1,0:T(8,128)(2,1)} %collective-permute-done.17.x_ref, ...), custom_call_target="tpu_custom_call", output_to_operand_aliasing={{0}: (4, {}), {1}: (5, {}), {2}: (6, {})} | custom-call | flops 1 | bytes 1 | tf_op jit(solution)/shard_map/pallas_call | solution.py:355
  726.9 21.5 %shard_map.236 = bf16[512,1536]{1,0:T(8,128)(2,1)} custom-call(bf16[1024,2048]{1,0:T(8,128)(2,1)} %get-tuple-element.284.refs_0_, bf16[1024,2048]{1,0:T(8,128)(2,1)} %get-tuple-element.256.refs_1_, bf16[1024,2048]{1,0:T(8,128)(2,1)} %get-tuple-element.275.refs_2_, bf16[1024,2048]{1,0:T(8,128)(2,1)} %get-tuple-element.253.refs_3_, ...), custom_call_target="tpu_custom_call" | custom-call | flops 1 | bytes 1 | tf_op jit(solution)/shard_map/pallas_call | solution.py:386
  748.4 19.9 %shard_map.237 = bf16[512,1536]{1,0:T(8,128)(2,1)S(1)} custom-call(bf16[1024,2048]{1,0:T(8,128)(2,1)} %get-tuple-element.284.refs_0_, bf16[1024,2048]{1,0:T(8,128)(2,1)} %get-tuple-element.256.refs_1_, bf16[1024,2048]{1,0:T(8,128)(2,1)} %get-tuple-element.275.refs_2_, bf16[1024,2048]{1,0:T(8,128)(2,1)} %get-tuple-element.253.refs_3_, ...), custom_call_target="tpu_custom_call" | custom-call | flops 1 | bytes 1 | tf_op jit(solution)/shard_map/pallas_call | solution.py:386
  769.5 19.0 %convolution_convert_fusion.4 = bf16[3072,2048]{1,0:T(8,128)(2,1)} fusion(bf16[1024,2048]{1,0:T(8,128)(2,1)S(1)} %copy-done.14, bf16[512,3072]{1,0:T(8,128)(2,1)} %collective-permute-done.17.x_ref, bf16[512,3072]{1,0:T(8,128)(2,1)} %multiply_convert_fusion.1.x_ref), kind=kOutput, calls=%fused_computation.21 | convolution fusion | flops 12903776256 | bytes 23068672 | tf_op jit(solution)/shard_map/dot_general | solution.py:25
  790.6 21.5 %shard_map.238.refs_1_ = f32[512,1536]{1,0:T(8,128)S(1)} custom-call(bf16[1024,2048]{1,0:T(8,128)(2,1)} %get-tuple-element.284.refs_0_, bf16[1024,2048]{1,0:T(8,128)(2,1)} %get-tuple-element.256.refs_1_, bf16[1024,2048]{1,0:T(8,128)(2,1)} %get-tuple-element.275.refs_2_, bf16[1024,2048]{1,0:T(8,128)(2,1)} %get-tuple-element.253.refs_3_, ...), custom_call_target="tpu_custom_call" | custom-call | flops 1 | bytes 1 | tf_op jit(solution)/shard_map/pallas_call | solution.py:386
  813.9 18.9 %convolution_convert_fusion.3 = bf16[3072,2048]{1,0:T(8,128)(2,1)} fusion(bf16[1024,2048]{1,0:T(8,128)(2,1)S(1)} %copy-done.13, bf16[512,3072]{1,0:T(8,128)(2,1)} %collective-permute-done.17.x_ref, bf16[512,3072]{1,0:T(8,128)(2,1)} %multiply_convert_fusion.1.x_ref), kind=kOutput, calls=%fused_computation.20 | convolution fusion | flops 12903776256 | bytes 23068672 | tf_op jit(solution)/shard_map/dot_general | solution.py:25
  837.3 10.6 shard_map.239
  853.8 21.9 %shard_map.240 = bf16[512,3072]{1,0:T(8,128)(2,1)} custom-call(bf16[1024,2048]{1,0:T(8,128)(2,1)} %get-tuple-element.274.refs_0_, bf16[1024,2048]{1,0:T(8,128)(2,1)} %get-tuple-element.243.refs_1_, bf16[3072,2048]{1,0:T(8,128)(2,1)} %all-gather.11.cloned.1.call-done.refs_2_, bf16[3072,2048]{1,0:T(8,128)(2,1)} %all-gather.15.cloned.1.call-done.refs_3_), custom_call_target="tpu_custom_call" | custom-call | flops 12884901888 | bytes 25165824 | tf_op jit(solution)/shard_map/pallas_call | solution.py:386
  875.7 7.0 convolution_convert_fusion.17.refs_0_
  882.7 17.7 %convolution_convert_fusion.2 = bf16[3072,2048]{1,0:T(8,128)(2,1)} fusion(bf16[1024,2048]{1,0:T(8,128)(2,1)S(1)} %copy-done.16, bf16[512,3072]{1,0:T(8,128)(2,1)} %copy-done.34, bf16[512,3072]{1,0:T(8,128)(2,1)S(1)} %copy-done.27), kind=kOutput, calls=%fused_computation.19 | convolution fusion | flops 12903776256 | bytes 23068672 | tf_op jit(solution)/shard_map/dot_general | solution.py:25
  900.4 10.8 collective-permute-done.20
  923.2 6.4 collective-permute-start.24
  935.5 22.8 %shard_map.241 = f32[512,3072]{1,0:T(8,128)} custom-call(bf16[1024,2048]{1,0:T(8,128)(2,1)} %get-tuple-element.274.refs_0_, bf16[1024,2048]{1,0:T(8,128)(2,1)} %get-tuple-element.243.refs_1_, bf16[3072,2048]{1,0:T(8,128)(2,1)} %all-gather.11.cloned.1.call-done.refs_2_, bf16[3072,2048]{1,0:T(8,128)(2,1)} %all-gather.15.cloned.1.call-done.refs_3_), custom_call_target="tpu_custom_call" | custom-call | flops 1 | bytes 1 | tf_op jit(solution)/shard_map/pallas_call | solution.py:386
  958.3 18.6 %convolution_convert_fusion.1 = bf16[3072,2048]{1,0:T(8,128)(2,1)} fusion(bf16[1024,2048]{1,0:T(8,128)(2,1)S(1)} %copy-done.12, bf16[512,3072]{1,0:T(8,128)(2,1)} %collective-permute-done.17.x_ref, bf16[512,3072]{1,0:T(8,128)(2,1)} %multiply_convert_fusion.1.x_ref), kind=kOutput, calls=%fused_computation.18 | convolution fusion | flops 12903776256 | bytes 23068672 | tf_op jit(solution)/shard_map/dot_general | solution.py:25
  980.9 7.2 collective-permute-done.23
  996.0 11.3 collective-permute-start.27
  1007.3 6.1 convolution_convert_fusion.15.refs_2_
  1013.4 18.6 %convolution_convert_fusion = bf16[3072,2048]{1,0:T(8,128)(2,1)} fusion(bf16[1024,2048]{1,0:T(8,128)(2,1)S(1)} %copy-done.11, bf16[512,3072]{1,0:T(8,128)(2,1)} %collective-permute-done.17.x_ref, bf16[512,3072]{1,0:T(8,128)(2,1)} %multiply_convert_fusion.1.x_ref), kind=kOutput, calls=%fused_computation.17 | convolution fusion | flops 12903776256 | bytes 23068672 | tf_op jit(solution)/shard_map/dot_general | solution.py:25
  1032.0 27.4 %collective-permute-done.26 = bf16[512,3072]{1,0:T(8,128)(2,1)} collective-permute-done((bf16[512,3072]{1,0:T(8,128)(2,1)}, bf16[512,3072]{1,0:T(8,128)(2,1)}, u32[]{:S(2)}, u32[]{:S(2)}) %collective-permute-start.26) | collective-permute-done | bytes 3145760 | tf_op jit(solution)/shard_map/ppermute | solution.py:55
  1079.7 55.5 %shard_map.242 = bf16[2048,1280]{1,0:T(8,128)(2,1)} custom-call(s32[8]{0:T(128)} %dynamic-slice_bitcast_fusion.place_ref, bf16[512,768]{1,0:T(8,128)(2,1)} %convolution_convert_fusion.17.refs_0_, bf16[512,768]{1,0:T(8,128)(2,1)} %convolution_convert_fusion.16.refs_1_, bf16[512,768]{1,0:T(8,128)(2,1)} %convolution_convert_fusion.15.refs_2_, ...), custom_call_target="tpu_custom_call" | custom-call | flops 32212254720 | bytes 26214400 | tf_op jit(solution)/shard_map/pallas_call | solution.py:711
  1138.2 9.6 convolution_convert_fusion.13
  1155.1 10.2 convolution_convert_fusion.12
  1165.3 21.7 %fusion.16 = bf16[3072,1280]{1,0:T(8,128)(2,1)} fusion(bf16[2048,1280]{1,0:T(8,128)(2,1)} %shard_map.242, bf16[512,3072]{1,0:T(8,128)(2,1)} %copy-done.32, bf16[512,3072]{1,0:T(8,128)(2,1)S(1)} %copy-done.31, bf16[512,3072]{1,0:T(8,128)(2,1)S(1)} %copy-done.29, bf16[512,3072]{1,0:T(8,128)(2,1)S(1)} %copy-done.24), kind=kOutput, calls=%fused_computation.16 | convolution fusion | flops 16160391168 | bytes 25690112 | tf_op jit(solution)/shard_map/dot_general | solution.py:25
  1187.0 30.6 %collective-permute-done.29 = bf16[512,3072]{1,0:T(8,128)(2,1)} collective-permute-done((bf16[512,3072]{1,0:T(8,128)(2,1)}, bf16[512,3072]{1,0:T(8,128)(2,1)}, u32[]{:S(2)}, u32[]{:S(2)}) %collective-permute-start.29) | collective-permute-done | bytes 3145760 | tf_op jit(solution)/shard_map/ppermute | solution.py:55
  1217.6 9.3 collective-permute-done.31
  1226.9 8.4 add_convert_fusion.2
  1242.3 10.0 convolution_convert_fusion.11
  1252.3 15.5 %fusion.22 = bf16[3072,768]{1,0:T(8,128)(2,1)} fusion(bf16[2048,768]{1,0:T(8,128)(2,1)} %get-tuple-element.307.refs_5_, bf16[512,3072]{1,0:T(8,128)(2,1)} %copy-done.37, bf16[512,3072]{1,0:T(8,128)(2,1)} %copy-done.36, bf16[512,3072]{1,0:T(8,128)(2,1)} %copy-done.33, bf16[512,3072]{1,0:T(8,128)(2,1)} %get-tuple-element.264), kind=kOutput, calls=%fused_computation.41 | convolution fusion | flops 9716367360 | bytes 20447232 | tf_op jit(solution)/shard_map/dot_general | solution.py:25
  1272.0 31.9 %collective-permute-done.32 = bf16[512,3072]{1,0:T(8,128)(2,1)} collective-permute-done((bf16[512,3072]{1,0:T(8,128)(2,1)}, bf16[512,3072]{1,0:T(8,128)(2,1)}, u32[]{:S(2)}, u32[]{:S(2)}) %collective-permute-start.32) | collective-permute-done | bytes 3145760 | tf_op jit(solution)/shard_map/ppermute | solution.py:55
  1304.0 8.3 collective-permute-done.34
  1312.3 8.5 add_convert_fusion
  1326.6 9.7 convolution_convert_fusion.10.refs_0_
  1357.0 7.0 multiply_convert_fusion
  1369.0 20.6 %collective-permute-done.35.refs_1_ = bf16[512,3072]{1,0:T(8,128)(2,1)} collective-permute-done((bf16[512,3072]{1,0:T(8,128)(2,1)}, bf16[512,3072]{1,0:T(8,128)(2,1)}, u32[]{:S(2)}, u32[]{:S(2)}) %collective-permute-start.35) | collective-permute-done | bytes 3145760 | tf_op jit(solution)/shard_map/ppermute | solution.py:55
  1395.4 9.4 shard_map.243
  1406.4 8.4 psum.7
  (276 shorter events, 268.3 us)
Async XLA Ops:
  7.2 75.6 %all-gather.7.cloned.1.call-start = ((), (), s32[]{:S(2)}) async-start(), calls=%async_computation.8 | async-start | bytes 8847360 | tf_op jit(solution)/shard_map/all_gather | solution.py:493
  30.2 244.1 %all-gather.9.cloned.1.call-start = ((), (), s32[]{:S(2)}) async-start(), calls=%async_computation.9 | async-start | bytes 5308416 | tf_op jit(solution)/shard_map/all_gather | solution.py:493
  43.6 68.7 %collective-permute-start = (bf16[512,3072]{1,0:T(8,128)(2,1)}, bf16[512,3072]{1,0:T(8,128)(2,1)}, u32[]{:S(2)}, u32[]{:S(2)}) collective-permute-start(bf16[512,3072]{1,0:T(8,128)(2,1)} %fusion.21), channel_id=1, source_target_pairs={{0,1},{1,2},{2,3},{4,5},{5,6},{6,7},{8,9},{9,10},{10,11},{12,13},{... | collective-permute-start | bytes 9437192 | tf_op jit(solution)/shard_map/ppermute | solution.py:55
  48.8 69.4 %collective-permute-start.1 = (bf16[512,3072]{1,0:T(8,128)(2,1)}, bf16[512,3072]{1,0:T(8,128)(2,1)}, u32[]{:S(2)}, u32[]{:S(2)}) collective-permute-start(bf16[512,3072]{1,0:T(8,128)(2,1)} %fusion.21), channel_id=1, source_target_pairs={{1,0},{2,1},{3,2},{5,4},{6,5},{7,6},{9,8},{10,9},{11,10},{13,12},{... | collective-permute-start | bytes 9437192 | tf_op jit(solution)/shard_map/ppermute | solution.py:55
  118.1 156.2 %all-gather.11.cloned.1.call-start = ((), (), s32[]{:S(2)}) async-start(), calls=%async_computation.10 | async-start | bytes 14155776 | tf_op jit(solution)/shard_map/all_gather | solution.py:493
  118.9 303.8 %all-gather.13.cloned.1.call-start = ((), (), s32[]{:S(2)}) async-start(), calls=%async_computation.11 | async-start | bytes 28311552 | tf_op jit(solution)/shard_map/all_gather | solution.py:493
  119.5 422.0 %all-gather.15.cloned.1.call-start = ((), (), s32[]{:S(2)}) async-start(), calls=%async_computation.12 | async-start | bytes 14155776 | tf_op jit(solution)/shard_map/all_gather | solution.py:493
  119.5 22.2 %collective-permute-start.2 = (bf16[512,3072]{1,0:T(8,128)(2,1)}, bf16[512,3072]{1,0:T(8,128)(2,1)}, u32[]{:S(2)}, u32[]{:S(2)}) collective-permute-start(bf16[512,3072]{1,0:T(8,128)(2,1)} %collective-permute-done), channel_id=1, source_target_pairs={{1,2},{2,3},{5,6},{6,7},{9,10},{10,11},{13,14},{14,15},{17,18},{18... | collective-permute-start | bytes 9437192 | tf_op jit(solution)/shard_map/ppermute | solution.py:55
  121.8 69.0 %collective-permute-start.3 = (bf16[512,3072]{1,0:T(8,128)(2,1)}, bf16[512,3072]{1,0:T(8,128)(2,1)}, u32[]{:S(2)}, u32[]{:S(2)}) collective-permute-start(bf16[512,3072]{1,0:T(8,128)(2,1)} %collective-permute-done.1), channel_id=1, source_target_pairs={{1,0},{2,1},{5,4},{6,5},{9,8},{10,9},{13,12},{14,13},{17,16},{18,1... | collective-permute-start | bytes 9437192 | tf_op jit(solution)/shard_map/ppermute | solution.py:55
  123.1 68.9 %collective-permute-start.4 = (bf16[512,3072]{1,0:T(8,128)(2,1)}, bf16[512,3072]{1,0:T(8,128)(2,1)}, u32[]{:S(2)}, u32[]{:S(2)}) collective-permute-start(bf16[512,3072]{1,0:T(8,128)(2,1)} %multiply_convert_fusion.2), channel_id=1, source_target_pairs={{0,1},{3,2},{4,5},{7,6},{8,9},{11,10},{12,13},{15,14},{16,17},{19,... | collective-permute-start | bytes 9437192 | tf_op jit(solution)/shard_map/ppermute | solution.py:55
  132.5 61.6 %copy-start.17 = (bf16[384,4096]{1,0:T(8,128)(2,1)S(1)}, bf16[384,4096]{1,0:T(8,128)(2,1)}, u32[]{:S(2)}) copy-start(bf16[384,4096]{1,0:T(8,128)(2,1)} %pad_maximum_fusion.2) | copy-start | bytes 9437188
  191.9 23.0 %collective-permute-start.5 = (bf16[512,3072]{1,0:T(8,128)(2,1)}, bf16[512,3072]{1,0:T(8,128)(2,1)S(1)}, u32[]{:S(2)}, u32[]{:S(2)}) collective-permute-start(bf16[512,3072]{1,0:T(8,128)(2,1)} %collective-permute-done.2), channel_id=1, source_target_pairs={{2,3},{6,7},{10,11},{14,15},{18,19},{22,23},{26,27},{30,31}} | collective-permute-start | bytes 9437192 | tf_op jit(solution)/shard_map/ppermute | solution.py:55
  192.8 67.2 %collective-permute-start.6 = (bf16[512,3072]{1,0:T(8,128)(2,1)}, bf16[512,3072]{1,0:T(8,128)(2,1)S(1)}, u32[]{:S(2)}, u32[]{:S(2)}) collective-permute-start(bf16[512,3072]{1,0:T(8,128)(2,1)} %collective-permute-done.3), channel_id=1, source_target_pairs={{1,0},{5,4},{9,8},{13,12},{17,16},{21,20},{25,24},{29,28}} | collective-permute-start | bytes 9437192 | tf_op jit(solution)/shard_map/ppermute | solution.py:55
  194.1 69.7 %collective-permute-start.7 = (bf16[384,4096]{1,0:T(8,128)(2,1)S(1)}, bf16[384,4096]{1,0:T(8,128)(2,1)}, u32[]{:S(2)}, u32[]{:S(2)}) collective-permute-start(bf16[384,4096]{1,0:T(8,128)(2,1)S(1)} %copy-done.17), channel_id=1, source_target_pairs={{3,1},{0,2},{7,5},{4,6},{11,9},{8,10},{15,13},{12,14},{19,17},{16,... | collective-permute-start | bytes 9437192 | tf_op jit(solution)/shard_map/ppermute | solution.py:55
  274.3 67.4 %collective-permute-start.8 = (bf16[384,2048]{1,0:T(8,128)(2,1)}, bf16[384,2048]{1,0:T(8,128)(2,1)}, u32[]{:S(2)}, u32[]{:S(2)}) collective-permute-start(bf16[384,2048]{1,0:T(8,128)(2,1)} %bitcast.58), channel_id=1, source_target_pairs={{3,1},{0,2},{2,0},{1,3},{7,5},{4,6},{6,4},{5,7},{11,9},{8,10},{10,... | collective-permute-start | bytes 4718600 | tf_op jit(solution)/shard_map/ppermute | solution.py:55
  341.8 275.8 %all-gather.17.cloned.1.call-start = ((), (), s32[]{:S(2)}) async-start(), calls=%async_computation.13 | async-start | bytes 28311552 | tf_op jit(solution)/shard_map/all_gather | solution.py:493
  347.4 16.3 %collective-permute-start.10 = (bf16[512,3072]{1,0:T(8,128)(2,1)S(1)}, bf16[512,3072]{1,0:T(8,128)(2,1)S(1)}, u32[]{:S(2)}, u32[]{:S(2)}) collective-permute-start(bf16[512,3072]{1,0:T(8,128)(2,1)S(1)} %convolution_convert_fusion.9), channel_id=1, source_target_pairs={{3,2},{7,6},{11,10},{15,14},{19,18},{23,22},{27,26},{31,30}} | collective-permute-start | bytes 9437192 | tf_op jit(solution)/shard_map/ppermute | solution.py:55
  348.2 72.8 %collective-permute-start.11 = (bf16[384,4096]{1,0:T(8,128)(2,1)S(1)}, bf16[384,4096]{1,0:T(8,128)(2,1)S(1)}, u32[]{:S(2)}, u32[]{:S(2)}) collective-permute-start(bf16[384,4096]{1,0:T(8,128)(2,1)S(1)} %copy-done.18), channel_id=1, source_target_pairs={{2,0},{1,3},{6,4},{5,7},{10,8},{9,11},{14,12},{13,15},{18,16},{17,... | collective-permute-start | bytes 9437192 | tf_op jit(solution)/shard_map/ppermute | solution.py:55
  349.5 73.1 %collective-permute-start.9 = (bf16[512,3072]{1,0:T(8,128)(2,1)S(1)}, bf16[512,3072]{1,0:T(8,128)(2,1)}, u32[]{:S(2)}, u32[]{:S(2)}) collective-permute-start(bf16[512,3072]{1,0:T(8,128)(2,1)S(1)} %convolution_convert_fusion.9), channel_id=1, source_target_pairs={{0,1},{4,5},{8,9},{12,13},{16,17},{20,21},{24,25},{28,29}} | collective-permute-start | bytes 9437192 | tf_op jit(solution)/shard_map/ppermute | solution.py:55
  363.6 57.4 %copy-start.39 = (bf16[512,3072]{1,0:T(8,128)(2,1)}, bf16[512,3072]{1,0:T(8,128)(2,1)S(1)}, u32[]{:S(2)}) copy-start(bf16[512,3072]{1,0:T(8,128)(2,1)S(1)} %collective-permute-done.10) | copy-start | bytes 9437188
  428.6 548.4 %reduce-scatter.11.cloned.1.call-start = ((), (), s32[]{:S(2)}) async-start(), calls=%async_computation.15 | async-start | bytes 14155776 | tf_op jit(solution)/shard_map/reduce_scatter | solution.py:658
  435.3 69.9 %collective-permute-start.12 = (bf16[512,3072]{1,0:T(8,128)(2,1)S(1)}, bf16[512,3072]{1,0:T(8,128)(2,1)S(1)}, u32[]{:S(2)}, u32[]{:S(2)}) collective-permute-start(bf16[512,3072]{1,0:T(8,128)(2,1)S(1)} %add_convert_fusion.5), channel_id=1, source_target_pairs={{0,1},{1,2},{4,5},{5,6},{8,9},{9,10},{12,13},{13,14},{16,17},{17,1... | collective-permute-start | bytes 9437192 | tf_op jit(solution)/shard_map/ppermute | solution.py:55
  439.2 66.0 %collective-permute-start.13 = (bf16[512,3072]{1,0:T(8,128)(2,1)S(1)}, bf16[512,3072]{1,0:T(8,128)(2,1)S(1)}, u32[]{:S(2)}, u32[]{:S(2)}) collective-permute-start(bf16[512,3072]{1,0:T(8,128)(2,1)S(1)} %add_convert_fusion.5), channel_id=1, source_target_pairs={{3,2},{2,1},{7,6},{6,5},{11,10},{10,9},{15,14},{14,13},{19,18},{18... | collective-permute-start | bytes 9437192 | tf_op jit(solution)/shard_map/ppermute | solution.py:55
  440.1 70.3 %collective-permute-start.14 = (bf16[512,3072]{1,0:T(8,128)(2,1)S(1)}, bf16[512,3072]{1,0:T(8,128)(2,1)S(1)}, u32[]{:S(2)}, u32[]{:S(2)}) collective-permute-start(bf16[512,3072]{1,0:T(8,128)(2,1)S(1)} %copy-done.25), channel_id=1, source_target_pairs={{1,0},{2,3},{5,4},{6,7},{9,8},{10,11},{13,12},{14,15},{17,16},{18,... | collective-permute-start | bytes 9437192 | tf_op jit(solution)/shard_map/ppermute | solution.py:55
  447.3 63.1 %copy-start.19 = (bf16[512,3072]{1,0:T(8,128)(2,1)S(1)}, bf16[512,3072]{1,0:T(8,128)(2,1)}, u32[]{:S(2)}) copy-start(bf16[512,3072]{1,0:T(8,128)(2,1)} %convolution_convert_fusion.8) | copy-start | bytes 9437188
  514.8 67.2 %collective-permute-start.15 = (bf16[512,3072]{1,0:T(8,128)(2,1)}, bf16[512,3072]{1,0:T(8,128)(2,1)}, u32[]{:S(2)}, u32[]{:S(2)}) collective-permute-start(bf16[512,3072]{1,0:T(8,128)(2,1)} %get-tuple-element.221), channel_id=1, source_target_pairs={{0,1},{1,2},{2,3},{4,5},{5,6},{6,7},{8,9},{9,10},{10,11},{12,13},{... | collective-permute-start | bytes 9437192 | tf_op jit(solution)/shard_map/ppermute | solution.py:55
  518.3 69.5 %collective-permute-start.16 = (bf16[512,3072]{1,0:T(8,128)(2,1)}, bf16[512,3072]{1,0:T(8,128)(2,1)}, u32[]{:S(2)}, u32[]{:S(2)}) collective-permute-start(bf16[512,3072]{1,0:T(8,128)(2,1)} %get-tuple-element.222), channel_id=1, source_target_pairs={{3,2},{2,1},{1,0},{7,6},{6,5},{5,4},{11,10},{10,9},{9,8},{15,14},{... | collective-permute-start | bytes 9437192 | tf_op jit(solution)/shard_map/ppermute | solution.py:55
  541.4 46.4 %copy-start.23 = (bf16[512,3072]{1,0:T(8,128)(2,1)S(1)}, bf16[512,3072]{1,0:T(8,128)(2,1)}, u32[]{:S(2)}) copy-start(bf16[512,3072]{1,0:T(8,128)(2,1)} %convolution_convert_fusion.6) | copy-start | bytes 9437188
  560.4 32.3 %copy-start.9 = (f32[1,3072]{1,0:T(1,128)S(1)}, f32[1,3072]{1,0:T(1,128)}, u32[]{:S(2)}) copy-start(f32[1,3072]{1,0:T(1,128)} %get-tuple-element.388.gain_ref) | copy-start | bytes 36868
  596.4 66.7 %collective-permute-start.17 = (bf16[512,3072]{1,0:T(8,128)(2,1)}, bf16[512,3072]{1,0:T(8,128)(2,1)}, u32[]{:S(2)}, u32[]{:S(2)}) collective-permute-start(bf16[512,3072]{1,0:T(8,128)(2,1)} %multiply_convert_fusion.1.x_ref), channel_id=1, source_target_pairs={{0,1},{3,2},{1,0},{2,3},{4,5},{7,6},{5,4},{6,7},{8,9},{11,10},{9,8... | collective-permute-start | bytes 9437192 | tf_op jit(solution)/shard_map/ppermute | solution.py:55
  663.1 21.2 %copy-start.26 = (bf16[512,3072]{1,0:T(8,128)(2,1)S(1)}, bf16[512,3072]{1,0:T(8,128)(2,1)}, u32[]{:S(2)}) copy-start(bf16[512,3072]{1,0:T(8,128)(2,1)} %multiply_convert_fusion.2) | copy-start | bytes 9437188
  663.1 21.2 %copy-start.35 = (bf16[512,3072]{1,0:T(8,128)(2,1)S(1)}, bf16[512,3072]{1,0:T(8,128)(2,1)}, u32[]{:S(2)}) copy-start(bf16[512,3072]{1,0:T(8,128)(2,1)} %copy-done.34) | copy-start | bytes 9437188
  702.2 274.7 %reduce-scatter.13.cloned.1.call-start = ((), (), s32[]{:S(2)}) async-start(), calls=%async_computation.16 | async-start | bytes 14155776 | tf_op jit(solution)/shard_map/reduce_scatter | solution.py:658
  748.4 21.1 %copy-start.14 = (bf16[1024,2048]{1,0:T(8,128)(2,1)S(1)}, bf16[1024,2048]{1,0:T(8,128)(2,1)}, u32[]{:S(2)}) copy-start(bf16[1024,2048]{1,0:T(8,128)(2,1)} %get-tuple-element.253.refs_3_) | copy-start | bytes 12582916
  748.4 40.1 %collective-permute-start.18 = (bf16[512,1536]{1,0:T(8,128)(2,1)}, bf16[512,1536]{1,0:T(8,128)(2,1)}, u32[]{:S(2)}, u32[]{:S(2)}) collective-permute-start(bf16[512,1536]{1,0:T(8,128)(2,1)} %shard_map.236), channel_id=1, source_target_pairs={{0,1},{3,2},{1,0},{2,3},{4,5},{7,6},{5,4},{6,7},{8,9},{11,10},{9,8... | collective-permute-start | bytes 4718600 | tf_op jit(solution)/shard_map/ppermute | solution.py:55
  788.6 286.6 %reduce-scatter.9.cloned.1.call-start = ((), (), s32[]{:S(2)}) async-start(), calls=%async_computation.14 | async-start | bytes 14155776 | tf_op jit(solution)/shard_map/reduce_scatter | solution.py:658
  788.6 25.3 %copy-start.13 = (bf16[1024,2048]{1,0:T(8,128)(2,1)S(1)}, bf16[1024,2048]{1,0:T(8,128)(2,1)}, u32[]{:S(2)}) copy-start(bf16[1024,2048]{1,0:T(8,128)(2,1)} %get-tuple-element.256.refs_1_) | copy-start | bytes 12582916
  788.6 44.2 %collective-permute-start.19 = (bf16[512,1536]{1,0:T(8,128)(2,1)}, bf16[512,1536]{1,0:T(8,128)(2,1)}, u32[]{:S(2)}, u32[]{:S(2)}) collective-permute-start(bf16[512,1536]{1,0:T(8,128)(2,1)} %copy-done.6), channel_id=1, source_target_pairs={{0,1},{3,2},{1,0},{2,3},{4,5},{7,6},{5,4},{6,7},{8,9},{11,10},{9,8... | collective-permute-start | bytes 4718600 | tf_op jit(solution)/shard_map/ppermute | solution.py:55
  832.9 305.4 %reduce-scatter.15.cloned.1.call-start = ((), (), s32[]{:S(2)}) async-start(), calls=%async_computation.17 | async-start | bytes 14155776 | tf_op jit(solution)/shard_map/reduce_scatter | solution.py:658
  848.0 63.2 %collective-permute-start.20 = (bf16[512,3072]{1,0:T(8,128)(2,1)}, bf16[512,3072]{1,0:T(8,128)(2,1)}, u32[]{:S(2)}, u32[]{:S(2)}) collective-permute-start(bf16[512,3072]{1,0:T(8,128)(2,1)} %get-tuple-element.264), channel_id=1, source_target_pairs={{0,1},{1,2},{2,3},{4,5},{5,6},{6,7},{8,9},{9,10},{10,11},{12,13},{... | collective-permute-start | bytes 9437192 | tf_op jit(solution)/shard_map/ppermute | solution.py:55
  852.5 64.4 %collective-permute-start.21 = (bf16[512,3072]{1,0:T(8,128)(2,1)}, bf16[512,3072]{1,0:T(8,128)(2,1)}, u32[]{:S(2)}, u32[]{:S(2)}) collective-permute-start(bf16[512,3072]{1,0:T(8,128)(2,1)} %get-tuple-element.264), channel_id=1, source_target_pairs={{1,0},{2,1},{3,2},{5,4},{6,5},{7,6},{9,8},{10,9},{11,10},{13,12},{... | collective-permute-start | bytes 9437192 | tf_op jit(solution)/shard_map/ppermute | solution.py:55
  917.0 309.9 %reduce-scatter.17.cloned.1.call-start = ((), (), s32[]{:S(2)}) async-start(), calls=%async_computation.18 | async-start | bytes 14155776 | tf_op jit(solution)/shard_map/reduce_scatter | solution.py:658
  917.0 63.9 %collective-permute-start.22 = (bf16[512,3072]{1,0:T(8,128)(2,1)}, bf16[512,3072]{1,0:T(8,128)(2,1)}, u32[]{:S(2)}, u32[]{:S(2)}) collective-permute-start(bf16[512,3072]{1,0:T(8,128)(2,1)} %collective-permute-done.20), channel_id=1, source_target_pairs={{1,2},{2,3},{5,6},{6,7},{9,10},{10,11},{13,14},{14,15},{17,18},{18... | collective-permute-start | bytes 9437192 | tf_op jit(solution)/shard_map/ppermute | solution.py:55
  921.9 66.2 %collective-permute-start.23 = (bf16[512,3072]{1,0:T(8,128)(2,1)}, bf16[512,3072]{1,0:T(8,128)(2,1)}, u32[]{:S(2)}, u32[]{:S(2)}) collective-permute-start(bf16[512,3072]{1,0:T(8,128)(2,1)} %collective-permute-done.21), channel_id=1, source_target_pairs={{1,0},{2,1},{5,4},{6,5},{9,8},{10,9},{13,12},{14,13},{17,16},{18,1... | collective-permute-start | bytes 9437192 | tf_op jit(solution)/shard_map/ppermute | solution.py:55
  923.2 66.1 %collective-permute-start.24 = (bf16[512,3072]{1,0:T(8,128)(2,1)}, bf16[512,3072]{1,0:T(8,128)(2,1)}, u32[]{:S(2)}, u32[]{:S(2)}) collective-permute-start(bf16[512,3072]{1,0:T(8,128)(2,1)} %shard_map.240), channel_id=1, source_target_pairs={{0,1},{3,2},{4,5},{7,6},{8,9},{11,10},{12,13},{15,14},{16,17},{19,... | collective-permute-start | bytes 9437192 | tf_op jit(solution)/shard_map/ppermute | solution.py:55
  935.5 22.8 %copy-start.12 = (bf16[1024,2048]{1,0:T(8,128)(2,1)S(1)}, bf16[1024,2048]{1,0:T(8,128)(2,1)}, u32[]{:S(2)}) copy-start(bf16[1024,2048]{1,0:T(8,128)(2,1)} %get-tuple-element.275.refs_2_) | copy-start | bytes 12582916
  989.4 282.7 %reduce-scatter.19.cloned.1.call-start = ((), (), s32[]{:S(2)}) async-start(), calls=%async_computation.19 | async-start | bytes 14155776 | tf_op jit(solution)/shard_map/reduce_scatter | solution.py:658
  989.4 42.6 %collective-permute-start.25 = (bf16[512,3072]{1,0:T(8,128)(2,1)}, bf16[512,3072]{1,0:T(8,128)(2,1)}, u32[]{:S(2)}, u32[]{:S(2)}) collective-permute-start(bf16[512,3072]{1,0:T(8,128)(2,1)} %collective-permute-done.22), channel_id=1, source_target_pairs={{2,3},{6,7},{10,11},{14,15},{18,19},{22,23},{26,27},{30,31}} | collective-permute-start | bytes 9437192 | tf_op jit(solution)/shard_map/ppermute | solution.py:55
  994.4 64.9 %collective-permute-start.26 = (bf16[512,3072]{1,0:T(8,128)(2,1)}, bf16[512,3072]{1,0:T(8,128)(2,1)}, u32[]{:S(2)}, u32[]{:S(2)}) collective-permute-start(bf16[512,3072]{1,0:T(8,128)(2,1)} %collective-permute-done.23), channel_id=1, source_target_pairs={{1,0},{5,4},{9,8},{13,12},{17,16},{21,20},{25,24},{29,28}} | collective-permute-start | bytes 9437192 | tf_op jit(solution)/shard_map/ppermute | solution.py:55
  996.0 68.7 %collective-permute-start.27 = (bf16[384,4096]{1,0:T(8,128)(2,1)}, bf16[384,4096]{1,0:T(8,128)(2,1)}, u32[]{:S(2)}, u32[]{:S(2)}) collective-permute-start(bf16[384,4096]{1,0:T(8,128)(2,1)} %pad_maximum_fusion.3), channel_id=1, source_target_pairs={{0,2},{3,1},{4,6},{7,5},{8,10},{11,9},{12,14},{15,13},{16,18},{19,... | collective-permute-start | bytes 9437192 | tf_op jit(solution)/shard_map/ppermute | solution.py:55
  1064.7 299.3 %reduce-scatter.21.cloned.1.call-start = ((), (), s32[]{:S(2)}) async-start(), calls=%async_computation.20 | async-start | bytes 8847360 | tf_op jit(solution)/shard_map/reduce_scatter | solution.py:658
  1075.2 63.1 %collective-permute-start.28 = (bf16[384,2048]{1,0:T(8,128)(2,1)}, bf16[384,2048]{1,0:T(8,128)(2,1)}, u32[]{:S(2)}, u32[]{:S(2)}) collective-permute-start(bf16[384,2048]{1,0:T(8,128)(2,1)} %reduce-scatter.9.cloned.1.call-done), channel_id=1, source_target_pairs={{0,2},{3,1},{1,3},{2,0},{4,6},{7,5},{5,7},{6,4},{8,10},{11,9},{9,1... | collective-permute-start | bytes 4718600 | tf_op jit(solution)/shard_map/ppermute | solution.py:55
  1147.8 69.7 %collective-permute-start.29 = (bf16[512,3072]{1,0:T(8,128)(2,1)}, bf16[512,3072]{1,0:T(8,128)(2,1)}, u32[]{:S(2)}, u32[]{:S(2)}) collective-permute-start(bf16[512,3072]{1,0:T(8,128)(2,1)} %convolution_convert_fusion.13), channel_id=1, source_target_pairs={{0,1},{4,5},{8,9},{12,13},{16,17},{20,21},{24,25},{28,29}} | collective-permute-start | bytes 9437192 | tf_op jit(solution)/shard_map/ppermute | solution.py:55
  1151.1 66.4 %collective-permute-start.30 = (bf16[512,3072]{1,0:T(8,128)(2,1)}, bf16[512,3072]{1,0:T(8,128)(2,1)}, u32[]{:S(2)}, u32[]{:S(2)}) collective-permute-start(bf16[512,3072]{1,0:T(8,128)(2,1)} %convolution_convert_fusion.13), channel_id=1, source_target_pairs={{3,2},{7,6},{11,10},{15,14},{19,18},{23,22},{27,26},{31,30}} | collective-permute-start | bytes 9437192 | tf_op jit(solution)/shard_map/ppermute | solution.py:55
  1153.6 73.2 %collective-permute-start.31 = (bf16[384,4096]{1,0:T(8,128)(2,1)}, bf16[384,4096]{1,0:T(8,128)(2,1)}, u32[]{:S(2)}, u32[]{:S(2)}) collective-permute-start(bf16[384,4096]{1,0:T(8,128)(2,1)} %pad_maximum_fusion.3), channel_id=1, source_target_pairs={{1,3},{2,0},{5,7},{6,4},{9,11},{10,8},{13,15},{14,12},{17,19},{18,... | collective-permute-start | bytes 9437192 | tf_op jit(solution)/shard_map/ppermute | solution.py:55
  1226.9 188.5 %reduce-scatter.23.cloned.1.call-start = ((), (), s32[]{:S(2)}) async-start(), calls=%async_computation.21 | async-start | bytes 5308416 | tf_op jit(solution)/shard_map/reduce_scatter | solution.py:658
  1235.3 68.6 %collective-permute-start.32 = (bf16[512,3072]{1,0:T(8,128)(2,1)}, bf16[512,3072]{1,0:T(8,128)(2,1)}, u32[]{:S(2)}, u32[]{:S(2)}) collective-permute-start(bf16[512,3072]{1,0:T(8,128)(2,1)} %add_convert_fusion.2), channel_id=1, source_target_pairs={{0,1},{1,2},{4,5},{5,6},{8,9},{9,10},{12,13},{13,14},{16,17},{17,1... | collective-permute-start | bytes 9437192 | tf_op jit(solution)/shard_map/ppermute | solution.py:55
  1238.4 65.6 %collective-permute-start.33 = (bf16[512,3072]{1,0:T(8,128)(2,1)}, bf16[512,3072]{1,0:T(8,128)(2,1)}, u32[]{:S(2)}, u32[]{:S(2)}) collective-permute-start(bf16[512,3072]{1,0:T(8,128)(2,1)} %add_convert_fusion.2), channel_id=1, source_target_pairs={{3,2},{2,1},{7,6},{6,5},{11,10},{10,9},{15,14},{14,13},{19,18},{18... | collective-permute-start | bytes 9437192 | tf_op jit(solution)/shard_map/ppermute | solution.py:55
  1240.8 71.5 %collective-permute-start.34 = (bf16[512,3072]{1,0:T(8,128)(2,1)}, bf16[512,3072]{1,0:T(8,128)(2,1)}, u32[]{:S(2)}, u32[]{:S(2)}) collective-permute-start(bf16[512,3072]{1,0:T(8,128)(2,1)} %shard_map.240), channel_id=1, source_target_pairs={{1,0},{2,3},{5,4},{6,7},{9,8},{10,11},{13,12},{14,15},{17,16},{18,... | collective-permute-start | bytes 9437192 | tf_op jit(solution)/shard_map/ppermute | solution.py:55
  1320.8 68.7 %collective-permute-start.35 = (bf16[512,3072]{1,0:T(8,128)(2,1)}, bf16[512,3072]{1,0:T(8,128)(2,1)}, u32[]{:S(2)}, u32[]{:S(2)}) collective-permute-start(bf16[512,3072]{1,0:T(8,128)(2,1)} %get-tuple-element.312), channel_id=1, source_target_pairs={{0,1},{1,2},{2,3},{4,5},{5,6},{6,7},{8,9},{9,10},{10,11},{12,13},{... | collective-permute-start | bytes 9437192 | tf_op jit(solution)/shard_map/ppermute | solution.py:55
  1325.1 70.2 %collective-permute-start.36 = (bf16[512,3072]{1,0:T(8,128)(2,1)}, bf16[512,3072]{1,0:T(8,128)(2,1)}, u32[]{:S(2)}, u32[]{:S(2)}) collective-permute-start(bf16[512,3072]{1,0:T(8,128)(2,1)} %get-tuple-element.313), channel_id=1, source_target_pairs={{3,2},{2,1},{1,0},{7,6},{6,5},{5,4},{11,10},{10,9},{9,8},{15,14},{... | collective-permute-start | bytes 9437192 | tf_op jit(solution)/shard_map/ppermute | solution.py:55
  1364.0 31.4 %copy-start.8 = (f32[1,3072]{1,0:T(1,128)S(1)}, f32[1,3072]{1,0:T(1,128)}, u32[]{:S(2)}) copy-start(f32[1,3072]{1,0:T(1,128)} %copy-done.7) | copy-start | bytes 36868
  1364.0 31.4 %copy-start.5 = (bf16[512,3072]{1,0:T(8,128)(2,1)S(1)}, bf16[512,3072]{1,0:T(8,128)(2,1)}, u32[]{:S(2)}) copy-start(bf16[512,3072]{1,0:T(8,128)(2,1)} %convolution_convert_fusion.10.refs_0_) | copy-start | bytes 9437188
  1395.3 19.4 %copy-start.49 = (bf16[1,384]{1,0:T(2,128)(2,1)S(1)}, bf16[1,384]{1,0:T(2,128)(2,1)}, u32[]{:S(2)}) copy-start(bf16[1,384]{1,0:T(2,128)(2,1)} %copy-done.48) | copy-start | bytes 2308
  (46 other events, 332.6 us)
Sparse Core Ops, SparseCore 0:
  30.3 52.4 all-gather.6
  118.3 37.3 all-gather.8
  157.5 72.1 all-gather.10
  231.4 125.3 all-gather.12
  358.5 72.1 all-gather.14
  432.5 125.3 all-gather.16
  702.4 90.2 reduce-scatter.10
  796.2 92.3 reduce-scatter.12
  892.1 92.3 reduce-scatter.8
  987.9 92.3 reduce-scatter.14
  1083.8 92.3 reduce-scatter.16
  1179.6 92.3 reduce-scatter.18
  1275.5 69.4 reduce-scatter.20
  1348.6 53.8 reduce-scatter.22

commit v9 on v5

--- a/solution.py
+++ b/solution.py
@@ -429,7 +429,7 @@
 
 def norm_back(grads, source, gain, straight, mask, low):
     rows, width = source.shape
-    tile = 64 if rows % 64 == 0 else rows
+    tile = 128 if rows % 128 == 0 else rows
     block = lambda wide: pl.BlockSpec((tile, wide), lambda i: (i, 0))
     masked = mask is not None
     out_shape = [jax.ShapeDtypeStruct((rows, width), F32)] + [jax.ShapeDtypeStruct((rows, width), BF16)] * low

time: 1420 us -> 1410 us (level)
  transfers between devices with their start and end apart: 50 -> 50, of which waited for: 28 -> 27; matrix products, arithmetic and copies ran while one was open for 30% -> 30% of each run, Pallas kernels for 22% -> 22%
where the time goes in v9:
time: 1410 us
  waiting for transfers between devices  441 us (31%)
  Pallas kernels  339 us (24%)
  matrix products  309 us (22%)
  other arithmetic  121 us (9%)
  starting transfers between devices  113 us (8%)
  local copies, waits for them, and re-layouts  37.4 us (3%)
  blocking collectives  33.7 us (2%)
  between operations  15.6 us (1%)
    ppermute x37, waiting for transfers between devices, travel(): lax.ppermute(array, 'tensor', pairs)  401 us
    dot_general x26, matrix products, dot(): return lax.dot_general(a, b, dims, preferred_element_type=F32).astype(out)  309 us
    pallas_call x6, Pallas kernels, spread(): pl.pallas_call(functools.partial(spread_kernel, count), grid=(tiles,), in...  127 us
    ppermute x37, starting transfers between devices, travel(): lax.ppermute(array, 'tensor', pairs)  112 us
    pallas_call x4, Pallas kernels, gated(): pl.pallas_call(gated_kernel, grid=(tiles,), in_specs=[pl.BlockSpec((rows,...  88 us
    pallas_call x1, Pallas kernels, attention_back(): attend_back(after(slot_table, gate), *grad_attended, rotated, attended, l...  55.6 us
    pallas_call x1, Pallas kernels, attention(): return attend(slot_table, *projected, *tables)  44.1 us
  transfers between devices with their start and end apart: 50, of which 27 were waited for; matrix products, arithmetic and copies ran while one was open for 30% of the time, Pallas kernels for 22%

profile of v9, /device:TPU:0, one launch (start us, length us, event | category | flops | bytes accessed | tf_op | source)
XLA Modules:
  0.0 1409.2 jit_solution(1848861810976832996)
XLA Ops:
  9.4 10.4 all_gather.24
  30.2 13.4 all_gather.25
  71.9 10.8 all-gather.7.cloned.1.call-done
  82.8 9.9 fusion.44.refs_0_
  92.7 19.6 %collective-permute-done = bf16[512,3072]{1,0:T(8,128)(2,1)} collective-permute-done((bf16[512,3072]{1,0:T(8,128)(2,1)}, bf16[512,3072]{1,0:T(8,128)(2,1)}, u32[]{:S(2)}, u32[]{:S(2)}) %collective-permute-start) | collective-permute-done | bytes 3145760 | tf_op jit(solution)/shard_map/ppermute | solution.py:55
  123.1 7.1 collective-permute-start.4
  132.4 9.2 fusion.45.refs_1_
  141.6 49.1 %collective-permute-done.3 = bf16[512,3072]{1,0:T(8,128)(2,1)} collective-permute-done((bf16[512,3072]{1,0:T(8,128)(2,1)}, bf16[512,3072]{1,0:T(8,128)(2,1)}, u32[]{:S(2)}, u32[]{:S(2)}) %collective-permute-start.3) | collective-permute-done | bytes 3145760 | tf_op jit(solution)/shard_map/ppermute | solution.py:55
  194.1 9.3 collective-permute-start.7
  205.7 9.2 fusion.46.refs_2_
  214.9 45.2 %collective-permute-done.6 = bf16[512,3072]{1,0:T(8,128)(2,1)S(1)} collective-permute-done((bf16[512,3072]{1,0:T(8,128)(2,1)}, bf16[512,3072]{1,0:T(8,128)(2,1)S(1)}, u32[]{:S(2)}, u32[]{:S(2)}) %collective-permute-start.6) | collective-permute-done | bytes 3145760 | tf_op jit(solution)/shard_map/ppermute | solution.py:55
  266.2 8.0 fusion.47.refs_3_
  280.7 44.1 %shard_map.230 = (bf16[2048,768]{1,0:T(8,128)(2,1)}, bf16[2048,1280]{1,0:T(8,128)(2,1)}, f32[2,8,2048]{2,1,0:T(8,128)}) custom-call(s32[8]{0:T(128)} %dynamic-slice_bitcast_fusion.place_ref, f32[512,1280]{1,0:T(8,128)} %fusion.44.refs_0_, f32[512,1280]{1,0:T(8,128)} %fusion.45.refs_1_, f32[512,1280]{1,0:T(8,128)} %fusion.46.refs_2_, ...), custom_call_target="tpu_custom_call" | custom-call | flops 1 | bytes 1 | tf_op jit(solution)/shard_map/pallas_call | solution.py:580
  324.8 16.8 %collective-permute-done.8 = bf16[384,2048]{1,0:T(8,128)(2,1)} collective-permute-done((bf16[384,2048]{1,0:T(8,128)(2,1)}, bf16[384,2048]{1,0:T(8,128)(2,1)}, u32[]{:S(2)}, u32[]{:S(2)}) %collective-permute-start.8) | collective-permute-done | bytes 1572896 | tf_op jit(solution)/shard_map/ppermute | solution.py:55
  349.5 7.2 collective-permute-start.9
  356.6 6.9 convolution_convert_fusion.8
  363.5 57.5 %collective-permute-done.11 = bf16[384,4096]{1,0:T(8,128)(2,1)S(1)} collective-permute-done((bf16[384,4096]{1,0:T(8,128)(2,1)S(1)}, bf16[384,4096]{1,0:T(8,128)(2,1)S(1)}, u32[]{:S(2)}, u32[]{:S(2)}) %collective-permute-start.11) | collective-permute-done | bytes 3145760 | tf_op jit(solution)/shard_map/ppermute | solution.py:55
  428.6 6.7 add_convert_fusion.5
  447.3 7.0 convolution_convert_fusion.6
  454.3 50.9 %collective-permute-done.12 = bf16[512,3072]{1,0:T(8,128)(2,1)S(1)} collective-permute-done((bf16[512,3072]{1,0:T(8,128)(2,1)S(1)}, bf16[512,3072]{1,0:T(8,128)(2,1)S(1)}, u32[]{:S(2)}, u32[]{:S(2)}) %collective-permute-start.12) | collective-permute-done | bytes 3145760 | tf_op jit(solution)/shard_map/ppermute | solution.py:55
  524.7 16.9 %fusion.40.gm_ref = f32[1024,2048]{1,0:T(8,128)} fusion(bf16[3072,2048]{1,0:T(8,128)(2,1)S(1)} %bitcast.56, bf16[512,3072]{1,0:T(8,128)(2,1)S(1)} %add.134, bf16[512,3072]{1,0:T(8,128)(2,1)S(1)} %copy-done.25), kind=kOutput, calls=%fused_computation.112 | convolution fusion | flops 12897484800 | bytes 27262976 | tf_op jit(solution)/shard_map/dot_general | solution.py:25
  541.6 19.0 %fusion.39.gm_ref = f32[1024,2048]{1,0:T(8,128)} fusion(bf16[3072,2048]{1,0:T(8,128)(2,1)} %all-gather.15.cloned.1.call-done.refs_3_, bf16[512,3072]{1,0:T(8,128)(2,1)} %copy-done.31, bf16[512,3072]{1,0:T(8,128)(2,1)} %multiply_convert_fusion.2), kind=kOutput, calls=%fused_computation.111 | convolution fusion | flops 12897484800 | bytes 27262976 | tf_op jit(solution)/shard_map/dot_general | solution.py:25
  560.6 21.4 %collective-permute-done.15 = bf16[512,3072]{1,0:T(8,128)(2,1)} collective-permute-done((bf16[512,3072]{1,0:T(8,128)(2,1)}, bf16[512,3072]{1,0:T(8,128)(2,1)}, u32[]{:S(2)}, u32[]{:S(2)}) %collective-permute-start.15) | collective-permute-done | bytes 3145760 | tf_op jit(solution)/shard_map/ppermute | solution.py:55
  596.2 21.2 %shard_map.231 = (bf16[1024,2048]{1,0:T(8,128)(2,1)}, bf16[1024,2048]{1,0:T(8,128)(2,1)}, bf16[1024,2048]{1,0:T(8,128)(2,1)}) custom-call(bf16[512,3072]{1,0:T(8,128)(2,1)} %multiply_convert_fusion.1.x_ref, bf16[3072,4096]{1,0:T(8,128)(2,1)} %all-gather.13.cloned.1.call-done.gate_ref.up_ref.refs_4_.refs_6_, ...), custom_call_target="tpu_custom_call" | custom-call | flops 1 | bytes 1 | tf_op jit(solution)/shard_map/pallas_call | solution.py:355
  617.5 21.0 %shard_map.232 = (bf16[1024,2048]{1,0:T(8,128)(2,1)}, bf16[1024,2048]{1,0:T(8,128)(2,1)}, bf16[1024,2048]{1,0:T(8,128)(2,1)}) custom-call(bf16[512,3072]{1,0:T(8,128)(2,1)} %multiply_convert_fusion.1.x_ref, bf16[3072,4096]{1,0:T(8,128)(2,1)} %all-gather.17.cloned.1.call-done.gate_ref.up_ref.refs_5_.refs_7_, ...), custom_call_target="tpu_custom_call" | custom-call | flops 1 | bytes 1 | tf_op jit(solution)/shard_map/pallas_call | solution.py:355
  638.5 19.5 %shard_map.233.refs_0_ = f32[512,1536]{1,0:T(8,128)S(1)} custom-call(bf16[1024,2048]{1,0:T(8,128)(2,1)} %get-tuple-element.246.refs_0_.refs_1_, bf16[1024,2048]{1,0:T(8,128)(2,1)} %get-tuple-element.241.refs_1_, bf16[1024,2048]{1,0:T(8,128)(2,1)} %get-tuple-element.247.refs_2_, bf16[1024,2048]{1,0:T(8,128)(2,1)} %get-tuple-element.242.refs_3_.refs_2_, ...), custom_call_target="tpu_custom_call" | custom-call | flops 1 | bytes 1 | tf_op jit(solution)/shard_map/pallas_call | solution.py:386
  662.9 21.2 %shard_map.234 = (bf16[1024,2048]{1,0:T(8,128)(2,1)}, bf16[1024,2048]{1,0:T(8,128)(2,1)}, bf16[1024,2048]{1,0:T(8,128)(2,1)}) custom-call(bf16[512,3072]{1,0:T(8,128)(2,1)} %collective-permute-done.17.x_ref, ...), custom_call_target="tpu_custom_call", output_to_operand_aliasing={{0}: (4, {}), {1}: (5, {}), {2}: (6, {})} | custom-call | flops 1 | bytes 1 | tf_op jit(solution)/shard_map/pallas_call | solution.py:355
  684.1 18.0 %convolution_convert_fusion.5 = bf16[3072,2048]{1,0:T(8,128)(2,1)} fusion(bf16[1024,2048]{1,0:T(8,128)(2,1)} %get-tuple-element.243.refs_1_, bf16[512,3072]{1,0:T(8,128)(2,1)S(1)} %copy-done.32, bf16[512,3072]{1,0:T(8,128)(2,1)S(1)} %copy-done.26), kind=kOutput, calls=%fused_computation.23 | convolution fusion | flops 12903776256 | bytes 23068672 | tf_op jit(solution)/shard_map/dot_general | solution.py:25
  702.2 24.6 %shard_map.235 = (bf16[1024,2048]{1,0:T(8,128)(2,1)}, bf16[1024,2048]{1,0:T(8,128)(2,1)}, bf16[1024,2048]{1,0:T(8,128)(2,1)}) custom-call(bf16[512,3072]{1,0:T(8,128)(2,1)} %collective-permute-done.17.x_ref, ...), custom_call_target="tpu_custom_call", output_to_operand_aliasing={{0}: (4, {}), {1}: (5, {}), {2}: (6, {})} | custom-call | flops 1 | bytes 1 | tf_op jit(solution)/shard_map/pallas_call | solution.py:355
  726.8 21.4 %shard_map.236 = bf16[512,1536]{1,0:T(8,128)(2,1)} custom-call(bf16[1024,2048]{1,0:T(8,128)(2,1)} %get-tuple-element.284.refs_0_, bf16[1024,2048]{1,0:T(8,128)(2,1)} %get-tuple-element.256.refs_1_, bf16[1024,2048]{1,0:T(8,128)(2,1)} %get-tuple-element.275.refs_2_, bf16[1024,2048]{1,0:T(8,128)(2,1)} %get-tuple-element.253.refs_3_, ...), custom_call_target="tpu_custom_call" | custom-call | flops 1 | bytes 1 | tf_op jit(solution)/shard_map/pallas_call | solution.py:386
  748.3 19.9 %shard_map.237 = bf16[512,1536]{1,0:T(8,128)(2,1)S(1)} custom-call(bf16[1024,2048]{1,0:T(8,128)(2,1)} %get-tuple-element.284.refs_0_, bf16[1024,2048]{1,0:T(8,128)(2,1)} %get-tuple-element.256.refs_1_, bf16[1024,2048]{1,0:T(8,128)(2,1)} %get-tuple-element.275.refs_2_, bf16[1024,2048]{1,0:T(8,128)(2,1)} %get-tuple-element.253.refs_3_, ...), custom_call_target="tpu_custom_call" | custom-call | flops 1 | bytes 1 | tf_op jit(solution)/shard_map/pallas_call | solution.py:386
  769.4 18.9 %convolution_convert_fusion.4 = bf16[3072,2048]{1,0:T(8,128)(2,1)} fusion(bf16[1024,2048]{1,0:T(8,128)(2,1)S(1)} %copy-done.14, bf16[512,3072]{1,0:T(8,128)(2,1)} %collective-permute-done.17.x_ref, bf16[512,3072]{1,0:T(8,128)(2,1)} %multiply_convert_fusion.1.x_ref), kind=kOutput, calls=%fused_computation.22 | convolution fusion | flops 12903776256 | bytes 23068672 | tf_op jit(solution)/shard_map/dot_general | solution.py:25
  790.4 21.6 %shard_map.238.refs_1_ = f32[512,1536]{1,0:T(8,128)S(1)} custom-call(bf16[1024,2048]{1,0:T(8,128)(2,1)} %get-tuple-element.284.refs_0_, bf16[1024,2048]{1,0:T(8,128)(2,1)} %get-tuple-element.256.refs_1_, bf16[1024,2048]{1,0:T(8,128)(2,1)} %get-tuple-element.275.refs_2_, bf16[1024,2048]{1,0:T(8,128)(2,1)} %get-tuple-element.253.refs_3_, ...), custom_call_target="tpu_custom_call" | custom-call | flops 1 | bytes 1 | tf_op jit(solution)/shard_map/pallas_call | solution.py:386
  813.8 19.0 %convolution_convert_fusion.3 = bf16[3072,2048]{1,0:T(8,128)(2,1)} fusion(bf16[1024,2048]{1,0:T(8,128)(2,1)S(1)} %copy-done.13, bf16[512,3072]{1,0:T(8,128)(2,1)} %collective-permute-done.17.x_ref, bf16[512,3072]{1,0:T(8,128)(2,1)} %multiply_convert_fusion.1.x_ref), kind=kOutput, calls=%fused_computation.21 | convolution fusion | flops 12903776256 | bytes 23068672 | tf_op jit(solution)/shard_map/dot_general | solution.py:25
  837.3 10.5 shard_map.239
  853.6 21.9 %shard_map.240 = bf16[512,3072]{1,0:T(8,128)(2,1)} custom-call(bf16[1024,2048]{1,0:T(8,128)(2,1)} %get-tuple-element.274.refs_0_, bf16[1024,2048]{1,0:T(8,128)(2,1)} %get-tuple-element.243.refs_1_, bf16[3072,2048]{1,0:T(8,128)(2,1)} %all-gather.11.cloned.1.call-done.refs_2_, bf16[3072,2048]{1,0:T(8,128)(2,1)} %all-gather.15.cloned.1.call-done.refs_3_), custom_call_target="tpu_custom_call" | custom-call | flops 12884901888 | bytes 25165824 | tf_op jit(solution)/shard_map/pallas_call | solution.py:386
  875.5 7.0 convolution_convert_fusion.17.refs_0_
  882.5 17.6 %convolution_convert_fusion.2 = bf16[3072,2048]{1,0:T(8,128)(2,1)} fusion(bf16[1024,2048]{1,0:T(8,128)(2,1)S(1)} %copy-done.16, bf16[512,3072]{1,0:T(8,128)(2,1)} %copy-done.31, bf16[512,3072]{1,0:T(8,128)(2,1)S(1)} %copy-done.27), kind=kOutput, calls=%fused_computation.20 | convolution fusion | flops 12903776256 | bytes 23068672 | tf_op jit(solution)/shard_map/dot_general | solution.py:25
  900.1 11.0 collective-permute-done.20
  923.0 6.8 collective-permute-start.24
  935.7 22.9 %shard_map.241 = f32[512,3072]{1,0:T(8,128)} custom-call(bf16[1024,2048]{1,0:T(8,128)(2,1)} %get-tuple-element.274.refs_0_, bf16[1024,2048]{1,0:T(8,128)(2,1)} %get-tuple-element.243.refs_1_, bf16[3072,2048]{1,0:T(8,128)(2,1)} %all-gather.11.cloned.1.call-done.refs_2_, bf16[3072,2048]{1,0:T(8,128)(2,1)} %all-gather.15.cloned.1.call-done.refs_3_), custom_call_target="tpu_custom_call" | custom-call | flops 1 | bytes 1 | tf_op jit(solution)/shard_map/pallas_call | solution.py:386
  958.6 18.6 %convolution_convert_fusion.1 = bf16[3072,2048]{1,0:T(8,128)(2,1)} fusion(bf16[1024,2048]{1,0:T(8,128)(2,1)S(1)} %copy-done.12, bf16[512,3072]{1,0:T(8,128)(2,1)} %collective-permute-done.17.x_ref, bf16[512,3072]{1,0:T(8,128)(2,1)} %multiply_convert_fusion.1.x_ref), kind=kOutput, calls=%fused_computation.19 | convolution fusion | flops 12903776256 | bytes 23068672 | tf_op jit(solution)/shard_map/dot_general | solution.py:25
  981.2 7.2 collective-permute-done.23
  996.7 11.0 collective-permute-start.27
  1013.7 18.5 %convolution_convert_fusion = bf16[3072,2048]{1,0:T(8,128)(2,1)} fusion(bf16[1024,2048]{1,0:T(8,128)(2,1)S(1)} %copy-done.11, bf16[512,3072]{1,0:T(8,128)(2,1)} %collective-permute-done.17.x_ref, bf16[512,3072]{1,0:T(8,128)(2,1)} %multiply_convert_fusion.1.x_ref), kind=kOutput, calls=%fused_computation.18 | convolution fusion | flops 12903776256 | bytes 23068672 | tf_op jit(solution)/shard_map/dot_general | solution.py:25
  1032.2 27.5 %collective-permute-done.26 = bf16[512,3072]{1,0:T(8,128)(2,1)} collective-permute-done((bf16[512,3072]{1,0:T(8,128)(2,1)}, bf16[512,3072]{1,0:T(8,128)(2,1)}, u32[]{:S(2)}, u32[]{:S(2)}) %collective-permute-start.26) | collective-permute-done | bytes 3145760 | tf_op jit(solution)/shard_map/ppermute | solution.py:55
  1080.1 55.6 %shard_map.242 = bf16[2048,1280]{1,0:T(8,128)(2,1)} custom-call(s32[8]{0:T(128)} %dynamic-slice_bitcast_fusion.place_ref, bf16[512,768]{1,0:T(8,128)(2,1)} %convolution_convert_fusion.17.refs_0_, bf16[512,768]{1,0:T(8,128)(2,1)} %convolution_convert_fusion.16.refs_1_, bf16[512,768]{1,0:T(8,128)(2,1)} %convolution_convert_fusion.15.refs_2_, ...), custom_call_target="tpu_custom_call" | custom-call | flops 32212254720 | bytes 26214400 | tf_op jit(solution)/shard_map/pallas_call | solution.py:711
  1135.7 15.8 %fusion.22 = bf16[3072,768]{1,0:T(8,128)(2,1)} fusion(bf16[2048,768]{1,0:T(8,128)(2,1)} %get-tuple-element.294.refs_5_, bf16[512,3072]{1,0:T(8,128)(2,1)} %copy-done.37, bf16[512,3072]{1,0:T(8,128)(2,1)} %copy-done.34, bf16[512,3072]{1,0:T(8,128)(2,1)} %copy-done.33, bf16[512,3072]{1,0:T(8,128)(2,1)} %get-tuple-element.264), kind=kOutput, calls=%fused_computation.42 | convolution fusion | flops 9716367360 | bytes 20447232 | tf_op jit(solution)/shard_map/dot_general | solution.py:25
  1151.6 9.7 convolution_convert_fusion.13
  1168.0 20.7 %fusion.16 = bf16[3072,1280]{1,0:T(8,128)(2,1)S(1)} fusion(bf16[2048,1280]{1,0:T(8,128)(2,1)} %shard_map.242, bf16[512,3072]{1,0:T(8,128)(2,1)} %copy-done.30, bf16[512,3072]{1,0:T(8,128)(2,1)} %copy-done.29, bf16[512,3072]{1,0:T(8,128)(2,1)} %copy-done.28, bf16[512,3072]{1,0:T(8,128)(2,1)S(1)} %copy-done.24), kind=kOutput, calls=%fused_computation.17 | convolution fusion | flops 16160391168 | bytes 25690112 | tf_op jit(solution)/shard_map/dot_general | solution.py:25
  1188.7 8.9 pad_maximum_fusion
  1197.7 10.0 convolution_convert_fusion.12
  1207.7 13.3 collective-permute-done.29
  1220.9 9.2 collective-permute-done.31
  1230.1 8.1 add_convert_fusion.2
  1245.3 9.6 convolution_convert_fusion.11
  1254.9 17.1 %reduce-scatter.18.cloned.1.call-done = bf16[384,2048]{1,0:T(8,128)(2,1)} async-done(((bf16[3072,2048]{1,0:T(8,128)(2,1)}), bf16[384,2048]{1,0:T(8,128)(2,1)}) %reduce-scatter.18.cloned.1.call-update) | async-done | bytes 1572880 | tf_op jit(solution)/shard_map/reduce_scatter | solution.py:658
  1272.0 25.3 %collective-permute-done.32 = bf16[512,3072]{1,0:T(8,128)(2,1)} collective-permute-done((bf16[512,3072]{1,0:T(8,128)(2,1)}, bf16[512,3072]{1,0:T(8,128)(2,1)}, u32[]{:S(2)}, u32[]{:S(2)}) %collective-permute-start.32) | collective-permute-done | bytes 3145760 | tf_op jit(solution)/shard_map/ppermute | solution.py:55
  1297.3 8.1 collective-permute-done.34
  1305.4 8.1 add_convert_fusion
  1319.6 10.0 convolution_convert_fusion.10.refs_0_
  1357.3 10.6 reduce-scatter.20.cloned.1.call-done.x_ref
  1380.6 10.0 psum.7
  1393.1 9.3 shard_map.244
  (270 shorter events, 271.9 us)
Async XLA Ops:
  7.2 75.6 %all-gather.7.cloned.1.call-start = ((), (), s32[]{:S(2)}) async-start(), calls=%async_computation.7 | async-start | bytes 8847360 | tf_op jit(solution)/shard_map/all_gather | solution.py:493
  30.1 244.0 %all-gather.9.cloned.1.call-start = ((), (), s32[]{:S(2)}) async-start(), calls=%async_computation.8 | async-start | bytes 5308416 | tf_op jit(solution)/shard_map/all_gather | solution.py:493
  43.6 68.7 %collective-permute-start = (bf16[512,3072]{1,0:T(8,128)(2,1)}, bf16[512,3072]{1,0:T(8,128)(2,1)}, u32[]{:S(2)}, u32[]{:S(2)}) collective-permute-start(bf16[512,3072]{1,0:T(8,128)(2,1)} %fusion.21), channel_id=1, source_target_pairs={{0,1},{1,2},{2,3},{4,5},{5,6},{6,7},{8,9},{9,10},{10,11},{12,13},{... | collective-permute-start | bytes 9437192 | tf_op jit(solution)/shard_map/ppermute | solution.py:55
  48.7 69.4 %collective-permute-start.1 = (bf16[512,3072]{1,0:T(8,128)(2,1)}, bf16[512,3072]{1,0:T(8,128)(2,1)}, u32[]{:S(2)}, u32[]{:S(2)}) collective-permute-start(bf16[512,3072]{1,0:T(8,128)(2,1)} %fusion.21), channel_id=1, source_target_pairs={{1,0},{2,1},{3,2},{5,4},{6,5},{7,6},{9,8},{10,9},{11,10},{13,12},{... | collective-permute-start | bytes 9437192 | tf_op jit(solution)/shard_map/ppermute | solution.py:55
  118.1 156.1 %all-gather.11.cloned.1.call-start = ((), (), s32[]{:S(2)}) async-start(), calls=%async_computation.9 | async-start | bytes 14155776 | tf_op jit(solution)/shard_map/all_gather | solution.py:493
  118.8 303.8 %all-gather.13.cloned.1.call-start = ((), (), s32[]{:S(2)}) async-start(), calls=%async_computation.10 | async-start | bytes 28311552 | tf_op jit(solution)/shard_map/all_gather | solution.py:493
  119.4 422.2 %all-gather.15.cloned.1.call-start = ((), (), s32[]{:S(2)}) async-start(), calls=%async_computation.11 | async-start | bytes 14155776 | tf_op jit(solution)/shard_map/all_gather | solution.py:493
  119.5 22.2 %collective-permute-start.2 = (bf16[512,3072]{1,0:T(8,128)(2,1)}, bf16[512,3072]{1,0:T(8,128)(2,1)}, u32[]{:S(2)}, u32[]{:S(2)}) collective-permute-start(bf16[512,3072]{1,0:T(8,128)(2,1)} %collective-permute-done), channel_id=1, source_target_pairs={{1,2},{2,3},{5,6},{6,7},{9,10},{10,11},{13,14},{14,15},{17,18},{18... | collective-permute-start | bytes 9437192 | tf_op jit(solution)/shard_map/ppermute | solution.py:55
  121.8 68.9 %collective-permute-start.3 = (bf16[512,3072]{1,0:T(8,128)(2,1)}, bf16[512,3072]{1,0:T(8,128)(2,1)}, u32[]{:S(2)}, u32[]{:S(2)}) collective-permute-start(bf16[512,3072]{1,0:T(8,128)(2,1)} %collective-permute-done.1), channel_id=1, source_target_pairs={{1,0},{2,1},{5,4},{6,5},{9,8},{10,9},{13,12},{14,13},{17,16},{18,1... | collective-permute-start | bytes 9437192 | tf_op jit(solution)/shard_map/ppermute | solution.py:55
  123.1 68.8 %collective-permute-start.4 = (bf16[512,3072]{1,0:T(8,128)(2,1)}, bf16[512,3072]{1,0:T(8,128)(2,1)}, u32[]{:S(2)}, u32[]{:S(2)}) collective-permute-start(bf16[512,3072]{1,0:T(8,128)(2,1)} %multiply_convert_fusion.2), channel_id=1, source_target_pairs={{0,1},{3,2},{4,5},{7,6},{8,9},{11,10},{12,13},{15,14},{16,17},{19,... | collective-permute-start | bytes 9437192 | tf_op jit(solution)/shard_map/ppermute | solution.py:55
  132.4 61.7 %copy-start.17 = (bf16[384,4096]{1,0:T(8,128)(2,1)S(1)}, bf16[384,4096]{1,0:T(8,128)(2,1)}, u32[]{:S(2)}) copy-start(bf16[384,4096]{1,0:T(8,128)(2,1)} %pad_maximum_fusion.3) | copy-start | bytes 9437188
  191.9 23.0 %collective-permute-start.5 = (bf16[512,3072]{1,0:T(8,128)(2,1)}, bf16[512,3072]{1,0:T(8,128)(2,1)S(1)}, u32[]{:S(2)}, u32[]{:S(2)}) collective-permute-start(bf16[512,3072]{1,0:T(8,128)(2,1)} %collective-permute-done.2), channel_id=1, source_target_pairs={{2,3},{6,7},{10,11},{14,15},{18,19},{22,23},{26,27},{30,31}} | collective-permute-start | bytes 9437192 | tf_op jit(solution)/shard_map/ppermute | solution.py:55
  192.8 67.3 %collective-permute-start.6 = (bf16[512,3072]{1,0:T(8,128)(2,1)}, bf16[512,3072]{1,0:T(8,128)(2,1)S(1)}, u32[]{:S(2)}, u32[]{:S(2)}) collective-permute-start(bf16[512,3072]{1,0:T(8,128)(2,1)} %collective-permute-done.3), channel_id=1, source_target_pairs={{1,0},{5,4},{9,8},{13,12},{17,16},{21,20},{25,24},{29,28}} | collective-permute-start | bytes 9437192 | tf_op jit(solution)/shard_map/ppermute | solution.py:55
  194.1 69.6 %collective-permute-start.7 = (bf16[384,4096]{1,0:T(8,128)(2,1)S(1)}, bf16[384,4096]{1,0:T(8,128)(2,1)}, u32[]{:S(2)}, u32[]{:S(2)}) collective-permute-start(bf16[384,4096]{1,0:T(8,128)(2,1)S(1)} %copy-done.17), channel_id=1, source_target_pairs={{3,1},{0,2},{7,5},{4,6},{11,9},{8,10},{15,13},{12,14},{19,17},{16,... | collective-permute-start | bytes 9437192 | tf_op jit(solution)/shard_map/ppermute | solution.py:55
  274.2 67.5 %collective-permute-start.8 = (bf16[384,2048]{1,0:T(8,128)(2,1)}, bf16[384,2048]{1,0:T(8,128)(2,1)}, u32[]{:S(2)}, u32[]{:S(2)}) collective-permute-start(bf16[384,2048]{1,0:T(8,128)(2,1)} %bitcast.58), channel_id=1, source_target_pairs={{3,1},{0,2},{2,0},{1,3},{7,5},{4,6},{6,4},{5,7},{11,9},{8,10},{10,... | collective-permute-start | bytes 4718600 | tf_op jit(solution)/shard_map/ppermute | solution.py:55
  341.7 275.8 %all-gather.17.cloned.1.call-start = ((), (), s32[]{:S(2)}) async-start(), calls=%async_computation.12 | async-start | bytes 28311552 | tf_op jit(solution)/shard_map/all_gather | solution.py:493
  347.3 16.2 %collective-permute-start.10 = (bf16[512,3072]{1,0:T(8,128)(2,1)S(1)}, bf16[512,3072]{1,0:T(8,128)(2,1)S(1)}, u32[]{:S(2)}, u32[]{:S(2)}) collective-permute-start(bf16[512,3072]{1,0:T(8,128)(2,1)S(1)} %convolution_convert_fusion.9), channel_id=1, source_target_pairs={{3,2},{7,6},{11,10},{15,14},{19,18},{23,22},{27,26},{31,30}} | collective-permute-start | bytes 9437192 | tf_op jit(solution)/shard_map/ppermute | solution.py:55
  348.2 72.8 %collective-permute-start.11 = (bf16[384,4096]{1,0:T(8,128)(2,1)S(1)}, bf16[384,4096]{1,0:T(8,128)(2,1)S(1)}, u32[]{:S(2)}, u32[]{:S(2)}) collective-permute-start(bf16[384,4096]{1,0:T(8,128)(2,1)S(1)} %copy-done.18), channel_id=1, source_target_pairs={{2,0},{1,3},{6,4},{5,7},{10,8},{9,11},{14,12},{13,15},{18,16},{17,... | collective-permute-start | bytes 9437192 | tf_op jit(solution)/shard_map/ppermute | solution.py:55
  349.5 73.2 %collective-permute-start.9 = (bf16[512,3072]{1,0:T(8,128)(2,1)S(1)}, bf16[512,3072]{1,0:T(8,128)(2,1)}, u32[]{:S(2)}, u32[]{:S(2)}) collective-permute-start(bf16[512,3072]{1,0:T(8,128)(2,1)S(1)} %convolution_convert_fusion.9), channel_id=1, source_target_pairs={{0,1},{4,5},{8,9},{12,13},{16,17},{20,21},{24,25},{28,29}} | collective-permute-start | bytes 9437192 | tf_op jit(solution)/shard_map/ppermute | solution.py:55
  363.5 57.5 %copy-start.36 = (bf16[512,3072]{1,0:T(8,128)(2,1)}, bf16[512,3072]{1,0:T(8,128)(2,1)S(1)}, u32[]{:S(2)}) copy-start(bf16[512,3072]{1,0:T(8,128)(2,1)S(1)} %collective-permute-done.10) | copy-start | bytes 9437188
  428.5 548.7 %reduce-scatter.10.cloned.1.call-start = ((), (), s32[]{:S(2)}) async-start(), calls=%async_computation.14 | async-start | bytes 14155776 | tf_op jit(solution)/shard_map/reduce_scatter | solution.py:658
  435.2 69.9 %collective-permute-start.12 = (bf16[512,3072]{1,0:T(8,128)(2,1)S(1)}, bf16[512,3072]{1,0:T(8,128)(2,1)S(1)}, u32[]{:S(2)}, u32[]{:S(2)}) collective-permute-start(bf16[512,3072]{1,0:T(8,128)(2,1)S(1)} %add_convert_fusion.5), channel_id=1, source_target_pairs={{0,1},{1,2},{4,5},{5,6},{8,9},{9,10},{12,13},{13,14},{16,17},{17,1... | collective-permute-start | bytes 9437192 | tf_op jit(solution)/shard_map/ppermute | solution.py:55
  439.1 66.0 %collective-permute-start.13 = (bf16[512,3072]{1,0:T(8,128)(2,1)S(1)}, bf16[512,3072]{1,0:T(8,128)(2,1)S(1)}, u32[]{:S(2)}, u32[]{:S(2)}) collective-permute-start(bf16[512,3072]{1,0:T(8,128)(2,1)S(1)} %add_convert_fusion.5), channel_id=1, source_target_pairs={{3,2},{2,1},{7,6},{6,5},{11,10},{10,9},{15,14},{14,13},{19,18},{18... | collective-permute-start | bytes 9437192 | tf_op jit(solution)/shard_map/ppermute | solution.py:55
  440.0 70.3 %collective-permute-start.14 = (bf16[512,3072]{1,0:T(8,128)(2,1)S(1)}, bf16[512,3072]{1,0:T(8,128)(2,1)S(1)}, u32[]{:S(2)}, u32[]{:S(2)}) collective-permute-start(bf16[512,3072]{1,0:T(8,128)(2,1)S(1)} %copy-done.25), channel_id=1, source_target_pairs={{1,0},{2,3},{5,4},{6,7},{9,8},{10,11},{13,12},{14,15},{17,16},{18,... | collective-permute-start | bytes 9437192 | tf_op jit(solution)/shard_map/ppermute | solution.py:55
  447.3 63.1 %copy-start.19 = (bf16[512,3072]{1,0:T(8,128)(2,1)S(1)}, bf16[512,3072]{1,0:T(8,128)(2,1)}, u32[]{:S(2)}) copy-start(bf16[512,3072]{1,0:T(8,128)(2,1)} %convolution_convert_fusion.8) | copy-start | bytes 9437188
  514.7 67.2 %collective-permute-start.15 = (bf16[512,3072]{1,0:T(8,128)(2,1)}, bf16[512,3072]{1,0:T(8,128)(2,1)}, u32[]{:S(2)}, u32[]{:S(2)}) collective-permute-start(bf16[512,3072]{1,0:T(8,128)(2,1)} %get-tuple-element.221), channel_id=1, source_target_pairs={{0,1},{1,2},{2,3},{4,5},{5,6},{6,7},{8,9},{9,10},{10,11},{12,13},{... | collective-permute-start | bytes 9437192 | tf_op jit(solution)/shard_map/ppermute | solution.py:55
  518.2 69.5 %collective-permute-start.16 = (bf16[512,3072]{1,0:T(8,128)(2,1)}, bf16[512,3072]{1,0:T(8,128)(2,1)}, u32[]{:S(2)}, u32[]{:S(2)}) collective-permute-start(bf16[512,3072]{1,0:T(8,128)(2,1)} %get-tuple-element.222), channel_id=1, source_target_pairs={{3,2},{2,1},{1,0},{7,6},{6,5},{5,4},{11,10},{10,9},{9,8},{15,14},{... | collective-permute-start | bytes 9437192 | tf_op jit(solution)/shard_map/ppermute | solution.py:55
  541.6 46.1 %copy-start.23 = (bf16[512,3072]{1,0:T(8,128)(2,1)S(1)}, bf16[512,3072]{1,0:T(8,128)(2,1)}, u32[]{:S(2)}) copy-start(bf16[512,3072]{1,0:T(8,128)(2,1)} %convolution_convert_fusion.6) | copy-start | bytes 9437188
  560.6 32.0 %copy-start.9 = (f32[1,3072]{1,0:T(1,128)S(1)}, f32[1,3072]{1,0:T(1,128)}, u32[]{:S(2)}) copy-start(f32[1,3072]{1,0:T(1,128)} %get-tuple-element.388.gain_ref) | copy-start | bytes 36868
  596.2 66.7 %collective-permute-start.17 = (bf16[512,3072]{1,0:T(8,128)(2,1)}, bf16[512,3072]{1,0:T(8,128)(2,1)}, u32[]{:S(2)}, u32[]{:S(2)}) collective-permute-start(bf16[512,3072]{1,0:T(8,128)(2,1)} %multiply_convert_fusion.1.x_ref), channel_id=1, source_target_pairs={{0,1},{3,2},{1,0},{2,3},{4,5},{7,6},{5,4},{6,7},{8,9},{11,10},{9,8... | collective-permute-start | bytes 9437192 | tf_op jit(solution)/shard_map/ppermute | solution.py:55
  662.9 21.2 %copy-start.26 = (bf16[512,3072]{1,0:T(8,128)(2,1)S(1)}, bf16[512,3072]{1,0:T(8,128)(2,1)}, u32[]{:S(2)}) copy-start(bf16[512,3072]{1,0:T(8,128)(2,1)} %multiply_convert_fusion.2) | copy-start | bytes 9437188
  662.9 21.2 %copy-start.32 = (bf16[512,3072]{1,0:T(8,128)(2,1)S(1)}, bf16[512,3072]{1,0:T(8,128)(2,1)}, u32[]{:S(2)}) copy-start(bf16[512,3072]{1,0:T(8,128)(2,1)} %copy-done.31) | copy-start | bytes 9437188
  702.2 275.1 %reduce-scatter.12.cloned.1.call-start = ((), (), s32[]{:S(2)}) async-start(), calls=%async_computation.15 | async-start | bytes 14155776 | tf_op jit(solution)/shard_map/reduce_scatter | solution.py:658
  748.2 21.1 %copy-start.14 = (bf16[1024,2048]{1,0:T(8,128)(2,1)S(1)}, bf16[1024,2048]{1,0:T(8,128)(2,1)}, u32[]{:S(2)}) copy-start(bf16[1024,2048]{1,0:T(8,128)(2,1)} %get-tuple-element.253.refs_3_) | copy-start | bytes 12582916
  748.2 40.0 %collective-permute-start.18 = (bf16[512,1536]{1,0:T(8,128)(2,1)}, bf16[512,1536]{1,0:T(8,128)(2,1)}, u32[]{:S(2)}, u32[]{:S(2)}) collective-permute-start(bf16[512,1536]{1,0:T(8,128)(2,1)} %shard_map.236), channel_id=1, source_target_pairs={{0,1},{3,2},{1,0},{2,3},{4,5},{7,6},{5,4},{6,7},{8,9},{11,10},{9,8... | collective-permute-start | bytes 4718600 | tf_op jit(solution)/shard_map/ppermute | solution.py:55
  788.3 287.4 %reduce-scatter.8.cloned.1.call-start = ((), (), s32[]{:S(2)}) async-start(), calls=%async_computation.13 | async-start | bytes 14155776 | tf_op jit(solution)/shard_map/reduce_scatter | solution.py:658
  788.4 25.4 %copy-start.13 = (bf16[1024,2048]{1,0:T(8,128)(2,1)S(1)}, bf16[1024,2048]{1,0:T(8,128)(2,1)}, u32[]{:S(2)}) copy-start(bf16[1024,2048]{1,0:T(8,128)(2,1)} %get-tuple-element.256.refs_1_) | copy-start | bytes 12582916
  788.4 44.4 %collective-permute-start.19 = (bf16[512,1536]{1,0:T(8,128)(2,1)}, bf16[512,1536]{1,0:T(8,128)(2,1)}, u32[]{:S(2)}, u32[]{:S(2)}) collective-permute-start(bf16[512,1536]{1,0:T(8,128)(2,1)} %copy-done.6), channel_id=1, source_target_pairs={{0,1},{3,2},{1,0},{2,3},{4,5},{7,6},{5,4},{6,7},{8,9},{11,10},{9,8... | collective-permute-start | bytes 4718600 | tf_op jit(solution)/shard_map/ppermute | solution.py:55
  832.8 318.7 %reduce-scatter.14.cloned.1.call-start = ((), (), s32[]{:S(2)}) async-start(), calls=%async_computation.16 | async-start | bytes 14155776 | tf_op jit(solution)/shard_map/reduce_scatter | solution.py:658
  847.8 63.3 %collective-permute-start.20 = (bf16[512,3072]{1,0:T(8,128)(2,1)}, bf16[512,3072]{1,0:T(8,128)(2,1)}, u32[]{:S(2)}, u32[]{:S(2)}) collective-permute-start(bf16[512,3072]{1,0:T(8,128)(2,1)} %get-tuple-element.264), channel_id=1, source_target_pairs={{0,1},{1,2},{2,3},{4,5},{5,6},{6,7},{8,9},{9,10},{10,11},{12,13},{... | collective-permute-start | bytes 9437192 | tf_op jit(solution)/shard_map/ppermute | solution.py:55
  852.4 64.5 %collective-permute-start.21 = (bf16[512,3072]{1,0:T(8,128)(2,1)}, bf16[512,3072]{1,0:T(8,128)(2,1)}, u32[]{:S(2)}, u32[]{:S(2)}) collective-permute-start(bf16[512,3072]{1,0:T(8,128)(2,1)} %get-tuple-element.264), channel_id=1, source_target_pairs={{1,0},{2,1},{3,2},{5,4},{6,5},{7,6},{9,8},{10,9},{11,10},{13,12},{... | collective-permute-start | bytes 9437192 | tf_op jit(solution)/shard_map/ppermute | solution.py:55
  916.8 313.3 %reduce-scatter.16.cloned.1.call-start = ((), (), s32[]{:S(2)}) async-start(), calls=%async_computation.17 | async-start | bytes 14155776 | tf_op jit(solution)/shard_map/reduce_scatter | solution.py:658
  916.9 64.3 %collective-permute-start.22 = (bf16[512,3072]{1,0:T(8,128)(2,1)}, bf16[512,3072]{1,0:T(8,128)(2,1)}, u32[]{:S(2)}, u32[]{:S(2)}) collective-permute-start(bf16[512,3072]{1,0:T(8,128)(2,1)} %collective-permute-done.20), channel_id=1, source_target_pairs={{1,2},{2,3},{5,6},{6,7},{9,10},{10,11},{13,14},{14,15},{17,18},{18... | collective-permute-start | bytes 9437192 | tf_op jit(solution)/shard_map/ppermute | solution.py:55
  921.7 66.7 %collective-permute-start.23 = (bf16[512,3072]{1,0:T(8,128)(2,1)}, bf16[512,3072]{1,0:T(8,128)(2,1)}, u32[]{:S(2)}, u32[]{:S(2)}) collective-permute-start(bf16[512,3072]{1,0:T(8,128)(2,1)} %collective-permute-done.21), channel_id=1, source_target_pairs={{1,0},{2,1},{5,4},{6,5},{9,8},{10,9},{13,12},{14,13},{17,16},{18,1... | collective-permute-start | bytes 9437192 | tf_op jit(solution)/shard_map/ppermute | solution.py:55
  923.0 66.6 %collective-permute-start.24 = (bf16[512,3072]{1,0:T(8,128)(2,1)}, bf16[512,3072]{1,0:T(8,128)(2,1)}, u32[]{:S(2)}, u32[]{:S(2)}) collective-permute-start(bf16[512,3072]{1,0:T(8,128)(2,1)} %shard_map.240), channel_id=1, source_target_pairs={{0,1},{3,2},{4,5},{7,6},{8,9},{11,10},{12,13},{15,14},{16,17},{19,... | collective-permute-start | bytes 9437192 | tf_op jit(solution)/shard_map/ppermute | solution.py:55
  935.7 22.9 %copy-start.12 = (bf16[1024,2048]{1,0:T(8,128)(2,1)S(1)}, bf16[1024,2048]{1,0:T(8,128)(2,1)}, u32[]{:S(2)}) copy-start(bf16[1024,2048]{1,0:T(8,128)(2,1)} %get-tuple-element.275.refs_2_) | copy-start | bytes 12582916
  989.6 282.4 %reduce-scatter.18.cloned.1.call-start = ((), (), s32[]{:S(2)}) async-start(), calls=%async_computation.18 | async-start | bytes 14155776 | tf_op jit(solution)/shard_map/reduce_scatter | solution.py:658
  989.7 42.5 %collective-permute-start.25 = (bf16[512,3072]{1,0:T(8,128)(2,1)}, bf16[512,3072]{1,0:T(8,128)(2,1)}, u32[]{:S(2)}, u32[]{:S(2)}) collective-permute-start(bf16[512,3072]{1,0:T(8,128)(2,1)} %collective-permute-done.22), channel_id=1, source_target_pairs={{2,3},{6,7},{10,11},{14,15},{18,19},{22,23},{26,27},{30,31}} | collective-permute-start | bytes 9437192 | tf_op jit(solution)/shard_map/ppermute | solution.py:55
  995.1 18.6 %copy-start.11 = (bf16[1024,2048]{1,0:T(8,128)(2,1)S(1)}, bf16[1024,2048]{1,0:T(8,128)(2,1)}, u32[]{:S(2)}) copy-start(bf16[1024,2048]{1,0:T(8,128)(2,1)} %get-tuple-element.284.refs_0_) | copy-start | bytes 12582916
  995.1 64.6 %collective-permute-start.26 = (bf16[512,3072]{1,0:T(8,128)(2,1)}, bf16[512,3072]{1,0:T(8,128)(2,1)}, u32[]{:S(2)}, u32[]{:S(2)}) collective-permute-start(bf16[512,3072]{1,0:T(8,128)(2,1)} %collective-permute-done.23), channel_id=1, source_target_pairs={{1,0},{5,4},{9,8},{13,12},{17,16},{21,20},{25,24},{29,28}} | collective-permute-start | bytes 9437192 | tf_op jit(solution)/shard_map/ppermute | solution.py:55
  996.7 68.5 %collective-permute-start.27 = (bf16[384,4096]{1,0:T(8,128)(2,1)}, bf16[384,4096]{1,0:T(8,128)(2,1)}, u32[]{:S(2)}, u32[]{:S(2)}) collective-permute-start(bf16[384,4096]{1,0:T(8,128)(2,1)} %pad_maximum_fusion.4), channel_id=1, source_target_pairs={{0,2},{3,1},{4,6},{7,5},{8,10},{11,9},{12,14},{15,13},{16,18},{19,... | collective-permute-start | bytes 9437192 | tf_op jit(solution)/shard_map/ppermute | solution.py:55
  1065.2 302.8 %reduce-scatter.20.cloned.1.call-start = ((), (), s32[]{:S(2)}) async-start(), calls=%async_computation.19 | async-start | bytes 14155776 | tf_op jit(solution)/shard_map/reduce_scatter | solution.py:658
  1075.7 75.8 %collective-permute-start.28 = (bf16[384,2048]{1,0:T(8,128)(2,1)}, bf16[384,2048]{1,0:T(8,128)(2,1)}, u32[]{:S(2)}, u32[]{:S(2)}) collective-permute-start(bf16[384,2048]{1,0:T(8,128)(2,1)} %reduce-scatter.8.cloned.1.call-done), channel_id=1, source_target_pairs={{0,2},{3,1},{1,3},{2,0},{4,6},{7,5},{5,7},{6,4},{8,10},{11,9},{9,1... | collective-permute-start | bytes 4718600 | tf_op jit(solution)/shard_map/ppermute | solution.py:55
  1161.3 59.6 %collective-permute-start.29 = (bf16[512,3072]{1,0:T(8,128)(2,1)}, bf16[512,3072]{1,0:T(8,128)(2,1)}, u32[]{:S(2)}, u32[]{:S(2)}) collective-permute-start(bf16[512,3072]{1,0:T(8,128)(2,1)} %convolution_convert_fusion.13), channel_id=1, source_target_pairs={{0,1},{4,5},{8,9},{12,13},{16,17},{20,21},{24,25},{28,29}} | collective-permute-start | bytes 9437192 | tf_op jit(solution)/shard_map/ppermute | solution.py:55
  1164.3 56.6 %collective-permute-start.30 = (bf16[512,3072]{1,0:T(8,128)(2,1)}, bf16[512,3072]{1,0:T(8,128)(2,1)}, u32[]{:S(2)}, u32[]{:S(2)}) collective-permute-start(bf16[512,3072]{1,0:T(8,128)(2,1)} %convolution_convert_fusion.13), channel_id=1, source_target_pairs={{3,2},{7,6},{11,10},{15,14},{19,18},{23,22},{27,26},{31,30}} | collective-permute-start | bytes 9437192 | tf_op jit(solution)/shard_map/ppermute | solution.py:55
  1166.7 63.4 %collective-permute-start.31 = (bf16[384,4096]{1,0:T(8,128)(2,1)}, bf16[384,4096]{1,0:T(8,128)(2,1)}, u32[]{:S(2)}, u32[]{:S(2)}) collective-permute-start(bf16[384,4096]{1,0:T(8,128)(2,1)} %pad_maximum_fusion.4), channel_id=1, source_target_pairs={{1,3},{2,0},{5,7},{6,4},{9,11},{10,8},{13,15},{14,12},{17,19},{18,... | collective-permute-start | bytes 9437192 | tf_op jit(solution)/shard_map/ppermute | solution.py:55
  1238.3 59.0 %collective-permute-start.32 = (bf16[512,3072]{1,0:T(8,128)(2,1)}, bf16[512,3072]{1,0:T(8,128)(2,1)}, u32[]{:S(2)}, u32[]{:S(2)}) collective-permute-start(bf16[512,3072]{1,0:T(8,128)(2,1)} %add_convert_fusion.2), channel_id=1, source_target_pairs={{0,1},{1,2},{4,5},{5,6},{8,9},{9,10},{12,13},{13,14},{16,17},{17,1... | collective-permute-start | bytes 9437192 | tf_op jit(solution)/shard_map/ppermute | solution.py:55
  1241.4 55.9 %collective-permute-start.33 = (bf16[512,3072]{1,0:T(8,128)(2,1)}, bf16[512,3072]{1,0:T(8,128)(2,1)}, u32[]{:S(2)}, u32[]{:S(2)}) collective-permute-start(bf16[512,3072]{1,0:T(8,128)(2,1)} %add_convert_fusion.2), channel_id=1, source_target_pairs={{3,2},{2,1},{7,6},{6,5},{11,10},{10,9},{15,14},{14,13},{19,18},{18... | collective-permute-start | bytes 9437192 | tf_op jit(solution)/shard_map/ppermute | solution.py:55
  1243.8 61.6 %collective-permute-start.34 = (bf16[512,3072]{1,0:T(8,128)(2,1)}, bf16[512,3072]{1,0:T(8,128)(2,1)}, u32[]{:S(2)}, u32[]{:S(2)}) collective-permute-start(bf16[512,3072]{1,0:T(8,128)(2,1)} %shard_map.240), channel_id=1, source_target_pairs={{1,0},{2,3},{5,4},{6,7},{9,8},{10,11},{13,12},{14,15},{17,16},{18,... | collective-permute-start | bytes 9437192 | tf_op jit(solution)/shard_map/ppermute | solution.py:55
  1313.5 63.8 %collective-permute-start.35 = (bf16[512,3072]{1,0:T(8,128)(2,1)}, bf16[512,3072]{1,0:T(8,128)(2,1)}, u32[]{:S(2)}, u32[]{:S(2)}) collective-permute-start(bf16[512,3072]{1,0:T(8,128)(2,1)} %get-tuple-element.313), channel_id=1, source_target_pairs={{0,1},{1,2},{2,3},{4,5},{5,6},{6,7},{8,9},{9,10},{10,11},{12,13},{... | collective-permute-start | bytes 9437192 | tf_op jit(solution)/shard_map/ppermute | solution.py:55
  1318.3 60.7 %collective-permute-start.36 = (bf16[512,3072]{1,0:T(8,128)(2,1)}, bf16[512,3072]{1,0:T(8,128)(2,1)}, u32[]{:S(2)}, u32[]{:S(2)}) collective-permute-start(bf16[512,3072]{1,0:T(8,128)(2,1)} %get-tuple-element.314), channel_id=1, source_target_pairs={{3,2},{2,1},{1,0},{7,6},{6,5},{5,4},{11,10},{10,9},{9,8},{15,14},{... | collective-permute-start | bytes 9437192 | tf_op jit(solution)/shard_map/ppermute | solution.py:55
  1373.6 17.0 %copy-start.47 = (bf16[1,384]{1,0:T(2,128)(2,1)S(1)}, bf16[1,384]{1,0:T(2,128)(2,1)}, u32[]{:S(2)}) copy-start(bf16[1,384]{1,0:T(2,128)(2,1)} %copy-done.46) | copy-start | bytes 2308
  1373.6 17.0 %copy-start.49 = (bf16[1,384]{1,0:T(2,128)(2,1)S(1)}, bf16[1,384]{1,0:T(2,128)(2,1)}, u32[]{:S(2)}) copy-start(bf16[1,384]{1,0:T(2,128)(2,1)} %copy-done.48) | copy-start | bytes 2308
  1373.6 17.7 %copy-start.8 = (f32[1,3072]{1,0:T(1,128)S(1)}, f32[1,3072]{1,0:T(1,128)}, u32[]{:S(2)}) copy-start(f32[1,3072]{1,0:T(1,128)} %copy-done.7) | copy-start | bytes 36868
  (43 other events, 259.4 us)
Sparse Core Ops, SparseCore 0:
  30.2 52.4 all-gather.6
  118.2 37.3 all-gather.8
  157.5 72.1 all-gather.10
  231.4 125.3 all-gather.12
  358.5 72.1 all-gather.14
  432.4 125.3 all-gather.16
  702.3 90.2 reduce-scatter.9
  796.1 92.3 reduce-scatter.11
  892.1 92.3 reduce-scatter.7
  987.8 92.3 reduce-scatter.13
  1083.8 92.4 reduce-scatter.15
  1179.6 92.3 reduce-scatter.17
  1275.5 92.3 reduce-scatter.19
